TPU v7x, 32 devices: a whole 2x2x4 slice. The times are simulated.
32 devices in a mesh: shot: 2 (over y), gx: 4 (over z), section: 2 (over x), gy: 2 (over core).
Axes of the slice: x: 2, y: 2, z: 4, core: 2. Of those that a mesh axis runs over, the one named last changes fastest.
Arguments:
- wave_now: float32 [256, 32, 512], P(('shot', 'gx'), 'section', 'gy'), parts along dimension 0, may hold values from -6 to 6
- wave_before: float32 [256, 32, 512], P(('shot', 'gx'), 'section', 'gy'), parts along dimension 0, may hold values from -6 to 6
- courant: float32 [256, 32, 512], P(('shot', 'gx'), 'section', 'gy'), parts along dimension 0, may hold values from 0.03 to 0.12
- anisotropy: float32 [256, 32, 512], P(('shot', 'gx'), 'section', 'gy'), parts along dimension 0, may hold values from 0 to 0.3
- tilt: float32 [256, 32, 512], P(('shot', 'gx'), 'section', 'gy'), parts along dimension 0, may hold values from -3.140625 to 3.140625
- reflectivity: bfloat16 [17, 256, 32, 512], P(None, ('shot', 'gx'), 'section', 'gy'), parts along dimension 1, may hold values from -2.5 to 2.5
- offsets: int32 [17], replicated, may hold values from -16 to 16, as said below
Outputs:
- background: float32 [256, 32, 512], P(('shot', 'gx'), 'section', 'gy'), parts along dimension 0
- scattered: float32 [256, 32, 512], P(('shot', 'gx'), 'section', 'gy'), parts along dimension 0
There are 2 independent parts, one for each index of `shot`. A program takes and returns all parts, laid end to end along the dimension named above; an argument that names none is the same for every part. Nothing has to cross between parts.
Inputs may be any that keep to these rules, and one draw needn't show every extreme that they name: 17 distinct offsets, among them 0, -16 and 16.
All inputs are finite; a program needn't handle non-finite values.
Results may differ from a plain program's by a relative error of at most 0.0003.
Values sent between devices are 32-bit elements; how exact they have to be, the bound alone decides.
No kernel may reach another device: no remote copies, remote signals or barrier semaphores. Data moves between devices by JAX's collectives and lax.ppermute only.
A program may use at most 64 MiB of HBM per device.

v0:
```python
import jax
import jax.numpy as jnp
from jax import lax
from jax.sharding import PartitionSpec as P

NOFF = 17
MARGIN = 16
ROUNDS = 3
STEPS = 2


def padded_2(cells, sides, width):
    for axis, dim in sides:
        count = lax.axis_size(axis)
        ends = count - 1
        head = lax.slice_in_dim(cells, 0, width, axis=dim)
        tail = lax.slice_in_dim(cells, cells.shape[dim] - width, cells.shape[dim], axis=dim)
        cells = jnp.concatenate(
            [
                lax.ppermute(tail, axis, [(i, (i + 1) % count) for i in range(ends)]),
                cells,
                lax.ppermute(head, axis, [((i + 1) % count, i) for i in range(ends)]),
            ],
            axis=dim,
        )
    return cells


def coefficients(courant, anisotropy, tilt):
    sine_tilt = jnp.sin(tilt)
    cosine_tilt = jnp.cos(tilt)
    stretch = 1.0 + 2.0 * anisotropy
    coef_xx = courant * (stretch * cosine_tilt * cosine_tilt + sine_tilt * sine_tilt)
    coef_zz = courant * (stretch * sine_tilt * sine_tilt + cosine_tilt * cosine_tilt)
    coef_yy = courant * stretch
    coef_xz = courant * 4.0 * anisotropy * sine_tilt * cosine_tilt
    return (coef_xx, coef_zz, coef_yy, coef_xz)


def apply_operator(padded, coef_set):
    centre = padded[1:-1, 1:-1, 1:-1]
    diff_xx = padded[2:, 1:-1, 1:-1] + padded[:-2, 1:-1, 1:-1] - 2.0 * centre
    diff_zz = padded[1:-1, 2:, 1:-1] + padded[1:-1, :-2, 1:-1] - 2.0 * centre
    diff_yy = padded[1:-1, 1:-1, 2:] + padded[1:-1, 1:-1, :-2] - 2.0 * centre
    diff_xz = 0.25 * (
        padded[2:, 2:, 1:-1]
        - padded[2:, :-2, 1:-1]
        - padded[:-2, 2:, 1:-1]
        + padded[:-2, :-2, 1:-1]
    )
    return (
        coef_set[0] * diff_xx
        + coef_set[1] * diff_zz
        + coef_set[2] * diff_yy
        + coef_set[3] * diff_xz
    )


def step_single(current, prior, coef_set):
    padded = padded_2(current, (("gx", 0), ("section", 1), ("gy", 2)), 1)
    return 2.0 * current - prior + apply_operator(padded, coef_set)


def shards(wave_now, wave_before, courant, anisotropy, tilt, reflectivity, offsets):
    cells_x = wave_now.shape[0]
    core_coefs = coefficients(courant, anisotropy, tilt)
    current = wave_now
    prior = wave_before
    wave_scat = jnp.zeros_like(wave_now)
    scat_prior = jnp.zeros_like(wave_now)
    for round_index in range(ROUNDS):
        run_current = current
        run_prior = prior
        for run_step_index in range(STEPS):
            run_advanced = step_single(run_current, run_prior, core_coefs)
            run_prior = run_current
            run_current = run_advanced
        current = run_current
        prior = run_prior
        extended = padded_2(current, (("gx", 0),), MARGIN)

        def accumulate(offset_index, running):
            start = MARGIN + offsets[offset_index]
            moved = lax.dynamic_slice_in_dim(extended, start, cells_x, 0)
            return running + reflectivity[offset_index].astype(jnp.float32) * moved

        source = lax.fori_loop(0, NOFF, accumulate, jnp.zeros_like(current))
        source, forcing = (source, courant * source)
        run_wave_scat = wave_scat
        run_scat_prior = scat_prior
        for step_index in range(STEPS):
            advanced = step_single(run_wave_scat, run_scat_prior, core_coefs) + forcing
            run_scat_prior = run_wave_scat
            run_wave_scat = advanced
        wave_scat = run_wave_scat
        scat_prior = run_scat_prior
    return (current, wave_scat)


def solution(mesh):
    return jax.shard_map(
        shards,
        mesh=mesh,
        in_specs=(
            P(("shot", "gx"), "section", "gy"),
            P(("shot", "gx"), "section", "gy"),
            P(("shot", "gx"), "section", "gy"),
            P(("shot", "gx"), "section", "gy"),
            P(("shot", "gx"), "section", "gy"),
            P(None, ("shot", "gx"), "section", "gy"),
            P(),
        ),
        out_specs=(P(("shot", "gx"), "section", "gy"), P(("shot", "gx"), "section", "gy")),
        check_vma=False,
    )
```

profile of v0, /device:TPU:0, one launch (start us, length us, event | category | flops | bytes accessed | tf_op | source)
XLA Modules:
  0.0 483.3 jit_solution(8201738399693499562)
XLA Ops:
  1.6 4.9 %collective-permute-start.1 = (f32[1,16,256]{2,1,0:T(8,128)S(1)}, f32[1,16,256]{2,1,0:T(8,128)S(1)}, u32[]{:S(2)}, u32[]{:S(2)}) collective-permute-start(f32[1,16,256]{2,1,0:T(8,128)S(1)} %get-tuple-element.595), channel_id=1, source_target_pairs={{0,4},{4,8},{8,12},{1,5},{5,9},{9,13},{2,6},{6,10},{10,14},{3,7},{... | collective-permute-start | bytes 49160 | tf_op jit(solution)/shard_map/ppermute | solution.py:20
  9.0 3.1 collective-permute-done
  13.5 4.5 collective-permute-start.3
  21.3 3.1 collective-permute-start.5
  26.3 2.5 fusion.20
  30.1 4.5 collective-permute-start.7
  37.4 4.5 collective-permute-start.9
  43.3 4.8 collective-permute-start.37
  49.8 3.1 collective-permute-start.11
  56.3 4.6 collective-permute-start.13
  62.3 4.5 collective-permute-start.39
  68.3 4.5 collective-permute-start.15
  76.0 3.1 collective-permute-start.17
  82.6 4.6 collective-permute-start.19
  89.5 4.6 collective-permute-start.41
  95.5 4.5 collective-permute-start.21
  103.2 3.1 collective-permute-start.23
  109.8 4.6 collective-permute-start.25
  114.4 3.9 collective-permute-start.42
  119.7 4.5 collective-permute-start.27
  126.4 5.3 %collective-permute-start.56 = (f32[16,16,256]{2,1,0:T(8,128)}, f32[16,16,256]{2,1,0:T(8,128)}, u32[]{:S(2)}, u32[]{:S(2)}) collective-permute-start(f32[16,16,256]{2,1,0:T(8,128)} %get-tuple-element.574), channel_id=1, source_target_pairs={{0,4},{4,8},{8,12},{1,5},{5,9},{9,13},{2,6},{6,10},{10,14},{3,7},{... | collective-permute-start | bytes 786440 | tf_op jit(solution)/shard_map/ppermute | solution.py:20
  137.8 70.0 %while.48 = (s32[]{:T(128)}, f32[32,16,256]{2,1,0:T(8,128)}, bf16[17,32,16,256]{3,2,1,0:T(8,128)(2,1)}, s32[17]{0:T(128)S(1)}, f32[64,16,256]{2,1,0:T(8,128)}, /...) while((s32[]{:T(128)}, f32[32,16,256]{2,1,0:T(8,128)}, bf16[17,32,16,256]{3,2,1,0:T(8,128)(2,1)}, ...), condition=%wide.region_1.0_spmd.clone, body=%wide.region_0.0_spmd.clone.sunk | while | flops 524295 | bytes 1835177 | solution.py:87
  207.9 4.1 collective-permute-start.29
  212.0 4.1 fusion.8
  217.4 5.2 %collective-permute-start.45 = (f32[1,16,256]{2,1,0:T(8,128)S(1)}, f32[1,16,256]{2,1,0:T(8,128)S(1)}, u32[]{:S(2)}, u32[]{:S(2)}) collective-permute-start(f32[1,16,256]{2,1,0:T(8,128)S(1)} %get-tuple-element.578), channel_id=1, source_target_pairs={{0,4},{4,8},{8,12},{1,5},{5,9},{9,13},{2,6},{6,10},{10,14},{3,7},{... | collective-permute-start | bytes 49160 | tf_op jit(solution)/shard_map/ppermute | solution.py:20
  225.8 4.5 collective-permute-start.47
  233.6 3.1 collective-permute-start.49
  236.8 4.3 collective-permute-start.31
  243.2 4.6 collective-permute-start.51
  249.2 4.5 collective-permute-start.33
  255.1 4.7 collective-permute-start.53
  263.9 4.6 collective-permute-start.55
  272.0 55.4 %while.49 = (s32[]{:T(128)}, f32[32,16,256]{2,1,0:T(8,128)S(1)}, bf16[17,32,16,256]{3,2,1,0:T(8,128)(2,1)}, s32[17]{0:T(128)S(1)}, f32[64,16,256]{2,1,0:T(8,128)...) while((s32[]{:T(128)}, f32[32,16,256]{2,1,0:T(8,128)S(1)}, ...), condition=%wide.region_3.0_spmd.clone, body=%wide.region_2.0_spmd.clone.sunk | while | flops 524295 | bytes 1835177 | solution.py:87
  328.2 5.0 %fusion.75 = (f32[32,16,256]{2,1,0:T(8,128)S(1)}, f32[32,16,256]{2,1,0:T(8,128)S(1)}) fusion(f32[32,16,256]{2,1,0:T(8,128)S(1)} %get-tuple-element.495, f32[34,17,256]{2,1,0:T(8,128)} %get-tuple-element.533, f32[34,17,256]{2,1,0:T(8,128)} %get-tuple-element.532, f32[32,16,256]{2,1,0:T(8,128)S(1)} %get-tuple-element.493, ...), kind=kLoop, calls=%fused_computation.182 | loop fusion | flops 4456448 | bytes 8495904 | tf_op jit(solution)/shard_map/add | solution.py:92
  334.5 4.6 collective-permute-start.59
  340.7 3.1 collective-permute-start.35
  345.2 4.5 collective-permute-start.61
  352.9 3.1 collective-permute-start.63
  359.6 4.6 collective-permute-start.65
  366.9 4.5 collective-permute-start.67
  371.5 4.2 collective-permute-start.70
  379.5 4.6 collective-permute-start.69
  386.5 69.7 %while.50 = (s32[]{:T(128)}, f32[32,16,256]{2,1,0:T(8,128)}, bf16[17,32,16,256]{3,2,1,0:T(8,128)(2,1)}, s32[17]{0:T(128)S(1)}, f32[64,16,256]{2,1,0:T(8,128)}, /...) while((s32[]{:T(128)}, f32[32,16,256]{2,1,0:T(8,128)}, bf16[17,32,16,256]{3,2,1,0:T(8,128)(2,1)}, ...), condition=%wide.region_5.0_spmd.clone, body=%wide.region_4.0_spmd.clone.sunk | while | flops 524295 | bytes 1835177 | solution.py:87
  400.6 2.2 fusion.212
  456.2 4.0 fusion.47
  461.5 5.2 %collective-permute-start.73 = (f32[1,16,256]{2,1,0:T(8,128)S(1)}, f32[1,16,256]{2,1,0:T(8,128)S(1)}, u32[]{:S(2)}, u32[]{:S(2)}) collective-permute-start(f32[1,16,256]{2,1,0:T(8,128)S(1)} %get-tuple-element.566), channel_id=1, source_target_pairs={{0,4},{4,8},{8,12},{1,5},{5,9},{9,13},{2,6},{6,10},{10,14},{3,7},{... | collective-permute-start | bytes 49160 | tf_op jit(solution)/shard_map/ppermute | solution.py:20
  469.4 4.5 collective-permute-start.75
  477.2 3.1 collective-permute-start.77
  (338 shorter events, 227.9 us)
Async XLA Ops:
  36.1 12.0 %collective-permute-start.8 = (f32[34,1,256]{2,1,0:T(1,128)S(1)}, f32[34,1,256]{2,1,0:T(1,128)S(1)}, u32[]{:S(2)}, u32[]{:S(2)}) collective-permute-start(f32[34,1,256]{2,1,0:T(1,128)S(1)} %get-tuple-element.562), channel_id=1, source_target_pairs={{2,0},{3,1},{6,4},{7,5},{10,8},{11,9},{14,12},{15,13},{18,16},{19,... | collective-permute-start | bytes 104456 | tf_op jit(solution)/shard_map/ppermute | solution.py:22
  37.4 10.7 %collective-permute-start.9 = (f32[34,1,256]{2,1,0:T(1,128)S(1)}, f32[34,1,256]{2,1,0:T(1,128)S(1)}, u32[]{:S(2)}, u32[]{:S(2)}) collective-permute-start(f32[34,1,256]{2,1,0:T(1,128)S(1)} %get-tuple-element.563), channel_id=1, source_target_pairs={{0,2},{1,3},{4,6},{5,7},{8,10},{9,11},{12,14},{13,15},{16,18},{17,... | collective-permute-start | bytes 104456 | tf_op jit(solution)/shard_map/ppermute | solution.py:20
  42.0 18.9 %collective-permute-start.36 = (f32[1,16,256]{2,1,0:T(8,128)S(1)}, f32[1,16,256]{2,1,0:T(8,128)S(1)}, u32[]{:S(2)}, u32[]{:S(2)}) collective-permute-start(f32[1,16,256]{2,1,0:T(8,128)S(1)} %broadcast.18), channel_id=1, source_target_pairs={{4,0},{8,4},{12,8},{5,1},{9,5},{13,9},{6,2},{10,6},{14,10},{7,3},{... | collective-permute-start | bytes 49160 | tf_op jit(solution)/shard_map/ppermute | solution.py:22
  43.3 17.6 %collective-permute-start.37 = (f32[1,16,256]{2,1,0:T(8,128)S(1)}, f32[1,16,256]{2,1,0:T(8,128)S(1)}, u32[]{:S(2)}, u32[]{:S(2)}) collective-permute-start(f32[1,16,256]{2,1,0:T(8,128)S(1)} %broadcast.18), channel_id=1, source_target_pairs={{0,4},{4,8},{8,12},{1,5},{5,9},{9,13},{2,6},{6,10},{10,14},{3,7},{... | collective-permute-start | bytes 49160 | tf_op jit(solution)/shard_map/ppermute | solution.py:20
  55.0 11.9 %collective-permute-start.12 = (f32[1,16,256]{2,1,0:T(8,128)S(1)}, f32[1,16,256]{2,1,0:T(8,128)S(1)}, u32[]{:S(2)}, u32[]{:S(2)}) collective-permute-start(f32[1,16,256]{2,1,0:T(8,128)S(1)} %get-tuple-element.589), channel_id=1, source_target_pairs={{4,0},{8,4},{12,8},{5,1},{9,5},{13,9},{6,2},{10,6},{14,10},{7,3},{... | collective-permute-start | bytes 49160 | tf_op jit(solution)/shard_map/ppermute | solution.py:22
  56.3 10.6 %collective-permute-start.13 = (f32[1,16,256]{2,1,0:T(8,128)S(1)}, f32[1,16,256]{2,1,0:T(8,128)S(1)}, u32[]{:S(2)}, u32[]{:S(2)}) collective-permute-start(f32[1,16,256]{2,1,0:T(8,128)S(1)} %get-tuple-element.588), channel_id=1, source_target_pairs={{0,4},{4,8},{8,12},{1,5},{5,9},{9,13},{2,6},{6,10},{10,14},{3,7},{... | collective-permute-start | bytes 49160 | tf_op jit(solution)/shard_map/ppermute | solution.py:20
  61.0 11.8 %collective-permute-start.38 = (f32[34,1,256]{2,1,0:T(1,128)S(1)}, f32[34,1,256]{2,1,0:T(1,128)S(1)}, u32[]{:S(2)}, u32[]{:S(2)}) collective-permute-start(f32[34,1,256]{2,1,0:T(1,128)S(1)} %get-tuple-element.542), channel_id=1, source_target_pairs={{2,0},{3,1},{6,4},{7,5},{10,8},{11,9},{14,12},{15,13},{18,16},{19,... | collective-permute-start | bytes 104456 | tf_op jit(solution)/shard_map/ppermute | solution.py:22
  62.3 10.5 %collective-permute-start.39 = (f32[34,1,256]{2,1,0:T(1,128)S(1)}, f32[34,1,256]{2,1,0:T(1,128)S(1)}, u32[]{:S(2)}, u32[]{:S(2)}) collective-permute-start(f32[34,1,256]{2,1,0:T(1,128)S(1)} %get-tuple-element.543), channel_id=1, source_target_pairs={{0,2},{1,3},{4,6},{5,7},{8,10},{9,11},{12,14},{13,15},{16,18},{17,... | collective-permute-start | bytes 104456 | tf_op jit(solution)/shard_map/ppermute | solution.py:20
  81.3 12.9 %collective-permute-start.18 = (f32[1,16,256]{2,1,0:T(8,128)S(1)}, f32[1,16,256]{2,1,0:T(8,128)S(1)}, u32[]{:S(2)}, u32[]{:S(2)}) collective-permute-start(f32[1,16,256]{2,1,0:T(8,128)S(1)} %get-tuple-element.587), channel_id=1, source_target_pairs={{4,0},{8,4},{12,8},{5,1},{9,5},{13,9},{6,2},{10,6},{14,10},{7,3},{... | collective-permute-start | bytes 49160 | tf_op jit(solution)/shard_map/ppermute | solution.py:22
  82.6 11.6 %collective-permute-start.19 = (f32[1,16,256]{2,1,0:T(8,128)S(1)}, f32[1,16,256]{2,1,0:T(8,128)S(1)}, u32[]{:S(2)}, u32[]{:S(2)}) collective-permute-start(f32[1,16,256]{2,1,0:T(8,128)S(1)} %get-tuple-element.586), channel_id=1, source_target_pairs={{0,4},{4,8},{8,12},{1,5},{5,9},{9,13},{2,6},{6,10},{10,14},{3,7},{... | collective-permute-start | bytes 49160 | tf_op jit(solution)/shard_map/ppermute | solution.py:20
  88.2 119.6 %collective-permute-start.40 = (f32[34,18,1]{2,1,0:T(8,128)}, f32[34,18,1]{2,1,0:T(8,128)}, u32[]{:S(2)}, u32[]{:S(2)}) collective-permute-start(f32[34,18,1]{2,1,0:T(8,128)} %get-tuple-element.506), channel_id=1, source_target_pairs={{1,0},{3,2},{5,4},{7,6},{9,8},{11,10},{13,12},{15,14},{17,16},{19,... | collective-permute-start | bytes 7352 | tf_op jit(solution)/shard_map/ppermute | solution.py:22
  89.5 122.5 %collective-permute-start.41 = (f32[34,18,1]{2,1,0:T(8,128)}, f32[34,18,1]{2,1,0:T(8,128)}, u32[]{:S(2)}, u32[]{:S(2)}) collective-permute-start(f32[34,18,1]{2,1,0:T(8,128)} %get-tuple-element.507), channel_id=1, source_target_pairs={{0,1},{2,3},{4,5},{6,7},{8,9},{10,11},{12,13},{14,15},{16,17},{18,... | collective-permute-start | bytes 7352 | tf_op jit(solution)/shard_map/ppermute | solution.py:20
  94.2 7.2 %collective-permute-start.20 = (f32[34,1,256]{2,1,0:T(1,128)S(1)}, f32[34,1,256]{2,1,0:T(1,128)S(1)}, u32[]{:S(2)}, u32[]{:S(2)}) collective-permute-start(f32[34,1,256]{2,1,0:T(1,128)S(1)} %get-tuple-element.554), channel_id=1, source_target_pairs={{2,0},{3,1},{6,4},{7,5},{10,8},{11,9},{14,12},{15,13},{18,16},{19,... | collective-permute-start | bytes 104456 | tf_op jit(solution)/shard_map/ppermute | solution.py:22
  108.5 9.9 %collective-permute-start.24 = (f32[1,16,256]{2,1,0:T(8,128)S(1)}, f32[1,16,256]{2,1,0:T(8,128)S(1)}, u32[]{:S(2)}, u32[]{:S(2)}) collective-permute-start(f32[1,16,256]{2,1,0:T(8,128)S(1)} %get-tuple-element.585), channel_id=1, source_target_pairs={{4,0},{8,4},{12,8},{5,1},{9,5},{13,9},{6,2},{10,6},{14,10},{7,3},{... | collective-permute-start | bytes 49160 | tf_op jit(solution)/shard_map/ppermute | solution.py:22
  109.8 8.6 %collective-permute-start.25 = (f32[1,16,256]{2,1,0:T(8,128)S(1)}, f32[1,16,256]{2,1,0:T(8,128)S(1)}, u32[]{:S(2)}, u32[]{:S(2)}) collective-permute-start(f32[1,16,256]{2,1,0:T(8,128)S(1)} %get-tuple-element.584), channel_id=1, source_target_pairs={{0,4},{4,8},{8,12},{1,5},{5,9},{9,13},{2,6},{6,10},{10,14},{3,7},{... | collective-permute-start | bytes 49160 | tf_op jit(solution)/shard_map/ppermute | solution.py:20
  114.4 19.8 %collective-permute-start.42 = (f32[16,16,256]{2,1,0:T(8,128)S(1)}, f32[16,16,256]{2,1,0:T(8,128)S(1)}, u32[]{:S(2)}, u32[]{:S(2)}) collective-permute-start(f32[16,16,256]{2,1,0:T(8,128)S(1)} %get-tuple-element.580), channel_id=1, source_target_pairs={{0,4},{4,8},{8,12},{1,5},{5,9},{9,13},{2,6},{6,10},{10,14},{3,7},{... | collective-permute-start | bytes 786440 | tf_op jit(solution)/shard_map/ppermute | solution.py:20
  118.4 6.7 %collective-permute-start.26 = (f32[34,1,256]{2,1,0:T(1,128)S(1)}, f32[34,1,256]{2,1,0:T(1,128)S(1)}, u32[]{:S(2)}, u32[]{:S(2)}) collective-permute-start(f32[34,1,256]{2,1,0:T(1,128)S(1)} %get-tuple-element.550), channel_id=1, source_target_pairs={{2,0},{3,1},{6,4},{7,5},{10,8},{11,9},{14,12},{15,13},{18,16},{19,... | collective-permute-start | bytes 104456 | tf_op jit(solution)/shard_map/ppermute | solution.py:22
  119.7 6.7 %collective-permute-start.27 = (f32[34,1,256]{2,1,0:T(1,128)S(1)}, f32[34,1,256]{2,1,0:T(1,128)S(1)}, u32[]{:S(2)}, u32[]{:S(2)}) collective-permute-start(f32[34,1,256]{2,1,0:T(1,128)S(1)} %get-tuple-element.551), channel_id=1, source_target_pairs={{0,2},{1,3},{4,6},{5,7},{8,10},{9,11},{12,14},{13,15},{16,18},{17,... | collective-permute-start | bytes 104456 | tf_op jit(solution)/shard_map/ppermute | solution.py:20
  125.1 10.4 %collective-permute-start.43 = (f32[16,16,256]{2,1,0:T(8,128)S(1)}, f32[16,16,256]{2,1,0:T(8,128)S(1)}, u32[]{:S(2)}, u32[]{:S(2)}) collective-permute-start(f32[16,16,256]{2,1,0:T(8,128)S(1)} %get-tuple-element.581), channel_id=1, source_target_pairs={{4,0},{8,4},{12,8},{5,1},{9,5},{13,9},{6,2},{10,6},{14,10},{7,3},{... | collective-permute-start | bytes 786440 | tf_op jit(solution)/shard_map/ppermute | solution.py:22
  126.4 143.5 %collective-permute-start.56 = (f32[16,16,256]{2,1,0:T(8,128)}, f32[16,16,256]{2,1,0:T(8,128)}, u32[]{:S(2)}, u32[]{:S(2)}) collective-permute-start(f32[16,16,256]{2,1,0:T(8,128)} %get-tuple-element.574), channel_id=1, source_target_pairs={{0,4},{4,8},{8,12},{1,5},{5,9},{9,13},{2,6},{6,10},{10,14},{3,7},{... | collective-permute-start | bytes 786440 | tf_op jit(solution)/shard_map/ppermute | solution.py:20
  134.2 135.7 %collective-permute-start.57 = (f32[16,16,256]{2,1,0:T(8,128)}, f32[16,16,256]{2,1,0:T(8,128)}, u32[]{:S(2)}, u32[]{:S(2)}) collective-permute-start(f32[16,16,256]{2,1,0:T(8,128)} %get-tuple-element.575), channel_id=1, source_target_pairs={{4,0},{8,4},{12,8},{5,1},{9,5},{13,9},{6,2},{10,6},{14,10},{7,3},{... | collective-permute-start | bytes 786440 | tf_op jit(solution)/shard_map/ppermute | solution.py:22
  135.5 82.0 %collective-permute-start.28 = (f32[34,18,1]{2,1,0:T(8,128)}, f32[34,18,1]{2,1,0:T(8,128)}, u32[]{:S(2)}, u32[]{:S(2)}) collective-permute-start(f32[34,18,1]{2,1,0:T(8,128)} %get-tuple-element.510), channel_id=1, source_target_pairs={{1,0},{3,2},{5,4},{7,6},{9,8},{11,10},{13,12},{15,14},{17,16},{19,... | collective-permute-start | bytes 7352 | tf_op jit(solution)/shard_map/ppermute | solution.py:22
  207.9 14.8 %collective-permute-start.29 = (f32[34,18,1]{2,1,0:T(8,128)}, f32[34,18,1]{2,1,0:T(8,128)S(1)}, u32[]{:S(2)}, u32[]{:S(2)}) collective-permute-start(f32[34,18,1]{2,1,0:T(8,128)} %get-tuple-element.511), channel_id=1, source_target_pairs={{0,1},{2,3},{4,5},{6,7},{8,9},{10,11},{12,13},{14,15},{16,17},{18,... | collective-permute-start | bytes 7352 | tf_op jit(solution)/shard_map/ppermute | solution.py:20
  216.1 8.3 %collective-permute-start.44 = (f32[1,16,256]{2,1,0:T(8,128)S(1)}, f32[1,16,256]{2,1,0:T(8,128)S(1)}, u32[]{:S(2)}, u32[]{:S(2)}) collective-permute-start(f32[1,16,256]{2,1,0:T(8,128)S(1)} %get-tuple-element.579), channel_id=1, source_target_pairs={{4,0},{8,4},{12,8},{5,1},{9,5},{13,9},{6,2},{10,6},{14,10},{7,3},{... | collective-permute-start | bytes 49160 | tf_op jit(solution)/shard_map/ppermute | solution.py:22
  217.4 7.0 %collective-permute-start.45 = (f32[1,16,256]{2,1,0:T(8,128)S(1)}, f32[1,16,256]{2,1,0:T(8,128)S(1)}, u32[]{:S(2)}, u32[]{:S(2)}) collective-permute-start(f32[1,16,256]{2,1,0:T(8,128)S(1)} %get-tuple-element.578), channel_id=1, source_target_pairs={{0,4},{4,8},{8,12},{1,5},{5,9},{9,13},{2,6},{6,10},{10,14},{3,7},{... | collective-permute-start | bytes 49160 | tf_op jit(solution)/shard_map/ppermute | solution.py:20
  224.5 7.2 %collective-permute-start.46 = (f32[34,1,256]{2,1,0:T(1,128)S(1)}, f32[34,1,256]{2,1,0:T(1,128)S(1)}, u32[]{:S(2)}, u32[]{:S(2)}) collective-permute-start(f32[34,1,256]{2,1,0:T(1,128)S(1)} %get-tuple-element.538), channel_id=1, source_target_pairs={{2,0},{3,1},{6,4},{7,5},{10,8},{11,9},{14,12},{15,13},{18,16},{19,... | collective-permute-start | bytes 104456 | tf_op jit(solution)/shard_map/ppermute | solution.py:22
  230.4 12.9 %collective-permute-start.30 = (f32[1,16,256]{2,1,0:T(8,128)S(1)}, f32[1,16,256]{2,1,0:T(8,128)S(1)}, u32[]{:S(2)}, u32[]{:S(2)}) collective-permute-start(f32[1,16,256]{2,1,0:T(8,128)S(1)} %get-tuple-element.583), channel_id=1, source_target_pairs={{4,0},{8,4},{12,8},{5,1},{9,5},{13,9},{6,2},{10,6},{14,10},{7,3},{... | collective-permute-start | bytes 49160 | tf_op jit(solution)/shard_map/ppermute | solution.py:22
  233.6 7.5 %collective-permute-start.49 = (f32[34,18,1]{2,1,0:T(8,128)S(1)}, f32[34,18,1]{2,1,0:T(8,128)S(1)}, u32[]{:S(2)}, u32[]{:S(2)}) collective-permute-start(f32[34,18,1]{2,1,0:T(8,128)S(1)} %get-tuple-element.505), channel_id=1, source_target_pairs={{0,1},{2,3},{4,5},{6,7},{8,9},{10,11},{12,13},{14,15},{16,17},{18,... | collective-permute-start | bytes 7352 | tf_op jit(solution)/shard_map/ppermute | solution.py:20
  236.8 11.0 %collective-permute-start.31 = (f32[1,16,256]{2,1,0:T(8,128)S(1)}, f32[1,16,256]{2,1,0:T(8,128)S(1)}, u32[]{:S(2)}, u32[]{:S(2)}) collective-permute-start(f32[1,16,256]{2,1,0:T(8,128)S(1)} %get-tuple-element.582), channel_id=1, source_target_pairs={{0,4},{4,8},{8,12},{1,5},{5,9},{9,13},{2,6},{6,10},{10,14},{3,7},{... | collective-permute-start | bytes 49160 | tf_op jit(solution)/shard_map/ppermute | solution.py:20
  241.9 7.2 %collective-permute-start.50 = (f32[1,16,256]{2,1,0:T(8,128)S(1)}, f32[1,16,256]{2,1,0:T(8,128)S(1)}, u32[]{:S(2)}, u32[]{:S(2)}) collective-permute-start(f32[1,16,256]{2,1,0:T(8,128)S(1)} %get-tuple-element.577), channel_id=1, source_target_pairs={{4,0},{8,4},{12,8},{5,1},{9,5},{13,9},{6,2},{10,6},{14,10},{7,3},{... | collective-permute-start | bytes 49160 | tf_op jit(solution)/shard_map/ppermute | solution.py:22
  243.2 10.5 %collective-permute-start.51 = (f32[1,16,256]{2,1,0:T(8,128)S(1)}, f32[1,16,256]{2,1,0:T(8,128)S(1)}, u32[]{:S(2)}, u32[]{:S(2)}) collective-permute-start(f32[1,16,256]{2,1,0:T(8,128)S(1)} %get-tuple-element.576), channel_id=1, source_target_pairs={{0,4},{4,8},{8,12},{1,5},{5,9},{9,13},{2,6},{6,10},{10,14},{3,7},{... | collective-permute-start | bytes 49160 | tf_op jit(solution)/shard_map/ppermute | solution.py:20
  247.9 7.2 %collective-permute-start.32 = (f32[34,1,256]{2,1,0:T(1,128)S(1)}, f32[34,1,256]{2,1,0:T(1,128)S(1)}, u32[]{:S(2)}, u32[]{:S(2)}) collective-permute-start(f32[34,1,256]{2,1,0:T(1,128)S(1)} %get-tuple-element.546), channel_id=1, source_target_pairs={{2,0},{3,1},{6,4},{7,5},{10,8},{11,9},{14,12},{15,13},{18,16},{19,... | collective-permute-start | bytes 104456 | tf_op jit(solution)/shard_map/ppermute | solution.py:22
  249.2 10.6 %collective-permute-start.33 = (f32[34,1,256]{2,1,0:T(1,128)S(1)}, f32[34,1,256]{2,1,0:T(1,128)S(1)}, u32[]{:S(2)}, u32[]{:S(2)}) collective-permute-start(f32[34,1,256]{2,1,0:T(1,128)S(1)} %get-tuple-element.547), channel_id=1, source_target_pairs={{0,2},{1,3},{4,6},{5,7},{8,10},{9,11},{12,14},{13,15},{16,18},{17,... | collective-permute-start | bytes 104456 | tf_op jit(solution)/shard_map/ppermute | solution.py:20
  253.8 7.1 %collective-permute-start.52 = (f32[34,1,256]{2,1,0:T(1,128)S(1)}, f32[34,1,256]{2,1,0:T(1,128)S(1)}, u32[]{:S(2)}, u32[]{:S(2)}) collective-permute-start(f32[34,1,256]{2,1,0:T(1,128)S(1)} %get-tuple-element.534), channel_id=1, source_target_pairs={{2,0},{3,1},{6,4},{7,5},{10,8},{11,9},{14,12},{15,13},{18,16},{19,... | collective-permute-start | bytes 104456 | tf_op jit(solution)/shard_map/ppermute | solution.py:22
  262.6 64.8 %collective-permute-start.54 = (f32[34,18,1]{2,1,0:T(8,128)}, f32[34,18,1]{2,1,0:T(8,128)}, u32[]{:S(2)}, u32[]{:S(2)}) collective-permute-start(f32[34,18,1]{2,1,0:T(8,128)} %get-tuple-element.502), channel_id=1, source_target_pairs={{1,0},{3,2},{5,4},{7,6},{9,8},{11,10},{13,12},{15,14},{17,16},{19,... | collective-permute-start | bytes 7352 | tf_op jit(solution)/shard_map/ppermute | solution.py:22
  263.9 63.5 %collective-permute-start.55 = (f32[34,18,1]{2,1,0:T(8,128)}, f32[34,18,1]{2,1,0:T(8,128)}, u32[]{:S(2)}, u32[]{:S(2)}) collective-permute-start(f32[34,18,1]{2,1,0:T(8,128)} %get-tuple-element.503), channel_id=1, source_target_pairs={{0,1},{2,3},{4,5},{6,7},{8,9},{10,11},{12,13},{14,15},{16,17},{18,... | collective-permute-start | bytes 7352 | tf_op jit(solution)/shard_map/ppermute | solution.py:20
  333.2 10.6 %collective-permute-start.58 = (f32[1,16,256]{2,1,0:T(8,128)S(1)}, f32[1,16,256]{2,1,0:T(8,128)S(1)}, u32[]{:S(2)}, u32[]{:S(2)}) collective-permute-start(f32[1,16,256]{2,1,0:T(8,128)S(1)} %get-tuple-element.573), channel_id=1, source_target_pairs={{4,0},{8,4},{12,8},{5,1},{9,5},{13,9},{6,2},{10,6},{14,10},{7,3},{... | collective-permute-start | bytes 49160 | tf_op jit(solution)/shard_map/ppermute | solution.py:22
  334.5 9.3 %collective-permute-start.59 = (f32[1,16,256]{2,1,0:T(8,128)S(1)}, f32[1,16,256]{2,1,0:T(8,128)S(1)}, u32[]{:S(2)}, u32[]{:S(2)}) collective-permute-start(f32[1,16,256]{2,1,0:T(8,128)S(1)} %get-tuple-element.572), channel_id=1, source_target_pairs={{0,4},{4,8},{8,12},{1,5},{5,9},{9,13},{2,6},{6,10},{10,14},{3,7},{... | collective-permute-start | bytes 49160 | tf_op jit(solution)/shard_map/ppermute | solution.py:20
  339.3 24.8 %collective-permute-start.34 = (f32[34,18,1]{2,1,0:T(8,128)S(1)}, f32[34,18,1]{2,1,0:T(8,128)S(1)}, u32[]{:S(2)}, u32[]{:S(2)}) collective-permute-start(f32[34,18,1]{2,1,0:T(8,128)S(1)} %get-tuple-element.508), channel_id=1, source_target_pairs={{1,0},{3,2},{5,4},{7,6},{9,8},{11,10},{13,12},{15,14},{17,16},{19,... | collective-permute-start | bytes 7352 | tf_op jit(solution)/shard_map/ppermute | solution.py:22
  340.7 23.4 %collective-permute-start.35 = (f32[34,18,1]{2,1,0:T(8,128)S(1)}, f32[34,18,1]{2,1,0:T(8,128)S(1)}, u32[]{:S(2)}, u32[]{:S(2)}) collective-permute-start(f32[34,18,1]{2,1,0:T(8,128)S(1)} %get-tuple-element.509), channel_id=1, source_target_pairs={{0,1},{2,3},{4,5},{6,7},{8,9},{10,11},{12,13},{14,15},{16,17},{18,... | collective-permute-start | bytes 7352 | tf_op jit(solution)/shard_map/ppermute | solution.py:20
  358.3 6.8 %collective-permute-start.64 = (f32[1,16,256]{2,1,0:T(8,128)S(1)}, f32[1,16,256]{2,1,0:T(8,128)S(1)}, u32[]{:S(2)}, u32[]{:S(2)}) collective-permute-start(f32[1,16,256]{2,1,0:T(8,128)S(1)} %get-tuple-element.571), channel_id=1, source_target_pairs={{4,0},{8,4},{12,8},{5,1},{9,5},{13,9},{6,2},{10,6},{14,10},{7,3},{... | collective-permute-start | bytes 49160 | tf_op jit(solution)/shard_map/ppermute | solution.py:22
  365.6 11.4 %collective-permute-start.66 = (f32[34,1,256]{2,1,0:T(1,128)S(1)}, f32[34,1,256]{2,1,0:T(1,128)S(1)}, u32[]{:S(2)}, u32[]{:S(2)}) collective-permute-start(f32[34,1,256]{2,1,0:T(1,128)S(1)} %get-tuple-element.526), channel_id=1, source_target_pairs={{2,0},{3,1},{6,4},{7,5},{10,8},{11,9},{14,12},{15,13},{18,16},{19,... | collective-permute-start | bytes 104456 | tf_op jit(solution)/shard_map/ppermute | solution.py:22
  366.9 10.1 %collective-permute-start.67 = (f32[34,1,256]{2,1,0:T(1,128)S(1)}, f32[34,1,256]{2,1,0:T(1,128)S(1)}, u32[]{:S(2)}, u32[]{:S(2)}) collective-permute-start(f32[34,1,256]{2,1,0:T(1,128)S(1)} %get-tuple-element.527), channel_id=1, source_target_pairs={{0,2},{1,3},{4,6},{5,7},{8,10},{9,11},{12,14},{13,15},{16,18},{17,... | collective-permute-start | bytes 104456 | tf_op jit(solution)/shard_map/ppermute | solution.py:20
  371.5 13.9 %collective-permute-start.70 = (f32[16,16,256]{2,1,0:T(8,128)S(1)}, f32[16,16,256]{2,1,0:T(8,128)S(1)}, u32[]{:S(2)}, u32[]{:S(2)}) collective-permute-start(f32[16,16,256]{2,1,0:T(8,128)S(1)} %get-tuple-element.568), channel_id=1, source_target_pairs={{0,4},{4,8},{8,12},{1,5},{5,9},{9,13},{2,6},{6,10},{10,14},{3,7},{... | collective-permute-start | bytes 786440 | tf_op jit(solution)/shard_map/ppermute | solution.py:20
  375.7 9.7 %collective-permute-start.71 = (f32[16,16,256]{2,1,0:T(8,128)S(1)}, f32[16,16,256]{2,1,0:T(8,128)S(1)}, u32[]{:S(2)}, u32[]{:S(2)}) collective-permute-start(f32[16,16,256]{2,1,0:T(8,128)S(1)} %get-tuple-element.569), channel_id=1, source_target_pairs={{4,0},{8,4},{12,8},{5,1},{9,5},{13,9},{6,2},{10,6},{14,10},{7,3},{... | collective-permute-start | bytes 786440 | tf_op jit(solution)/shard_map/ppermute | solution.py:22
  378.2 78.0 %collective-permute-start.68 = (f32[34,18,1]{2,1,0:T(8,128)}, f32[34,18,1]{2,1,0:T(8,128)}, u32[]{:S(2)}, u32[]{:S(2)}) collective-permute-start(f32[34,18,1]{2,1,0:T(8,128)} %get-tuple-element.498), channel_id=1, source_target_pairs={{1,0},{3,2},{5,4},{7,6},{9,8},{11,10},{13,12},{15,14},{17,16},{19,... | collective-permute-start | bytes 7352 | tf_op jit(solution)/shard_map/ppermute | solution.py:22
  379.5 76.7 %collective-permute-start.69 = (f32[34,18,1]{2,1,0:T(8,128)}, f32[34,18,1]{2,1,0:T(8,128)}, u32[]{:S(2)}, u32[]{:S(2)}) collective-permute-start(f32[34,18,1]{2,1,0:T(8,128)} %get-tuple-element.499), channel_id=1, source_target_pairs={{0,1},{2,3},{4,5},{6,7},{8,9},{10,11},{12,13},{14,15},{16,17},{18,... | collective-permute-start | bytes 7352 | tf_op jit(solution)/shard_map/ppermute | solution.py:20
  461.5 6.6 %collective-permute-start.73 = (f32[1,16,256]{2,1,0:T(8,128)S(1)}, f32[1,16,256]{2,1,0:T(8,128)S(1)}, u32[]{:S(2)}, u32[]{:S(2)}) collective-permute-start(f32[1,16,256]{2,1,0:T(8,128)S(1)} %get-tuple-element.566), channel_id=1, source_target_pairs={{0,4},{4,8},{8,12},{1,5},{5,9},{9,13},{2,6},{6,10},{10,14},{3,7},{... | collective-permute-start | bytes 49160 | tf_op jit(solution)/shard_map/ppermute | solution.py:20
  (50 other events, 657.8 us)
where the time goes:
time: 489 us; the launch traced here: 483 us
  starting transfers between devices  217 us (44%)
  other arithmetic  135 us (28%)
  loops' own time  65.4 us (13%)
  local copies, waits for them, and re-layouts  43.2 us (9%)
  waiting for transfers between devices  19.8 us (4%)
    ppermute x39, starting transfers between devices, padded_2(): lax.ppermute(tail, axis, [(i, (i + 1) % count) for i in range(ends)])  167 us
    add x51, other arithmetic, accumulate(): return running + reflectivity[offset_index].astype(jnp.float32) * moved  97.9 us
    another operation x3, loops' own time, shards(): source = lax.fori_loop(0, NOFF, accumulate, jnp.zeros_like(current))  65.4 us
    ppermute x39, starting transfers between devices, padded_2(): lax.ppermute(head, axis, [((i + 1) % count, i) for i in range(ends)])  50.5 us
    dynamic_slice x51, local copies, waits for them, and re-layouts, accumulate(): start = MARGIN + offsets[offset_index]  31.8 us
    ppermute x39, waiting for transfers between devices, padded_2(): lax.ppermute(tail, axis, [(i, (i + 1) % count) for i in range(ends)])  16.6 us
    add x6, other arithmetic, shards(): advanced = step_single(run_wave_scat, run_scat_prior, core_coefs) + forcing  16.4 us
    concatenate x26, other arithmetic, padded_2(): jnp.concatenate([lax.ppermute(tail, axis, [(i, (i + 1) % count) for i in...  13 us
  transfers between devices with their start and end apart: 78, of which 17 were waited for; matrix products, arithmetic and copies ran while one was open for 33% of the time, Pallas kernels for 0%

commit v1 on v0

v1 whole, which is shorter than its diff:
```python
import functools

import jax
import jax.numpy as jnp
from jax import lax
from jax.experimental import pallas as pl
from jax.experimental.pallas import tpu as pltpu
from jax.sharding import PartitionSpec as P

NOFF = 17
MARGIN = 16
TILE = 8
F32 = jnp.float32


class Geometry:
    def __init__(self, rows, depth, half, sections):
        self.B, self.Z, self.H, self.Y = rows // 2, depth, half, 2 * half
        self.two = sections == 2
        self.sides = 1 if self.two else 2
        self.ZE = depth + TILE * self.sides
        assert self.B >= MARGIN and depth % TILE == 0 and half % 128 == 0


def near_side(side, geo):
    first = (geo.B - 2) + side * (geo.B + 2)
    return first, first + 1 - side


def tile_mask(sender, depth, turn, width):
    place = lax.broadcasted_iota(jnp.int32, (TILE, width), 0)
    place = lax.rem(place + (TILE - turn), TILE)
    start = (1 - sender) * (TILE - depth)
    return (place >= start) & (place < start + depth)


def turned(value, turn):
    turn = turn % TILE
    return value if turn == 0 else pltpu.roll(value, turn, 0)


def senders(s, geo):
    return [s] if geo.two else [0, 1]


def receivers(s, geo):
    return [(geo.Z, 1 - s)] if geo.two else [(geo.ZE - TILE, 0), (geo.Z, 1)]


def edge_tile(ref, row, sender, geo):
    start = pl.multiple_of((1 - sender) * (geo.Z - TILE), TILE)
    return ref[row, pl.ds(start, TILE), :]


def packed(items, row, sender, geo):
    out = jnp.zeros((TILE, geo.Y), F32)
    for ref, depth, turn in items:
        out = jnp.where(
            tile_mask(sender, depth, turn, geo.Y), turned(edge_tile(ref, row, sender, geo), turn), out
        )
    return out


def unpacked(tile, depth, turn, sender, geo):
    return jnp.where(tile_mask(sender, depth, 0, geo.Y), turned(tile, TILE - turn), 0.0)


def pack_tiles(items, g, s, tiles, corners, geo):
    for sender, tile_ref, corner_ref in zip(senders(s, geo), tiles, corners):

        def one(row, carry):
            tile_ref[row] = packed(items, row, sender, geo)
            return carry

        lax.fori_loop(0, geo.B, one, 0)
        for k in range(2):
            corner_ref[k] = tile_ref[g * (geo.B - 2) + k]


def put_tiles(dst, place, tiles, index, depth, turn, s, geo):
    for (offset, sender), ref in zip(receivers(s, geo), tiles):
        dst[place, offset : offset + TILE, :] = unpacked(ref[index], depth, turn, sender, geo)


def fill(dst, own, xrow, crow, tiles, xtiles, ctiles, depth, turn, g, s, geo):
    def one(row, carry):
        dst[geo.B + row, 0 : geo.Z, :] = own[row]
        put_tiles(dst, geo.B + row, tiles, row, depth, turn, s, geo)
        return carry

    lax.fori_loop(0, geo.B, one, 0)
    for side, get, edge in ((g, xrow, xtiles), (1 - g, crow, ctiles)):
        first, nearest = near_side(side, geo)
        for k in range(depth):
            place = first + k if depth == 2 else nearest
            index = k if depth == 2 else 1 - side
            if get is not None:
                dst[place, 0 : geo.Z, :] = get(k)
            put_tiles(dst, place, edge, index, depth, turn, s, geo)


def fill_blocks(dst, xblock, cblock, g, geo):
    def one(row, carry):
        dst[g * 2 * geo.B + row, 0 : geo.Z, :] = xblock[row]
        dst[(1 - g) * 2 * geo.B + row, 0 : geo.Z, :] = cblock[row]
        return carry

    lax.fori_loop(0, geo.B, one, 0)


def advance(src, first, count, prior, extra, store, coefs, dif, tot, geo):
    xx, zz, yy, xz = coefs

    def rolls(row, carry):
        value = src[row]
        above = pltpu.roll(value, geo.ZE - 1, 0)
        below = pltpu.roll(value, 1, 0)
        dif[row] = above - below
        tot[row] = above + below
        return carry

    lax.fori_loop(first - 1, first + count + 1, rolls, 0)
    lane = lax.broadcasted_iota(jnp.int32, (geo.ZE, geo.Y), 1)

    def one(row, carry):
        at = row - (geo.B - 1)
        value = src[row]
        right = jnp.where(lane == geo.Y - 1, 0.0, pltpu.roll(value, geo.Y - 1, 1))
        left = jnp.where(lane == 0, 0.0, pltpu.roll(value, 1, 1))
        cx, cz, cy = xx[at], zz[at], yy[at]
        out = (2.0 - 2.0 * (cx + cz + cy)) * value - prior(row)
        out = out + cx * (src[row + 1] + src[row - 1]) + cz * tot[row] + cy * (right + left)
        out = out + xz[at] * (dif[row + 1] - dif[row - 1])
        if extra is not None:
            out = out + extra(row)
        store(row, out)
        return carry

    lax.fori_loop(first, first + count, one, 0)


def make_source(ext, refl, refl_far, offsets, courant, out, g, geo):
    near = pl.multiple_of(g * geo.H, 128)
    far = pl.multiple_of((1 - g) * geo.H, 128)

    def one(row, carry):
        acc = jnp.zeros((geo.Z, geo.H), F32)
        acc_far = jnp.zeros((geo.Z, geo.H), F32)
        for h in range(NOFF):
            place = geo.B + row + offsets[h]
            acc = acc + refl[h, g * geo.B + row].astype(F32) * ext[place, 0 : geo.Z, pl.ds(near, geo.H)]
            acc_far = acc_far + refl_far[h, row] * ext[place, 0 : geo.Z, pl.ds(far, geo.H)]
        out[row, :, pl.ds(near, geo.H)] = courant[row, :, pl.ds(near, geo.H)] * acc
        out[row, :, pl.ds(far, geo.H)] = courant[row, :, pl.ds(far, geo.H)] * acc_far
        return carry

    lax.fori_loop(0, geo.B, one, 0)


def edge_rows(ref, depth, side, geo):
    return side * (geo.B - depth)


def trig_products(angle):
    turns = jnp.floor(angle * 0.6366197723675814 + 0.5)
    rest = angle - turns * 1.5703125
    rest = rest - turns * 4.837512969970703125e-4
    rest = rest - turns * 7.549789954891882e-8
    odd = (turns - 2.0 * jnp.floor(turns * 0.5)) > 0.5
    square = rest * rest
    sine = rest + rest * square * (
        -1.6666654611e-1 + square * (8.3321608736e-3 + square * -1.9515295891e-4)
    )
    cosine = 1.0 - 0.5 * square + square * square * (
        4.166664568298827e-2 + square * (-1.388731625493765e-3 + square * 2.443315711809948e-5)
    )
    sine_square = jnp.where(odd, cosine * cosine, sine * sine)
    cosine_square = jnp.where(odd, sine * sine, cosine * cosine)
    product = sine * cosine
    return sine_square, cosine_square, jnp.where(odd, -product, product)


def join_kernel(geo, scal, *refs):
    raw, far = refs[:5], refs[5]
    own = refs[6:11]
    px, pc = refs[11], refs[12]
    tiles, corners = refs[13 : 13 + geo.sides], refs[13 + geo.sides :]
    g, s = scal[0], scal[1]
    near_y = pl.multiple_of(g * geo.H, 128)
    far_y = pl.multiple_of((1 - g) * geo.H, 128)

    def one(row, carry):
        for k in range(5):
            own[k][row, :, pl.ds(near_y, geo.H)] = raw[k][g * geo.B + row]
            own[k][row, :, pl.ds(far_y, geo.H)] = far[k, row]
        return carry

    lax.fori_loop(0, geo.B, one, 0)
    for side, out in ((g, px), (1 - g, pc)):
        for k in range(2):
            out[k] = own[0][edge_rows(own[0], 2, side, geo) + k]
        for k in range(1, 5):
            out[1 + k] = own[k][edge_rows(own[k], 1, side, geo)]
    items = [(own[0], 2, 0)] + [(own[k], 1, 1 + k) for k in range(1, 5)]
    pack_tiles(items, g, s, tiles, corners, geo)


def first_kernel(geo, scal, *refs):
    n = geo.sides
    now, before, courant, aniso, tilt, xr, cr = refs[:7]
    tiles, xtiles, ctiles = refs[7 : 7 + n], refs[7 + n : 7 + 2 * n], refs[7 + 2 * n : 7 + 3 * n]
    out_block, prior_ext, xx, zz, yy, xz = refs[7 + 3 * n : 13 + 3 * n]
    out_tiles, out_corners = refs[13 + 3 * n : 13 + 4 * n], refs[13 + 4 * n : 13 + 5 * n]
    ext, old, dif, tot, mid, ca, cb, cc = refs[13 + 5 * n :]
    g, s = scal[0], scal[1]
    for k, (dst, own) in enumerate(((old, before), (ca, courant), (cb, aniso), (cc, tilt)), 1):
        fill(dst, own, lambda _, k=k: xr[1 + k], lambda _, k=k: cr[1 + k], tiles, xtiles, ctiles, 1, 1 + k, g, s, geo)
    fill(ext, now, lambda k: xr[k], lambda k: cr[k], tiles, xtiles, ctiles, 2, 0, g, s, geo)

    def coefficients(row, carry):
        at = row - (geo.B - 1)
        speed, stretch = ca[row], 2.0 * cb[row]
        sine_square, cosine_square, product = trig_products(cc[row])
        xx[at] = speed * (1.0 + stretch * cosine_square)
        zz[at] = speed * (1.0 + stretch * sine_square)
        yy[at] = speed * (1.0 + stretch)
        xz[at] = (0.5 * speed) * (stretch * product)
        return carry

    lax.fori_loop(geo.B - 1, 2 * geo.B + 1, coefficients, 0)
    two_steps(ext, mid, lambda row: old[row], prior_ext, out_block, (xx, zz, yy, xz), dif, tot, geo)
    pack_tiles([(out_block, 2, 0)], g, s, out_tiles, out_corners, geo)


def two_steps(ext, mid, prior, prior_ext, out_block, coefs, dif, tot, geo):
    def keep(row, value):
        mid[row] = value
        prior_ext[row - (geo.B - 1)] = value

    def keep_block(row, value):
        out_block[row - geo.B] = value[0 : geo.Z]

    advance(ext, geo.B - 1, geo.B + 2, prior, None, keep, coefs, dif, tot, geo)
    advance(mid, geo.B, geo.B, lambda row: ext[row], None, keep_block, coefs, dif, tot, geo)


def second_kernel(geo, scal, offsets, *refs):
    n = geo.sides
    now, before, xr, cr, courant, refl, refl_far, *coefs = refs[:11]
    tiles, xtiles, ctiles = refs[11 : 11 + n], refs[11 + n : 11 + 2 * n], refs[11 + 2 * n : 11 + 3 * n]
    px, pc, prior_ext, force = refs[11 + 3 * n : 15 + 3 * n]
    out_tiles, out_corners = refs[15 + 3 * n : 15 + 4 * n], refs[15 + 4 * n : 15 + 5 * n]
    ext, dif, tot, mid = refs[15 + 5 * n :]
    g, s = scal[0], scal[1]
    fill(ext, now, None, None, tiles, xtiles, ctiles, 2, 0, g, s, geo)
    fill_blocks(ext, xr, cr, g, geo)
    two_steps(ext, mid, lambda row: before[row - (geo.B - 1)], prior_ext, px, coefs, dif, tot, geo)
    make_source(ext, refl, refl_far, offsets, courant, force, g, geo)

    def one(row, carry):
        pc[row] = px[row]
        return carry

    lax.fori_loop(0, geo.B, one, 0)
    for side, out in ((g, px), (1 - g, pc)):
        for k in range(2):
            out[geo.B + k] = force[edge_rows(force, 2, side, geo) + k]
    pack_tiles([(px, 2, 0), (force, 2, 4)], g, s, out_tiles, out_corners, geo)


def third_kernel(geo, scal, offsets, *refs):
    n = geo.sides
    now, before, xr, cr, courant, refl, refl_far, *coefs = refs[:11]
    force = refs[11]
    tiles, xtiles, ctiles = refs[12 : 12 + n], refs[12 + n : 12 + 2 * n], refs[12 + 2 * n : 12 + 3 * n]
    px, pc, force_out, scat, scat_prior = refs[12 + 3 * n : 17 + 3 * n]
    out_tiles, out_corners = refs[17 + 3 * n : 17 + 4 * n], refs[17 + 4 * n : 17 + 5 * n]
    ext, dif, tot, mid, wave = refs[17 + 5 * n :]
    g, s = scal[0], scal[1]
    B = geo.B
    fill(ext, now, None, None, tiles, xtiles, ctiles, 2, 0, g, s, geo)
    fill_blocks(ext, xr, cr, g, geo)
    def keep_mid(row, value):
        mid[row] = value

    def keep_block(row, value):
        px[row - B] = value[0 : geo.Z]
        pc[row - B] = value[0 : geo.Z]

    advance(ext, B - 1, B + 2, lambda row: before[row - (B - 1)], None, keep_mid, coefs, dif, tot, geo)
    advance(mid, B, B, lambda row: ext[row], None, keep_block, coefs, dif, tot, geo)
    make_source(ext, refl, refl_far, offsets, courant, force_out, g, geo)
    fill(wave, force, lambda k: xr[B + k], lambda k: cr[B + k], tiles, xtiles, ctiles, 2, 4, g, s, geo)

    def keep_wave(row, value):
        mid[row] = value
        scat_prior[row - (B - 1)] = value

    def keep_scat(row, value):
        scat[row - B] = value[0 : geo.Z] + force_out[row - B]

    advance(wave, B - 1, B + 2, lambda row: -wave[row], None, keep_wave, coefs, dif, tot, geo)
    advance(mid, B, B, lambda row: wave[row], None, keep_scat, coefs, dif, tot, geo)
    for side, out in ((g, px), (1 - g, pc)):
        for k in range(2):
            out[B + k] = scat[edge_rows(scat, 2, side, geo) + k]
        out[B + 2] = force_out[edge_rows(force_out, 1, side, geo)]
    pack_tiles([(scat, 2, 0), (force_out, 1, 2)], g, s, out_tiles, out_corners, geo)


def fourth_kernel(geo, scal, offsets, *refs):
    n = geo.sides
    now, scat, before, xr, cr, courant, refl, refl_far, *coefs = refs[:12]
    force2 = refs[12]
    tiles, xtiles, ctiles = refs[13 : 13 + n], refs[13 + n : 13 + 2 * n], refs[13 + 2 * n : 13 + 3 * n]
    scat_out, scat_prior, force_out, px, pc, back = refs[13 + 3 * n : 19 + 3 * n]
    out_rows, out_corners = refs[19 + 3 * n : 19 + 4 * n], refs[19 + 4 * n : 19 + 5 * n]
    ext, dif, tot, mid, wave = refs[19 + 5 * n :]
    g, s = scal[0], scal[1]
    B = geo.B

    def own(row, carry):
        ext[B + row, 0 : geo.Z, :] = now[row]
        back[row] = now[row, :, pl.ds(pl.multiple_of((1 - g) * geo.H, 128), geo.H)]
        return carry

    lax.fori_loop(0, B, own, 0)
    fill_blocks(ext, xr, cr, g, geo)
    make_source(ext, refl, refl_far, offsets, courant, force_out, g, geo)
    fill(wave, scat, lambda k: xr[B + k], lambda k: cr[B + k], tiles, xtiles, ctiles, 2, 0, g, s, geo)
    fill(ext, force2, lambda k: xr[B + 2], lambda k: cr[B + 2], tiles, xtiles, ctiles, 1, 2, g, s, geo)

    def keep_wave(row, value):
        mid[row] = value

    def keep_scat(row, value):
        scat_out[row - B] = value[0 : geo.Z] + force_out[row - B]
        scat_prior[row - B] = mid[row, 0 : geo.Z, :]

    advance(wave, B - 1, B + 2, lambda row: before[row - (B - 1)], lambda row: ext[row], keep_wave, coefs, dif, tot, geo)
    advance(mid, B, B, lambda row: wave[row], None, keep_scat, coefs, dif, tot, geo)
    px[0] = scat_out[edge_rows(scat_out, 1, g, geo)]
    pc[0] = scat_out[edge_rows(scat_out, 1, 1 - g, geo)]
    for sender, rows, corner in zip(senders(s, geo), out_rows, out_corners):
        for row in range(B):
            tile = edge_tile(scat_out, row, sender, geo)
            rows[row : row + 1, :] = jnp.where(sender == 0, tile[TILE - 1 : TILE], tile[0:1])
        tile = edge_tile(scat_out, g * (B - 1), sender, geo)
        corner[...] = jnp.where(sender == 0, tile[TILE - 1 : TILE], tile[0:1])


def fifth_kernel(geo, scal, *refs):
    n = geo.sides
    scat, before, force, xr, cr, *coefs = refs[:9]
    rows, xrows, crows = refs[9 : 9 + n], refs[9 + n : 9 + 2 * n], refs[9 + 2 * n : 9 + 3 * n]
    out_near, out_far = refs[9 + 3 * n : 11 + 3 * n]
    ext, dif, tot = refs[11 + 3 * n :]
    g, s = scal[0], scal[1]
    B = geo.B
    places = [(row, rows, row) for row in range(B)]

    def halo(place, offset, sender, value):
        whole = jnp.broadcast_to(value, (TILE, geo.Y))
        ext[place, offset : offset + TILE, :] = jnp.where(tile_mask(sender, 1, 0, geo.Y), whole, 0.0)

    def own(row, carry):
        ext[B + row, 0 : geo.Z, :] = scat[row]
        return carry

    lax.fori_loop(0, B, own, 0)
    for (offset, sender), ref in zip(receivers(s, geo), rows):
        for row in range(B):
            halo(B + row, offset, sender, ref[row : row + 1, :])
    for side, line, edge in ((g, xr, xrows), (1 - g, cr, crows)):
        _, place = near_side(side, geo)
        ext[place, 0 : geo.Z, :] = line[0]
        for (offset, sender), ref in zip(receivers(s, geo), edge):
            halo(place, offset, sender, ref[...])
    near = pl.multiple_of(g * geo.H, 128)
    far = pl.multiple_of((1 - g) * geo.H, 128)

    def keep(row, value):
        ext[row, 0 : geo.Z, :] = ext[row, 0 : geo.Z, :]
        dif[0, 0 : geo.Z, :] = value[0 : geo.Z] - before[row - B] + force[row - B]
        out_near[row - B] = dif[0, 0 : geo.Z, pl.ds(near, geo.H)]
        out_far[row - B] = dif[0, 0 : geo.Z, pl.ds(far, geo.H)]

    advance(ext, B, B, lambda row: 0.0, None, keep, coefs, dif, tot, geo)


def shards(sections, gx, wave_now, wave_before, courant, anisotropy, tilt, reflectivity, offsets):
    rows, depth, half = wave_now.shape
    geo = Geometry(rows, depth, half, sections)
    B, Z, H, Y, ZE, n = geo.B, geo.Z, geo.H, geo.Y, geo.ZE, geo.sides
    g = lax.axis_index("gy")
    s = lax.axis_index("section")
    scal = jnp.stack([g, s]).astype(jnp.int32)
    swap = [(0, 1), (1, 0)]
    pairs_x = [p for i in range(gx - 1) for p in ((2 * i + 1, 2 * i + 2), (2 * i + 2, 2 * i + 1))]

    def z_moves():
        if geo.two:
            return [[(0, 1), (1, 0)]]
        return [[(i, i + 1) for i in range(sections - 1)], [(i + 1, i) for i in range(sections - 1)]]

    def corner_pairs(move):
        out = []
        for a, b in pairs_x:
            for i, j in move:
                out.append((((a // 2) * sections + i) * 2 + a % 2, ((b // 2) * sections + j) * 2 + b % 2))
        return out

    def chip(value):
        return lax.ppermute(value, "gy", swap)

    def exchange(px, pc, tiles, corners, depth):
        xr = lax.ppermute(px, ("gx", "gy"), pairs_x)
        zr = [lax.ppermute(t, "section", m) for t, m in zip(tiles, z_moves())]
        xz = [lax.ppermute(t, ("gx", "section", "gy"), corner_pairs(m)) for t, m in zip(corners, z_moves())]
        cr = chip(pc)
        start = (1 - g) * (B - depth)
        cz = [chip(lax.dynamic_slice_in_dim(t, start, depth, 0)) for t in zr]
        return xr, cr, [*zr, *xz, *cz]

    def shape(*dims):
        return jax.ShapeDtypeStruct(dims, F32)

    def call(kernel, inputs, outs, scratch, smem=1):
        specs = [pl.BlockSpec(memory_space=pltpu.SMEM)] * smem
        specs += [pl.BlockSpec(memory_space=pltpu.VMEM)] * (len(inputs) - smem)
        return pl.pallas_call(
            functools.partial(kernel, geo),
            out_shape=outs,
            in_specs=specs,
            out_specs=[pl.BlockSpec(memory_space=pltpu.VMEM)] * len(outs),
            scratch_shapes=[pltpu.VMEM(d, F32) for d in scratch],
        )(*inputs)

    block, wide, ext = (B, Z, Y), (B + 2, ZE, Y), (3 * B, ZE, Y)
    tile_outs = [shape(B, TILE, Y)] * n + [shape(2, TILE, Y)] * n
    fields = (wave_now, wave_before, courant, anisotropy, tilt)
    other = (1 - g) * B
    far = chip(jnp.stack([lax.dynamic_slice_in_dim(f, other, B, 0) for f in fields]))
    *own, px, pc, r0, r1 = _split(
        call(join_kernel, [scal, *fields, far], [shape(*block)] * 5 + [shape(6, Z, Y)] * 2 + tile_outs, []), 7, n
    )
    xr, cr, halo = exchange(px, pc, r0, r1, 2)
    refl_far = chip(lax.dynamic_slice_in_dim(reflectivity, other, B, 1).astype(F32))
    now, prior, *coefs, r0, r1 = _split(
        call(first_kernel, [scal, *own, xr, cr, *halo], [shape(*block)] + [shape(*wide)] * 5 + tile_outs, [ext] * 8), 6, n
    )
    xr, cr, halo = exchange(now, now, r0, r1, 2)
    px, pc, prior, force, r0, r1 = _split(
        call(
            second_kernel,
            [scal, offsets, now, prior, xr, cr, own[2], reflectivity, refl_far, *coefs, *halo],
            [shape(B + 2, Z, Y)] * 2 + [shape(*wide), shape(*block)] + tile_outs,
            [ext] * 4,
            2,
        ),
        4,
        n,
    )
    xr, cr, halo = exchange(px, pc, r0, r1, 2)
    px, pc, force2, scat, scat_prior, r0, r1 = _split(
        call(
            third_kernel,
            [scal, offsets, px, prior, xr, cr, own[2], reflectivity, refl_far, *coefs, force, *halo],
            [shape(B + 3, Z, Y)] * 2 + [shape(*block)] * 2 + [shape(*wide)] + tile_outs,
            [ext] * 5,
            2,
        ),
        5,
        n,
    )
    xr, cr, halo = exchange(px, pc, r0, r1, 2)
    scat, scat_prior, force3, qx, qc, back, r0, r1 = _split(
        call(
            fourth_kernel,
            [scal, offsets, px, scat, scat_prior, xr, cr, own[2], reflectivity, refl_far, *coefs, force2, *halo],
            [shape(*block)] * 3
            + [shape(1, Z, Y)] * 2
            + [shape(B, Z, H)]
            + [shape(B, Y)] * n
            + [shape(1, Y)] * n,
            [ext] * 5,
            2,
        ),
        6,
        n,
    )
    xr, cr, halo = exchange(qx, qc, r0, r1, 1)
    near_w, far_w = call(fifth_kernel, [scal, scat, scat_prior, force3, xr, cr, *coefs, *halo], [shape(B, Z, H)] * 2, [ext] * 3)
    near_u = lax.dynamic_slice_in_dim(px[:B], g * H, H, 2)

    def joined(near, other):
        return jnp.where(g == 0, jnp.concatenate([near, other], 0), jnp.concatenate([other, near], 0))

    return joined(near_u, chip(back)), joined(near_w, chip(far_w))


def _split(values, count, n):
    return [*values[:count], values[count : count + n], values[count + n :]]


def solution(mesh):
    spec = P(("shot", "gx"), "section", "gy")
    assert mesh.shape["gy"] == 2
    return jax.shard_map(
        functools.partial(shards, mesh.shape["section"], mesh.shape["gx"]),
        mesh=mesh,
        in_specs=(spec,) * 5 + (P(None, ("shot", "gx"), "section", "gy"), P()),
        out_specs=(spec, spec),
        check_vma=False,
    )
```

time: 489 us -> 149 us (0.30); the launches traced: 483 us -> 149 us
  starting transfers between devices: 217 us -> 34.7 us
  other arithmetic: 135 us -> 6.82 us
  loops' own time: 65.4 us -> 0 us
  Pallas kernels: 0 us -> 62.3 us
  local copies, waits for them, and re-layouts: 43.2 us -> 8.97 us
  waiting for transfers between devices: 19.8 us -> 35.1 us
    ppermute x78 -> x29, starting transfers between devices: 217 us -> 34.7 us  [the longest x14 21.9 us: chip(): return lax.ppermute(value, 'gy', swap)]
    add x63 -> x0, other arithmetic: 122 us -> none  [the longest x51 97.9 us: accumulate(): return running + reflectivity[offset_index].astype(jnp.float32) * moved]
    another operation x3 -> x0, loops' own time: 65.4 us -> none  [shards(): source = lax.fori_loop(0, NOFF, accumulate, jnp.zeros_like(current))]
    pallas_call x0 -> x6, Pallas kernels: none -> 62.3 us  [call(): pl.pallas_call(functools.partial(kernel, geo), out_shape=outs, in_specs=s...]
    dynamic_slice x51 -> x6, local copies, waits for them, and re-layouts: 31.8 us -> 0.05 us  [the longest x1 0.03 us: shards(): near_u = lax.dynamic_slice_in_dim(px[:B], g * H, H, 2)]
    ppermute x78 -> x29, waiting for transfers between devices: 19.8 us -> 35.1 us  [the longest x5 24.6 us: exchange(): zr = [lax.ppermute(t, 'section', m) for t, m in zip(tiles, z_moves())]]
    concatenate x26 -> x0, other arithmetic: 13 us -> none  [padded_2(): jnp.concatenate([lax.ppermute(tail, axis, [(i, (i + 1) % count) for i in...]
    slice x27 -> x1, local copies, waits for them, and re-layouts: 7.59 us -> 0.04 us  [shards(): near_u = lax.dynamic_slice_in_dim(px[:B], g * H, H, 2)]
  transfers between devices with their start and end apart: 78 -> 29, of which waited for: 17 -> 11; matrix products, arithmetic and copies ran while one was open for 33% -> 3% of each run, Pallas kernels for 0% -> 13%
where the time goes in v1:
time: 149 us
  Pallas kernels  62.3 us (42%)
  waiting for transfers between devices  35.1 us (24%)
  starting transfers between devices  34.7 us (23%)
  local copies, waits for them, and re-layouts  8.97 us (6%)
  other arithmetic  6.82 us (5%)
    pallas_call x6, Pallas kernels, call(): pl.pallas_call(functools.partial(kernel, geo), out_shape=outs, in_specs=s...  62.3 us
    ppermute x5, waiting for transfers between devices, exchange(): zr = [lax.ppermute(t, 'section', m) for t, m in zip(tiles, z_moves())]  24.6 us
    ppermute x14, starting transfers between devices, chip(): return lax.ppermute(value, 'gy', swap)  21.9 us
    ppermute x14, waiting for transfers between devices, chip(): return lax.ppermute(value, 'gy', swap)  10.5 us
    unnamed x70, local copies, waits for them, and re-layouts  8.16 us
    ppermute x5, starting transfers between devices, exchange(): zr = [lax.ppermute(t, 'section', m) for t, m in zip(tiles, z_moves())]  6.15 us
    convert_element_type x1, other arithmetic, shards(): lax.dynamic_slice_in_dim(reflectivity, other, B, 1).astype(F32)  4.48 us
    ppermute x5, starting transfers between devices, exchange(): xr = lax.ppermute(px, ('gx', 'gy'), pairs_x)  3.38 us
  transfers between devices with their start and end apart: 29, of which 11 were waited for; matrix products, arithmetic and copies ran while one was open for 3% of the time, Pallas kernels for 13%

profile of v1, /device:TPU:0, one launch (start us, length us, event | category | flops | bytes accessed | tf_op | source)
XLA Modules:
  0.0 149.0 jit_solution(1971194398852571148)
XLA Ops:
  0.7 4.5 %dynamic-slice_convert_fusion = f32[17,16,16,256]{3,2,1,0:T(8,128)} fusion(bf16[17,32,16,256]{3,2,1,0:T(8,128)(2,1)} %refs_6_.1, s32[]{:T(128)S(6)} %select_n.33), kind=kLoop, calls=%fused_computation | loop fusion | flops 1114112 | bytes 6684676 | tf_op jit(solution)/shard_map/convert_element_type | solution.py:448
  5.7 0.7 bitcast_dynamic-update-slice_fusion.4
  6.4 0.7 bitcast_dynamic-update-slice_fusion.3
  7.1 0.7 bitcast_dynamic-update-slice_fusion.2
  7.8 0.7 bitcast_dynamic-update-slice_fusion.1
  8.6 0.7 bitcast_dynamic-update-slice_fusion
  9.3 0.7 pad_add_fusion.scal
  9.9 5.0 %collective-permute-done.refs_5_ = f32[5,16,16,256]{3,2,1,0:T(8,128)S(1)} collective-permute-done((f32[5,16,16,256]{3,2,1,0:T(8,128)}, f32[5,16,16,256]{3,2,1,0:T(8,128)S(1)}, u32[]{:S(2)}, u32[]{:S(2)}) %collective-permute-start) | collective-permute-done | bytes 1310752 | tf_op jit(solution)/shard_map/ppermute | solution.py:414
  14.9 1.0 copy-done.1
  15.9 4.3 %shard_map.86 = (f32[16,16,512]{2,1,0:T(8,128)}, f32[16,16,512]{2,1,0:T(8,128)}, f32[16,16,512]{2,1,0:T(8,128)}, f32[16,16,512]{2,1,0:T(8,128)}, f32[16,16,512]{...) custom-call(s32[2]{0:T(128)} %pad_add_fusion.scal, ...), custom_call_target="tpu_custom_call" | custom-call | tf_op jit(solution)/shard_map/pallas_call | solution.py:431
  20.2 2.8 %collective-permute-start.3 = (f32[16,8,512]{2,1,0:T(8,128)}, f32[16,8,512]{2,1,0:T(8,128)S(1)}, u32[]{:S(2)}, u32[]{:S(2)}) collective-permute-start(f32[16,8,512]{2,1,0:T(8,128)} %get-tuple-element.49), channel_id=1, source_target_pairs={{0,2},{2,0},{1,3},{3,1},{4,6},{6,4},{5,7},{7,5},{8,10},{10,8},{9,1... | collective-permute-start | bytes 786440 | tf_op jit(solution)/shard_map/ppermute | solution.py:418
  23.1 0.7 collective-permute-start.1
  23.8 3.0 %collective-permute-start.2 = (f32[6,16,512]{2,1,0:T(8,128)}, f32[6,16,512]{2,1,0:T(8,128)S(1)}, u32[]{:S(2)}, u32[]{:S(2)}) collective-permute-start(f32[6,16,512]{2,1,0:T(8,128)} %get-tuple-element.48), channel_id=1, source_target_pairs={{0,1},{1,0},{2,3},{3,2},{4,5},{5,4},{6,7},{7,6},{8,9},{9,8},{10,11... | collective-permute-start | bytes 589832 | tf_op jit(solution)/shard_map/ppermute | solution.py:414
  26.7 0.7 collective-permute-start.4
  27.4 2.5 %collective-permute-done.3.refs_7_ = f32[16,8,512]{2,1,0:T(8,128)S(1)} collective-permute-done((f32[16,8,512]{2,1,0:T(8,128)}, f32[16,8,512]{2,1,0:T(8,128)S(1)}, u32[]{:S(2)}, u32[]{:S(2)}) %collective-permute-start.3) | collective-permute-done | bytes 262176 | tf_op jit(solution)/shard_map/ppermute | solution.py:418
  30.5 0.8 collective-permute-done.5.refs_9_
  31.3 0.6 copy-done.27
  31.9 10.4 %shard_map.87 = (f32[16,16,512]{2,1,0:T(8,128)}, f32[18,24,512]{2,1,0:T(8,128)}, f32[18,24,512]{2,1,0:T(8,128)}, f32[18,24,512]{2,1,0:T(8,128)}, f32[18,24,512]{...) custom-call(s32[2]{0:T(128)} %pad_add_fusion.scal, ...), custom_call_target="tpu_custom_call" | custom-call | tf_op jit(solution)/shard_map/pallas_call | solution.py:431
  42.3 0.7 collective-permute-start.6
  42.9 5.1 %collective-permute-start.7 = (f32[16,16,512]{2,1,0:T(8,128)}, f32[16,16,512]{2,1,0:T(8,128)S(1)}, u32[]{:S(2)}, u32[]{:S(2)}) collective-permute-start(f32[16,16,512]{2,1,0:T(8,128)} %get-tuple-element.51.refs_0_), channel_id=1, source_target_pairs={{0,1},{1,0},{2,3},{3,2},{4,5},{5,4},{6,7},{7,6},{8,9},{9,8},{10,11... | collective-permute-start | bytes 1572872 | tf_op jit(solution)/shard_map/ppermute | solution.py:414
  48.6 0.7 collective-permute-start.10
  49.2 7.7 %collective-permute-done.9.refs_11_ = f32[16,8,512]{2,1,0:T(8,128)S(1)} collective-permute-done((f32[16,8,512]{2,1,0:T(8,128)}, f32[16,8,512]{2,1,0:T(8,128)S(1)}, u32[]{:S(2)}, u32[]{:S(2)}) %collective-permute-start.9) | collective-permute-done | bytes 262176 | tf_op jit(solution)/shard_map/ppermute | solution.py:418
  56.9 1.2 collective-permute-done.11.refs_13_
  59.1 12.8 %shard_map.88 = (f32[18,16,512]{2,1,0:T(8,128)}, f32[18,16,512]{2,1,0:T(8,128)}, f32[18,24,512]{2,1,0:T(8,128)}, f32[16,16,512]{2,1,0:T(8,128)}, f32[16,8,512]{2,1,0:T(8,128)}, /*index=5*/f32[2,8,512]{2,1,0:T(8,128)}) custom-call(s32[2]{0:T(128)} %pad_add_fusion.scal, s32[17]{0:T(128)} %offsets.5, f32[16,16,512]{2,1,0:T(8,128)} %get-tuple-element.51.refs_0_, ...), custom_call_target="tpu_custom_call" | custom-call | tf_op jit(solution)/shard_map/pallas_call | solution.py:431
  71.9 0.7 collective-permute-start.12
  72.6 3.3 %collective-permute-start.13 = (f32[18,16,512]{2,1,0:T(8,128)}, f32[18,16,512]{2,1,0:T(8,128)S(1)}, u32[]{:S(2)}, u32[]{:S(2)}) collective-permute-start(f32[18,16,512]{2,1,0:T(8,128)} %get-tuple-element.61), channel_id=1, source_target_pairs={{0,1},{1,0},{2,3},{3,2},{4,5},{5,4},{6,7},{7,6},{8,9},{9,8},{10,11... | collective-permute-start | bytes 1769480 | tf_op jit(solution)/shard_map/ppermute | solution.py:414
  76.4 0.7 collective-permute-start.15
  77.1 7.7 %collective-permute-done.14.refs_12_ = f32[16,8,512]{2,1,0:T(8,128)S(1)} collective-permute-done((f32[16,8,512]{2,1,0:T(8,128)}, f32[16,8,512]{2,1,0:T(8,128)S(1)}, u32[]{:S(2)}, u32[]{:S(2)}) %collective-permute-start.14) | collective-permute-done | bytes 262176 | tf_op jit(solution)/shard_map/ppermute | solution.py:418
  84.8 1.2 collective-permute-done.16.refs_14_
  87.0 16.9 %shard_map.89 = (f32[19,16,512]{2,1,0:T(8,128)}, f32[19,16,512]{2,1,0:T(8,128)}, f32[16,16,512]{2,1,0:T(8,128)}, f32[16,16,512]{2,1,0:T(8,128)}, f32[18,24,512]{...) custom-call(s32[2]{0:T(128)} %pad_add_fusion.scal, s32[17]{0:T(128)} %offsets.5, ...), custom_call_target="tpu_custom_call" | custom-call | tf_op jit(solution)/shard_map/pallas_call | solution.py:431
  103.9 0.7 collective-permute-start.17
  104.6 1.4 collective-permute-start.18
  106.0 1.1 collective-permute-start.19
  107.1 0.7 collective-permute-start.20
  107.7 6.8 %collective-permute-done.19.refs_13_ = f32[16,8,512]{2,1,0:T(8,128)S(1)} collective-permute-done((f32[16,8,512]{2,1,0:T(8,128)}, f32[16,8,512]{2,1,0:T(8,128)S(1)}, u32[]{:S(2)}, u32[]{:S(2)}) %collective-permute-start.19) | collective-permute-done | bytes 262176 | tf_op jit(solution)/shard_map/ppermute | solution.py:418
  114.5 1.2 collective-permute-done.21.refs_15_
  116.8 12.7 %shard_map.90 = (f32[16,16,512]{2,1,0:T(8,128)}, f32[16,16,512]{2,1,0:T(8,128)}, f32[16,16,512]{2,1,0:T(8,128)}, f32[1,16,512]{2,1,0:T(8,128)}, f32[1,16,512]{2,...) custom-call(s32[2]{0:T(128)} %pad_add_fusion.scal, s32[17]{0:T(128)} %offsets.5, ...), custom_call_target="tpu_custom_call" | custom-call | tf_op jit(solution)/shard_map/pallas_call | solution.py:431
  129.5 1.2 collective-permute-start.25
  131.1 0.7 collective-permute-start.23
  131.8 3.1 %collective-permute-start.24 = (f32[1,16,512]{2,1,0:T(8,128)}, f32[1,16,512]{2,1,0:T(8,128)S(1)}, u32[]{:S(2)}, u32[]{:S(2)}) collective-permute-start(f32[1,16,512]{2,1,0:T(8,128)} %get-tuple-element.77), channel_id=1, source_target_pairs={{0,1},{1,0},{2,3},{3,2},{4,5},{5,4},{6,7},{7,6},{8,9},{9,8},{10,11... | collective-permute-start | bytes 98312 | tf_op jit(solution)/shard_map/ppermute | solution.py:414
  134.9 0.6 collective-permute-start.26
  135.6 3.1 %collective-permute-start.27 = (f32[1,512]{1,0:T(1,128)S(1)}, f32[1,512]{1,0:T(1,128)S(1)}, u32[]{:S(2)}, u32[]{:S(2)}) collective-permute-start(f32[1,512]{1,0:T(1,128)S(1)} %constant_dynamic-slice_fusion), channel_id=1, source_target_pairs={{0,1},{1,0},{2,3},{3,2},{4,5},{5,4},{6,7},{7,6},{8,9},{9,8},{10,11... | collective-permute-start | bytes 6152 | tf_op jit(solution)/shard_map/ppermute | solution.py:414
  138.8 0.8 collective-permute-done.27.refs_11_
  139.6 0.6 copy-done.32
  140.1 5.3 %shard_map.91 = (f32[16,16,256]{2,1,0:T(8,128)}, f32[16,16,256]{2,1,0:T(8,128)}) custom-call(s32[2]{0:T(128)} %pad_add_fusion.scal, f32[16,16,512]{2,1,0:T(8,128)} %get-tuple-element.73.refs_0_, f32[16,16,512]{2,1,0:T(8,128)} %get-tuple-element.74.refs_1_, f32[16,16,512]{2,1,0:T(8,128)} %get-tuple-element.75.refs_2_, f32[1,16,512]{2,1,0:T(8,128)} %copy-done.21, ...), custom_call_target="tpu_custom_call" | custom-call | tf_op jit(solution)/shard_map/pallas_call | solution.py:431
  145.4 1.3 collective-permute-start.28
  146.9 0.8 maximum_select_fusion
  148.1 0.8 maximum_select_fusion.1
  (98 shorter events, 6.2 us)
Async XLA Ops:
  0.6 5.0 %copy-start.2 = (f32[32,16,256]{2,1,0:T(8,128)S(1)}, f32[32,16,256]{2,1,0:T(8,128)}, u32[]{:S(2)}) copy-start(f32[32,16,256]{2,1,0:T(8,128)} %refs_0_.1) | copy-start | bytes 1572868
  0.6 5.7 %copy-start.3 = (f32[32,16,256]{2,1,0:T(8,128)S(1)}, f32[32,16,256]{2,1,0:T(8,128)}, u32[]{:S(2)}) copy-start(f32[32,16,256]{2,1,0:T(8,128)} %refs_1_.1) | copy-start | bytes 1572868
  0.7 6.4 %copy-start.4 = (f32[32,16,256]{2,1,0:T(8,128)S(1)}, f32[32,16,256]{2,1,0:T(8,128)}, u32[]{:S(2)}) copy-start(f32[32,16,256]{2,1,0:T(8,128)} %refs_2_.1) | copy-start | bytes 1572868
  5.2 2.7 %copy-start.5 = (f32[32,16,256]{2,1,0:T(8,128)S(1)}, f32[32,16,256]{2,1,0:T(8,128)}, u32[]{:S(2)}) copy-start(f32[32,16,256]{2,1,0:T(8,128)} %refs_3_.1) | copy-start | bytes 1572868
  5.2 3.4 %copy-start.6 = (f32[32,16,256]{2,1,0:T(8,128)S(1)}, f32[32,16,256]{2,1,0:T(8,128)}, u32[]{:S(2)}) copy-start(f32[32,16,256]{2,1,0:T(8,128)} %refs_4_.1) | copy-start | bytes 1572868
  5.2 53.0 %collective-permute-start.8 = (f32[17,16,16,256]{3,2,1,0:T(8,128)}, f32[17,16,16,256]{3,2,1,0:T(8,128)}, u32[]{:S(2)}, u32[]{:S(2)}) collective-permute-start(f32[17,16,16,256]{3,2,1,0:T(8,128)} %dynamic-slice_convert_fusion), channel_id=1, source_target_pairs={{0,1},{1,0},{2,3},{3,2},{4,5},{5,4},{6,7},{7,6},{8,9},{9,8},{10,11... | collective-permute-start | bytes 13369352 | tf_op jit(solution)/shard_map/ppermute | solution.py:414
  9.3 5.6 %collective-permute-start = (f32[5,16,16,256]{3,2,1,0:T(8,128)}, f32[5,16,16,256]{3,2,1,0:T(8,128)S(1)}, u32[]{:S(2)}, u32[]{:S(2)}) collective-permute-start(f32[5,16,16,256]{3,2,1,0:T(8,128)} %bitcast_dynamic-update-slice_fusion), channel_id=1, source_target_pairs={{0,1},{1,0},{2,3},{3,2},{4,5},{5,4},{6,7},{7,6},{8,9},{9,8},{10,11... | collective-permute-start | bytes 3932168 | tf_op jit(solution)/shard_map/ppermute | solution.py:414
  14.9 1.1 copy-start.1
  20.2 9.7 %collective-permute-start.3 = (f32[16,8,512]{2,1,0:T(8,128)}, f32[16,8,512]{2,1,0:T(8,128)S(1)}, u32[]{:S(2)}, u32[]{:S(2)}) collective-permute-start(f32[16,8,512]{2,1,0:T(8,128)} %get-tuple-element.49), channel_id=1, source_target_pairs={{0,2},{2,0},{1,3},{3,1},{4,6},{6,4},{5,7},{7,5},{8,10},{10,8},{9,1... | collective-permute-start | bytes 786440 | tf_op jit(solution)/shard_map/ppermute | solution.py:418
  23.1 7.3 %collective-permute-start.1 = (f32[6,16,512]{2,1,0:T(8,128)}, f32[6,16,512]{2,1,0:T(8,128)S(1)}, u32[]{:S(2)}, u32[]{:S(2)}) collective-permute-start(f32[6,16,512]{2,1,0:T(8,128)} %get-tuple-element.47), channel_id=1, source_target_pairs={{1,4},{4,1},{5,8},{8,5},{9,12},{12,9},{3,6},{6,3},{7,10},{10,7},{1... | collective-permute-start | bytes 589832 | tf_op jit(solution)/shard_map/ppermute | solution.py:417
  23.8 6.7 %collective-permute-start.2 = (f32[6,16,512]{2,1,0:T(8,128)}, f32[6,16,512]{2,1,0:T(8,128)S(1)}, u32[]{:S(2)}, u32[]{:S(2)}) collective-permute-start(f32[6,16,512]{2,1,0:T(8,128)} %get-tuple-element.48), channel_id=1, source_target_pairs={{0,1},{1,0},{2,3},{3,2},{4,5},{5,4},{6,7},{7,6},{8,9},{9,8},{10,11... | collective-permute-start | bytes 589832 | tf_op jit(solution)/shard_map/ppermute | solution.py:414
  26.7 3.7 %collective-permute-start.4 = (f32[2,8,512]{2,1,0:T(8,128)}, f32[2,8,512]{2,1,0:T(8,128)S(1)}, u32[]{:S(2)}, u32[]{:S(2)}) collective-permute-start(f32[2,8,512]{2,1,0:T(8,128)} %get-tuple-element.50), channel_id=1, source_target_pairs={{1,6},{3,4},{4,3},{6,1},{5,10},{7,8},{8,7},{10,5},{9,14},{11,12},{... | collective-permute-start | bytes 98312 | tf_op jit(solution)/shard_map/ppermute | solution.py:419
  29.9 1.4 copy-start.16
  29.9 1.4 collective-permute-start.5
  42.3 15.8 %collective-permute-start.6 = (f32[16,16,512]{2,1,0:T(8,128)}, f32[16,16,512]{2,1,0:T(8,128)S(1)}, u32[]{:S(2)}, u32[]{:S(2)}) collective-permute-start(f32[16,16,512]{2,1,0:T(8,128)} %get-tuple-element.51.refs_0_), channel_id=1, source_target_pairs={{1,4},{4,1},{5,8},{8,5},{9,12},{12,9},{3,6},{6,3},{7,10},{10,7},{1... | collective-permute-start | bytes 1572872 | tf_op jit(solution)/shard_map/ppermute | solution.py:417
  42.9 15.2 %collective-permute-start.7 = (f32[16,16,512]{2,1,0:T(8,128)}, f32[16,16,512]{2,1,0:T(8,128)S(1)}, u32[]{:S(2)}, u32[]{:S(2)}) collective-permute-start(f32[16,16,512]{2,1,0:T(8,128)} %get-tuple-element.51.refs_0_), channel_id=1, source_target_pairs={{0,1},{1,0},{2,3},{3,2},{4,5},{5,4},{6,7},{7,6},{8,9},{9,8},{10,11... | collective-permute-start | bytes 1572872 | tf_op jit(solution)/shard_map/ppermute | solution.py:414
  48.0 8.9 %collective-permute-start.9 = (f32[16,8,512]{2,1,0:T(8,128)}, f32[16,8,512]{2,1,0:T(8,128)S(1)}, u32[]{:S(2)}, u32[]{:S(2)}) collective-permute-start(f32[16,8,512]{2,1,0:T(8,128)} %get-tuple-element.57), channel_id=1, source_target_pairs={{0,2},{2,0},{1,3},{3,1},{4,6},{6,4},{5,7},{7,5},{8,10},{10,8},{9,1... | collective-permute-start | bytes 786440 | tf_op jit(solution)/shard_map/ppermute | solution.py:418
  48.6 8.3 %collective-permute-start.10 = (f32[2,8,512]{2,1,0:T(8,128)}, f32[2,8,512]{2,1,0:T(8,128)S(1)}, u32[]{:S(2)}, u32[]{:S(2)}) collective-permute-start(f32[2,8,512]{2,1,0:T(8,128)} %get-tuple-element.58), channel_id=1, source_target_pairs={{1,6},{3,4},{4,3},{6,1},{5,10},{7,8},{8,7},{10,5},{9,14},{11,12},{... | collective-permute-start | bytes 98312 | tf_op jit(solution)/shard_map/ppermute | solution.py:419
  56.9 1.3 copy-start.14
  56.9 1.2 collective-permute-start.11
  56.9 1.2 copy-start.25
  58.1 1.0 copy-start.12
  71.9 14.1 %collective-permute-start.12 = (f32[18,16,512]{2,1,0:T(8,128)}, f32[18,16,512]{2,1,0:T(8,128)S(1)}, u32[]{:S(2)}, u32[]{:S(2)}) collective-permute-start(f32[18,16,512]{2,1,0:T(8,128)} %get-tuple-element.59.refs_0_), channel_id=1, source_target_pairs={{1,4},{4,1},{5,8},{8,5},{9,12},{12,9},{3,6},{6,3},{7,10},{10,7},{1... | collective-permute-start | bytes 1769480 | tf_op jit(solution)/shard_map/ppermute | solution.py:417
  72.6 13.4 %collective-permute-start.13 = (f32[18,16,512]{2,1,0:T(8,128)}, f32[18,16,512]{2,1,0:T(8,128)S(1)}, u32[]{:S(2)}, u32[]{:S(2)}) collective-permute-start(f32[18,16,512]{2,1,0:T(8,128)} %get-tuple-element.61), channel_id=1, source_target_pairs={{0,1},{1,0},{2,3},{3,2},{4,5},{5,4},{6,7},{7,6},{8,9},{9,8},{10,11... | collective-permute-start | bytes 1769480 | tf_op jit(solution)/shard_map/ppermute | solution.py:414
  75.9 8.9 %collective-permute-start.14 = (f32[16,8,512]{2,1,0:T(8,128)}, f32[16,8,512]{2,1,0:T(8,128)S(1)}, u32[]{:S(2)}, u32[]{:S(2)}) collective-permute-start(f32[16,8,512]{2,1,0:T(8,128)} %get-tuple-element.63), channel_id=1, source_target_pairs={{0,2},{2,0},{1,3},{3,1},{4,6},{6,4},{5,7},{7,5},{8,10},{10,8},{9,1... | collective-permute-start | bytes 786440 | tf_op jit(solution)/shard_map/ppermute | solution.py:418
  76.4 8.3 %collective-permute-start.15 = (f32[2,8,512]{2,1,0:T(8,128)}, f32[2,8,512]{2,1,0:T(8,128)S(1)}, u32[]{:S(2)}, u32[]{:S(2)}) collective-permute-start(f32[2,8,512]{2,1,0:T(8,128)} %get-tuple-element.64), channel_id=1, source_target_pairs={{1,6},{3,4},{4,3},{6,1},{5,10},{7,8},{8,7},{10,5},{9,14},{11,12},{... | collective-permute-start | bytes 98312 | tf_op jit(solution)/shard_map/ppermute | solution.py:419
  84.7 1.2 copy-start.15
  84.7 1.2 collective-permute-start.16
  84.8 1.2 copy-start.26
  86.0 1.0 copy-start.10
  103.9 11.9 %collective-permute-start.17 = (f32[19,16,512]{2,1,0:T(8,128)}, f32[19,16,512]{2,1,0:T(8,128)S(1)}, u32[]{:S(2)}, u32[]{:S(2)}) collective-permute-start(f32[19,16,512]{2,1,0:T(8,128)} %get-tuple-element.65.refs_0_), channel_id=1, source_target_pairs={{1,4},{4,1},{5,8},{8,5},{9,12},{12,9},{3,6},{6,3},{7,10},{10,7},{1... | collective-permute-start | bytes 1867784 | tf_op jit(solution)/shard_map/ppermute | solution.py:417
  104.6 11.2 %collective-permute-start.18 = (f32[19,16,512]{2,1,0:T(8,128)}, f32[19,16,512]{2,1,0:T(8,128)S(1)}, u32[]{:S(2)}, u32[]{:S(2)}) collective-permute-start(f32[19,16,512]{2,1,0:T(8,128)} %get-tuple-element.68), channel_id=1, source_target_pairs={{0,1},{1,0},{2,3},{3,2},{4,5},{5,4},{6,7},{7,6},{8,9},{9,8},{10,11... | collective-permute-start | bytes 1867784 | tf_op jit(solution)/shard_map/ppermute | solution.py:414
  106.0 8.5 %collective-permute-start.19 = (f32[16,8,512]{2,1,0:T(8,128)}, f32[16,8,512]{2,1,0:T(8,128)S(1)}, u32[]{:S(2)}, u32[]{:S(2)}) collective-permute-start(f32[16,8,512]{2,1,0:T(8,128)} %get-tuple-element.70), channel_id=1, source_target_pairs={{0,2},{2,0},{1,3},{3,1},{4,6},{6,4},{5,7},{7,5},{8,10},{10,8},{9,1... | collective-permute-start | bytes 786440 | tf_op jit(solution)/shard_map/ppermute | solution.py:418
  107.1 7.4 %collective-permute-start.20 = (f32[2,8,512]{2,1,0:T(8,128)}, f32[2,8,512]{2,1,0:T(8,128)S(1)}, u32[]{:S(2)}, u32[]{:S(2)}) collective-permute-start(f32[2,8,512]{2,1,0:T(8,128)} %get-tuple-element.71), channel_id=1, source_target_pairs={{1,6},{3,4},{4,3},{6,1},{5,10},{7,8},{8,7},{10,5},{9,14},{11,12},{... | collective-permute-start | bytes 98312 | tf_op jit(solution)/shard_map/ppermute | solution.py:419
  114.5 1.2 copy-start.13
  114.5 1.2 collective-permute-start.21
  114.5 1.2 copy-start.23
  115.7 1.1 copy-start.8
  129.5 6.1 %collective-permute-start.25 = (f32[16,512]{1,0:T(8,128)}, f32[16,512]{1,0:T(8,128)S(1)}, u32[]{:S(2)}, u32[]{:S(2)}) collective-permute-start(f32[16,512]{1,0:T(8,128)} %get-tuple-element.78), channel_id=1, source_target_pairs={{0,2},{2,0},{1,3},{3,1},{4,6},{6,4},{5,7},{7,5},{8,10},{10,8},{9,1... | collective-permute-start | bytes 98312 | tf_op jit(solution)/shard_map/ppermute | solution.py:418
  130.7 16.2 %collective-permute-start.22 = (f32[16,16,256]{2,1,0:T(8,128)}, f32[16,16,256]{2,1,0:T(8,128)S(1)}, u32[]{:S(2)}, u32[]{:S(2)}) collective-permute-start(f32[16,16,256]{2,1,0:T(8,128)} %get-tuple-element.72), channel_id=1, source_target_pairs={{0,1},{1,0},{2,3},{3,2},{4,5},{5,4},{6,7},{7,6},{8,9},{9,8},{10,11... | collective-permute-start | bytes 786440 | tf_op jit(solution)/shard_map/ppermute | solution.py:414
  131.1 7.6 %collective-permute-start.23 = (f32[1,16,512]{2,1,0:T(8,128)}, f32[1,16,512]{2,1,0:T(8,128)S(1)}, u32[]{:S(2)}, u32[]{:S(2)}) collective-permute-start(f32[1,16,512]{2,1,0:T(8,128)} %get-tuple-element.76), channel_id=1, source_target_pairs={{1,4},{4,1},{5,8},{8,5},{9,12},{12,9},{3,6},{6,3},{7,10},{10,7},{1... | collective-permute-start | bytes 98312 | tf_op jit(solution)/shard_map/ppermute | solution.py:417
  131.8 7.0 %collective-permute-start.24 = (f32[1,16,512]{2,1,0:T(8,128)}, f32[1,16,512]{2,1,0:T(8,128)S(1)}, u32[]{:S(2)}, u32[]{:S(2)}) collective-permute-start(f32[1,16,512]{2,1,0:T(8,128)} %get-tuple-element.77), channel_id=1, source_target_pairs={{0,1},{1,0},{2,3},{3,2},{4,5},{5,4},{6,7},{7,6},{8,9},{9,8},{10,11... | collective-permute-start | bytes 98312 | tf_op jit(solution)/shard_map/ppermute | solution.py:414
  134.9 3.8 %collective-permute-start.26 = (f32[1,512]{1,0:T(1,128)}, f32[1,512]{1,0:T(1,128)S(1)}, u32[]{:S(2)}, u32[]{:S(2)}) collective-permute-start(f32[1,512]{1,0:T(1,128)} %get-tuple-element.79), channel_id=1, source_target_pairs={{1,6},{3,4},{4,3},{6,1},{5,10},{7,8},{8,7},{10,5},{9,14},{11,12},{... | collective-permute-start | bytes 6152 | tf_op jit(solution)/shard_map/ppermute | solution.py:419
  135.6 4.0 %copy-start.20 = (f32[16,512]{1,0:T(8,128)}, f32[16,512]{1,0:T(8,128)S(1)}, u32[]{:S(2)}) copy-start(f32[16,512]{1,0:T(8,128)S(1)} %collective-permute-done.25.refs_9_) | copy-start | bytes 98308
  135.6 3.9 %collective-permute-start.27 = (f32[1,512]{1,0:T(1,128)S(1)}, f32[1,512]{1,0:T(1,128)S(1)}, u32[]{:S(2)}, u32[]{:S(2)}) collective-permute-start(f32[1,512]{1,0:T(1,128)S(1)} %constant_dynamic-slice_fusion), channel_id=1, source_target_pairs={{0,1},{1,0},{2,3},{3,2},{4,5},{5,4},{6,7},{7,6},{8,9},{9,8},{10,11... | collective-permute-start | bytes 6152 | tf_op jit(solution)/shard_map/ppermute | solution.py:414
  140.1 6.6 %copy-start = (f32[19,16,512]{2,1,0:T(8,128)S(1)}, f32[19,16,512]{2,1,0:T(8,128)}, u32[]{:S(2)}) copy-start(f32[19,16,512]{2,1,0:T(8,128)} %get-tuple-element.65.refs_0_) | copy-start | bytes 1867780
  145.4 2.7 %collective-permute-start.28 = (f32[16,16,256]{2,1,0:T(8,128)}, f32[16,16,256]{2,1,0:T(8,128)S(1)}, u32[]{:S(2)}, u32[]{:S(2)}) collective-permute-start(f32[16,16,256]{2,1,0:T(8,128)} %get-tuple-element.81), channel_id=1, source_target_pairs={{0,1},{1,0},{2,3},{3,2},{4,5},{5,4},{6,7},{7,6},{8,9},{9,8},{10,11... | collective-permute-start | bytes 786440 | tf_op jit(solution)/shard_map/ppermute | solution.py:414
  146.8 1.4 copy-start.17
  (14 other events, 10.5 us)

commit v2 on v1

v2 whole, which is shorter than its diff:
```python
import functools

import jax
import jax.numpy as jnp
from jax import lax
from jax.experimental import pallas as pl
from jax.experimental.pallas import tpu as pltpu
from jax.sharding import PartitionSpec as P


NOFF = 17
MARGIN = 16
TILE = 8
F32 = jnp.float32
UNROLL = 4
SLACK = 8 << 20


class Geometry:
    def __init__(self, rows, depth, half, sections):
        self.B, self.Z, self.H, self.Y = rows // 2, depth, half, 2 * half
        self.two = sections == 2
        self.sides = 1 if self.two else 2
        self.ZE = depth + TILE * self.sides
        assert self.B >= MARGIN and depth % TILE == 0 and half % 128 == 0


def near_side(side, geo):
    first = (geo.B - 2) + side * (geo.B + 2)
    return first, first + 1 - side


def tile_mask(sender, depth, turn, width):
    place = lax.broadcasted_iota(jnp.int32, (TILE, width), 0)
    place = lax.rem(place + (TILE - turn), TILE)
    start = (1 - sender) * (TILE - depth)
    return (place >= start) & (place < start + depth)


def turned(value, turn):
    turn = turn % TILE
    return value if turn == 0 else pltpu.roll(value, turn, 0)


def senders(s, geo):
    return [s] if geo.two else [0, 1]


def receivers(s, geo):
    return [(geo.Z, 1 - s)] if geo.two else [(geo.ZE - TILE, 0), (geo.Z, 1)]


def edge_tile(ref, row, sender, geo):
    start = pl.multiple_of((1 - sender) * (geo.Z - TILE), TILE)
    return ref[row, pl.ds(start, TILE), :]


def pack_corner(items, row, sender, geo):
    out = jnp.zeros((TILE, geo.Y), F32)
    for ref, depth, turn in items:
        value = turned(edge_tile(ref, row, sender, geo), turn)
        out = jnp.where(tile_mask(sender, depth, turn, geo.Y), value, out)
    return out


def tiles_of(depths, geo):
    starts, total = [], 0
    for depth in depths:
        starts.append(total)
        total += geo.B * depth // TILE
    return starts, total


def pack_tiles(items, g, s, tiles, corners, geo):
    starts, _ = tiles_of([depth for _, depth, _ in items], geo)
    for sender, tile_ref, corner_ref in zip(senders(s, geo), tiles, corners):
        for (ref, depth, _), start in zip(items, starts):
            per = TILE // depth
            masks = [tile_mask(sender, depth, k * depth, geo.Y) for k in range(1, per)]
            for q in range(geo.B // per):
                out = edge_tile(ref, q * per, sender, geo)
                for k in range(1, per):
                    value = turned(edge_tile(ref, q * per + k, sender, geo), k * depth)
                    out = jnp.where(masks[k - 1], value, out)
                tile_ref[start + q] = out
        for k in range(corner_ref.shape[0]):
            row = g * (geo.B - corner_ref.shape[0]) + k
            corner_ref[k] = pack_corner(items, row, sender, geo)


def unpack_row(ref, start, x, depth, sender, geo):
    per = TILE // depth
    value = turned(ref[start + x // per], TILE - (x % per) * depth)
    return jnp.where(tile_mask(sender, depth, 0, geo.Y), value, 0.0)


def fill(dst, own, xrow, crow, tiles, xtiles, ctiles, start, depth, turn, g, s, geo):
    ends = list(zip(receivers(s, geo), tiles, xtiles, ctiles))

    def one(row, carry):
        dst[geo.B + row, 0 : geo.Z, :] = own[row]
        return carry

    lax.fori_loop(0, geo.B, one, 0, unroll=4)
    for (offset, sender), tile, _, _ in ends:
        for row in range(geo.B):
            dst[geo.B + row, offset : offset + TILE, :] = unpack_row(tile, start, row, depth, sender, geo)
    for side, get, is_x in ((g, xrow, True), (1 - g, crow, False)):
        first, nearest = near_side(side, geo)
        for k in range(depth):
            place = first + k if depth == 2 else nearest
            if get is not None:
                dst[place, 0 : geo.Z, :] = get(k)
            for (offset, sender), _, xtile, ctile in ends:
                if is_x:
                    index = k if depth == xtile.shape[0] else 1 - side
                    value = turned(xtile[index], TILE - turn)
                    value = jnp.where(tile_mask(sender, depth, 0, geo.Y), value, 0.0)
                else:
                    low = unpack_row(ctile, start, k, depth, sender, geo)
                    high = unpack_row(ctile, start, geo.B - depth + k, depth, sender, geo)
                    value = jnp.where(side == 1, low, high)
                dst[place, offset : offset + TILE, :] = value


def fill_blocks(dst, xblock, cblock, g, geo):
    def one(row, carry):
        dst[g * 2 * geo.B + row, 0 : geo.Z, :] = xblock[row]
        dst[(1 - g) * 2 * geo.B + row, 0 : geo.Z, :] = cblock[row]
        return carry

    lax.fori_loop(0, geo.B, one, 0)


def each(first, count, body, group):
    group = max(k for k in range(1, group + 1) if count % k == 0)

    def trip(index, carry):
        for k in range(group):
            body(first + index * group + k)
        return carry

    lax.fori_loop(0, count // group, trip, 0)


def advance(src, first, count, prior, extra, store, coefs, dif, tot, geo):
    xx, zz, yy, xz = coefs

    def rolls(row):
        value = src[row]
        above = pltpu.roll(value, geo.ZE - 1, 0)
        below = pltpu.roll(value, 1, 0)
        dif[row] = above - below
        tot[row] = above + below

    each(first - 1, count + 2, rolls, 6)
    lane = lax.broadcasted_iota(jnp.int32, (geo.ZE, geo.Y), 1)

    def one(row):
        at = row - (geo.B - 1)
        value = src[row]
        right = jnp.where(lane == geo.Y - 1, 0.0, pltpu.roll(value, geo.Y - 1, 1))
        left = jnp.where(lane == 0, 0.0, pltpu.roll(value, 1, 1))
        cx, cz, cy = xx[at], zz[at], yy[at]
        out = (2.0 - 2.0 * (cx + cz + cy)) * value - prior(row)
        out = out + cx * (src[row + 1] + src[row - 1]) + cz * tot[row] + cy * (right + left)
        out = out + xz[at] * (dif[row + 1] - dif[row - 1])
        if extra is not None:
            out = out + extra(row)
        store(row, out)

    each(first, count, one, UNROLL)


def make_source(ext, refl, refl_far, offsets, courant, out, g, geo):
    near = pl.multiple_of(g * geo.H, 128)
    far = pl.multiple_of((1 - g) * geo.H, 128)

    def one(row):
        acc = jnp.zeros((geo.Z, geo.H), F32)
        acc_far = jnp.zeros((geo.Z, geo.H), F32)
        for h in range(NOFF):
            place = geo.B + row + offsets[h]
            acc = acc + refl[h, g * geo.B + row].astype(F32) * ext[place, 0 : geo.Z, pl.ds(near, geo.H)]
            acc_far = acc_far + refl_far[h, row] * ext[place, 0 : geo.Z, pl.ds(far, geo.H)]
        out[row, :, pl.ds(near, geo.H)] = courant[row, :, pl.ds(near, geo.H)] * acc
        out[row, :, pl.ds(far, geo.H)] = courant[row, :, pl.ds(far, geo.H)] * acc_far

    each(0, geo.B, one, 2)


def edge_rows(depth, side, geo):
    return side * (geo.B - depth)


def trig_products(angle):
    turns = jnp.floor(angle * 0.6366197723675814 + 0.5)
    rest = angle - turns * 1.5703125
    rest = rest - turns * 4.837512969970703125e-4
    rest = rest - turns * 7.549789954891882e-8
    odd = (turns - 2.0 * jnp.floor(turns * 0.5)) > 0.5
    square = rest * rest
    sine = rest + rest * square * (
        -1.6666654611e-1 + square * (8.3321608736e-3 + square * -1.9515295891e-4)
    )
    cosine = 1.0 - 0.5 * square + square * square * (
        4.166664568298827e-2 + square * (-1.388731625493765e-3 + square * 2.443315711809948e-5)
    )
    sine_square = jnp.where(odd, cosine * cosine, sine * sine)
    cosine_square = jnp.where(odd, sine * sine, cosine * cosine)
    product = sine * cosine
    return sine_square, cosine_square, jnp.where(odd, -product, product)


def half_kernel(geo, scal, *refs):
    *fields, out = refs

    def one(row, carry):
        for k, field in enumerate(fields):
            out[k, row] = field[row]
        return carry

    lax.fori_loop(0, geo.B, one, 0, unroll=4)


def widen_kernel(geo, scal, refl, out):
    def one(h, carry):
        for row in range(geo.B):
            out[h, row] = refl[h, row].astype(F32)
        return carry

    lax.fori_loop(0, NOFF, one, 0)


def join_kernel(geo, scal, *refs):
    raw, far = refs[:5], refs[5]
    own = refs[6:11]
    px, pc = refs[11], refs[12]
    tiles, corners = refs[13 : 13 + geo.sides], refs[13 + geo.sides :]
    g, s = scal[0], scal[1]
    near_y = pl.multiple_of(g * geo.H, 128)
    far_y = pl.multiple_of((1 - g) * geo.H, 128)

    def one(row, carry):
        for k in range(5):
            own[k][row, :, pl.ds(near_y, geo.H)] = raw[k][row]
            own[k][row, :, pl.ds(far_y, geo.H)] = far[k, row]
        return carry

    lax.fori_loop(0, geo.B, one, 0, unroll=2)
    for side, out in ((g, px), (1 - g, pc)):
        for k in range(2):
            out[k] = own[0][edge_rows(2, side, geo) + k]
        for k in range(1, 5):
            out[1 + k] = own[k][edge_rows(1, side, geo)]
    items = [(own[0], 2, 0)] + [(own[k], 1, 1 + k) for k in range(1, 5)]
    pack_tiles(items, g, s, tiles, corners, geo)


def first_kernel(geo, scal, *refs):
    n = geo.sides
    now, before, courant, aniso, tilt, xr, cr = refs[:7]
    tiles, xtiles, ctiles = refs[7 : 7 + n], refs[7 + n : 7 + 2 * n], refs[7 + 2 * n : 7 + 3 * n]
    out_block, prior_ext, xx, zz, yy, xz = refs[7 + 3 * n : 13 + 3 * n]
    out_tiles, out_corners = refs[13 + 3 * n : 13 + 4 * n], refs[13 + 4 * n : 13 + 5 * n]
    ext, old, dif, tot, mid, ca, cb, cc = refs[13 + 5 * n :]
    g, s = scal[0], scal[1]
    starts, _ = tiles_of([2, 1, 1, 1, 1], geo)
    for k, (dst, own) in enumerate(((old, before), (ca, courant), (cb, aniso), (cc, tilt)), 1):
        xrow, crow = (lambda _, k=k: xr[1 + k]), (lambda _, k=k: cr[1 + k])
        fill(dst, own, xrow, crow, tiles, xtiles, ctiles, starts[k], 1, 1 + k, g, s, geo)
    fill(ext, now, lambda k: xr[k], lambda k: cr[k], tiles, xtiles, ctiles, 0, 2, 0, g, s, geo)

    def coefficients(row, carry):
        at = row - (geo.B - 1)
        speed, stretch = ca[row], 2.0 * cb[row]
        sine_square, cosine_square, product = trig_products(cc[row])
        xx[at] = speed * (1.0 + stretch * cosine_square)
        zz[at] = speed * (1.0 + stretch * sine_square)
        yy[at] = speed * (1.0 + stretch)
        xz[at] = (0.5 * speed) * (stretch * product)
        return carry

    lax.fori_loop(geo.B - 1, 2 * geo.B + 1, coefficients, 0)
    two_steps(ext, mid, lambda row: old[row], prior_ext, out_block, (xx, zz, yy, xz), dif, tot, geo)
    pack_tiles([(out_block, 2, 0)], g, s, out_tiles, out_corners, geo)


def two_steps(ext, mid, prior, prior_ext, out_block, coefs, dif, tot, geo):
    def keep(row, value):
        mid[row] = value
        prior_ext[row - (geo.B - 1)] = value

    def keep_block(row, value):
        out_block[row - geo.B] = value[0 : geo.Z]

    advance(ext, geo.B - 1, geo.B + 2, prior, None, keep, coefs, dif, tot, geo)
    advance(mid, geo.B, geo.B, lambda row: ext[row], None, keep_block, coefs, dif, tot, geo)


def second_kernel(geo, scal, offsets, *refs):
    n = geo.sides
    now, before, xr, cr, courant, refl, refl_far, *coefs = refs[:11]
    tiles, xtiles, ctiles = refs[11 : 11 + n], refs[11 + n : 11 + 2 * n], refs[11 + 2 * n : 11 + 3 * n]
    px, pc, prior_ext, force = refs[11 + 3 * n : 15 + 3 * n]
    out_tiles, out_corners = refs[15 + 3 * n : 15 + 4 * n], refs[15 + 4 * n : 15 + 5 * n]
    ext, dif, tot, mid = refs[15 + 5 * n :]
    g, s = scal[0], scal[1]
    fill(ext, now, None, None, tiles, xtiles, ctiles, 0, 2, 0, g, s, geo)
    fill_blocks(ext, xr, cr, g, geo)
    two_steps(ext, mid, lambda row: before[row - (geo.B - 1)], prior_ext, px, coefs, dif, tot, geo)
    make_source(ext, refl, refl_far, offsets, courant, force, g, geo)

    def one(row, carry):
        pc[row] = px[row]
        return carry

    lax.fori_loop(0, geo.B, one, 0)
    for side, out in ((g, px), (1 - g, pc)):
        for k in range(2):
            out[geo.B + k] = force[edge_rows(2, side, geo) + k]
    pack_tiles([(px, 2, 0), (force, 2, 4)], g, s, out_tiles, out_corners, geo)


def third_kernel(geo, scal, offsets, *refs):
    n = geo.sides
    now, before, xr, cr, courant, refl, refl_far, *coefs = refs[:11]
    force = refs[11]
    tiles, xtiles, ctiles = refs[12 : 12 + n], refs[12 + n : 12 + 2 * n], refs[12 + 2 * n : 12 + 3 * n]
    px, pc, force_out, scat, scat_prior = refs[12 + 3 * n : 17 + 3 * n]
    out_tiles, out_corners = refs[17 + 3 * n : 17 + 4 * n], refs[17 + 4 * n : 17 + 5 * n]
    ext, dif, tot, mid, wave = refs[17 + 5 * n :]
    g, s = scal[0], scal[1]
    B = geo.B
    fill(ext, now, None, None, tiles, xtiles, ctiles, 0, 2, 0, g, s, geo)
    fill_blocks(ext, xr, cr, g, geo)

    def keep_mid(row, value):
        mid[row] = value

    def keep_block(row, value):
        px[row - B] = value[0 : geo.Z]
        pc[row - B] = value[0 : geo.Z]

    advance(ext, B - 1, B + 2, lambda row: before[row - (B - 1)], None, keep_mid, coefs, dif, tot, geo)
    advance(mid, B, B, lambda row: ext[row], None, keep_block, coefs, dif, tot, geo)
    make_source(ext, refl, refl_far, offsets, courant, force_out, g, geo)
    start = tiles_of([2, 2], geo)[0][1]
    fill(wave, force, lambda k: xr[B + k], lambda k: cr[B + k], tiles, xtiles, ctiles, start, 2, 4, g, s, geo)

    def keep_wave(row, value):
        mid[row] = value
        scat_prior[row - (B - 1)] = value

    def keep_scat(row, value):
        scat[row - B] = value[0 : geo.Z] + force_out[row - B]

    advance(wave, B - 1, B + 2, lambda row: -wave[row], None, keep_wave, coefs, dif, tot, geo)
    advance(mid, B, B, lambda row: wave[row], None, keep_scat, coefs, dif, tot, geo)
    for side, out in ((g, px), (1 - g, pc)):
        for k in range(2):
            out[B + k] = scat[edge_rows(2, side, geo) + k]
        out[B + 2] = force_out[edge_rows(1, side, geo)]
    pack_tiles([(scat, 2, 0), (force_out, 1, 2)], g, s, out_tiles, out_corners, geo)


def fourth_kernel(geo, scal, offsets, *refs):
    n = geo.sides
    now, scat, before, xr, cr, courant, refl, refl_far, *coefs = refs[:12]
    force2 = refs[12]
    tiles, xtiles, ctiles = refs[13 : 13 + n], refs[13 + n : 13 + 2 * n], refs[13 + 2 * n : 13 + 3 * n]
    scat_out, scat_prior, force_out, px, pc, near, back = refs[13 + 3 * n : 20 + 3 * n]
    out_tiles, out_corners = refs[20 + 3 * n : 20 + 4 * n], refs[20 + 4 * n : 20 + 5 * n]
    ext, dif, tot, mid, wave = refs[20 + 5 * n :]
    g, s = scal[0], scal[1]
    B = geo.B

    def own(row, carry):
        ext[B + row, 0 : geo.Z, :] = now[row]
        back[row] = now[row, :, pl.ds(pl.multiple_of((1 - g) * geo.H, 128), geo.H)]
        near[row] = now[row, :, pl.ds(pl.multiple_of(g * geo.H, 128), geo.H)]
        return carry

    lax.fori_loop(0, B, own, 0)
    fill_blocks(ext, xr, cr, g, geo)
    make_source(ext, refl, refl_far, offsets, courant, force_out, g, geo)
    fill(wave, scat, lambda k: xr[B + k], lambda k: cr[B + k], tiles, xtiles, ctiles, 0, 2, 0, g, s, geo)
    start = tiles_of([2, 1], geo)[0][1]
    fill(ext, force2, lambda _: xr[B + 2], lambda _: cr[B + 2], tiles, xtiles, ctiles, start, 1, 2, g, s, geo)

    def keep_wave(row, value):
        mid[row] = value

    def keep_scat(row, value):
        scat_out[row - B] = value[0 : geo.Z] + force_out[row - B]
        scat_prior[row - B] = mid[row, 0 : geo.Z, :]

    advance(wave, B - 1, B + 2, lambda row: before[row - (B - 1)], lambda row: ext[row], keep_wave, coefs, dif, tot, geo)
    advance(mid, B, B, lambda row: wave[row], None, keep_scat, coefs, dif, tot, geo)
    px[0] = scat_out[edge_rows(1, g, geo)]
    pc[0] = scat_out[edge_rows(1, 1 - g, geo)]
    pack_tiles([(scat_out, 1, 0)], g, s, out_tiles, out_corners, geo)


def fifth_kernel(geo, scal, *refs):
    n = geo.sides
    scat, before, force, xr, cr, *coefs = refs[:9]
    tiles, xtiles, ctiles = refs[9 : 9 + n], refs[9 + n : 9 + 2 * n], refs[9 + 2 * n : 9 + 3 * n]
    out_near, out_far = refs[9 + 3 * n : 11 + 3 * n]
    ext, dif, tot = refs[11 + 3 * n :]
    g, s = scal[0], scal[1]
    B = geo.B
    fill(ext, scat, lambda _: xr[0], lambda _: cr[0], tiles, xtiles, ctiles, 0, 1, 0, g, s, geo)
    low, high = slice(0, geo.H), slice(geo.H, geo.Y)

    def keep(row, value):
        at = row - B
        value = value[0 : geo.Z] - before[at] + force[at]
        out_near[at] = jnp.where(g == 0, value[:, low], value[:, high])
        out_far[at] = jnp.where(g == 0, value[:, high], value[:, low])

    advance(ext, B, B, lambda row: 0.0, None, keep, coefs, dif, tot, geo)


def finish_kernel(geo, scal, near, far, out):
    g = scal[0]

    def one(row, carry):
        out[g * geo.B + row] = near[row]
        out[(1 - g) * geo.B + row] = far[row]
        return carry

    lax.fori_loop(0, geo.B, one, 0, unroll=4)


def shards(sections, gx, wave_now, wave_before, courant, anisotropy, tilt, reflectivity, offsets):
    rows, depth, half = wave_now.shape
    geo = Geometry(rows, depth, half, sections)
    B, Z, H, Y, ZE, n = geo.B, geo.Z, geo.H, geo.Y, geo.ZE, geo.sides
    g = lax.axis_index("gy")
    s = lax.axis_index("section")
    scal = jnp.stack([g, s]).astype(jnp.int32)
    swap = [(0, 1), (1, 0)]
    pairs_x = [p for i in range(gx - 1) for p in ((2 * i + 1, 2 * i + 2), (2 * i + 2, 2 * i + 1))]

    def z_moves():
        if geo.two:
            return [[(0, 1), (1, 0)]]
        return [[(i, i + 1) for i in range(sections - 1)], [(i + 1, i) for i in range(sections - 1)]]

    def corner_pairs(move):
        out = []
        for a, b in pairs_x:
            for i, j in move:
                out.append((((a // 2) * sections + i) * 2 + a % 2, ((b // 2) * sections + j) * 2 + b % 2))
        return out

    def chip(value):
        return lax.ppermute(value, "gy", swap)

    def exchange(px, pc, tiles, corners):
        xr = lax.ppermute(px, ("gx", "gy"), pairs_x)
        xz = [
            lax.ppermute(t, ("gx", "section", "gy"), corner_pairs(m)) for t, m in zip(corners, z_moves())
        ]
        zr = [lax.ppermute(t, "section", m) for t, m in zip(tiles, z_moves())]
        cr = chip(pc)
        cz = [chip(t) for t in zr]
        return xr, cr, [*zr, *xz, *cz]

    def shape(*dims):
        return jax.ShapeDtypeStruct(dims, F32)

    def call(kernel, inputs, outs, scratch, smem=1, specs=None):
        if specs is None:
            specs = [pl.BlockSpec(memory_space=pltpu.SMEM)] * (smem - 1)
            specs += [pl.BlockSpec(memory_space=pltpu.VMEM)] * (len(inputs) - smem)
        used = sum(4 * d[0] * d[1] * d[2] for d in scratch)
        return pl.pallas_call(
            functools.partial(kernel, geo),
            out_shape=outs,
            grid_spec=pltpu.PrefetchScalarGridSpec(
                num_scalar_prefetch=1,
                grid=(1,),
                in_specs=specs,
                out_specs=[pl.BlockSpec(memory_space=pltpu.VMEM)] * len(outs),
                scratch_shapes=[pltpu.VMEM(d, F32) for d in scratch],
            ),
            compiler_params=pltpu.CompilerParams(vmem_limit_bytes=used + SLACK),
        )(*inputs)

    block, wide, ext = (B, Z, Y), (B + 2, ZE, Y), (3 * B, ZE, Y)

    def tile_outs(depths, corner=2):
        return [shape(tiles_of(depths, geo)[1], TILE, Y)] * n + [shape(corner, TILE, Y)] * n

    fields = (wave_now, wave_before, courant, anisotropy, tilt)
    near_half = pl.BlockSpec((B, Z, H), lambda i, scal: (scal[0], 0, 0))
    far_half = pl.BlockSpec((B, Z, H), lambda i, scal: (1 - scal[0], 0, 0))
    whole = pl.BlockSpec(memory_space=pltpu.VMEM)
    (sent,) = call(half_kernel, [scal, *fields], [shape(5, B, Z, H)], [], specs=[far_half] * 5)
    far = chip(sent)
    *own, px, pc, r0, r1 = _split(
        call(
            join_kernel,
            [scal, *fields, far],
            [shape(*block)] * 5 + [shape(6, Z, Y)] * 2 + tile_outs([2, 1, 1, 1, 1]),
            [],
            specs=[near_half] * 5 + [whole],
        ),
        7,
        n,
    )
    xr, cr, halo = exchange(px, pc, r0, r1)
    refl_half = pl.BlockSpec((NOFF, B, Z, H), lambda i, scal: (0, 1 - scal[0], 0, 0))
    (refl_far,) = call(widen_kernel, [scal, reflectivity], [shape(NOFF, B, Z, H)], [], specs=[refl_half])
    refl_far = chip(refl_far)
    now, prior, *coefs, r0, r1 = _split(
        call(
            first_kernel, [scal, *own, xr, cr, *halo], [shape(*block)] + [shape(*wide)] * 5 + tile_outs([2]), [ext] * 8
        ),
        6,
        n,
    )
    xr, cr, halo = exchange(now, now, r0, r1)
    px, pc, prior, force, r0, r1 = _split(
        call(
            second_kernel,
            [scal, offsets, now, prior, xr, cr, own[2], reflectivity, refl_far, *coefs, *halo],
            [shape(B + 2, Z, Y)] * 2 + [shape(*wide), shape(*block)] + tile_outs([2, 2]),
            [ext] * 4,
            2,
        ),
        4,
        n,
    )
    xr, cr, halo = exchange(px, pc, r0, r1)
    px, pc, force2, scat, scat_prior, r0, r1 = _split(
        call(
            third_kernel,
            [scal, offsets, px, prior, xr, cr, own[2], reflectivity, refl_far, *coefs, force, *halo],
            [shape(B + 3, Z, Y)] * 2 + [shape(*block)] * 2 + [shape(*wide)] + tile_outs([2, 1]),
            [ext] * 5,
            2,
        ),
        5,
        n,
    )
    xr, cr, halo = exchange(px, pc, r0, r1)
    scat, scat_prior, force3, qx, qc, near_u, back, r0, r1 = _split(
        call(
            fourth_kernel,
            [scal, offsets, px, scat, scat_prior, xr, cr, own[2], reflectivity, refl_far, *coefs, force2, *halo],
            [shape(*block)] * 3 + [shape(1, Z, Y)] * 2 + [shape(B, Z, H)] * 2 + tile_outs([1], 1),
            [ext] * 5,
            2,
        ),
        7,
        n,
    )
    xr, cr, halo = exchange(qx, qc, r0, r1)
    back = chip(back)
    (background,) = call(finish_kernel, [scal, near_u, back], [shape(rows, Z, H)], [])
    near_w, far_w = call(
        fifth_kernel, [scal, scat, scat_prior, force3, xr, cr, *coefs, *halo], [shape(B, Z, H)] * 2, [ext] * 3
    )
    (scattered,) = call(finish_kernel, [scal, near_w, chip(far_w)], [shape(rows, Z, H)], [])
    return background, scattered


def _split(values, count, n):
    return [*values[:count], values[count : count + n], values[count + n :]]


def solution(mesh):
    spec = P(("shot", "gx"), "section", "gy")
    assert mesh.shape["gy"] == 2
    return jax.shard_map(
        functools.partial(shards, mesh.shape["section"], mesh.shape["gx"]),
        mesh=mesh,
        in_specs=(spec,) * 5 + (P(None, ("shot", "gx"), "section", "gy"), P()),
        out_specs=(spec, spec),
        check_vma=False,
    )
```

time: 149 us -> 110 us (0.74)
  Pallas kernels: 62.3 us -> 28 us
  starting transfers between devices: 34.7 us -> 56.3 us
  waiting for transfers between devices: 35.1 us -> 22.1 us
  other arithmetic: 6.82 us -> 0.08 us
  local copies, waits for them, and re-layouts: 8.97 us -> 2.31 us
    pallas_call x6 -> x10, Pallas kernels: 62.3 us -> 28 us  [call(): pl.pallas_call(functools.partial(kernel, geo), out_shape=outs, grid_spec=...]
    ppermute x14, starting transfers between devices: 21.9 us -> 40.7 us  [chip(): return lax.ppermute(value, 'gy', swap)]
    ppermute x5, waiting for transfers between devices: 24.6 us -> 11.6 us  [exchange(): zr = [lax.ppermute(t, 'section', m) for t, m in zip(tiles, z_moves())]]
    unnamed x70 -> x18, local copies, waits for them, and re-layouts: 8.16 us -> 2.31 us
    convert_element_type x1 -> x0, other arithmetic: 4.48 us -> none  [shards(): lax.dynamic_slice_in_dim(reflectivity, other, B, 1).astype(F32)]
    ppermute x5, starting transfers between devices: 6.15 us -> 8.94 us  [exchange(): zr = [lax.ppermute(t, 'section', m) for t, m in zip(tiles, z_moves())]]
    select_n x2 -> x0, other arithmetic: 1.69 us -> none  [joined(): jnp.where(g == 0, jnp.concatenate([near, other], 0), jnp.concatenate([oth...]
  transfers between devices with their start and end apart: 29 -> 29, of which waited for: 11 -> 9; matrix products, arithmetic and copies ran while one was open for 3% -> 0% of each run, Pallas kernels for 13% -> 8%
where the time goes in v2:
time: 110 us
  starting transfers between devices  56.3 us (51%)
  Pallas kernels  28 us (25%)
  waiting for transfers between devices  22.1 us (20%)
  local copies, waits for them, and re-layouts  2.31 us (2%)
    ppermute x14, starting transfers between devices, chip(): return lax.ppermute(value, 'gy', swap)  40.7 us
    pallas_call x10, Pallas kernels, call(): pl.pallas_call(functools.partial(kernel, geo), out_shape=outs, grid_spec=...  28 us
    ppermute x5, waiting for transfers between devices, exchange(): zr = [lax.ppermute(t, 'section', m) for t, m in zip(tiles, z_moves())]  11.6 us
    ppermute x14, waiting for transfers between devices, chip(): return lax.ppermute(value, 'gy', swap)  10.5 us
    ppermute x5, starting transfers between devices, exchange(): zr = [lax.ppermute(t, 'section', m) for t, m in zip(tiles, z_moves())]  8.94 us
    ppermute x5, starting transfers between devices, exchange(): xr = lax.ppermute(px, ('gx', 'gy'), pairs_x)  3.41 us
    ppermute x5, starting transfers between devices, exchange(): lax.ppermute(t, ('gx', 'section', 'gy'), corner_pairs(m))  3.26 us
    unnamed x18, local copies, waits for them, and re-layouts  2.31 us
  transfers between devices with their start and end apart: 29, of which 9 were waited for; matrix products, arithmetic and copies ran while one was open for 0% of the time, Pallas kernels for 8%

profile of v2, /device:TPU:0, one launch (start us, length us, event | category | flops | bytes accessed | tf_op | source)
XLA Modules:
  0.0 109.7 jit_solution(12326013826068696057)
XLA Ops:
  0.6 0.1 pad_add_fusion.scal
  0.7 2.3 %copy-done = bf16[17,32,16,256]{3,2,1,0:T(8,128)(2,1)S(1)} copy-done((bf16[17,32,16,256]{3,2,1,0:T(8,128)(2,1)S(1)}, bf16[17,32,16,256]{3,2,1,0:T(8,128)(2,1)}, u32[]{:S(2)}) %copy-start) | copy-done | bytes 4456472
  3.0 1.0 shard_map.89
  4.1 0.0 slice-start.1
  4.1 0.6 collective-permute-start.8
  4.6 0.0 copy-done.5
  4.7 0.6 shard_map.86
  5.3 0.6 collective-permute-start
  5.9 7.8 %collective-permute-done.refs_5_ = f32[5,16,16,256]{3,2,1,0:T(8,128)S(1)} collective-permute-done((f32[5,16,16,256]{3,2,1,0:T(8,128)S(1)}, f32[5,16,16,256]{3,2,1,0:T(8,128)S(1)}, u32[]{:S(2)}, u32[]{:S(2)}) %collective-permute-start) | collective-permute-done | bytes 1310752 | tf_op jit(solution)/shard_map/ppermute | solution.py:459
  13.7 0.9 shard_map.87
  14.5 2.9 %collective-permute-start.3 = (f32[12,8,512]{2,1,0:T(8,128)S(1)}, f32[12,8,512]{2,1,0:T(8,128)S(1)}, u32[]{:S(2)}, u32[]{:S(2)}) collective-permute-start(f32[12,8,512]{2,1,0:T(8,128)S(1)} %get-tuple-element.50), channel_id=1, source_target_pairs={{0,2},{2,0},{1,3},{3,1},{4,6},{6,4},{5,7},{7,5},{8,10},{10,8},{9,1... | collective-permute-start | bytes 589832 | tf_op jit(solution)/shard_map/ppermute | solution.py:466
  17.5 0.7 collective-permute-start.1
  18.1 3.0 %collective-permute-start.2 = (f32[6,16,512]{2,1,0:T(8,128)S(1)}, f32[6,16,512]{2,1,0:T(8,128)S(1)}, u32[]{:S(2)}, u32[]{:S(2)}) collective-permute-start(f32[6,16,512]{2,1,0:T(8,128)S(1)} %get-tuple-element.49), channel_id=1, source_target_pairs={{0,1},{1,0},{2,3},{3,2},{4,5},{5,4},{6,7},{7,6},{8,9},{9,8},{10,11... | collective-permute-start | bytes 589832 | tf_op jit(solution)/shard_map/ppermute | solution.py:459
  21.1 1.5 %collective-permute-done.3.refs_7_ = f32[12,8,512]{2,1,0:T(8,128)S(1)} collective-permute-done((f32[12,8,512]{2,1,0:T(8,128)S(1)}, f32[12,8,512]{2,1,0:T(8,128)S(1)}, u32[]{:S(2)}, u32[]{:S(2)}) %collective-permute-start.3) | collective-permute-done | bytes 196640 | tf_op jit(solution)/shard_map/ppermute | solution.py:466
  22.7 0.7 collective-permute-start.4
  23.4 0.7 collective-permute-done.5.refs_9_
  24.1 4.6 %shard_map.88 = (f32[16,16,512]{2,1,0:T(8,128)S(1)}, f32[18,24,512]{2,1,0:T(8,128)S(1)}, f32[18,24,512]{2,1,0:T(8,128)S(1)}, f32[18,24,512]{2,1,0:T(8,128)S(1)},...) custom-call(s32[2]{0:T(128)S(1)} %pad_add_fusion.scal, ...), custom_call_target="tpu_custom_call" | custom-call | tf_op jit(solution)/shard_map/pallas_call | solution.py:479
  28.8 0.7 collective-permute-start.6
  29.5 7.9 %collective-permute-start.7 = (f32[16,16,512]{2,1,0:T(8,128)S(1)}, f32[16,16,512]{2,1,0:T(8,128)S(1)}, u32[]{:S(2)}, u32[]{:S(2)}) collective-permute-start(f32[16,16,512]{2,1,0:T(8,128)S(1)} %get-tuple-element.52.refs_0_), channel_id=1, source_target_pairs={{0,1},{1,0},{2,3},{3,2},{4,5},{5,4},{6,7},{7,6},{8,9},{9,8},{10,11... | collective-permute-start | bytes 1572872 | tf_op jit(solution)/shard_map/ppermute | solution.py:459
  37.4 1.5 %collective-permute-start.9 = (f32[4,8,512]{2,1,0:T(8,128)S(1)}, f32[4,8,512]{2,1,0:T(8,128)S(1)}, u32[]{:S(2)}, u32[]{:S(2)}) collective-permute-start(f32[4,8,512]{2,1,0:T(8,128)S(1)} %get-tuple-element.58), channel_id=1, source_target_pairs={{0,2},{2,0},{1,3},{3,1},{4,6},{6,4},{5,7},{7,5},{8,10},{10,8},{9,1... | collective-permute-start | bytes 196616 | tf_op jit(solution)/shard_map/ppermute | solution.py:466
  38.9 2.8 %collective-permute-done.9.refs_11_ = f32[4,8,512]{2,1,0:T(8,128)S(1)} collective-permute-done((f32[4,8,512]{2,1,0:T(8,128)S(1)}, f32[4,8,512]{2,1,0:T(8,128)S(1)}, u32[]{:S(2)}, u32[]{:S(2)}) %collective-permute-start.9) | collective-permute-done | bytes 65568 | tf_op jit(solution)/shard_map/ppermute | solution.py:466
  41.7 0.7 collective-permute-start.10
  42.3 0.6 collective-permute-done.11.refs_13_
  43.0 4.8 %shard_map.90 = (f32[18,16,512]{2,1,0:T(8,128)S(1)}, f32[18,16,512]{2,1,0:T(8,128)S(1)}, f32[18,24,512]{2,1,0:T(8,128)S(1)}, f32[16,16,512]{2,1,0:T(8,128)S(1)},...) custom-call(s32[2]{0:T(128)S(1)} %pad_add_fusion.scal, s32[17]{0:T(128)S(1)} %copy-done.6, ...), custom_call_target="tpu_custom_call" | custom-call | tf_op jit(solution)/shard_map/pallas_call | solution.py:479
  47.8 0.7 collective-permute-start.12
  48.5 7.8 %collective-permute-start.13 = (f32[18,16,512]{2,1,0:T(8,128)S(1)}, f32[18,16,512]{2,1,0:T(8,128)S(1)}, u32[]{:S(2)}, u32[]{:S(2)}) collective-permute-start(f32[18,16,512]{2,1,0:T(8,128)S(1)} %get-tuple-element.62), channel_id=1, source_target_pairs={{0,1},{1,0},{2,3},{3,2},{4,5},{5,4},{6,7},{7,6},{8,9},{9,8},{10,11... | collective-permute-start | bytes 1769480 | tf_op jit(solution)/shard_map/ppermute | solution.py:459
  56.3 1.5 %collective-permute-start.14 = (f32[8,8,512]{2,1,0:T(8,128)S(1)}, f32[8,8,512]{2,1,0:T(8,128)S(1)}, u32[]{:S(2)}, u32[]{:S(2)}) collective-permute-start(f32[8,8,512]{2,1,0:T(8,128)S(1)} %get-tuple-element.64), channel_id=1, source_target_pairs={{0,2},{2,0},{1,3},{3,1},{4,6},{6,4},{5,7},{7,5},{8,10},{10,8},{9,1... | collective-permute-start | bytes 393224 | tf_op jit(solution)/shard_map/ppermute | solution.py:466
  57.8 4.0 %collective-permute-done.14.refs_12_ = f32[8,8,512]{2,1,0:T(8,128)S(1)} collective-permute-done((f32[8,8,512]{2,1,0:T(8,128)S(1)}, f32[8,8,512]{2,1,0:T(8,128)S(1)}, u32[]{:S(2)}, u32[]{:S(2)}) %collective-permute-start.14) | collective-permute-done | bytes 131104 | tf_op jit(solution)/shard_map/ppermute | solution.py:466
  61.8 0.7 collective-permute-start.15
  62.5 0.7 collective-permute-done.16.refs_14_
  63.1 6.9 %shard_map.91 = (f32[19,16,512]{2,1,0:T(8,128)S(1)}, f32[19,16,512]{2,1,0:T(8,128)S(1)}, f32[16,16,512]{2,1,0:T(8,128)S(1)}, f32[16,16,512]{2,1,0:T(8,128)S(1)},...) custom-call(s32[2]{0:T(128)S(1)} %pad_add_fusion.scal, s32[17]{0:T(128)S(1)} %copy-done.6, ...), custom_call_target="tpu_custom_call" | custom-call | tf_op jit(solution)/shard_map/pallas_call | solution.py:479
  70.1 0.7 collective-permute-start.17
  70.8 7.8 %collective-permute-start.18 = (f32[19,16,512]{2,1,0:T(8,128)S(1)}, f32[19,16,512]{2,1,0:T(8,128)S(1)}, u32[]{:S(2)}, u32[]{:S(2)}) collective-permute-start(f32[19,16,512]{2,1,0:T(8,128)S(1)} %get-tuple-element.69), channel_id=1, source_target_pairs={{0,1},{1,0},{2,3},{3,2},{4,5},{5,4},{6,7},{7,6},{8,9},{9,8},{10,11... | collective-permute-start | bytes 1867784 | tf_op jit(solution)/shard_map/ppermute | solution.py:459
  78.5 1.5 %collective-permute-start.19 = (f32[6,8,512]{2,1,0:T(8,128)S(1)}, f32[6,8,512]{2,1,0:T(8,128)S(1)}, u32[]{:S(2)}, u32[]{:S(2)}) collective-permute-start(f32[6,8,512]{2,1,0:T(8,128)S(1)} %get-tuple-element.71), channel_id=1, source_target_pairs={{0,2},{2,0},{1,3},{3,1},{4,6},{6,4},{5,7},{7,5},{8,10},{10,8},{9,1... | collective-permute-start | bytes 294920 | tf_op jit(solution)/shard_map/ppermute | solution.py:466
  80.0 3.3 %collective-permute-done.19.refs_13_ = f32[6,8,512]{2,1,0:T(8,128)S(1)} collective-permute-done((f32[6,8,512]{2,1,0:T(8,128)S(1)}, f32[6,8,512]{2,1,0:T(8,128)S(1)}, u32[]{:S(2)}, u32[]{:S(2)}) %collective-permute-start.19) | collective-permute-done | bytes 98336 | tf_op jit(solution)/shard_map/ppermute | solution.py:466
  83.3 0.7 collective-permute-start.20
  84.0 0.6 collective-permute-done.21.refs_15_
  84.6 4.9 %shard_map.92 = (f32[16,16,512]{2,1,0:T(8,128)S(1)}, f32[16,16,512]{2,1,0:T(8,128)S(1)}, f32[16,16,512]{2,1,0:T(8,128)S(1)}, f32[1,16,512]{2,1,0:T(8,128)S(1)}, ...) custom-call(s32[2]{0:T(128)S(1)} %pad_add_fusion.scal, ...), custom_call_target="tpu_custom_call" | custom-call | tf_op jit(solution)/shard_map/pallas_call | solution.py:479
  89.5 1.6 %collective-permute-start.25 = (f32[2,8,512]{2,1,0:T(8,128)S(1)}, f32[2,8,512]{2,1,0:T(8,128)S(1)}, u32[]{:S(2)}, u32[]{:S(2)}) collective-permute-start(f32[2,8,512]{2,1,0:T(8,128)S(1)} %get-tuple-element.80), channel_id=1, source_target_pairs={{0,2},{2,0},{1,3},{3,1},{4,6},{6,4},{5,7},{7,5},{8,10},{10,8},{9,1... | collective-permute-start | bytes 98312 | tf_op jit(solution)/shard_map/ppermute | solution.py:466
  91.1 0.7 collective-permute-start.23
  91.8 7.2 %collective-permute-start.24 = (f32[1,16,512]{2,1,0:T(8,128)S(1)}, f32[1,16,512]{2,1,0:T(8,128)S(1)}, u32[]{:S(2)}, u32[]{:S(2)}) collective-permute-start(f32[1,16,512]{2,1,0:T(8,128)S(1)} %get-tuple-element.79), channel_id=1, source_target_pairs={{0,1},{1,0},{2,3},{3,2},{4,5},{5,4},{6,7},{7,6},{8,9},{9,8},{10,11... | collective-permute-start | bytes 98312 | tf_op jit(solution)/shard_map/ppermute | solution.py:459
  98.9 0.1 collective-permute-start.27
  99.0 0.7 collective-permute-start.26
  99.7 3.0 %collective-permute-start.22 = (f32[16,16,256]{2,1,0:T(8,128)S(1)}, f32[16,16,256]{2,1,0:T(8,128)S(1)}, u32[]{:S(2)}, u32[]{:S(2)}) collective-permute-start(f32[16,16,256]{2,1,0:T(8,128)S(1)} %get-tuple-element.74), channel_id=1, source_target_pairs={{0,1},{1,0},{2,3},{3,2},{4,5},{5,4},{6,7},{7,6},{8,9},{9,8},{10,11... | collective-permute-start | bytes 786440 | tf_op jit(solution)/shard_map/ppermute | solution.py:459
  102.7 1.5 %shard_map.94 = (f32[16,16,256]{2,1,0:T(8,128)S(1)}, f32[16,16,256]{2,1,0:T(8,128)S(1)}) custom-call(s32[2]{0:T(128)S(1)} %pad_add_fusion.scal, f32[16,16,512]{2,1,0:T(8,128)S(1)} %get-tuple-element.75.refs_0_, f32[16,16,512]{2,1,0:T(8,128)S(1)} %get-tuple-element.76.refs_1_, f32[16,16,512]{2,1,0:T(8,128)S(1)} %get-tuple-element.77.refs_2_, ...), custom_call_target="tpu_custom_call" | custom-call | tf_op jit(solution)/shard_map/pallas_call | solution.py:479
  104.1 2.8 %collective-permute-start.28 = (f32[16,16,256]{2,1,0:T(8,128)S(1)}, f32[16,16,256]{2,1,0:T(8,128)S(1)}, u32[]{:S(2)}, u32[]{:S(2)}) collective-permute-start(f32[16,16,256]{2,1,0:T(8,128)S(1)} %get-tuple-element.83), channel_id=1, source_target_pairs={{0,1},{1,0},{2,3},{3,2},{4,5},{5,4},{6,7},{7,6},{8,9},{9,8},{10,11... | collective-permute-start | bytes 786440 | tf_op jit(solution)/shard_map/ppermute | solution.py:459
  106.9 1.4 %shard_map.93 = f32[32,16,256]{2,1,0:T(8,128)} custom-call(s32[2]{0:T(128)S(1)} %pad_add_fusion.scal, f32[16,16,256]{2,1,0:T(8,128)S(1)} %get-tuple-element.73.near, f32[16,16,256]{2,1,0:T(8,128)S(1)} %collective-permute-done.22.far), custom_call_target="tpu_custom_call" | custom-call | tf_op jit(solution)/shard_map/pallas_call | solution.py:479
  108.3 1.4 %shard_map.95 = f32[32,16,256]{2,1,0:T(8,128)} custom-call(s32[2]{0:T(128)S(1)} %pad_add_fusion.scal, f32[16,16,256]{2,1,0:T(8,128)S(1)} %get-tuple-element.82.near, f32[16,16,256]{2,1,0:T(8,128)S(1)} %collective-permute-done.28.far), custom_call_target="tpu_custom_call" | custom-call | tf_op jit(solution)/shard_map/pallas_call | solution.py:479
  (40 shorter events, 0.1 us)
Async XLA Ops:
  0.7 2.3 %copy-start = (bf16[17,32,16,256]{3,2,1,0:T(8,128)(2,1)S(1)}, bf16[17,32,16,256]{3,2,1,0:T(8,128)(2,1)}, u32[]{:S(2)}) copy-start(bf16[17,32,16,256]{3,2,1,0:T(8,128)(2,1)} %refs_6_.1) | copy-start | bytes 13369348
  3.0 1.7 %copy-start.1 = (f32[32,16,256]{2,1,0:T(8,128)S(1)}, f32[32,16,256]{2,1,0:T(8,128)}, u32[]{:S(2)}) copy-start(f32[32,16,256]{2,1,0:T(8,128)} %refs_0_.3) | copy-start | bytes 1572868
  3.0 1.7 %copy-start.2 = (f32[32,16,256]{2,1,0:T(8,128)S(1)}, f32[32,16,256]{2,1,0:T(8,128)}, u32[]{:S(2)}) copy-start(f32[32,16,256]{2,1,0:T(8,128)} %refs_1_.3) | copy-start | bytes 1572868
  3.0 1.7 %copy-start.3 = (f32[32,16,256]{2,1,0:T(8,128)S(1)}, f32[32,16,256]{2,1,0:T(8,128)}, u32[]{:S(2)}) copy-start(f32[32,16,256]{2,1,0:T(8,128)} %refs_2_.3) | copy-start | bytes 1572868
  3.0 1.7 %copy-start.4 = (f32[32,16,256]{2,1,0:T(8,128)S(1)}, f32[32,16,256]{2,1,0:T(8,128)}, u32[]{:S(2)}) copy-start(f32[32,16,256]{2,1,0:T(8,128)} %refs_3_.3) | copy-start | bytes 1572868
  3.0 1.7 %copy-start.5 = (f32[32,16,256]{2,1,0:T(8,128)S(1)}, f32[32,16,256]{2,1,0:T(8,128)}, u32[]{:S(2)}) copy-start(f32[32,16,256]{2,1,0:T(8,128)} %refs_4_.3) | copy-start | bytes 1572868
  3.0 39.9 %slice-start = ((s8[4456448]{0:T(1024)(128)(4,1)}), s8[4194304]{0:T(1024)(128)(4,1)S(1)}, s32[]{:S(2)}) async-start(s8[4456448]{0:T(1024)(128)(4,1)} %bitcast.2), calls=%async_computation | async-start | bytes 8388608
  4.1 38.9 %slice-start.1 = ((s8[4456448]{0:T(1024)(128)(4,1)}), s8[262144]{0:T(1024)(128)(4,1)S(1)}, s32[]{:S(2)}) async-start(s8[4456448]{0:T(1024)(128)(4,1)} %bitcast.2), calls=%async_computation.1 | async-start | bytes 524288
  4.1 38.8 %collective-permute-start.8 = (f32[17,16,16,256]{3,2,1,0:T(8,128)S(1)}, f32[17,16,16,256]{3,2,1,0:T(8,128)S(1)}, u32[]{:S(2)}, u32[]{:S(2)}) collective-permute-start(f32[17,16,16,256]{3,2,1,0:T(8,128)S(1)} %shard_map.89), channel_id=1, source_target_pairs={{0,1},{1,0},{2,3},{3,2},{4,5},{5,4},{6,7},{7,6},{8,9},{9,8},{10,11... | collective-permute-start | bytes 13369352 | tf_op jit(solution)/shard_map/ppermute | solution.py:459
  5.3 37.6 %copy-start.6 = (s32[17]{0:T(128)S(1)}, s32[17]{0:T(128)}, u32[]{:S(2)}) copy-start(s32[17]{0:T(128)} %offsets.5) | copy-start | bytes 208
  5.3 8.4 %collective-permute-start = (f32[5,16,16,256]{3,2,1,0:T(8,128)S(1)}, f32[5,16,16,256]{3,2,1,0:T(8,128)S(1)}, u32[]{:S(2)}, u32[]{:S(2)}) collective-permute-start(f32[5,16,16,256]{3,2,1,0:T(8,128)S(1)} %shard_map.86), channel_id=1, source_target_pairs={{0,1},{1,0},{2,3},{3,2},{4,5},{5,4},{6,7},{7,6},{8,9},{9,8},{10,11... | collective-permute-start | bytes 3932168 | tf_op jit(solution)/shard_map/ppermute | solution.py:459
  14.5 8.1 %collective-permute-start.3 = (f32[12,8,512]{2,1,0:T(8,128)S(1)}, f32[12,8,512]{2,1,0:T(8,128)S(1)}, u32[]{:S(2)}, u32[]{:S(2)}) collective-permute-start(f32[12,8,512]{2,1,0:T(8,128)S(1)} %get-tuple-element.50), channel_id=1, source_target_pairs={{0,2},{2,0},{1,3},{3,1},{4,6},{6,4},{5,7},{7,5},{8,10},{10,8},{9,1... | collective-permute-start | bytes 589832 | tf_op jit(solution)/shard_map/ppermute | solution.py:466
  17.5 5.9 %collective-permute-start.1 = (f32[6,16,512]{2,1,0:T(8,128)S(1)}, f32[6,16,512]{2,1,0:T(8,128)S(1)}, u32[]{:S(2)}, u32[]{:S(2)}) collective-permute-start(f32[6,16,512]{2,1,0:T(8,128)S(1)} %get-tuple-element.48), channel_id=1, source_target_pairs={{1,4},{4,1},{5,8},{8,5},{9,12},{12,9},{3,6},{6,3},{7,10},{10,7},{1... | collective-permute-start | bytes 589832 | tf_op jit(solution)/shard_map/ppermute | solution.py:462
  18.1 5.2 %collective-permute-start.2 = (f32[6,16,512]{2,1,0:T(8,128)S(1)}, f32[6,16,512]{2,1,0:T(8,128)S(1)}, u32[]{:S(2)}, u32[]{:S(2)}) collective-permute-start(f32[6,16,512]{2,1,0:T(8,128)S(1)} %get-tuple-element.49), channel_id=1, source_target_pairs={{0,1},{1,0},{2,3},{3,2},{4,5},{5,4},{6,7},{7,6},{8,9},{9,8},{10,11... | collective-permute-start | bytes 589832 | tf_op jit(solution)/shard_map/ppermute | solution.py:459
  22.7 1.4 %collective-permute-start.5 = (f32[12,8,512]{2,1,0:T(8,128)S(1)}, f32[12,8,512]{2,1,0:T(8,128)S(1)}, u32[]{:S(2)}, u32[]{:S(2)}) collective-permute-start(f32[12,8,512]{2,1,0:T(8,128)S(1)} %collective-permute-done.3.refs_7_), channel_id=1, source_target_pairs={{0,1},{1,0},{2,3},{3,2},{4,5},{5,4},{6,7},{7,6},{8,9},{9,8},{10,11... | collective-permute-start | bytes 589832 | tf_op jit(solution)/shard_map/ppermute | solution.py:459
  22.7 0.7 collective-permute-start.4
  28.8 14.2 %collective-permute-start.6 = (f32[16,16,512]{2,1,0:T(8,128)S(1)}, f32[16,16,512]{2,1,0:T(8,128)S(1)}, u32[]{:S(2)}, u32[]{:S(2)}) collective-permute-start(f32[16,16,512]{2,1,0:T(8,128)S(1)} %get-tuple-element.52.refs_0_), channel_id=1, source_target_pairs={{1,4},{4,1},{5,8},{8,5},{9,12},{12,9},{3,6},{6,3},{7,10},{10,7},{1... | collective-permute-start | bytes 1572872 | tf_op jit(solution)/shard_map/ppermute | solution.py:462
  29.5 13.5 %collective-permute-start.7 = (f32[16,16,512]{2,1,0:T(8,128)S(1)}, f32[16,16,512]{2,1,0:T(8,128)S(1)}, u32[]{:S(2)}, u32[]{:S(2)}) collective-permute-start(f32[16,16,512]{2,1,0:T(8,128)S(1)} %get-tuple-element.52.refs_0_), channel_id=1, source_target_pairs={{0,1},{1,0},{2,3},{3,2},{4,5},{5,4},{6,7},{7,6},{8,9},{9,8},{10,11... | collective-permute-start | bytes 1572872 | tf_op jit(solution)/shard_map/ppermute | solution.py:459
  37.4 4.3 %collective-permute-start.9 = (f32[4,8,512]{2,1,0:T(8,128)S(1)}, f32[4,8,512]{2,1,0:T(8,128)S(1)}, u32[]{:S(2)}, u32[]{:S(2)}) collective-permute-start(f32[4,8,512]{2,1,0:T(8,128)S(1)} %get-tuple-element.58), channel_id=1, source_target_pairs={{0,2},{2,0},{1,3},{3,1},{4,6},{6,4},{5,7},{7,5},{8,10},{10,8},{9,1... | collective-permute-start | bytes 196616 | tf_op jit(solution)/shard_map/ppermute | solution.py:466
  41.6 1.3 %collective-permute-start.11 = (f32[4,8,512]{2,1,0:T(8,128)S(1)}, f32[4,8,512]{2,1,0:T(8,128)S(1)}, u32[]{:S(2)}, u32[]{:S(2)}) collective-permute-start(f32[4,8,512]{2,1,0:T(8,128)S(1)} %collective-permute-done.9.refs_11_), channel_id=1, source_target_pairs={{0,1},{1,0},{2,3},{3,2},{4,5},{5,4},{6,7},{7,6},{8,9},{9,8},{10,11... | collective-permute-start | bytes 196616 | tf_op jit(solution)/shard_map/ppermute | solution.py:459
  41.7 0.7 collective-permute-start.10
  47.8 15.4 %collective-permute-start.12 = (f32[18,16,512]{2,1,0:T(8,128)S(1)}, f32[18,16,512]{2,1,0:T(8,128)S(1)}, u32[]{:S(2)}, u32[]{:S(2)}) collective-permute-start(f32[18,16,512]{2,1,0:T(8,128)S(1)} %get-tuple-element.60.refs_0_), channel_id=1, source_target_pairs={{1,4},{4,1},{5,8},{8,5},{9,12},{12,9},{3,6},{6,3},{7,10},{10,7},{1... | collective-permute-start | bytes 1769480 | tf_op jit(solution)/shard_map/ppermute | solution.py:462
  48.5 14.7 %collective-permute-start.13 = (f32[18,16,512]{2,1,0:T(8,128)S(1)}, f32[18,16,512]{2,1,0:T(8,128)S(1)}, u32[]{:S(2)}, u32[]{:S(2)}) collective-permute-start(f32[18,16,512]{2,1,0:T(8,128)S(1)} %get-tuple-element.62), channel_id=1, source_target_pairs={{0,1},{1,0},{2,3},{3,2},{4,5},{5,4},{6,7},{7,6},{8,9},{9,8},{10,11... | collective-permute-start | bytes 1769480 | tf_op jit(solution)/shard_map/ppermute | solution.py:459
  56.3 5.5 %collective-permute-start.14 = (f32[8,8,512]{2,1,0:T(8,128)S(1)}, f32[8,8,512]{2,1,0:T(8,128)S(1)}, u32[]{:S(2)}, u32[]{:S(2)}) collective-permute-start(f32[8,8,512]{2,1,0:T(8,128)S(1)} %get-tuple-element.64), channel_id=1, source_target_pairs={{0,2},{2,0},{1,3},{3,1},{4,6},{6,4},{5,7},{7,5},{8,10},{10,8},{9,1... | collective-permute-start | bytes 393224 | tf_op jit(solution)/shard_map/ppermute | solution.py:466
  61.8 1.3 %collective-permute-start.16 = (f32[8,8,512]{2,1,0:T(8,128)S(1)}, f32[8,8,512]{2,1,0:T(8,128)S(1)}, u32[]{:S(2)}, u32[]{:S(2)}) collective-permute-start(f32[8,8,512]{2,1,0:T(8,128)S(1)} %collective-permute-done.14.refs_12_), channel_id=1, source_target_pairs={{0,1},{1,0},{2,3},{3,2},{4,5},{5,4},{6,7},{7,6},{8,9},{9,8},{10,11... | collective-permute-start | bytes 393224 | tf_op jit(solution)/shard_map/ppermute | solution.py:459
  61.8 0.7 collective-permute-start.15
  70.1 14.6 %collective-permute-start.17 = (f32[19,16,512]{2,1,0:T(8,128)S(1)}, f32[19,16,512]{2,1,0:T(8,128)S(1)}, u32[]{:S(2)}, u32[]{:S(2)}) collective-permute-start(f32[19,16,512]{2,1,0:T(8,128)S(1)} %get-tuple-element.66.refs_0_), channel_id=1, source_target_pairs={{1,4},{4,1},{5,8},{8,5},{9,12},{12,9},{3,6},{6,3},{7,10},{10,7},{1... | collective-permute-start | bytes 1867784 | tf_op jit(solution)/shard_map/ppermute | solution.py:462
  70.8 13.9 %collective-permute-start.18 = (f32[19,16,512]{2,1,0:T(8,128)S(1)}, f32[19,16,512]{2,1,0:T(8,128)S(1)}, u32[]{:S(2)}, u32[]{:S(2)}) collective-permute-start(f32[19,16,512]{2,1,0:T(8,128)S(1)} %get-tuple-element.69), channel_id=1, source_target_pairs={{0,1},{1,0},{2,3},{3,2},{4,5},{5,4},{6,7},{7,6},{8,9},{9,8},{10,11... | collective-permute-start | bytes 1867784 | tf_op jit(solution)/shard_map/ppermute | solution.py:459
  78.5 4.8 %collective-permute-start.19 = (f32[6,8,512]{2,1,0:T(8,128)S(1)}, f32[6,8,512]{2,1,0:T(8,128)S(1)}, u32[]{:S(2)}, u32[]{:S(2)}) collective-permute-start(f32[6,8,512]{2,1,0:T(8,128)S(1)} %get-tuple-element.71), channel_id=1, source_target_pairs={{0,2},{2,0},{1,3},{3,1},{4,6},{6,4},{5,7},{7,5},{8,10},{10,8},{9,1... | collective-permute-start | bytes 294920 | tf_op jit(solution)/shard_map/ppermute | solution.py:466
  83.3 1.3 %collective-permute-start.21 = (f32[6,8,512]{2,1,0:T(8,128)S(1)}, f32[6,8,512]{2,1,0:T(8,128)S(1)}, u32[]{:S(2)}, u32[]{:S(2)}) collective-permute-start(f32[6,8,512]{2,1,0:T(8,128)S(1)} %collective-permute-done.19.refs_13_), channel_id=1, source_target_pairs={{0,1},{1,0},{2,3},{3,2},{4,5},{5,4},{6,7},{7,6},{8,9},{9,8},{10,11... | collective-permute-start | bytes 294920 | tf_op jit(solution)/shard_map/ppermute | solution.py:459
  83.3 0.7 collective-permute-start.20
  89.5 9.4 %collective-permute-start.25 = (f32[2,8,512]{2,1,0:T(8,128)S(1)}, f32[2,8,512]{2,1,0:T(8,128)S(1)}, u32[]{:S(2)}, u32[]{:S(2)}) collective-permute-start(f32[2,8,512]{2,1,0:T(8,128)S(1)} %get-tuple-element.80), channel_id=1, source_target_pairs={{0,2},{2,0},{1,3},{3,1},{4,6},{6,4},{5,7},{7,5},{8,10},{10,8},{9,1... | collective-permute-start | bytes 98312 | tf_op jit(solution)/shard_map/ppermute | solution.py:466
  91.1 11.6 %collective-permute-start.23 = (f32[1,16,512]{2,1,0:T(8,128)S(1)}, f32[1,16,512]{2,1,0:T(8,128)S(1)}, u32[]{:S(2)}, u32[]{:S(2)}) collective-permute-start(f32[1,16,512]{2,1,0:T(8,128)S(1)} %get-tuple-element.78), channel_id=1, source_target_pairs={{1,4},{4,1},{5,8},{8,5},{9,12},{12,9},{3,6},{6,3},{7,10},{10,7},{1... | collective-permute-start | bytes 98312 | tf_op jit(solution)/shard_map/ppermute | solution.py:462
  91.8 10.9 %collective-permute-start.24 = (f32[1,16,512]{2,1,0:T(8,128)S(1)}, f32[1,16,512]{2,1,0:T(8,128)S(1)}, u32[]{:S(2)}, u32[]{:S(2)}) collective-permute-start(f32[1,16,512]{2,1,0:T(8,128)S(1)} %get-tuple-element.79), channel_id=1, source_target_pairs={{0,1},{1,0},{2,3},{3,2},{4,5},{5,4},{6,7},{7,6},{8,9},{9,8},{10,11... | collective-permute-start | bytes 98312 | tf_op jit(solution)/shard_map/ppermute | solution.py:459
  98.9 3.7 %collective-permute-start.27 = (f32[2,8,512]{2,1,0:T(8,128)S(1)}, f32[2,8,512]{2,1,0:T(8,128)S(1)}, u32[]{:S(2)}, u32[]{:S(2)}) collective-permute-start(f32[2,8,512]{2,1,0:T(8,128)S(1)} %collective-permute-done.25.refs_9_), channel_id=1, source_target_pairs={{0,1},{1,0},{2,3},{3,2},{4,5},{5,4},{6,7},{7,6},{8,9},{9,8},{10,11... | collective-permute-start | bytes 98312 | tf_op jit(solution)/shard_map/ppermute | solution.py:459
  99.0 3.6 %collective-permute-start.26 = (f32[1,8,512]{2,1,0:T(8,128)S(1)}, f32[1,8,512]{2,1,0:T(8,128)S(1)}, u32[]{:S(2)}, u32[]{:S(2)}) collective-permute-start(f32[1,8,512]{2,1,0:T(8,128)S(1)} %get-tuple-element.81), channel_id=1, source_target_pairs={{1,6},{3,4},{4,3},{6,1},{5,10},{7,8},{8,7},{10,5},{9,14},{11,12},{... | collective-permute-start | bytes 49160 | tf_op jit(solution)/shard_map/ppermute | solution.py:464
  99.7 7.3 %collective-permute-start.22 = (f32[16,16,256]{2,1,0:T(8,128)S(1)}, f32[16,16,256]{2,1,0:T(8,128)S(1)}, u32[]{:S(2)}, u32[]{:S(2)}) collective-permute-start(f32[16,16,256]{2,1,0:T(8,128)S(1)} %get-tuple-element.74), channel_id=1, source_target_pairs={{0,1},{1,0},{2,3},{3,2},{4,5},{5,4},{6,7},{7,6},{8,9},{9,8},{10,11... | collective-permute-start | bytes 786440 | tf_op jit(solution)/shard_map/ppermute | solution.py:459
  104.1 4.2 %collective-permute-start.28 = (f32[16,16,256]{2,1,0:T(8,128)S(1)}, f32[16,16,256]{2,1,0:T(8,128)S(1)}, u32[]{:S(2)}, u32[]{:S(2)}) collective-permute-start(f32[16,16,256]{2,1,0:T(8,128)S(1)} %get-tuple-element.83), channel_id=1, source_target_pairs={{0,1},{1,0},{2,3},{3,2},{4,5},{5,4},{6,7},{7,6},{8,9},{9,8},{10,11... | collective-permute-start | bytes 786440 | tf_op jit(solution)/shard_map/ppermute | solution.py:459

commit v3 on v2

--- a/solution.py
+++ b/solution.py
@@ -181,7 +181,7 @@
         acc_far = jnp.zeros((geo.Z, geo.H), F32)
         for h in range(NOFF):
             place = geo.B + row + offsets[h]
-            acc = acc + refl[h, g * geo.B + row].astype(F32) * ext[place, 0 : geo.Z, pl.ds(near, geo.H)]
+            acc = acc + refl[h, row].astype(F32) * ext[place, 0 : geo.Z, pl.ds(near, geo.H)]
             acc_far = acc_far + refl_far[h, row] * ext[place, 0 : geo.Z, pl.ds(far, geo.H)]
         out[row, :, pl.ds(near, geo.H)] = courant[row, :, pl.ds(near, geo.H)] * acc
         out[row, :, pl.ds(far, geo.H)] = courant[row, :, pl.ds(far, geo.H)] * acc_far
@@ -212,38 +212,49 @@
     return sine_square, cosine_square, jnp.where(odd, -product, product)
 
 
-def half_kernel(geo, scal, *refs):
-    *fields, out = refs
-
-    def one(row, carry):
-        for k, field in enumerate(fields):
-            out[k, row] = field[row]
-        return carry
-
-    lax.fori_loop(0, geo.B, one, 0, unroll=4)
-
-
-def widen_kernel(geo, scal, refl, out):
+def half_kernel(geo, scal, *refs, other):
+    *fields, out, sems = refs
+    half = 1 - scal[0] if other else scal[0]
+    start = pl.multiple_of(half * geo.B, TILE)
+    copies = [
+        pltpu.make_async_copy(field.at[pl.ds(start, geo.B)], out.at[k], sems.at[k]) for k, field in enumerate(fields)
+    ]
+    for copy in copies:
+        copy.start()
+    for copy in copies:
+        copy.wait()
+
+
+def widen_kernel(geo, scal, refl, near, out, held, sems):
+    start = pl.multiple_of(scal[0] * geo.B, TILE)
+    other = pl.multiple_of((1 - scal[0]) * geo.B, TILE)
+    first = pltpu.make_async_copy(refl.at[:, pl.ds(other, geo.B)], held, sems.at[0])
+    second = pltpu.make_async_copy(refl.at[:, pl.ds(start, geo.B)], near, sems.at[1])
+    first.start()
+    second.start()
+    first.wait()
+
     def one(h, carry):
         for row in range(geo.B):
-            out[h, row] = refl[h, row].astype(F32)
+            out[h, row] = held[h, row].astype(F32)
         return carry
 
     lax.fori_loop(0, NOFF, one, 0)
+    second.wait()
 
 
 def join_kernel(geo, scal, *refs):
-    raw, far = refs[:5], refs[5]
-    own = refs[6:11]
-    px, pc = refs[11], refs[12]
-    tiles, corners = refs[13 : 13 + geo.sides], refs[13 + geo.sides :]
+    near, far = refs[:2]
+    own = refs[2:7]
+    px, pc = refs[7:9]
+    tiles, corners = refs[9 : 9 + geo.sides], refs[9 + geo.sides :]
     g, s = scal[0], scal[1]
     near_y = pl.multiple_of(g * geo.H, 128)
     far_y = pl.multiple_of((1 - g) * geo.H, 128)
 
     def one(row, carry):
         for k in range(5):
-            own[k][row, :, pl.ds(near_y, geo.H)] = raw[k][row]
+            own[k][row, :, pl.ds(near_y, geo.H)] = near[k, row]
             own[k][row, :, pl.ds(far_y, geo.H)] = far[k, row]
         return carry
 
@@ -327,9 +338,9 @@
     now, before, xr, cr, courant, refl, refl_far, *coefs = refs[:11]
     force = refs[11]
     tiles, xtiles, ctiles = refs[12 : 12 + n], refs[12 + n : 12 + 2 * n], refs[12 + 2 * n : 12 + 3 * n]
-    px, pc, force_out, scat, scat_prior = refs[12 + 3 * n : 17 + 3 * n]
-    out_tiles, out_corners = refs[17 + 3 * n : 17 + 4 * n], refs[17 + 4 * n : 17 + 5 * n]
-    ext, dif, tot, mid, wave = refs[17 + 5 * n :]
+    px, pc, force_out, scat, scat_prior, near, back = refs[12 + 3 * n : 19 + 3 * n]
+    out_tiles, out_corners = refs[19 + 3 * n : 19 + 4 * n], refs[19 + 4 * n : 19 + 5 * n]
+    ext, dif, tot, mid, wave = refs[19 + 5 * n :]
     g, s = scal[0], scal[1]
     B = geo.B
     fill(ext, now, None, None, tiles, xtiles, ctiles, 0, 2, 0, g, s, geo)
@@ -339,8 +350,12 @@
         mid[row] = value
 
     def keep_block(row, value):
-        px[row - B] = value[0 : geo.Z]
-        pc[row - B] = value[0 : geo.Z]
+        value = value[0 : geo.Z]
+        px[row - B] = value
+        pc[row - B] = value
+        low, high = value[:, 0 : geo.H], value[:, geo.H : geo.Y]
+        near[row - B] = jnp.where(g == 0, low, high)
+        back[row - B] = jnp.where(g == 0, high, low)
 
     advance(ext, B - 1, B + 2, lambda row: before[row - (B - 1)], None, keep_mid, coefs, dif, tot, geo)
     advance(mid, B, B, lambda row: ext[row], None, keep_block, coefs, dif, tot, geo)
@@ -369,16 +384,14 @@
     now, scat, before, xr, cr, courant, refl, refl_far, *coefs = refs[:12]
     force2 = refs[12]
     tiles, xtiles, ctiles = refs[13 : 13 + n], refs[13 + n : 13 + 2 * n], refs[13 + 2 * n : 13 + 3 * n]
-    scat_out, scat_prior, force_out, px, pc, near, back = refs[13 + 3 * n : 20 + 3 * n]
-    out_tiles, out_corners = refs[20 + 3 * n : 20 + 4 * n], refs[20 + 4 * n : 20 + 5 * n]
-    ext, dif, tot, mid, wave = refs[20 + 5 * n :]
+    scat_out, scat_prior, force_out, px, pc = refs[13 + 3 * n : 18 + 3 * n]
+    out_tiles, out_corners = refs[18 + 3 * n : 18 + 4 * n], refs[18 + 4 * n : 18 + 5 * n]
+    ext, dif, tot, mid, wave = refs[18 + 5 * n :]
     g, s = scal[0], scal[1]
     B = geo.B
 
     def own(row, carry):
         ext[B + row, 0 : geo.Z, :] = now[row]
-        back[row] = now[row, :, pl.ds(pl.multiple_of((1 - g) * geo.H, 128), geo.H)]
-        near[row] = now[row, :, pl.ds(pl.multiple_of(g * geo.H, 128), geo.H)]
         return carry
 
     lax.fori_loop(0, B, own, 0)
@@ -471,7 +484,7 @@
     def shape(*dims):
         return jax.ShapeDtypeStruct(dims, F32)
 
-    def call(kernel, inputs, outs, scratch, smem=1, specs=None):
+    def call(kernel, inputs, outs, scratch, smem=1, specs=None, extra=()):
         if specs is None:
             specs = [pl.BlockSpec(memory_space=pltpu.SMEM)] * (smem - 1)
             specs += [pl.BlockSpec(memory_space=pltpu.VMEM)] * (len(inputs) - smem)
@@ -484,7 +497,7 @@
                 grid=(1,),
                 in_specs=specs,
                 out_specs=[pl.BlockSpec(memory_space=pltpu.VMEM)] * len(outs),
-                scratch_shapes=[pltpu.VMEM(d, F32) for d in scratch],
+                scratch_shapes=[*(pltpu.VMEM(d, F32) for d in scratch), *extra],
             ),
             compiler_params=pltpu.CompilerParams(vmem_limit_bytes=used + SLACK),
         )(*inputs)
@@ -494,26 +507,38 @@
     def tile_outs(depths, corner=2):
         return [shape(tiles_of(depths, geo)[1], TILE, Y)] * n + [shape(corner, TILE, Y)] * n
 
-    fields = (wave_now, wave_before, courant, anisotropy, tilt)
-    near_half = pl.BlockSpec((B, Z, H), lambda i, scal: (scal[0], 0, 0))
-    far_half = pl.BlockSpec((B, Z, H), lambda i, scal: (1 - scal[0], 0, 0))
-    whole = pl.BlockSpec(memory_space=pltpu.VMEM)
-    (sent,) = call(half_kernel, [scal, *fields], [shape(5, B, Z, H)], [], specs=[far_half] * 5)
-    far = chip(sent)
+    in_hbm = lambda value: pltpu.with_memory_space_constraint(value, pltpu.HBM)
+    fields = [in_hbm(f) for f in (wave_now, wave_before, courant, anisotropy, tilt)]
+    reflectivity = in_hbm(reflectivity)
+    hbm = pl.BlockSpec(memory_space=pltpu.HBM)
+
+    def half_of(other):
+        kernel = functools.partial(half_kernel, other=other)
+        copies = [pltpu.SemaphoreType.DMA((5,))]
+        (out,) = call(kernel, [scal, *fields], [shape(5, B, Z, H)], [], specs=[hbm] * 5, extra=copies)
+        return out
+
+    far = chip(half_of(True))
+    near = half_of(False)
     *own, px, pc, r0, r1 = _split(
         call(
             join_kernel,
-            [scal, *fields, far],
+            [scal, near, far],
             [shape(*block)] * 5 + [shape(6, Z, Y)] * 2 + tile_outs([2, 1, 1, 1, 1]),
             [],
-            specs=[near_half] * 5 + [whole],
         ),
         7,
         n,
     )
     xr, cr, halo = exchange(px, pc, r0, r1)
-    refl_half = pl.BlockSpec((NOFF, B, Z, H), lambda i, scal: (0, 1 - scal[0], 0, 0))
-    (refl_far,) = call(widen_kernel, [scal, reflectivity], [shape(NOFF, B, Z, H)], [], specs=[refl_half])
+    refl, refl_far = call(
+        widen_kernel,
+        [scal, reflectivity],
+        [jax.ShapeDtypeStruct((NOFF, B, Z, H), reflectivity.dtype), shape(NOFF, B, Z, H)],
+        [],
+        specs=[hbm],
+        extra=[pltpu.VMEM((NOFF, B, Z, H), reflectivity.dtype), pltpu.SemaphoreType.DMA((2,))],
+    )
     refl_far = chip(refl_far)
     now, prior, *coefs, r0, r1 = _split(
         call(
@@ -526,7 +551,7 @@
     px, pc, prior, force, r0, r1 = _split(
         call(
             second_kernel,
-            [scal, offsets, now, prior, xr, cr, own[2], reflectivity, refl_far, *coefs, *halo],
+            [scal, offsets, now, prior, xr, cr, own[2], refl, refl_far, *coefs, *halo],
             [shape(B + 2, Z, Y)] * 2 + [shape(*wide), shape(*block)] + tile_outs([2, 2]),
             [ext] * 4,
             2,
@@ -535,27 +560,31 @@
         n,
     )
     xr, cr, halo = exchange(px, pc, r0, r1)
-    px, pc, force2, scat, scat_prior, r0, r1 = _split(
+    px, pc, force2, scat, scat_prior, near_u, back, r0, r1 = _split(
         call(
             third_kernel,
-            [scal, offsets, px, prior, xr, cr, own[2], reflectivity, refl_far, *coefs, force, *halo],
-            [shape(B + 3, Z, Y)] * 2 + [shape(*block)] * 2 + [shape(*wide)] + tile_outs([2, 1]),
+            [scal, offsets, px, prior, xr, cr, own[2], refl, refl_far, *coefs, force, *halo],
+            [shape(B + 3, Z, Y)] * 2
+            + [shape(*block)] * 2
+            + [shape(*wide)]
+            + [shape(B, Z, H)] * 2
+            + tile_outs([2, 1]),
+            [ext] * 5,
+            2,
+        ),
+        7,
+        n,
+    )
+    xr, cr, halo = exchange(px, pc, r0, r1)
+    scat, scat_prior, force3, qx, qc, r0, r1 = _split(
+        call(
+            fourth_kernel,
+            [scal, offsets, px, scat, scat_prior, xr, cr, own[2], refl, refl_far, *coefs, force2, *halo],
+            [shape(*block)] * 3 + [shape(1, Z, Y)] * 2 + tile_outs([1], 1),
             [ext] * 5,
             2,
         ),
         5,
-        n,
-    )
-    xr, cr, halo = exchange(px, pc, r0, r1)
-    scat, scat_prior, force3, qx, qc, near_u, back, r0, r1 = _split(
-        call(
-            fourth_kernel,
-            [scal, offsets, px, scat, scat_prior, xr, cr, own[2], reflectivity, refl_far, *coefs, force2, *halo],
-            [shape(*block)] * 3 + [shape(1, Z, Y)] * 2 + [shape(B, Z, H)] * 2 + tile_outs([1], 1),
-            [ext] * 5,
-            2,
-        ),
-        7,
         n,
     )
     xr, cr, halo = exchange(qx, qc, r0, r1)

time: 110 us -> 109 us (level)
  Pallas kernels: 28 us -> 32.7 us
  waiting for transfers between devices: 22.1 us -> 18.8 us
  local copies, waits for them, and re-layouts: 2.31 us -> 0.01 us
    pallas_call x10 -> x11, Pallas kernels: 28 us -> 32.7 us  [call(): pl.pallas_call(functools.partial(kernel, geo), out_shape=outs, grid_spec=...]
    ppermute x14, waiting for transfers between devices: 10.5 us -> 6.83 us  [chip(): return lax.ppermute(value, 'gy', swap)]
    unnamed x18 -> x2, local copies, waits for them, and re-layouts: 2.31 us -> 0.01 us
  transfers between devices with their start and end apart: 29 -> 29, of which waited for: 9 -> 9; matrix products, arithmetic and copies ran while one was open for 0% -> 0% of each run, Pallas kernels for 8% -> 11%
where the time goes in v3:
time: 109 us
  starting transfers between devices  56.2 us (52%)
  Pallas kernels  32.7 us (30%)
  waiting for transfers between devices  18.8 us (17%)
    ppermute x14, starting transfers between devices, chip(): return lax.ppermute(value, 'gy', swap)  41.5 us
    pallas_call x11, Pallas kernels, call(): pl.pallas_call(functools.partial(kernel, geo), out_shape=outs, grid_spec=...  32.7 us
    ppermute x5, waiting for transfers between devices, exchange(): zr = [lax.ppermute(t, 'section', m) for t, m in zip(tiles, z_moves())]  12 us
    ppermute x5, starting transfers between devices, exchange(): zr = [lax.ppermute(t, 'section', m) for t, m in zip(tiles, z_moves())]  8.14 us
    ppermute x14, waiting for transfers between devices, chip(): return lax.ppermute(value, 'gy', swap)  6.83 us
    ppermute x5, starting transfers between devices, exchange(): xr = lax.ppermute(px, ('gx', 'gy'), pairs_x)  3.37 us
    ppermute x5, starting transfers between devices, exchange(): lax.ppermute(t, ('gx', 'section', 'gy'), corner_pairs(m))  3.26 us
  transfers between devices with their start and end apart: 29, of which 9 were waited for; matrix products, arithmetic and copies ran while one was open for 0% of the time, Pallas kernels for 11%

profile of v3, /device:TPU:0, one launch (start us, length us, event | category | flops | bytes accessed | tf_op | source)
XLA Modules:
  0.0 108.7 jit_solution(15166823477433774881)
XLA Ops:
  0.7 2.9 %shard_map.90 = (bf16[17,16,16,256]{3,2,1,0:T(8,128)(2,1)S(1)}, f32[17,16,16,256]{3,2,1,0:T(8,128)S(1)}) custom-call(s32[2]{0:T(128)S(1)} %pad_add_fusion.scal, bf16[17,32,16,256]{3,2,1,0:T(8,128)(2,1)} %refl.1), custom_call_target="tpu_custom_call" | custom-call | tf_op jit(solution)/shard_map/pallas_call | solution.py:492
  3.6 0.6 collective-permute-start.8
  4.1 1.9 %shard_map.87 = f32[5,16,16,256]{3,2,1,0:T(8,128)S(1)} custom-call(s32[2]{0:T(128)S(1)} %pad_add_fusion.scal, f32[32,16,256]{2,1,0:T(8,128)} %refs_0_.3, f32[32,16,256]{2,1,0:T(8,128)} %refs_1_.3, f32[32,16,256]{2,1,0:T(8,128)} %refs_2_.3, f32[32,16,256]{2,1,0:T(8,128)} %refs_3_.3, f32[32,16,256]{2,1,0:T(8,128)} %refs_4_.3), custom_call_target="tpu_custom_call" | custom-call | tf_op jit(solution)/shard_map/pallas_call | solution.py:492
  6.0 0.1 collective-permute-start
  6.1 1.9 %shard_map.86.refs_0_ = f32[5,16,16,256]{3,2,1,0:T(8,128)S(1)} custom-call(s32[2]{0:T(128)S(1)} %pad_add_fusion.scal, f32[32,16,256]{2,1,0:T(8,128)} %refs_0_.3, f32[32,16,256]{2,1,0:T(8,128)} %refs_1_.3, f32[32,16,256]{2,1,0:T(8,128)} %refs_2_.3, f32[32,16,256]{2,1,0:T(8,128)} %refs_3_.3, f32[32,16,256]{2,1,0:T(8,128)} %refs_4_.3), custom_call_target="tpu_custom_call" | custom-call | tf_op jit(solution)/shard_map/pallas_call | solution.py:492
  7.9 5.2 %collective-permute-done.refs_1_ = f32[5,16,16,256]{3,2,1,0:T(8,128)S(1)} collective-permute-done((f32[5,16,16,256]{3,2,1,0:T(8,128)S(1)}, f32[5,16,16,256]{3,2,1,0:T(8,128)S(1)}, u32[]{:S(2)}, u32[]{:S(2)}) %collective-permute-start) | collective-permute-done | bytes 1310752 | tf_op jit(solution)/shard_map/ppermute | solution.py:472
  13.2 0.9 shard_map.88
  14.0 2.9 %collective-permute-start.3 = (f32[12,8,512]{2,1,0:T(8,128)S(1)}, f32[12,8,512]{2,1,0:T(8,128)S(1)}, u32[]{:S(2)}, u32[]{:S(2)}) collective-permute-start(f32[12,8,512]{2,1,0:T(8,128)S(1)} %get-tuple-element.52), channel_id=1, source_target_pairs={{0,2},{2,0},{1,3},{3,1},{4,6},{6,4},{5,7},{7,5},{8,10},{10,8},{9,1... | collective-permute-start | bytes 589832 | tf_op jit(solution)/shard_map/ppermute | solution.py:479
  17.0 0.7 collective-permute-start.1
  17.6 3.0 %collective-permute-start.2 = (f32[6,16,512]{2,1,0:T(8,128)S(1)}, f32[6,16,512]{2,1,0:T(8,128)S(1)}, u32[]{:S(2)}, u32[]{:S(2)}) collective-permute-start(f32[6,16,512]{2,1,0:T(8,128)S(1)} %get-tuple-element.51), channel_id=1, source_target_pairs={{0,1},{1,0},{2,3},{3,2},{4,5},{5,4},{6,7},{7,6},{8,9},{9,8},{10,11... | collective-permute-start | bytes 589832 | tf_op jit(solution)/shard_map/ppermute | solution.py:472
  20.6 1.5 %collective-permute-done.3.refs_7_ = f32[12,8,512]{2,1,0:T(8,128)S(1)} collective-permute-done((f32[12,8,512]{2,1,0:T(8,128)S(1)}, f32[12,8,512]{2,1,0:T(8,128)S(1)}, u32[]{:S(2)}, u32[]{:S(2)}) %collective-permute-start.3) | collective-permute-done | bytes 196640 | tf_op jit(solution)/shard_map/ppermute | solution.py:479
  22.2 0.7 collective-permute-start.4
  22.9 0.7 collective-permute-done.5.refs_9_
  23.6 4.6 %shard_map.89 = (f32[16,16,512]{2,1,0:T(8,128)S(1)}, f32[18,24,512]{2,1,0:T(8,128)S(1)}, f32[18,24,512]{2,1,0:T(8,128)S(1)}, f32[18,24,512]{2,1,0:T(8,128)S(1)},...) custom-call(s32[2]{0:T(128)S(1)} %pad_add_fusion.scal, ...), custom_call_target="tpu_custom_call" | custom-call | tf_op jit(solution)/shard_map/pallas_call | solution.py:492
  28.2 5.3 %collective-permute-start.7 = (f32[16,16,512]{2,1,0:T(8,128)S(1)}, f32[16,16,512]{2,1,0:T(8,128)S(1)}, u32[]{:S(2)}, u32[]{:S(2)}) collective-permute-start(f32[16,16,512]{2,1,0:T(8,128)S(1)} %get-tuple-element.54.refs_0_), channel_id=1, source_target_pairs={{0,1},{1,0},{2,3},{3,2},{4,5},{5,4},{6,7},{7,6},{8,9},{9,8},{10,11... | collective-permute-start | bytes 1572872 | tf_op jit(solution)/shard_map/ppermute | solution.py:472
  33.5 0.7 collective-permute-start.6
  34.2 1.8 %collective-permute-start.9 = (f32[4,8,512]{2,1,0:T(8,128)S(1)}, f32[4,8,512]{2,1,0:T(8,128)S(1)}, u32[]{:S(2)}, u32[]{:S(2)}) collective-permute-start(f32[4,8,512]{2,1,0:T(8,128)S(1)} %get-tuple-element.62), channel_id=1, source_target_pairs={{0,2},{2,0},{1,3},{3,1},{4,6},{6,4},{5,7},{7,5},{8,10},{10,8},{9,1... | collective-permute-start | bytes 196616 | tf_op jit(solution)/shard_map/ppermute | solution.py:479
  36.0 2.5 %collective-permute-done.9.refs_11_ = f32[4,8,512]{2,1,0:T(8,128)S(1)} collective-permute-done((f32[4,8,512]{2,1,0:T(8,128)S(1)}, f32[4,8,512]{2,1,0:T(8,128)S(1)}, u32[]{:S(2)}, u32[]{:S(2)}) %collective-permute-start.9) | collective-permute-done | bytes 65568 | tf_op jit(solution)/shard_map/ppermute | solution.py:479
  38.5 2.0 %collective-permute-start.11 = (f32[4,8,512]{2,1,0:T(8,128)S(1)}, f32[4,8,512]{2,1,0:T(8,128)S(1)}, u32[]{:S(2)}, u32[]{:S(2)}) collective-permute-start(f32[4,8,512]{2,1,0:T(8,128)S(1)} %collective-permute-done.9.refs_11_), channel_id=1, source_target_pairs={{0,1},{1,0},{2,3},{3,2},{4,5},{5,4},{6,7},{7,6},{8,9},{9,8},{10,11... | collective-permute-start | bytes 196616 | tf_op jit(solution)/shard_map/ppermute | solution.py:472
  40.5 0.7 collective-permute-start.10
  41.2 0.2 collective-permute-done.11.refs_13_
  41.5 4.7 %shard_map.91 = (f32[18,16,512]{2,1,0:T(8,128)S(1)}, f32[18,16,512]{2,1,0:T(8,128)S(1)}, f32[18,24,512]{2,1,0:T(8,128)S(1)}, f32[16,16,512]{2,1,0:T(8,128)S(1)},...) custom-call(s32[2]{0:T(128)S(1)} %pad_add_fusion.scal, s32[17]{0:T(128)S(1)} %copy-done, ...), custom_call_target="tpu_custom_call" | custom-call | tf_op jit(solution)/shard_map/pallas_call | solution.py:492
  46.2 5.7 %collective-permute-start.13 = (f32[18,16,512]{2,1,0:T(8,128)S(1)}, f32[18,16,512]{2,1,0:T(8,128)S(1)}, u32[]{:S(2)}, u32[]{:S(2)}) collective-permute-start(f32[18,16,512]{2,1,0:T(8,128)S(1)} %get-tuple-element.66), channel_id=1, source_target_pairs={{0,1},{1,0},{2,3},{3,2},{4,5},{5,4},{6,7},{7,6},{8,9},{9,8},{10,11... | collective-permute-start | bytes 1769480 | tf_op jit(solution)/shard_map/ppermute | solution.py:472
  51.9 0.7 collective-permute-start.12
  52.5 1.2 %collective-permute-start.14 = (f32[8,8,512]{2,1,0:T(8,128)S(1)}, f32[8,8,512]{2,1,0:T(8,128)S(1)}, u32[]{:S(2)}, u32[]{:S(2)}) collective-permute-start(f32[8,8,512]{2,1,0:T(8,128)S(1)} %get-tuple-element.68), channel_id=1, source_target_pairs={{0,2},{2,0},{1,3},{3,1},{4,6},{6,4},{5,7},{7,5},{8,10},{10,8},{9,1... | collective-permute-start | bytes 393224 | tf_op jit(solution)/shard_map/ppermute | solution.py:479
  53.8 3.8 %collective-permute-done.14.refs_12_ = f32[8,8,512]{2,1,0:T(8,128)S(1)} collective-permute-done((f32[8,8,512]{2,1,0:T(8,128)S(1)}, f32[8,8,512]{2,1,0:T(8,128)S(1)}, u32[]{:S(2)}, u32[]{:S(2)}) %collective-permute-start.14) | collective-permute-done | bytes 131104 | tf_op jit(solution)/shard_map/ppermute | solution.py:479
  57.6 1.9 %collective-permute-start.16 = (f32[8,8,512]{2,1,0:T(8,128)S(1)}, f32[8,8,512]{2,1,0:T(8,128)S(1)}, u32[]{:S(2)}, u32[]{:S(2)}) collective-permute-start(f32[8,8,512]{2,1,0:T(8,128)S(1)} %collective-permute-done.14.refs_12_), channel_id=1, source_target_pairs={{0,1},{1,0},{2,3},{3,2},{4,5},{5,4},{6,7},{7,6},{8,9},{9,8},{10,11... | collective-permute-start | bytes 393224 | tf_op jit(solution)/shard_map/ppermute | solution.py:472
  59.5 0.7 collective-permute-start.15
  60.1 0.3 collective-permute-done.16.refs_14_
  60.5 6.9 %shard_map.92 = (f32[19,16,512]{2,1,0:T(8,128)S(1)}, f32[19,16,512]{2,1,0:T(8,128)S(1)}, f32[16,16,512]{2,1,0:T(8,128)S(1)}, f32[16,16,512]{2,1,0:T(8,128)S(1)},...) custom-call(s32[2]{0:T(128)S(1)} %pad_add_fusion.scal, ...), custom_call_target="tpu_custom_call" | custom-call | tf_op jit(solution)/shard_map/pallas_call | solution.py:492
  67.3 6.3 %collective-permute-start.19 = (f32[19,16,512]{2,1,0:T(8,128)S(1)}, f32[19,16,512]{2,1,0:T(8,128)S(1)}, u32[]{:S(2)}, u32[]{:S(2)}) collective-permute-start(f32[19,16,512]{2,1,0:T(8,128)S(1)} %get-tuple-element.75), channel_id=1, source_target_pairs={{0,1},{1,0},{2,3},{3,2},{4,5},{5,4},{6,7},{7,6},{8,9},{9,8},{10,11... | collective-permute-start | bytes 1867784 | tf_op jit(solution)/shard_map/ppermute | solution.py:472
  73.6 0.7 collective-permute-start.18
  74.3 0.6 collective-permute-start.20
  74.9 4.1 %collective-permute-done.20.refs_13_ = f32[6,8,512]{2,1,0:T(8,128)S(1)} collective-permute-done((f32[6,8,512]{2,1,0:T(8,128)S(1)}, f32[6,8,512]{2,1,0:T(8,128)S(1)}, u32[]{:S(2)}, u32[]{:S(2)}) %collective-permute-start.20) | collective-permute-done | bytes 98336 | tf_op jit(solution)/shard_map/ppermute | solution.py:479
  79.0 1.9 %collective-permute-start.22 = (f32[6,8,512]{2,1,0:T(8,128)S(1)}, f32[6,8,512]{2,1,0:T(8,128)S(1)}, u32[]{:S(2)}, u32[]{:S(2)}) collective-permute-start(f32[6,8,512]{2,1,0:T(8,128)S(1)} %collective-permute-done.20.refs_13_), channel_id=1, source_target_pairs={{0,1},{1,0},{2,3},{3,2},{4,5},{5,4},{6,7},{7,6},{8,9},{9,8},{10,11... | collective-permute-start | bytes 294920 | tf_op jit(solution)/shard_map/ppermute | solution.py:472
  80.9 0.7 collective-permute-start.21
  81.5 0.3 collective-permute-done.22.refs_15_
  81.8 4.8 %shard_map.94 = (f32[16,16,512]{2,1,0:T(8,128)S(1)}, f32[16,16,512]{2,1,0:T(8,128)S(1)}, f32[16,16,512]{2,1,0:T(8,128)S(1)}, f32[1,16,512]{2,1,0:T(8,128)S(1)}, ...) custom-call(s32[2]{0:T(128)S(1)} %pad_add_fusion.scal, s32[17]{0:T(128)S(1)} %copy-done, ...), custom_call_target="tpu_custom_call" | custom-call | tf_op jit(solution)/shard_map/pallas_call | solution.py:492
  86.6 1.6 %collective-permute-start.25 = (f32[2,8,512]{2,1,0:T(8,128)S(1)}, f32[2,8,512]{2,1,0:T(8,128)S(1)}, u32[]{:S(2)}, u32[]{:S(2)}) collective-permute-start(f32[2,8,512]{2,1,0:T(8,128)S(1)} %get-tuple-element.84), channel_id=1, source_target_pairs={{0,2},{2,0},{1,3},{3,1},{4,6},{6,4},{5,7},{7,5},{8,10},{10,8},{9,1... | collective-permute-start | bytes 98312 | tf_op jit(solution)/shard_map/ppermute | solution.py:479
  88.3 0.7 collective-permute-start.23
  88.9 9.0 %collective-permute-start.24 = (f32[1,16,512]{2,1,0:T(8,128)S(1)}, f32[1,16,512]{2,1,0:T(8,128)S(1)}, u32[]{:S(2)}, u32[]{:S(2)}) collective-permute-start(f32[1,16,512]{2,1,0:T(8,128)S(1)} %get-tuple-element.83), channel_id=1, source_target_pairs={{0,1},{1,0},{2,3},{3,2},{4,5},{5,4},{6,7},{7,6},{8,9},{9,8},{10,11... | collective-permute-start | bytes 98312 | tf_op jit(solution)/shard_map/ppermute | solution.py:472
  97.9 0.1 collective-permute-start.27
  98.0 0.7 collective-permute-start.26
  98.7 2.6 %collective-permute-start.17 = (f32[16,16,256]{2,1,0:T(8,128)S(1)}, f32[16,16,256]{2,1,0:T(8,128)S(1)}, u32[]{:S(2)}, u32[]{:S(2)}) collective-permute-start(f32[16,16,256]{2,1,0:T(8,128)S(1)} %get-tuple-element.71), channel_id=1, source_target_pairs={{0,1},{1,0},{2,3},{3,2},{4,5},{5,4},{6,7},{7,6},{8,9},{9,8},{10,11... | collective-permute-start | bytes 786440 | tf_op jit(solution)/shard_map/ppermute | solution.py:472
  101.3 1.4 %shard_map.95 = (f32[16,16,256]{2,1,0:T(8,128)S(1)}, f32[16,16,256]{2,1,0:T(8,128)S(1)}) custom-call(s32[2]{0:T(128)S(1)} %pad_add_fusion.scal, f32[16,16,512]{2,1,0:T(8,128)S(1)} %get-tuple-element.79.refs_0_, f32[16,16,512]{2,1,0:T(8,128)S(1)} %get-tuple-element.80.refs_1_, f32[16,16,512]{2,1,0:T(8,128)S(1)} %get-tuple-element.81.refs_2_, ...), custom_call_target="tpu_custom_call" | custom-call | tf_op jit(solution)/shard_map/pallas_call | solution.py:492
  102.8 3.2 %collective-permute-start.28 = (f32[16,16,256]{2,1,0:T(8,128)S(1)}, f32[16,16,256]{2,1,0:T(8,128)S(1)}, u32[]{:S(2)}, u32[]{:S(2)}) collective-permute-start(f32[16,16,256]{2,1,0:T(8,128)S(1)} %get-tuple-element.87), channel_id=1, source_target_pairs={{0,1},{1,0},{2,3},{3,2},{4,5},{5,4},{6,7},{7,6},{8,9},{9,8},{10,11... | collective-permute-start | bytes 786440 | tf_op jit(solution)/shard_map/ppermute | solution.py:472
  105.9 1.4 %shard_map.93 = f32[32,16,256]{2,1,0:T(8,128)} custom-call(s32[2]{0:T(128)S(1)} %pad_add_fusion.scal, f32[16,16,256]{2,1,0:T(8,128)S(1)} %get-tuple-element.70.near, f32[16,16,256]{2,1,0:T(8,128)S(1)} %collective-permute-done.17.far), custom_call_target="tpu_custom_call" | custom-call | tf_op jit(solution)/shard_map/pallas_call | solution.py:492
  107.3 1.4 %shard_map.96 = f32[32,16,256]{2,1,0:T(8,128)} custom-call(s32[2]{0:T(128)S(1)} %pad_add_fusion.scal, f32[16,16,256]{2,1,0:T(8,128)S(1)} %get-tuple-element.86.near, f32[16,16,256]{2,1,0:T(8,128)S(1)} %collective-permute-done.28.far), custom_call_target="tpu_custom_call" | custom-call | tf_op jit(solution)/shard_map/pallas_call | solution.py:492
  (24 shorter events, 0.1 us)
Async XLA Ops:
  3.6 37.9 %collective-permute-start.8 = (f32[17,16,16,256]{3,2,1,0:T(8,128)S(1)}, f32[17,16,16,256]{3,2,1,0:T(8,128)S(1)}, u32[]{:S(2)}, u32[]{:S(2)}) collective-permute-start(f32[17,16,16,256]{3,2,1,0:T(8,128)S(1)} %get-tuple-element.57), channel_id=1, source_target_pairs={{0,1},{1,0},{2,3},{3,2},{4,5},{5,4},{6,7},{7,6},{8,9},{9,8},{10,11... | collective-permute-start | bytes 13369352 | tf_op jit(solution)/shard_map/ppermute | solution.py:472
  6.0 7.2 %collective-permute-start = (f32[5,16,16,256]{3,2,1,0:T(8,128)S(1)}, f32[5,16,16,256]{3,2,1,0:T(8,128)S(1)}, u32[]{:S(2)}, u32[]{:S(2)}) collective-permute-start(f32[5,16,16,256]{3,2,1,0:T(8,128)S(1)} %shard_map.87), channel_id=1, source_target_pairs={{0,1},{1,0},{2,3},{3,2},{4,5},{5,4},{6,7},{7,6},{8,9},{9,8},{10,11... | collective-permute-start | bytes 3932168 | tf_op jit(solution)/shard_map/ppermute | solution.py:472
  14.0 27.4 %copy-start = (s32[17]{0:T(128)S(1)}, s32[17]{0:T(128)}, u32[]{:S(2)}) copy-start(s32[17]{0:T(128)} %offsets.5) | copy-start | bytes 208
  14.0 8.1 %collective-permute-start.3 = (f32[12,8,512]{2,1,0:T(8,128)S(1)}, f32[12,8,512]{2,1,0:T(8,128)S(1)}, u32[]{:S(2)}, u32[]{:S(2)}) collective-permute-start(f32[12,8,512]{2,1,0:T(8,128)S(1)} %get-tuple-element.52), channel_id=1, source_target_pairs={{0,2},{2,0},{1,3},{3,1},{4,6},{6,4},{5,7},{7,5},{8,10},{10,8},{9,1... | collective-permute-start | bytes 589832 | tf_op jit(solution)/shard_map/ppermute | solution.py:479
  17.0 5.9 %collective-permute-start.1 = (f32[6,16,512]{2,1,0:T(8,128)S(1)}, f32[6,16,512]{2,1,0:T(8,128)S(1)}, u32[]{:S(2)}, u32[]{:S(2)}) collective-permute-start(f32[6,16,512]{2,1,0:T(8,128)S(1)} %get-tuple-element.50), channel_id=1, source_target_pairs={{1,4},{4,1},{5,8},{8,5},{9,12},{12,9},{3,6},{6,3},{7,10},{10,7},{1... | collective-permute-start | bytes 589832 | tf_op jit(solution)/shard_map/ppermute | solution.py:475
  17.6 5.2 %collective-permute-start.2 = (f32[6,16,512]{2,1,0:T(8,128)S(1)}, f32[6,16,512]{2,1,0:T(8,128)S(1)}, u32[]{:S(2)}, u32[]{:S(2)}) collective-permute-start(f32[6,16,512]{2,1,0:T(8,128)S(1)} %get-tuple-element.51), channel_id=1, source_target_pairs={{0,1},{1,0},{2,3},{3,2},{4,5},{5,4},{6,7},{7,6},{8,9},{9,8},{10,11... | collective-permute-start | bytes 589832 | tf_op jit(solution)/shard_map/ppermute | solution.py:472
  22.2 1.4 %collective-permute-start.5 = (f32[12,8,512]{2,1,0:T(8,128)S(1)}, f32[12,8,512]{2,1,0:T(8,128)S(1)}, u32[]{:S(2)}, u32[]{:S(2)}) collective-permute-start(f32[12,8,512]{2,1,0:T(8,128)S(1)} %collective-permute-done.3.refs_7_), channel_id=1, source_target_pairs={{0,1},{1,0},{2,3},{3,2},{4,5},{5,4},{6,7},{7,6},{8,9},{9,8},{10,11... | collective-permute-start | bytes 589832 | tf_op jit(solution)/shard_map/ppermute | solution.py:472
  22.2 0.7 collective-permute-start.4
  28.2 13.2 %collective-permute-start.7 = (f32[16,16,512]{2,1,0:T(8,128)S(1)}, f32[16,16,512]{2,1,0:T(8,128)S(1)}, u32[]{:S(2)}, u32[]{:S(2)}) collective-permute-start(f32[16,16,512]{2,1,0:T(8,128)S(1)} %get-tuple-element.54.refs_0_), channel_id=1, source_target_pairs={{0,1},{1,0},{2,3},{3,2},{4,5},{5,4},{6,7},{7,6},{8,9},{9,8},{10,11... | collective-permute-start | bytes 1572872 | tf_op jit(solution)/shard_map/ppermute | solution.py:472
  33.5 7.9 %collective-permute-start.6 = (f32[16,16,512]{2,1,0:T(8,128)S(1)}, f32[16,16,512]{2,1,0:T(8,128)S(1)}, u32[]{:S(2)}, u32[]{:S(2)}) collective-permute-start(f32[16,16,512]{2,1,0:T(8,128)S(1)} %get-tuple-element.54.refs_0_), channel_id=1, source_target_pairs={{1,4},{4,1},{5,8},{8,5},{9,12},{12,9},{3,6},{6,3},{7,10},{10,7},{1... | collective-permute-start | bytes 1572872 | tf_op jit(solution)/shard_map/ppermute | solution.py:475
  34.2 4.3 %collective-permute-start.9 = (f32[4,8,512]{2,1,0:T(8,128)S(1)}, f32[4,8,512]{2,1,0:T(8,128)S(1)}, u32[]{:S(2)}, u32[]{:S(2)}) collective-permute-start(f32[4,8,512]{2,1,0:T(8,128)S(1)} %get-tuple-element.62), channel_id=1, source_target_pairs={{0,2},{2,0},{1,3},{3,1},{4,6},{6,4},{5,7},{7,5},{8,10},{10,8},{9,1... | collective-permute-start | bytes 196616 | tf_op jit(solution)/shard_map/ppermute | solution.py:479
  38.5 2.9 %collective-permute-start.11 = (f32[4,8,512]{2,1,0:T(8,128)S(1)}, f32[4,8,512]{2,1,0:T(8,128)S(1)}, u32[]{:S(2)}, u32[]{:S(2)}) collective-permute-start(f32[4,8,512]{2,1,0:T(8,128)S(1)} %collective-permute-done.9.refs_11_), channel_id=1, source_target_pairs={{0,1},{1,0},{2,3},{3,2},{4,5},{5,4},{6,7},{7,6},{8,9},{9,8},{10,11... | collective-permute-start | bytes 196616 | tf_op jit(solution)/shard_map/ppermute | solution.py:472
  40.5 0.7 collective-permute-start.10
  46.2 14.2 %collective-permute-start.13 = (f32[18,16,512]{2,1,0:T(8,128)S(1)}, f32[18,16,512]{2,1,0:T(8,128)S(1)}, u32[]{:S(2)}, u32[]{:S(2)}) collective-permute-start(f32[18,16,512]{2,1,0:T(8,128)S(1)} %get-tuple-element.66), channel_id=1, source_target_pairs={{0,1},{1,0},{2,3},{3,2},{4,5},{5,4},{6,7},{7,6},{8,9},{9,8},{10,11... | collective-permute-start | bytes 1769480 | tf_op jit(solution)/shard_map/ppermute | solution.py:472
  51.9 8.6 %collective-permute-start.12 = (f32[18,16,512]{2,1,0:T(8,128)S(1)}, f32[18,16,512]{2,1,0:T(8,128)S(1)}, u32[]{:S(2)}, u32[]{:S(2)}) collective-permute-start(f32[18,16,512]{2,1,0:T(8,128)S(1)} %get-tuple-element.64.refs_0_), channel_id=1, source_target_pairs={{1,4},{4,1},{5,8},{8,5},{9,12},{12,9},{3,6},{6,3},{7,10},{10,7},{1... | collective-permute-start | bytes 1769480 | tf_op jit(solution)/shard_map/ppermute | solution.py:475
  52.5 5.0 %collective-permute-start.14 = (f32[8,8,512]{2,1,0:T(8,128)S(1)}, f32[8,8,512]{2,1,0:T(8,128)S(1)}, u32[]{:S(2)}, u32[]{:S(2)}) collective-permute-start(f32[8,8,512]{2,1,0:T(8,128)S(1)} %get-tuple-element.68), channel_id=1, source_target_pairs={{0,2},{2,0},{1,3},{3,1},{4,6},{6,4},{5,7},{7,5},{8,10},{10,8},{9,1... | collective-permute-start | bytes 393224 | tf_op jit(solution)/shard_map/ppermute | solution.py:479
  57.6 2.9 %collective-permute-start.16 = (f32[8,8,512]{2,1,0:T(8,128)S(1)}, f32[8,8,512]{2,1,0:T(8,128)S(1)}, u32[]{:S(2)}, u32[]{:S(2)}) collective-permute-start(f32[8,8,512]{2,1,0:T(8,128)S(1)} %collective-permute-done.14.refs_12_), channel_id=1, source_target_pairs={{0,1},{1,0},{2,3},{3,2},{4,5},{5,4},{6,7},{7,6},{8,9},{9,8},{10,11... | collective-permute-start | bytes 393224 | tf_op jit(solution)/shard_map/ppermute | solution.py:472
  59.5 0.7 collective-permute-start.15
  67.3 14.5 %collective-permute-start.19 = (f32[19,16,512]{2,1,0:T(8,128)S(1)}, f32[19,16,512]{2,1,0:T(8,128)S(1)}, u32[]{:S(2)}, u32[]{:S(2)}) collective-permute-start(f32[19,16,512]{2,1,0:T(8,128)S(1)} %get-tuple-element.75), channel_id=1, source_target_pairs={{0,1},{1,0},{2,3},{3,2},{4,5},{5,4},{6,7},{7,6},{8,9},{9,8},{10,11... | collective-permute-start | bytes 1867784 | tf_op jit(solution)/shard_map/ppermute | solution.py:472
  73.6 8.2 %collective-permute-start.18 = (f32[19,16,512]{2,1,0:T(8,128)S(1)}, f32[19,16,512]{2,1,0:T(8,128)S(1)}, u32[]{:S(2)}, u32[]{:S(2)}) collective-permute-start(f32[19,16,512]{2,1,0:T(8,128)S(1)} %get-tuple-element.72.refs_0_), channel_id=1, source_target_pairs={{1,4},{4,1},{5,8},{8,5},{9,12},{12,9},{3,6},{6,3},{7,10},{10,7},{1... | collective-permute-start | bytes 1867784 | tf_op jit(solution)/shard_map/ppermute | solution.py:475
  74.3 4.7 %collective-permute-start.20 = (f32[6,8,512]{2,1,0:T(8,128)S(1)}, f32[6,8,512]{2,1,0:T(8,128)S(1)}, u32[]{:S(2)}, u32[]{:S(2)}) collective-permute-start(f32[6,8,512]{2,1,0:T(8,128)S(1)} %get-tuple-element.77), channel_id=1, source_target_pairs={{0,2},{2,0},{1,3},{3,1},{4,6},{6,4},{5,7},{7,5},{8,10},{10,8},{9,1... | collective-permute-start | bytes 294920 | tf_op jit(solution)/shard_map/ppermute | solution.py:479
  79.0 2.8 %collective-permute-start.22 = (f32[6,8,512]{2,1,0:T(8,128)S(1)}, f32[6,8,512]{2,1,0:T(8,128)S(1)}, u32[]{:S(2)}, u32[]{:S(2)}) collective-permute-start(f32[6,8,512]{2,1,0:T(8,128)S(1)} %collective-permute-done.20.refs_13_), channel_id=1, source_target_pairs={{0,1},{1,0},{2,3},{3,2},{4,5},{5,4},{6,7},{7,6},{8,9},{9,8},{10,11... | collective-permute-start | bytes 294920 | tf_op jit(solution)/shard_map/ppermute | solution.py:472
  80.9 0.7 collective-permute-start.21
  86.6 11.3 %collective-permute-start.25 = (f32[2,8,512]{2,1,0:T(8,128)S(1)}, f32[2,8,512]{2,1,0:T(8,128)S(1)}, u32[]{:S(2)}, u32[]{:S(2)}) collective-permute-start(f32[2,8,512]{2,1,0:T(8,128)S(1)} %get-tuple-element.84), channel_id=1, source_target_pairs={{0,2},{2,0},{1,3},{3,1},{4,6},{6,4},{5,7},{7,5},{8,10},{10,8},{9,1... | collective-permute-start | bytes 98312 | tf_op jit(solution)/shard_map/ppermute | solution.py:479
  88.3 13.0 %collective-permute-start.23 = (f32[1,16,512]{2,1,0:T(8,128)S(1)}, f32[1,16,512]{2,1,0:T(8,128)S(1)}, u32[]{:S(2)}, u32[]{:S(2)}) collective-permute-start(f32[1,16,512]{2,1,0:T(8,128)S(1)} %get-tuple-element.82), channel_id=1, source_target_pairs={{1,4},{4,1},{5,8},{8,5},{9,12},{12,9},{3,6},{6,3},{7,10},{10,7},{1... | collective-permute-start | bytes 98312 | tf_op jit(solution)/shard_map/ppermute | solution.py:475
  88.9 12.4 %collective-permute-start.24 = (f32[1,16,512]{2,1,0:T(8,128)S(1)}, f32[1,16,512]{2,1,0:T(8,128)S(1)}, u32[]{:S(2)}, u32[]{:S(2)}) collective-permute-start(f32[1,16,512]{2,1,0:T(8,128)S(1)} %get-tuple-element.83), channel_id=1, source_target_pairs={{0,1},{1,0},{2,3},{3,2},{4,5},{5,4},{6,7},{7,6},{8,9},{9,8},{10,11... | collective-permute-start | bytes 98312 | tf_op jit(solution)/shard_map/ppermute | solution.py:472
  97.9 3.4 %collective-permute-start.27 = (f32[2,8,512]{2,1,0:T(8,128)S(1)}, f32[2,8,512]{2,1,0:T(8,128)S(1)}, u32[]{:S(2)}, u32[]{:S(2)}) collective-permute-start(f32[2,8,512]{2,1,0:T(8,128)S(1)} %collective-permute-done.25.refs_9_), channel_id=1, source_target_pairs={{0,1},{1,0},{2,3},{3,2},{4,5},{5,4},{6,7},{7,6},{8,9},{9,8},{10,11... | collective-permute-start | bytes 98312 | tf_op jit(solution)/shard_map/ppermute | solution.py:472
  98.0 3.3 %collective-permute-start.26 = (f32[1,8,512]{2,1,0:T(8,128)S(1)}, f32[1,8,512]{2,1,0:T(8,128)S(1)}, u32[]{:S(2)}, u32[]{:S(2)}) collective-permute-start(f32[1,8,512]{2,1,0:T(8,128)S(1)} %get-tuple-element.85), channel_id=1, source_target_pairs={{1,6},{3,4},{4,3},{6,1},{5,10},{7,8},{8,7},{10,5},{9,14},{11,12},{... | collective-permute-start | bytes 49160 | tf_op jit(solution)/shard_map/ppermute | solution.py:477
  98.7 7.2 %collective-permute-start.17 = (f32[16,16,256]{2,1,0:T(8,128)S(1)}, f32[16,16,256]{2,1,0:T(8,128)S(1)}, u32[]{:S(2)}, u32[]{:S(2)}) collective-permute-start(f32[16,16,256]{2,1,0:T(8,128)S(1)} %get-tuple-element.71), channel_id=1, source_target_pairs={{0,1},{1,0},{2,3},{3,2},{4,5},{5,4},{6,7},{7,6},{8,9},{9,8},{10,11... | collective-permute-start | bytes 786440 | tf_op jit(solution)/shard_map/ppermute | solution.py:472
  102.8 4.6 %collective-permute-start.28 = (f32[16,16,256]{2,1,0:T(8,128)S(1)}, f32[16,16,256]{2,1,0:T(8,128)S(1)}, u32[]{:S(2)}, u32[]{:S(2)}) collective-permute-start(f32[16,16,256]{2,1,0:T(8,128)S(1)} %get-tuple-element.87), channel_id=1, source_target_pairs={{0,1},{1,0},{2,3},{3,2},{4,5},{5,4},{6,7},{7,6},{8,9},{9,8},{10,11... | collective-permute-start | bytes 786440 | tf_op jit(solution)/shard_map/ppermute | solution.py:472

commit v4 on v3

--- a/solution.py
+++ b/solution.py
@@ -12,7 +12,7 @@
 MARGIN = 16
 TILE = 8
 F32 = jnp.float32
-UNROLL = 4
+UNROLL = 8
 SLACK = 8 << 20
 
 
@@ -123,13 +123,15 @@
                 dst[place, offset : offset + TILE, :] = value
 
 
-def fill_blocks(dst, xblock, cblock, g, geo):
+def fill_blocks(dst, xblock, cblock, g, geo, own=None):
     def one(row, carry):
         dst[g * 2 * geo.B + row, 0 : geo.Z, :] = xblock[row]
         dst[(1 - g) * 2 * geo.B + row, 0 : geo.Z, :] = cblock[row]
+        if own is not None:
+            dst[geo.B + row, 0 : geo.Z, :] = own[row]
         return carry
 
-    lax.fori_loop(0, geo.B, one, 0)
+    lax.fori_loop(0, geo.B, one, 0, unroll=2)
 
 
 def each(first, count, body, group):
@@ -143,33 +145,47 @@
     lax.fori_loop(0, count // group, trip, 0)
 
 
-def advance(src, first, count, prior, extra, store, coefs, dif, tot, geo):
-    xx, zz, yy, xz = coefs
-
-    def rolls(row):
-        value = src[row]
-        above = pltpu.roll(value, geo.ZE - 1, 0)
-        below = pltpu.roll(value, 1, 0)
-        dif[row] = above - below
-        tot[row] = above + below
-
-    each(first - 1, count + 2, rolls, 6)
-    lane = lax.broadcasted_iota(jnp.int32, (geo.ZE, geo.Y), 1)
+def advance(src, off, first, count, top, prior, extra, store, coefs, dif, tot, geo, group=None):
+    xx, zz, yy, xz, mid = coefs
+    lane = lax.broadcasted_iota(jnp.int32, (top, 128), 1)
+    low_edge, high_edge = lane == 0, lane == 127
+    spans = [slice(k, k + 128) for k in range(0, geo.Y, 128)]
+
+    def slopes(row):
+        value = src[row - off]
+        above = pltpu.roll(value, geo.ZE - 1, 0)[0:top]
+        below = pltpu.roll(value, 1, 0)[0:top]
+        dif[row, 0:top] = above - below
+        return value[0:top], above + below
+
+    def local(row):
+        at = jnp.minimum(row - (geo.B - 1), geo.B + 1)
+        whole, total = slopes(row)
+        value = [whole[:, span] for span in spans]
+        zero = jnp.zeros_like(value[0])
+        right = [pltpu.roll(v, 127, 1) for v in value] + [zero]
+        left = [zero] + [pltpu.roll(v, 1, 1) for v in value]
+        for k, span in enumerate(spans):
+            side = jnp.where(high_edge, right[k + 1], right[k]) + jnp.where(low_edge, left[k], left[k + 1])
+            new = mid[at, 0:top, span] * value[k] + zz[at, 0:top, span] * total[:, span]
+            tot[row, 0:top, span] = new + yy[at, 0:top, span] * side
+
+    slopes(first - 1)
+    local(first)
 
     def one(row):
+        local(row + 1)
         at = row - (geo.B - 1)
-        value = src[row]
-        right = jnp.where(lane == geo.Y - 1, 0.0, pltpu.roll(value, geo.Y - 1, 1))
-        left = jnp.where(lane == 0, 0.0, pltpu.roll(value, 1, 1))
-        cx, cz, cy = xx[at], zz[at], yy[at]
-        out = (2.0 - 2.0 * (cx + cz + cy)) * value - prior(row)
-        out = out + cx * (src[row + 1] + src[row - 1]) + cz * tot[row] + cy * (right + left)
-        out = out + xz[at] * (dif[row + 1] - dif[row - 1])
+        new = tot[row, 0:top] + xx[at, 0:top] * (src[row + 1 - off, 0:top] + src[row - 1 - off, 0:top])
+        new = new + xz[at, 0:top] * (dif[row + 1, 0:top] - dif[row - 1, 0:top])
+        last = prior(row)
+        if last is not None:
+            new = new - last[0:top]
         if extra is not None:
-            out = out + extra(row)
-        store(row, out)
-
-    each(first, count, one, UNROLL)
+            new = new + extra(row)[0:top]
+        store(row, new)
+
+    each(first, count, one, group or UNROLL)
 
 
 def make_source(ext, refl, refl_far, offsets, courant, out, g, geo):
@@ -225,22 +241,31 @@
         copy.wait()
 
 
-def widen_kernel(geo, scal, refl, near, out, held, sems):
+def widen_kernel(geo, scal, refl, out, held, sems):
+    other = pl.multiple_of((1 - scal[0]) * geo.B, TILE)
+    cuts = [0, 5, 9, 13, NOFF]
+    copies = [
+        pltpu.make_async_copy(refl.at[pl.ds(a, b - a), pl.ds(other, geo.B)], held.at[pl.ds(a, b - a)], sems.at[k])
+        for k, (a, b) in enumerate(zip(cuts, cuts[1:]))
+    ]
+    for copy in copies:
+        copy.start()
+    for copy, a, b in zip(copies, cuts, cuts[1:]):
+        copy.wait()
+
+        def one(h, carry):
+            for row in range(geo.B):
+                out[h, row] = held[h, row].astype(F32)
+            return carry
+
+        lax.fori_loop(a, b, one, 0)
+
+
+def own_refl_kernel(geo, scal, refl, out, sem):
     start = pl.multiple_of(scal[0] * geo.B, TILE)
-    other = pl.multiple_of((1 - scal[0]) * geo.B, TILE)
-    first = pltpu.make_async_copy(refl.at[:, pl.ds(other, geo.B)], held, sems.at[0])
-    second = pltpu.make_async_copy(refl.at[:, pl.ds(start, geo.B)], near, sems.at[1])
-    first.start()
-    second.start()
-    first.wait()
-
-    def one(h, carry):
-        for row in range(geo.B):
-            out[h, row] = held[h, row].astype(F32)
-        return carry
-
-    lax.fori_loop(0, NOFF, one, 0)
-    second.wait()
+    copy = pltpu.make_async_copy(refl.at[:, pl.ds(start, geo.B)], out, sem)
+    copy.start()
+    copy.wait()
 
 
 def join_kernel(geo, scal, *refs):
@@ -268,148 +293,186 @@
     pack_tiles(items, g, s, tiles, corners, geo)
 
 
+def coefficients(speed, aniso, angle):
+    stretch = 2.0 * aniso
+    sine_square, cosine_square, product = trig_products(angle)
+    cx = speed * (1.0 + stretch * cosine_square)
+    cz = speed * (1.0 + stretch * sine_square)
+    cy = speed * (1.0 + stretch)
+    return cx, cz, cy, (0.5 * speed) * (stretch * product), 2.0 - 2.0 * (cx + cz + cy)
+
+
+def coef_kernel(geo, scal, courant, aniso, tilt, *coefs):
+    def one(row):
+        for ref, value in zip(coefs, coefficients(courant[row], aniso[row], tilt[row])):
+            ref[row + 1, 0 : geo.Z, :] = value
+
+    each(0, geo.B, one, 2)
+
+
+def coef_halo(coefs, xr, cr, tiles, xtiles, ctiles, starts, g, s, geo):
+    ends = list(zip(receivers(s, geo), tiles, xtiles, ctiles))
+    for (offset, sender), tile, _, _ in ends:
+        keep = tile_mask(sender, 1, 0, geo.Y)
+        for q in range(geo.B // TILE):
+            values = coefficients(*(tile[start + q] for start in starts))
+            for k in range(TILE):
+                for ref, value in zip(coefs, values):
+                    place = (q * TILE + k + 1, slice(offset, offset + TILE))
+                    ref[place] = jnp.where(keep, turned(value, TILE - k), 0.0)
+    for side, line, is_x in ((g, xr, True), (1 - g, cr, False)):
+        at = side * (geo.B + 1)
+        for ref, value in zip(coefs, coefficients(line[3], line[4], line[5])):
+            ref[at, 0 : geo.Z, :] = value
+        for (offset, sender), _, xtile, ctile in ends:
+            if is_x:
+                fields = [turned(xtile[1 - side], TILE - turn) for turn in (3, 4, 5)]
+            else:
+                fields = [
+                    jnp.where(
+                        side == 1,
+                        unpack_row(ctile, start, 0, 1, sender, geo),
+                        unpack_row(ctile, start, geo.B - 1, 1, sender, geo),
+                    )
+                    for start in starts
+                ]
+            keep = tile_mask(sender, 1, 0, geo.Y)
+            for ref, value in zip(coefs, coefficients(*fields)):
+                ref[at, offset : offset + TILE, :] = jnp.where(keep, value, 0.0)
+
+
 def first_kernel(geo, scal, *refs):
     n = geo.sides
-    now, before, courant, aniso, tilt, xr, cr = refs[:7]
-    tiles, xtiles, ctiles = refs[7 : 7 + n], refs[7 + n : 7 + 2 * n], refs[7 + 2 * n : 7 + 3 * n]
-    out_block, prior_ext, xx, zz, yy, xz = refs[7 + 3 * n : 13 + 3 * n]
-    out_tiles, out_corners = refs[13 + 3 * n : 13 + 4 * n], refs[13 + 4 * n : 13 + 5 * n]
-    ext, old, dif, tot, mid, ca, cb, cc = refs[13 + 5 * n :]
+    now, before, xr, cr = refs[:4]
+    tiles, xtiles, ctiles = refs[4 : 4 + n], refs[4 + n : 4 + 2 * n], refs[4 + 2 * n : 4 + 3 * n]
+    out_block, prior_ext, *coefs = refs[9 + 3 * n : 16 + 3 * n]
+    out_tiles, out_corners = refs[16 + 3 * n : 16 + 4 * n], refs[16 + 4 * n : 16 + 5 * n]
+    ext, old, dif, tot = refs[16 + 5 * n :]
     g, s = scal[0], scal[1]
     starts, _ = tiles_of([2, 1, 1, 1, 1], geo)
-    for k, (dst, own) in enumerate(((old, before), (ca, courant), (cb, aniso), (cc, tilt)), 1):
-        xrow, crow = (lambda _, k=k: xr[1 + k]), (lambda _, k=k: cr[1 + k])
-        fill(dst, own, xrow, crow, tiles, xtiles, ctiles, starts[k], 1, 1 + k, g, s, geo)
+    coef_halo(coefs, xr, cr, tiles, xtiles, ctiles, starts[2:], g, s, geo)
+    fill(old, before, lambda _: xr[2], lambda _: cr[2], tiles, xtiles, ctiles, starts[1], 1, 2, g, s, geo)
     fill(ext, now, lambda k: xr[k], lambda k: cr[k], tiles, xtiles, ctiles, 0, 2, 0, g, s, geo)
-
-    def coefficients(row, carry):
-        at = row - (geo.B - 1)
-        speed, stretch = ca[row], 2.0 * cb[row]
-        sine_square, cosine_square, product = trig_products(cc[row])
-        xx[at] = speed * (1.0 + stretch * cosine_square)
-        zz[at] = speed * (1.0 + stretch * sine_square)
-        yy[at] = speed * (1.0 + stretch)
-        xz[at] = (0.5 * speed) * (stretch * product)
-        return carry
-
-    lax.fori_loop(geo.B - 1, 2 * geo.B + 1, coefficients, 0)
-    two_steps(ext, mid, lambda row: old[row], prior_ext, out_block, (xx, zz, yy, xz), dif, tot, geo)
-    pack_tiles([(out_block, 2, 0)], g, s, out_tiles, out_corners, geo)
-
-
-def two_steps(ext, mid, prior, prior_ext, out_block, coefs, dif, tot, geo):
-    def keep(row, value):
-        mid[row] = value
-        prior_ext[row - (geo.B - 1)] = value
 
     def keep_block(row, value):
         out_block[row - geo.B] = value[0 : geo.Z]
 
-    advance(ext, geo.B - 1, geo.B + 2, prior, None, keep, coefs, dif, tot, geo)
-    advance(mid, geo.B, geo.B, lambda row: ext[row], None, keep_block, coefs, dif, tot, geo)
+    two_steps(ext, lambda row: old[row], prior_ext, keep_block, coefs, dif, tot, geo)
+    pack_tiles([(out_block, 2, 0)], g, s, out_tiles, out_corners, geo)
+
+
+def two_steps(ext, prior, mid, store, coefs, dif, tot, geo):
+    off = geo.B - 1
+
+    def keep(row, value):
+        mid[row - off] = value
+
+    advance(ext, 0, off, geo.B + 2, geo.ZE, prior, None, keep, coefs, dif, tot, geo)
+    advance(mid, off, geo.B, geo.B, geo.Z, lambda row: ext[row], None, store, coefs, dif, tot, geo)
 
 
 def second_kernel(geo, scal, offsets, *refs):
     n = geo.sides
-    now, before, xr, cr, courant, refl, refl_far, *coefs = refs[:11]
-    tiles, xtiles, ctiles = refs[11 : 11 + n], refs[11 + n : 11 + 2 * n], refs[11 + 2 * n : 11 + 3 * n]
-    px, pc, prior_ext, force = refs[11 + 3 * n : 15 + 3 * n]
-    out_tiles, out_corners = refs[15 + 3 * n : 15 + 4 * n], refs[15 + 4 * n : 15 + 5 * n]
-    ext, dif, tot, mid = refs[15 + 5 * n :]
+    now, before, xr, cr, courant, refl, refl_far, *coefs = refs[:12]
+    tiles, xtiles, ctiles = refs[12 : 12 + n], refs[12 + n : 12 + 2 * n], refs[12 + 2 * n : 12 + 3 * n]
+    px, pc, prior_ext, force = refs[12 + 3 * n : 16 + 3 * n]
+    out_tiles, out_corners = refs[16 + 3 * n : 16 + 4 * n], refs[16 + 4 * n : 16 + 5 * n]
+    ext, dif, tot = refs[16 + 5 * n :]
     g, s = scal[0], scal[1]
+    B = geo.B
+    fill_blocks(ext, xr, cr, g, geo)
     fill(ext, now, None, None, tiles, xtiles, ctiles, 0, 2, 0, g, s, geo)
-    fill_blocks(ext, xr, cr, g, geo)
-    two_steps(ext, mid, lambda row: before[row - (geo.B - 1)], prior_ext, px, coefs, dif, tot, geo)
+
+    def keep_block(row, value):
+        px[row - B] = value[0 : geo.Z]
+        pc[row - B] = value[0 : geo.Z]
+
+    two_steps(ext, lambda row: before[row - (B - 1)], prior_ext, keep_block, coefs, dif, tot, geo)
     make_source(ext, refl, refl_far, offsets, courant, force, g, geo)
-
-    def one(row, carry):
-        pc[row] = px[row]
-        return carry
-
-    lax.fori_loop(0, geo.B, one, 0)
     for side, out in ((g, px), (1 - g, pc)):
         for k in range(2):
-            out[geo.B + k] = force[edge_rows(2, side, geo) + k]
+            out[B + k] = force[edge_rows(2, side, geo) + k]
     pack_tiles([(px, 2, 0), (force, 2, 4)], g, s, out_tiles, out_corners, geo)
 
 
-def third_kernel(geo, scal, offsets, *refs):
+def third_kernel(geo, scal, *refs):
     n = geo.sides
-    now, before, xr, cr, courant, refl, refl_far, *coefs = refs[:11]
-    force = refs[11]
-    tiles, xtiles, ctiles = refs[12 : 12 + n], refs[12 + n : 12 + 2 * n], refs[12 + 2 * n : 12 + 3 * n]
-    px, pc, force_out, scat, scat_prior, near, back = refs[12 + 3 * n : 19 + 3 * n]
-    out_tiles, out_corners = refs[19 + 3 * n : 19 + 4 * n], refs[19 + 4 * n : 19 + 5 * n]
-    ext, dif, tot, mid, wave = refs[19 + 5 * n :]
+    now, before, xr, cr, *coefs = refs[:9]
+    tiles, xtiles, ctiles = refs[9 : 9 + n], refs[9 + n : 9 + 2 * n], refs[9 + 2 * n : 9 + 3 * n]
+    block, near, back = refs[9 + 3 * n : 12 + 3 * n]
+    ext, dif, tot, mid = refs[12 + 3 * n :]
     g, s = scal[0], scal[1]
     B = geo.B
-    fill(ext, now, None, None, tiles, xtiles, ctiles, 0, 2, 0, g, s, geo)
-    fill_blocks(ext, xr, cr, g, geo)
-
-    def keep_mid(row, value):
-        mid[row] = value
+    fill(ext, now, lambda k: xr[near_row(g, k, geo)], lambda k: cr[near_row(1 - g, k, geo)], tiles, xtiles, ctiles, 0, 2, 0, g, s, geo)
 
     def keep_block(row, value):
         value = value[0 : geo.Z]
-        px[row - B] = value
-        pc[row - B] = value
+        block[row - B] = value
         low, high = value[:, 0 : geo.H], value[:, geo.H : geo.Y]
         near[row - B] = jnp.where(g == 0, low, high)
         back[row - B] = jnp.where(g == 0, high, low)
 
-    advance(ext, B - 1, B + 2, lambda row: before[row - (B - 1)], None, keep_mid, coefs, dif, tot, geo)
-    advance(mid, B, B, lambda row: ext[row], None, keep_block, coefs, dif, tot, geo)
+    two_steps(ext, lambda row: before[row - (B - 1)], mid, keep_block, coefs, dif, tot, geo)
+
+
+def near_row(side, k, geo):
+    return (1 - side) * (geo.B - 2) + k
+
+
+def scatter_kernel(geo, scal, offsets, *refs):
+    n = geo.sides
+    now, xr, cr, courant, refl, refl_far, *coefs = refs[:11]
+    force = refs[11]
+    tiles, xtiles, ctiles = refs[12 : 12 + n], refs[12 + n : 12 + 2 * n], refs[12 + 2 * n : 12 + 3 * n]
+    px, pc, force_out, scat, scat_prior = refs[12 + 3 * n : 17 + 3 * n]
+    out_tiles, out_corners = refs[17 + 3 * n : 17 + 4 * n], refs[17 + 4 * n : 17 + 5 * n]
+    ext, dif, tot, wave = refs[17 + 5 * n :]
+    g, s = scal[0], scal[1]
+    B = geo.B
+    fill_blocks(ext, xr, cr, g, geo, now)
     make_source(ext, refl, refl_far, offsets, courant, force_out, g, geo)
     start = tiles_of([2, 2], geo)[0][1]
     fill(wave, force, lambda k: xr[B + k], lambda k: cr[B + k], tiles, xtiles, ctiles, start, 2, 4, g, s, geo)
 
-    def keep_wave(row, value):
-        mid[row] = value
-        scat_prior[row - (B - 1)] = value
-
     def keep_scat(row, value):
         scat[row - B] = value[0 : geo.Z] + force_out[row - B]
 
-    advance(wave, B - 1, B + 2, lambda row: -wave[row], None, keep_wave, coefs, dif, tot, geo)
-    advance(mid, B, B, lambda row: wave[row], None, keep_scat, coefs, dif, tot, geo)
+    two_steps(wave, lambda row: -wave[row], scat_prior, keep_scat, coefs, dif, tot, geo)
     for side, out in ((g, px), (1 - g, pc)):
         for k in range(2):
-            out[B + k] = scat[edge_rows(2, side, geo) + k]
-        out[B + 2] = force_out[edge_rows(1, side, geo)]
+            out[k] = scat[edge_rows(2, side, geo) + k]
+        out[2] = force_out[edge_rows(1, side, geo)]
     pack_tiles([(scat, 2, 0), (force_out, 1, 2)], g, s, out_tiles, out_corners, geo)
 
 
-def fourth_kernel(geo, scal, offsets, *refs):
+def source_kernel(geo, scal, offsets, now, xr, cr, courant, refl, refl_far, force, ext):
+    g = scal[0]
+    fill_blocks(ext, xr, cr, g, geo, now)
+    make_source(ext, refl, refl_far, offsets, courant, force, g, geo)
+
+
+def fourth_kernel(geo, scal, *refs):
     n = geo.sides
-    now, scat, before, xr, cr, courant, refl, refl_far, *coefs = refs[:12]
-    force2 = refs[12]
-    tiles, xtiles, ctiles = refs[13 : 13 + n], refs[13 + n : 13 + 2 * n], refs[13 + 2 * n : 13 + 3 * n]
-    scat_out, scat_prior, force_out, px, pc = refs[13 + 3 * n : 18 + 3 * n]
-    out_tiles, out_corners = refs[18 + 3 * n : 18 + 4 * n], refs[18 + 4 * n : 18 + 5 * n]
-    ext, dif, tot, mid, wave = refs[18 + 5 * n :]
+    scat, before, xr, cr, force2, force3, *coefs = refs[:11]
+    tiles, xtiles, ctiles = refs[11 : 11 + n], refs[11 + n : 11 + 2 * n], refs[11 + 2 * n : 11 + 3 * n]
+    scat_out, scat_prior, px, pc = refs[11 + 3 * n : 15 + 3 * n]
+    out_tiles, out_corners = refs[15 + 3 * n : 15 + 4 * n], refs[15 + 4 * n : 15 + 5 * n]
+    wave, extra, dif, tot, mid = refs[15 + 5 * n :]
     g, s = scal[0], scal[1]
     B = geo.B
-
-    def own(row, carry):
-        ext[B + row, 0 : geo.Z, :] = now[row]
-        return carry
-
-    lax.fori_loop(0, B, own, 0)
-    fill_blocks(ext, xr, cr, g, geo)
-    make_source(ext, refl, refl_far, offsets, courant, force_out, g, geo)
-    fill(wave, scat, lambda k: xr[B + k], lambda k: cr[B + k], tiles, xtiles, ctiles, 0, 2, 0, g, s, geo)
+    fill(wave, scat, lambda k: xr[k], lambda k: cr[k], tiles, xtiles, ctiles, 0, 2, 0, g, s, geo)
     start = tiles_of([2, 1], geo)[0][1]
-    fill(ext, force2, lambda _: xr[B + 2], lambda _: cr[B + 2], tiles, xtiles, ctiles, start, 1, 2, g, s, geo)
+    fill(extra, force2, lambda _: xr[2], lambda _: cr[2], tiles, xtiles, ctiles, start, 1, 2, g, s, geo)
 
     def keep_wave(row, value):
-        mid[row] = value
+        mid[row - (B - 1)] = value
 
     def keep_scat(row, value):
-        scat_out[row - B] = value[0 : geo.Z] + force_out[row - B]
-        scat_prior[row - B] = mid[row, 0 : geo.Z, :]
-
-    advance(wave, B - 1, B + 2, lambda row: before[row - (B - 1)], lambda row: ext[row], keep_wave, coefs, dif, tot, geo)
-    advance(mid, B, B, lambda row: wave[row], None, keep_scat, coefs, dif, tot, geo)
+        scat_out[row - B] = value[0 : geo.Z] + force3[row - B]
+        scat_prior[row - B] = mid[row - (B - 1), 0 : geo.Z, :]
+
+    advance(wave, 0, B - 1, B + 2, geo.ZE, lambda row: before[row - (B - 1)], lambda row: extra[row], keep_wave, coefs, dif, tot, geo)
+    advance(mid, B - 1, B, B, geo.Z, lambda row: wave[row], None, keep_scat, coefs, dif, tot, geo)
     px[0] = scat_out[edge_rows(1, g, geo)]
     pc[0] = scat_out[edge_rows(1, 1 - g, geo)]
     pack_tiles([(scat_out, 1, 0)], g, s, out_tiles, out_corners, geo)
@@ -417,10 +480,10 @@
 
 def fifth_kernel(geo, scal, *refs):
     n = geo.sides
-    scat, before, force, xr, cr, *coefs = refs[:9]
-    tiles, xtiles, ctiles = refs[9 : 9 + n], refs[9 + n : 9 + 2 * n], refs[9 + 2 * n : 9 + 3 * n]
-    out_near, out_far = refs[9 + 3 * n : 11 + 3 * n]
-    ext, dif, tot = refs[11 + 3 * n :]
+    scat, before, force, xr, cr, *coefs = refs[:10]
+    tiles, xtiles, ctiles = refs[10 : 10 + n], refs[10 + n : 10 + 2 * n], refs[10 + 2 * n : 10 + 3 * n]
+    out_near, out_far = refs[10 + 3 * n : 12 + 3 * n]
+    ext, dif, tot = refs[12 + 3 * n :]
     g, s = scal[0], scal[1]
     B = geo.B
     fill(ext, scat, lambda _: xr[0], lambda _: cr[0], tiles, xtiles, ctiles, 0, 1, 0, g, s, geo)
@@ -432,7 +495,7 @@
         out_near[at] = jnp.where(g == 0, value[:, low], value[:, high])
         out_far[at] = jnp.where(g == 0, value[:, high], value[:, low])
 
-    advance(ext, B, B, lambda row: 0.0, None, keep, coefs, dif, tot, geo)
+    advance(ext, 0, B, B, geo.Z, lambda row: None, None, keep, coefs, dif, tot, geo, 16)
 
 
 def finish_kernel(geo, scal, near, far, out):
@@ -444,6 +507,14 @@
         return carry
 
     lax.fori_loop(0, geo.B, one, 0, unroll=4)
+
+
+def place_kernel(geo, scal, *refs, other):
+    half, out, sem = refs[0], refs[-2], refs[-1]
+    start = pl.multiple_of((1 - scal[0] if other else scal[0]) * geo.B, TILE)
+    copy = pltpu.make_async_copy(half, out.at[pl.ds(start, geo.B)], sem)
+    copy.start()
+    copy.wait()
 
 
 def shards(sections, gx, wave_now, wave_before, courant, anisotropy, tilt, reflectivity, offsets):
@@ -484,7 +555,7 @@
     def shape(*dims):
         return jax.ShapeDtypeStruct(dims, F32)
 
-    def call(kernel, inputs, outs, scratch, smem=1, specs=None, extra=()):
+    def call(kernel, inputs, outs, scratch, smem=1, specs=None, extra=(), aliases=None, out_specs=None):
         if specs is None:
             specs = [pl.BlockSpec(memory_space=pltpu.SMEM)] * (smem - 1)
             specs += [pl.BlockSpec(memory_space=pltpu.VMEM)] * (len(inputs) - smem)
@@ -496,9 +567,10 @@
                 num_scalar_prefetch=1,
                 grid=(1,),
                 in_specs=specs,
-                out_specs=[pl.BlockSpec(memory_space=pltpu.VMEM)] * len(outs),
+                out_specs=out_specs or [pl.BlockSpec(memory_space=pltpu.VMEM)] * len(outs),
                 scratch_shapes=[*(pltpu.VMEM(d, F32) for d in scratch), *extra],
             ),
+            input_output_aliases=aliases or {},
             compiler_params=pltpu.CompilerParams(vmem_limit_bytes=used + SLACK),
         )(*inputs)
 
@@ -511,6 +583,7 @@
     fields = [in_hbm(f) for f in (wave_now, wave_before, courant, anisotropy, tilt)]
     reflectivity = in_hbm(reflectivity)
     hbm = pl.BlockSpec(memory_space=pltpu.HBM)
+    whole = pl.BlockSpec(memory_space=pltpu.VMEM)
 
     def half_of(other):
         kernel = functools.partial(half_kernel, other=other)
@@ -531,57 +604,62 @@
         n,
     )
     xr, cr, halo = exchange(px, pc, r0, r1)
-    refl, refl_far = call(
+    (refl_far,) = call(
         widen_kernel,
         [scal, reflectivity],
-        [jax.ShapeDtypeStruct((NOFF, B, Z, H), reflectivity.dtype), shape(NOFF, B, Z, H)],
+        [shape(NOFF, B, Z, H)],
         [],
         specs=[hbm],
-        extra=[pltpu.VMEM((NOFF, B, Z, H), reflectivity.dtype), pltpu.SemaphoreType.DMA((2,))],
+        extra=[pltpu.VMEM((NOFF, B, Z, H), reflectivity.dtype), pltpu.SemaphoreType.DMA((4,))],
     )
     refl_far = chip(refl_far)
+    coefs = call(coef_kernel, [scal, *own[2:]], [shape(*wide)] * 5, [])
+    inputs = [scal, *own[:2], xr, cr, *halo, *coefs]
+    first = len(inputs) - 5
     now, prior, *coefs, r0, r1 = _split(
         call(
-            first_kernel, [scal, *own, xr, cr, *halo], [shape(*block)] + [shape(*wide)] * 5 + tile_outs([2]), [ext] * 8
+            first_kernel,
+            inputs,
+            [shape(*block)] + [shape(*wide)] * 6 + tile_outs([2]),
+            [ext] * 4,
+            aliases={first + k: 2 + k for k in range(5)},
         ),
-        6,
+        7,
         n,
     )
+    courant_own = own[2]
     xr, cr, halo = exchange(now, now, r0, r1)
+    (refl,) = call(
+        own_refl_kernel,
+        [scal, reflectivity],
+        [jax.ShapeDtypeStruct((NOFF, B, Z, H), reflectivity.dtype)],
+        [],
+        specs=[hbm],
+        extra=[pltpu.SemaphoreType.DMA],
+    )
     px, pc, prior, force, r0, r1 = _split(
         call(
             second_kernel,
-            [scal, offsets, now, prior, xr, cr, own[2], refl, refl_far, *coefs, *halo],
+            [scal, offsets, now, prior, xr, cr, courant_own, refl, refl_far, *coefs, *halo],
             [shape(B + 2, Z, Y)] * 2 + [shape(*wide), shape(*block)] + tile_outs([2, 2]),
-            [ext] * 4,
+            [ext] * 3,
             2,
         ),
         4,
         n,
     )
     xr, cr, halo = exchange(px, pc, r0, r1)
-    px, pc, force2, scat, scat_prior, near_u, back, r0, r1 = _split(
+    wave, near_u, back = call(
+        third_kernel, [scal, px, prior, xr, cr, *coefs, *halo], [shape(*block)] + [shape(B, Z, H)] * 2, [ext] * 3 + [wide]
+    )
+    wave_x = lax.ppermute(wave, ("gx", "gy"), pairs_x)
+    wave_c = chip(wave)
+    qx, qc, force2, scat, scat_prior, r0, r1 = _split(
         call(
-            third_kernel,
-            [scal, offsets, px, prior, xr, cr, own[2], refl, refl_far, *coefs, force, *halo],
-            [shape(B + 3, Z, Y)] * 2
-            + [shape(*block)] * 2
-            + [shape(*wide)]
-            + [shape(B, Z, H)] * 2
-            + tile_outs([2, 1]),
-            [ext] * 5,
-            2,
-        ),
-        7,
-        n,
-    )
-    xr, cr, halo = exchange(px, pc, r0, r1)
-    scat, scat_prior, force3, qx, qc, r0, r1 = _split(
-        call(
-            fourth_kernel,
-            [scal, offsets, px, scat, scat_prior, xr, cr, own[2], refl, refl_far, *coefs, force2, *halo],
-            [shape(*block)] * 3 + [shape(1, Z, Y)] * 2 + tile_outs([1], 1),
-            [ext] * 5,
+            scatter_kernel,
+            [scal, offsets, px, xr, cr, courant_own, refl, refl_far, *coefs, force, *halo],
+            [shape(3, Z, Y)] * 2 + [shape(*block)] * 2 + [shape(*wide)] + tile_outs([2, 1]),
+            [ext] * 4,
             2,
         ),
         5,
@@ -589,11 +667,44 @@
     )
     xr, cr, halo = exchange(qx, qc, r0, r1)
     back = chip(back)
+    (force3,) = call(
+        source_kernel,
+        [scal, offsets, wave, wave_x, wave_c, courant_own, refl, refl_far],
+        [shape(*block)],
+        [ext],
+        2,
+    )
+    scat, scat_prior, qx, qc, r0, r1 = _split(
+        call(
+            fourth_kernel,
+            [scal, scat, scat_prior, xr, cr, force2, force3, *coefs, *halo],
+            [shape(*block)] * 2 + [shape(1, Z, Y)] * 2 + tile_outs([1], 1),
+            [ext] * 4 + [wide],
+        ),
+        4,
+        n,
+    )
+    xr, cr, halo = exchange(qx, qc, r0, r1)
+
+    def placed(half, other, into=None):
+        return call(
+            functools.partial(place_kernel, other=other),
+            [scal, half] + ([] if into is None else [into]),
+            [shape(rows, Z, H)],
+            [],
+            specs=[whole] + ([] if into is None else [hbm]),
+            extra=[pltpu.SemaphoreType.DMA],
+            aliases={} if into is None else {2: 0},
+            out_specs=[hbm],
+        )[0]
+
     (background,) = call(finish_kernel, [scal, near_u, back], [shape(rows, Z, H)], [])
     near_w, far_w = call(
         fifth_kernel, [scal, scat, scat_prior, force3, xr, cr, *coefs, *halo], [shape(B, Z, H)] * 2, [ext] * 3
     )
-    (scattered,) = call(finish_kernel, [scal, near_w, chip(far_w)], [shape(rows, Z, H)], [])
+    far_w = chip(far_w)
+    scattered = placed(near_w, False)
+    scattered = placed(far_w, True, scattered)
     return background, scattered
 
 

time: 109 us -> 105 us (0.963)
  waiting for transfers between devices: 18.8 us -> 14.6 us
  starting transfers between devices: 56.2 us -> 54.8 us
  Pallas kernels: 32.7 us -> 33.9 us
    ppermute x5, waiting for transfers between devices: 12 us -> 8.58 us  [exchange(): zr = [lax.ppermute(t, 'section', m) for t, m in zip(tiles, z_moves())]]
    ppermute x14 -> x15, starting transfers between devices: 41.5 us -> 38.3 us  [chip(): return lax.ppermute(value, 'gy', swap)]
    pallas_call x11 -> x16, Pallas kernels: 32.7 us -> 33.9 us  [call(): pl.pallas_call(functools.partial(kernel, geo), out_shape=outs, grid_spec=...]
    ppermute x14 -> x15, waiting for transfers between devices: 6.83 us -> 5.94 us  [chip(): return lax.ppermute(value, 'gy', swap)]
  transfers between devices with their start and end apart: 29 -> 31, of which waited for: 9 -> 6; matrix products, arithmetic and copies ran while one was open for 0% -> 0% of each run, Pallas kernels for 11% -> 21%
where the time goes in v4:
time: 105 us; the launch traced here: 104 us
  starting transfers between devices  54.8 us (52%)
  Pallas kernels  33.9 us (32%)
  waiting for transfers between devices  14.6 us (14%)
    ppermute x15, starting transfers between devices, chip(): return lax.ppermute(value, 'gy', swap)  38.3 us
    pallas_call x16, Pallas kernels, call(): pl.pallas_call(functools.partial(kernel, geo), out_shape=outs, grid_spec=...  33.9 us
    ppermute x5, starting transfers between devices, exchange(): zr = [lax.ppermute(t, 'section', m) for t, m in zip(tiles, z_moves())]  9.01 us
    ppermute x5, waiting for transfers between devices, exchange(): zr = [lax.ppermute(t, 'section', m) for t, m in zip(tiles, z_moves())]  8.58 us
    ppermute x15, waiting for transfers between devices, chip(): return lax.ppermute(value, 'gy', swap)  5.94 us
    ppermute x5, starting transfers between devices, exchange(): lax.ppermute(t, ('gx', 'section', 'gy'), corner_pairs(m))  3.39 us
    ppermute x5, starting transfers between devices, exchange(): xr = lax.ppermute(px, ('gx', 'gy'), pairs_x)  3.36 us
  transfers between devices with their start and end apart: 31, of which 6 were waited for; matrix products, arithmetic and copies ran while one was open for 0% of the time, Pallas kernels for 21%

profile of v4, /device:TPU:0, one launch (start us, length us, event | category | flops | bytes accessed | tf_op | source)
XLA Modules:
  0.0 104.3 jit_solution(6951963641162761953)
XLA Ops:
  0.7 2.2 %shard_map.92 = f32[17,16,16,256]{3,2,1,0:T(8,128)S(1)} custom-call(s32[2]{0:T(128)S(1)} %pad_add_fusion.scal, bf16[17,32,16,256]{3,2,1,0:T(8,128)(2,1)} %refl.3), custom_call_target="tpu_custom_call" | custom-call | tf_op jit(solution)/shard_map/pallas_call | solution.py:563
  2.9 0.6 collective-permute-start.8
  3.5 1.9 %shard_map.87 = f32[5,16,16,256]{3,2,1,0:T(8,128)S(1)} custom-call(s32[2]{0:T(128)S(1)} %pad_add_fusion.scal, f32[32,16,256]{2,1,0:T(8,128)} %refs_0_.3, f32[32,16,256]{2,1,0:T(8,128)} %refs_1_.3, f32[32,16,256]{2,1,0:T(8,128)} %refs_2_.3, f32[32,16,256]{2,1,0:T(8,128)} %refs_3_.3, f32[32,16,256]{2,1,0:T(8,128)} %refs_4_.3), custom_call_target="tpu_custom_call" | custom-call | tf_op jit(solution)/shard_map/pallas_call | solution.py:563
  5.4 1.9 %shard_map.86.refs_0_ = f32[5,16,16,256]{3,2,1,0:T(8,128)S(1)} custom-call(s32[2]{0:T(128)S(1)} %pad_add_fusion.scal, f32[32,16,256]{2,1,0:T(8,128)} %refs_0_.3, f32[32,16,256]{2,1,0:T(8,128)} %refs_1_.3, f32[32,16,256]{2,1,0:T(8,128)} %refs_2_.3, f32[32,16,256]{2,1,0:T(8,128)} %refs_3_.3, f32[32,16,256]{2,1,0:T(8,128)} %refs_4_.3), custom_call_target="tpu_custom_call" | custom-call | tf_op jit(solution)/shard_map/pallas_call | solution.py:563
  7.3 5.2 %collective-permute-done.refs_1_ = f32[5,16,16,256]{3,2,1,0:T(8,128)S(1)} collective-permute-done((f32[5,16,16,256]{3,2,1,0:T(8,128)S(1)}, f32[5,16,16,256]{3,2,1,0:T(8,128)S(1)}, u32[]{:S(2)}, u32[]{:S(2)}) %collective-permute-start) | collective-permute-done | bytes 1310752 | tf_op jit(solution)/shard_map/ppermute | solution.py:543
  12.5 0.9 shard_map.88
  13.4 2.9 %collective-permute-start.3 = (f32[12,8,512]{2,1,0:T(8,128)S(1)}, f32[12,8,512]{2,1,0:T(8,128)S(1)}, u32[]{:S(2)}, u32[]{:S(2)}) collective-permute-start(f32[12,8,512]{2,1,0:T(8,128)S(1)} %get-tuple-element.53), channel_id=1, source_target_pairs={{0,2},{2,0},{1,3},{3,1},{4,6},{6,4},{5,7},{7,5},{8,10},{10,8},{9,1... | collective-permute-start | bytes 589832 | tf_op jit(solution)/shard_map/ppermute | solution.py:550
  16.3 0.7 collective-permute-start.1
  17.0 3.0 %collective-permute-start.2 = (f32[6,16,512]{2,1,0:T(8,128)S(1)}, f32[6,16,512]{2,1,0:T(8,128)S(1)}, u32[]{:S(2)}, u32[]{:S(2)}) collective-permute-start(f32[6,16,512]{2,1,0:T(8,128)S(1)} %get-tuple-element.52), channel_id=1, source_target_pairs={{0,1},{1,0},{2,3},{3,2},{4,5},{5,4},{6,7},{7,6},{8,9},{9,8},{10,11... | collective-permute-start | bytes 589832 | tf_op jit(solution)/shard_map/ppermute | solution.py:543
  20.0 1.5 %collective-permute-done.3.refs_4_ = f32[12,8,512]{2,1,0:T(8,128)S(1)} collective-permute-done((f32[12,8,512]{2,1,0:T(8,128)S(1)}, f32[12,8,512]{2,1,0:T(8,128)S(1)}, u32[]{:S(2)}, u32[]{:S(2)}) %collective-permute-start.3) | collective-permute-done | bytes 196640 | tf_op jit(solution)/shard_map/ppermute | solution.py:550
  21.5 0.7 collective-permute-start.4
  22.2 1.6 %shard_map.89 = (f32[18,24,512]{2,1,0:T(8,128)S(1)}, f32[18,24,512]{2,1,0:T(8,128)S(1)}, f32[18,24,512]{2,1,0:T(8,128)S(1)}, f32[18,24,512]{2,1,0:T(8,128)S(1)}, f32[18,24,512]{2,1,0:T(8,128)S(1)}) custom-call(s32[2]{0:T(128)S(1)} %pad_add_fusion.scal, f32[16,16,512]{2,1,0:T(8,128)S(1)} %get-tuple-element.55.courant.refs_4_.refs_3_, ...), custom_call_target="tpu_custom_call" | custom-call | tf_op jit(solution)/shard_map/pallas_call | solution.py:563
  23.8 2.8 %shard_map.90 = (f32[16,16,512]{2,1,0:T(8,128)S(1)}, f32[18,24,512]{2,1,0:T(8,128)S(1)}, f32[18,24,512]{2,1,0:T(8,128)S(1)}, f32[18,24,512]{2,1,0:T(8,128)S(1)},...) custom-call(s32[2]{0:T(128)S(1)} %pad_add_fusion.scal, ...), custom_call_target="tpu_custom_call", output_to_operand_aliasing={{2}: (8, {}), {3}: (9, {}), {4}: (10, {}), {5}: (11, {}), {... | custom-call | tf_op jit(solution)/shard_map/pallas_call | solution.py:563
  26.6 0.7 collective-permute-start.6
  27.3 7.1 %collective-permute-start.7 = (f32[16,16,512]{2,1,0:T(8,128)S(1)}, f32[16,16,512]{2,1,0:T(8,128)S(1)}, u32[]{:S(2)}, u32[]{:S(2)}) collective-permute-start(f32[16,16,512]{2,1,0:T(8,128)S(1)} %get-tuple-element.63.refs_0_), channel_id=1, source_target_pairs={{0,1},{1,0},{2,3},{3,2},{4,5},{5,4},{6,7},{7,6},{8,9},{9,8},{10,11... | collective-permute-start | bytes 1572872 | tf_op jit(solution)/shard_map/ppermute | solution.py:543
  34.4 1.5 %collective-permute-start.9 = (f32[4,8,512]{2,1,0:T(8,128)S(1)}, f32[4,8,512]{2,1,0:T(8,128)S(1)}, u32[]{:S(2)}, u32[]{:S(2)}) collective-permute-start(f32[4,8,512]{2,1,0:T(8,128)S(1)} %get-tuple-element.70), channel_id=1, source_target_pairs={{0,2},{2,0},{1,3},{3,1},{4,6},{6,4},{5,7},{7,5},{8,10},{10,8},{9,1... | collective-permute-start | bytes 196616 | tf_op jit(solution)/shard_map/ppermute | solution.py:550
  35.8 2.8 %collective-permute-done.9.refs_12_ = f32[4,8,512]{2,1,0:T(8,128)S(1)} collective-permute-done((f32[4,8,512]{2,1,0:T(8,128)S(1)}, f32[4,8,512]{2,1,0:T(8,128)S(1)}, u32[]{:S(2)}, u32[]{:S(2)}) %collective-permute-start.9) | collective-permute-done | bytes 65568 | tf_op jit(solution)/shard_map/ppermute | solution.py:550
  38.6 0.8 collective-permute-start.10
  39.4 2.2 %shard_map.91.refs_5_.refs_4_.refl = bf16[17,16,16,256]{3,2,1,0:T(8,128)(2,1)S(1)} custom-call(s32[2]{0:T(128)S(1)} %pad_add_fusion.scal, bf16[17,32,16,256]{3,2,1,0:T(8,128)(2,1)} %refl.3), custom_call_target="tpu_custom_call" | custom-call | tf_op jit(solution)/shard_map/pallas_call | solution.py:563
  41.7 4.1 %shard_map.93 = (f32[18,16,512]{2,1,0:T(8,128)S(1)}, f32[18,16,512]{2,1,0:T(8,128)S(1)}, f32[18,24,512]{2,1,0:T(8,128)S(1)}, f32[16,16,512]{2,1,0:T(8,128)S(1)},...) custom-call(s32[2]{0:T(128)S(1)} %pad_add_fusion.scal, s32[17]{0:T(128)S(1)} %copy-done, ...), custom_call_target="tpu_custom_call" | custom-call | tf_op jit(solution)/shard_map/pallas_call | solution.py:563
  45.8 0.7 collective-permute-start.12
  46.5 6.2 %collective-permute-start.13 = (f32[18,16,512]{2,1,0:T(8,128)S(1)}, f32[18,16,512]{2,1,0:T(8,128)S(1)}, u32[]{:S(2)}, u32[]{:S(2)}) collective-permute-start(f32[18,16,512]{2,1,0:T(8,128)S(1)} %get-tuple-element.74), channel_id=1, source_target_pairs={{0,1},{1,0},{2,3},{3,2},{4,5},{5,4},{6,7},{7,6},{8,9},{9,8},{10,11... | collective-permute-start | bytes 1769480 | tf_op jit(solution)/shard_map/ppermute | solution.py:543
  52.7 1.5 %collective-permute-start.14 = (f32[8,8,512]{2,1,0:T(8,128)S(1)}, f32[8,8,512]{2,1,0:T(8,128)S(1)}, u32[]{:S(2)}, u32[]{:S(2)}) collective-permute-start(f32[8,8,512]{2,1,0:T(8,128)S(1)} %get-tuple-element.75), channel_id=1, source_target_pairs={{0,2},{2,0},{1,3},{3,1},{4,6},{6,4},{5,7},{7,5},{8,10},{10,8},{9,1... | collective-permute-start | bytes 393224 | tf_op jit(solution)/shard_map/ppermute | solution.py:550
  54.2 4.0 %collective-permute-done.14.refs_9_.refs_12_ = f32[8,8,512]{2,1,0:T(8,128)S(1)} collective-permute-done((f32[8,8,512]{2,1,0:T(8,128)S(1)}, f32[8,8,512]{2,1,0:T(8,128)S(1)}, u32[]{:S(2)}, u32[]{:S(2)}) %collective-permute-start.14) | collective-permute-done | bytes 131104 | tf_op jit(solution)/shard_map/ppermute | solution.py:550
  58.2 0.7 collective-permute-start.15
  58.9 0.7 collective-permute-done.16.refs_11_.refs_14_
  59.6 2.3 %shard_map.94 = (f32[16,16,512]{2,1,0:T(8,128)S(1)}, f32[16,16,256]{2,1,0:T(8,128)S(1)}, f32[16,16,256]{2,1,0:T(8,128)S(1)}) custom-call(s32[2]{0:T(128)S(1)} %pad_add_fusion.scal, f32[18,16,512]{2,1,0:T(8,128)S(1)} %get-tuple-element.72.refs_0_, f32[18,24,512]{2,1,0:T(8,128)S(1)} %get-tuple-element.73.refs_1_, ...), custom_call_target="tpu_custom_call" | custom-call | tf_op jit(solution)/shard_map/pallas_call | solution.py:563
  61.9 0.7 collective-permute-start.20
  62.6 7.8 %collective-permute-start.21 = (f32[16,16,512]{2,1,0:T(8,128)S(1)}, f32[16,16,512]{2,1,0:T(8,128)S(1)}, u32[]{:S(2)}, u32[]{:S(2)}) collective-permute-start(f32[16,16,512]{2,1,0:T(8,128)S(1)} %get-tuple-element.85.now), channel_id=1, source_target_pairs={{0,1},{1,0},{2,3},{3,2},{4,5},{5,4},{6,7},{7,6},{8,9},{9,8},{10,11... | collective-permute-start | bytes 1572872 | tf_op jit(solution)/shard_map/ppermute | solution.py:543
  70.4 4.2 %shard_map.96 = (f32[3,16,512]{2,1,0:T(8,128)S(1)}, f32[3,16,512]{2,1,0:T(8,128)S(1)}, f32[16,16,512]{2,1,0:T(8,128)S(1)}, f32[16,16,512]{2,1,0:T(8,128)S(1)}, f...) custom-call(s32[2]{0:T(128)S(1)} %pad_add_fusion.scal, s32[17]{0:T(128)S(1)} %copy-done, ...), custom_call_target="tpu_custom_call" | custom-call | tf_op jit(solution)/shard_map/pallas_call | solution.py:563
  74.5 1.6 %collective-permute-start.22 = (f32[6,8,512]{2,1,0:T(8,128)S(1)}, f32[6,8,512]{2,1,0:T(8,128)S(1)}, u32[]{:S(2)}, u32[]{:S(2)}) collective-permute-start(f32[6,8,512]{2,1,0:T(8,128)S(1)} %get-tuple-element.86), channel_id=1, source_target_pairs={{0,2},{2,0},{1,3},{3,1},{4,6},{6,4},{5,7},{7,5},{8,10},{10,8},{9,1... | collective-permute-start | bytes 294920 | tf_op jit(solution)/shard_map/ppermute | solution.py:550
  76.1 0.7 collective-permute-start.18
  76.7 2.3 %collective-permute-start.19 = (f32[3,16,512]{2,1,0:T(8,128)S(1)}, f32[3,16,512]{2,1,0:T(8,128)S(1)}, u32[]{:S(2)}, u32[]{:S(2)}) collective-permute-start(f32[3,16,512]{2,1,0:T(8,128)S(1)} %get-tuple-element.83), channel_id=1, source_target_pairs={{0,1},{1,0},{2,3},{3,2},{4,5},{5,4},{6,7},{7,6},{8,9},{9,8},{10,11... | collective-permute-start | bytes 294920 | tf_op jit(solution)/shard_map/ppermute | solution.py:543
  79.1 0.3 collective-permute-done.22.refs_11_
  79.3 0.7 collective-permute-start.23
  80.0 2.3 %shard_map.97.refs_5_.refs_2_ = f32[16,16,512]{2,1,0:T(8,128)S(1)} custom-call(s32[2]{0:T(128)S(1)} %pad_add_fusion.scal, s32[17]{0:T(128)S(1)} %copy-done, f32[16,16,512]{2,1,0:T(8,128)S(1)} %get-tuple-element.85.now, f32[16,16,512]{2,1,0:T(8,128)S(1)} %collective-permute-done.20.xr, f32[16,16,512]{2,1,0:T(8,128)S(1)} %collective-permute-done.21.cr, ...), custom_call_target="tpu_custom_call" | custom-call | tf_op jit(solution)/shard_map/pallas_call | solution.py:563
  82.4 2.5 %shard_map.98 = (f32[16,16,512]{2,1,0:T(8,128)S(1)}, f32[16,16,512]{2,1,0:T(8,128)S(1)}, f32[1,16,512]{2,1,0:T(8,128)S(1)}, f32[1,16,512]{2,1,0:T(8,128)S(1)}, f...) custom-call(s32[2]{0:T(128)S(1)} %pad_add_fusion.scal, f32[16,16,512]{2,1,0:T(8,128)S(1)} %get-tuple-element.80.refs_0_, ...), custom_call_target="tpu_custom_call" | custom-call | tf_op jit(solution)/shard_map/pallas_call | solution.py:563
  84.9 1.6 %collective-permute-start.27 = (f32[2,8,512]{2,1,0:T(8,128)S(1)}, f32[2,8,512]{2,1,0:T(8,128)S(1)}, u32[]{:S(2)}, u32[]{:S(2)}) collective-permute-start(f32[2,8,512]{2,1,0:T(8,128)S(1)} %get-tuple-element.92), channel_id=1, source_target_pairs={{0,2},{2,0},{1,3},{3,1},{4,6},{6,4},{5,7},{7,5},{8,10},{10,8},{9,1... | collective-permute-start | bytes 98312 | tf_op jit(solution)/shard_map/ppermute | solution.py:550
  86.5 0.7 collective-permute-start.25
  87.1 5.5 %collective-permute-start.26 = (f32[1,16,512]{2,1,0:T(8,128)S(1)}, f32[1,16,512]{2,1,0:T(8,128)S(1)}, u32[]{:S(2)}, u32[]{:S(2)}) collective-permute-start(f32[1,16,512]{2,1,0:T(8,128)S(1)} %get-tuple-element.91), channel_id=1, source_target_pairs={{0,1},{1,0},{2,3},{3,2},{4,5},{5,4},{6,7},{7,6},{8,9},{9,8},{10,11... | collective-permute-start | bytes 98312 | tf_op jit(solution)/shard_map/ppermute | solution.py:543
  92.6 0.1 collective-permute-start.29
  92.7 0.7 collective-permute-start.28
  93.3 3.0 %collective-permute-start.17 = (f32[16,16,256]{2,1,0:T(8,128)S(1)}, f32[16,16,256]{2,1,0:T(8,128)S(1)}, u32[]{:S(2)}, u32[]{:S(2)}) collective-permute-start(f32[16,16,256]{2,1,0:T(8,128)S(1)} %get-tuple-element.78), channel_id=1, source_target_pairs={{0,1},{1,0},{2,3},{3,2},{4,5},{5,4},{6,7},{7,6},{8,9},{9,8},{10,11... | collective-permute-start | bytes 786440 | tf_op jit(solution)/shard_map/ppermute | solution.py:543
  96.3 1.2 %shard_map.99 = (f32[16,16,256]{2,1,0:T(8,128)S(1)}, f32[16,16,256]{2,1,0:T(8,128)S(1)}) custom-call(s32[2]{0:T(128)S(1)} %pad_add_fusion.scal, f32[16,16,512]{2,1,0:T(8,128)S(1)} %get-tuple-element.88.refs_0_, f32[16,16,512]{2,1,0:T(8,128)S(1)} %get-tuple-element.89.refs_1_, f32[16,16,512]{2,1,0:T(8,128)S(1)} %shard_map.97.refs_5_.refs_2_, ...), custom_call_target="tpu_custom_call" | custom-call | tf_op jit(solution)/shard_map/pallas_call | solution.py:563
  97.6 2.8 %collective-permute-start.30 = (f32[16,16,256]{2,1,0:T(8,128)S(1)}, f32[16,16,256]{2,1,0:T(8,128)S(1)}, u32[]{:S(2)}, u32[]{:S(2)}) collective-permute-start(f32[16,16,256]{2,1,0:T(8,128)S(1)} %get-tuple-element.94), channel_id=1, source_target_pairs={{0,1},{1,0},{2,3},{3,2},{4,5},{5,4},{6,7},{7,6},{8,9},{9,8},{10,11... | collective-permute-start | bytes 786440 | tf_op jit(solution)/shard_map/ppermute | solution.py:543
  100.4 1.4 %shard_map.95 = f32[32,16,256]{2,1,0:T(8,128)} custom-call(s32[2]{0:T(128)S(1)} %pad_add_fusion.scal, f32[16,16,256]{2,1,0:T(8,128)S(1)} %get-tuple-element.77.near, f32[16,16,256]{2,1,0:T(8,128)S(1)} %collective-permute-done.17.far), custom_call_target="tpu_custom_call" | custom-call | tf_op jit(solution)/shard_map/pallas_call | solution.py:563
  101.8 1.3 %shard_map.100.refs_1_ = f32[32,16,256]{2,1,0:T(8,128)} custom-call(s32[2]{0:T(128)S(1)} %pad_add_fusion.scal, f32[16,16,256]{2,1,0:T(8,128)S(1)} %get-tuple-element.95.refs_0_), custom_call_target="tpu_custom_call" | custom-call | tf_op jit(solution)/shard_map/pallas_call | solution.py:563
  103.0 1.3 %shard_map.101 = f32[32,16,256]{2,1,0:T(8,128)} custom-call(s32[2]{0:T(128)S(1)} %pad_add_fusion.scal, f32[16,16,256]{2,1,0:T(8,128)S(1)} %collective-permute-done.30.refs_0_, f32[32,16,256]{2,1,0:T(8,128)} %shard_map.100.refs_1_), custom_call_target="tpu_custom_call", output_to_operand_aliasing={{}: (2, {})} | custom-call | tf_op jit(solution)/shard_map/pallas_call | solution.py:563
  (33 shorter events, 0.2 us)
Async XLA Ops:
  2.9 38.7 %collective-permute-start.8 = (f32[17,16,16,256]{3,2,1,0:T(8,128)S(1)}, f32[17,16,16,256]{3,2,1,0:T(8,128)S(1)}, u32[]{:S(2)}, u32[]{:S(2)}) collective-permute-start(f32[17,16,16,256]{3,2,1,0:T(8,128)S(1)} %shard_map.92), channel_id=1, source_target_pairs={{0,1},{1,0},{2,3},{3,2},{4,5},{5,4},{6,7},{7,6},{8,9},{9,8},{10,11... | collective-permute-start | bytes 13369352 | tf_op jit(solution)/shard_map/ppermute | solution.py:543
  5.3 7.2 %collective-permute-start = (f32[5,16,16,256]{3,2,1,0:T(8,128)S(1)}, f32[5,16,16,256]{3,2,1,0:T(8,128)S(1)}, u32[]{:S(2)}, u32[]{:S(2)}) collective-permute-start(f32[5,16,16,256]{3,2,1,0:T(8,128)S(1)} %shard_map.87), channel_id=1, source_target_pairs={{0,1},{1,0},{2,3},{3,2},{4,5},{5,4},{6,7},{7,6},{8,9},{9,8},{10,11... | collective-permute-start | bytes 3932168 | tf_op jit(solution)/shard_map/ppermute | solution.py:543
  13.4 8.1 %collective-permute-start.3 = (f32[12,8,512]{2,1,0:T(8,128)S(1)}, f32[12,8,512]{2,1,0:T(8,128)S(1)}, u32[]{:S(2)}, u32[]{:S(2)}) collective-permute-start(f32[12,8,512]{2,1,0:T(8,128)S(1)} %get-tuple-element.53), channel_id=1, source_target_pairs={{0,2},{2,0},{1,3},{3,1},{4,6},{6,4},{5,7},{7,5},{8,10},{10,8},{9,1... | collective-permute-start | bytes 589832 | tf_op jit(solution)/shard_map/ppermute | solution.py:550
  16.3 7.4 %collective-permute-start.1 = (f32[6,16,512]{2,1,0:T(8,128)S(1)}, f32[6,16,512]{2,1,0:T(8,128)S(1)}, u32[]{:S(2)}, u32[]{:S(2)}) collective-permute-start(f32[6,16,512]{2,1,0:T(8,128)S(1)} %get-tuple-element.51), channel_id=1, source_target_pairs={{1,4},{4,1},{5,8},{8,5},{9,12},{12,9},{3,6},{6,3},{7,10},{10,7},{1... | collective-permute-start | bytes 589832 | tf_op jit(solution)/shard_map/ppermute | solution.py:546
  17.0 6.8 %collective-permute-start.2 = (f32[6,16,512]{2,1,0:T(8,128)S(1)}, f32[6,16,512]{2,1,0:T(8,128)S(1)}, u32[]{:S(2)}, u32[]{:S(2)}) collective-permute-start(f32[6,16,512]{2,1,0:T(8,128)S(1)} %get-tuple-element.52), channel_id=1, source_target_pairs={{0,1},{1,0},{2,3},{3,2},{4,5},{5,4},{6,7},{7,6},{8,9},{9,8},{10,11... | collective-permute-start | bytes 589832 | tf_op jit(solution)/shard_map/ppermute | solution.py:543
  21.5 2.3 %collective-permute-start.5 = (f32[12,8,512]{2,1,0:T(8,128)S(1)}, f32[12,8,512]{2,1,0:T(8,128)S(1)}, u32[]{:S(2)}, u32[]{:S(2)}) collective-permute-start(f32[12,8,512]{2,1,0:T(8,128)S(1)} %collective-permute-done.3.refs_4_), channel_id=1, source_target_pairs={{0,1},{1,0},{2,3},{3,2},{4,5},{5,4},{6,7},{7,6},{8,9},{9,8},{10,11... | collective-permute-start | bytes 589832 | tf_op jit(solution)/shard_map/ppermute | solution.py:543
  21.5 2.2 %collective-permute-start.4 = (f32[2,8,512]{2,1,0:T(8,128)S(1)}, f32[2,8,512]{2,1,0:T(8,128)S(1)}, u32[]{:S(2)}, u32[]{:S(2)}) collective-permute-start(f32[2,8,512]{2,1,0:T(8,128)S(1)} %get-tuple-element.54), channel_id=1, source_target_pairs={{1,6},{3,4},{4,3},{6,1},{5,10},{7,8},{8,7},{10,5},{9,14},{11,12},{... | collective-permute-start | bytes 98312 | tf_op jit(solution)/shard_map/ppermute | solution.py:548
  26.6 15.1 %collective-permute-start.6 = (f32[16,16,512]{2,1,0:T(8,128)S(1)}, f32[16,16,512]{2,1,0:T(8,128)S(1)}, u32[]{:S(2)}, u32[]{:S(2)}) collective-permute-start(f32[16,16,512]{2,1,0:T(8,128)S(1)} %get-tuple-element.63.refs_0_), channel_id=1, source_target_pairs={{1,4},{4,1},{5,8},{8,5},{9,12},{12,9},{3,6},{6,3},{7,10},{10,7},{1... | collective-permute-start | bytes 1572872 | tf_op jit(solution)/shard_map/ppermute | solution.py:546
  27.3 14.4 %collective-permute-start.7 = (f32[16,16,512]{2,1,0:T(8,128)S(1)}, f32[16,16,512]{2,1,0:T(8,128)S(1)}, u32[]{:S(2)}, u32[]{:S(2)}) collective-permute-start(f32[16,16,512]{2,1,0:T(8,128)S(1)} %get-tuple-element.63.refs_0_), channel_id=1, source_target_pairs={{0,1},{1,0},{2,3},{3,2},{4,5},{5,4},{6,7},{7,6},{8,9},{9,8},{10,11... | collective-permute-start | bytes 1572872 | tf_op jit(solution)/shard_map/ppermute | solution.py:543
  34.4 4.3 %collective-permute-start.9 = (f32[4,8,512]{2,1,0:T(8,128)S(1)}, f32[4,8,512]{2,1,0:T(8,128)S(1)}, u32[]{:S(2)}, u32[]{:S(2)}) collective-permute-start(f32[4,8,512]{2,1,0:T(8,128)S(1)} %get-tuple-element.70), channel_id=1, source_target_pairs={{0,2},{2,0},{1,3},{3,1},{4,6},{6,4},{5,7},{7,5},{8,10},{10,8},{9,1... | collective-permute-start | bytes 196616 | tf_op jit(solution)/shard_map/ppermute | solution.py:550
  38.6 3.0 %collective-permute-start.11 = (f32[4,8,512]{2,1,0:T(8,128)S(1)}, f32[4,8,512]{2,1,0:T(8,128)S(1)}, u32[]{:S(2)}, u32[]{:S(2)}) collective-permute-start(f32[4,8,512]{2,1,0:T(8,128)S(1)} %collective-permute-done.9.refs_12_), channel_id=1, source_target_pairs={{0,1},{1,0},{2,3},{3,2},{4,5},{5,4},{6,7},{7,6},{8,9},{9,8},{10,11... | collective-permute-start | bytes 196616 | tf_op jit(solution)/shard_map/ppermute | solution.py:543
  38.6 3.0 %copy-start = (s32[17]{0:T(128)S(1)}, s32[17]{0:T(128)}, u32[]{:S(2)}) copy-start(s32[17]{0:T(128)} %offsets.5) | copy-start | bytes 208
  38.6 3.0 %collective-permute-start.10 = (f32[2,8,512]{2,1,0:T(8,128)S(1)}, f32[2,8,512]{2,1,0:T(8,128)S(1)}, u32[]{:S(2)}, u32[]{:S(2)}) collective-permute-start(f32[2,8,512]{2,1,0:T(8,128)S(1)} %get-tuple-element.71), channel_id=1, source_target_pairs={{1,6},{3,4},{4,3},{6,1},{5,10},{7,8},{8,7},{10,5},{9,14},{11,12},{... | collective-permute-start | bytes 98312 | tf_op jit(solution)/shard_map/ppermute | solution.py:548
  45.8 13.8 %collective-permute-start.12 = (f32[18,16,512]{2,1,0:T(8,128)S(1)}, f32[18,16,512]{2,1,0:T(8,128)S(1)}, u32[]{:S(2)}, u32[]{:S(2)}) collective-permute-start(f32[18,16,512]{2,1,0:T(8,128)S(1)} %get-tuple-element.72.refs_0_), channel_id=1, source_target_pairs={{1,4},{4,1},{5,8},{8,5},{9,12},{12,9},{3,6},{6,3},{7,10},{10,7},{1... | collective-permute-start | bytes 1769480 | tf_op jit(solution)/shard_map/ppermute | solution.py:546
  46.5 13.0 %collective-permute-start.13 = (f32[18,16,512]{2,1,0:T(8,128)S(1)}, f32[18,16,512]{2,1,0:T(8,128)S(1)}, u32[]{:S(2)}, u32[]{:S(2)}) collective-permute-start(f32[18,16,512]{2,1,0:T(8,128)S(1)} %get-tuple-element.74), channel_id=1, source_target_pairs={{0,1},{1,0},{2,3},{3,2},{4,5},{5,4},{6,7},{7,6},{8,9},{9,8},{10,11... | collective-permute-start | bytes 1769480 | tf_op jit(solution)/shard_map/ppermute | solution.py:543
  52.7 5.5 %collective-permute-start.14 = (f32[8,8,512]{2,1,0:T(8,128)S(1)}, f32[8,8,512]{2,1,0:T(8,128)S(1)}, u32[]{:S(2)}, u32[]{:S(2)}) collective-permute-start(f32[8,8,512]{2,1,0:T(8,128)S(1)} %get-tuple-element.75), channel_id=1, source_target_pairs={{0,2},{2,0},{1,3},{3,1},{4,6},{6,4},{5,7},{7,5},{8,10},{10,8},{9,1... | collective-permute-start | bytes 393224 | tf_op jit(solution)/shard_map/ppermute | solution.py:550
  58.2 1.3 %collective-permute-start.16 = (f32[8,8,512]{2,1,0:T(8,128)S(1)}, f32[8,8,512]{2,1,0:T(8,128)S(1)}, u32[]{:S(2)}, u32[]{:S(2)}) collective-permute-start(f32[8,8,512]{2,1,0:T(8,128)S(1)} %collective-permute-done.14.refs_9_.refs_12_), channel_id=1, source_target_pairs={{0,1},{1,0},{2,3},{3,2},{4,5},{5,4},{6,7},{7,6},{8,9},{9,8},{10,11... | collective-permute-start | bytes 393224 | tf_op jit(solution)/shard_map/ppermute | solution.py:543
  58.2 0.7 collective-permute-start.15
  61.9 17.4 %collective-permute-start.20 = (f32[16,16,512]{2,1,0:T(8,128)S(1)}, f32[16,16,512]{2,1,0:T(8,128)S(1)}, u32[]{:S(2)}, u32[]{:S(2)}) collective-permute-start(f32[16,16,512]{2,1,0:T(8,128)S(1)} %get-tuple-element.85.now), channel_id=1, source_target_pairs={{1,4},{4,1},{5,8},{8,5},{9,12},{12,9},{3,6},{6,3},{7,10},{10,7},{1... | collective-permute-start | bytes 1572872 | tf_op jit(solution)/shard_map/ppermute | solution.py:655
  62.6 17.4 %collective-permute-start.21 = (f32[16,16,512]{2,1,0:T(8,128)S(1)}, f32[16,16,512]{2,1,0:T(8,128)S(1)}, u32[]{:S(2)}, u32[]{:S(2)}) collective-permute-start(f32[16,16,512]{2,1,0:T(8,128)S(1)} %get-tuple-element.85.now), channel_id=1, source_target_pairs={{0,1},{1,0},{2,3},{3,2},{4,5},{5,4},{6,7},{7,6},{8,9},{9,8},{10,11... | collective-permute-start | bytes 1572872 | tf_op jit(solution)/shard_map/ppermute | solution.py:543
  74.5 4.8 %collective-permute-start.22 = (f32[6,8,512]{2,1,0:T(8,128)S(1)}, f32[6,8,512]{2,1,0:T(8,128)S(1)}, u32[]{:S(2)}, u32[]{:S(2)}) collective-permute-start(f32[6,8,512]{2,1,0:T(8,128)S(1)} %get-tuple-element.86), channel_id=1, source_target_pairs={{0,2},{2,0},{1,3},{3,1},{4,6},{6,4},{5,7},{7,5},{8,10},{10,8},{9,1... | collective-permute-start | bytes 294920 | tf_op jit(solution)/shard_map/ppermute | solution.py:550
  76.1 6.3 %collective-permute-start.18 = (f32[3,16,512]{2,1,0:T(8,128)S(1)}, f32[3,16,512]{2,1,0:T(8,128)S(1)}, u32[]{:S(2)}, u32[]{:S(2)}) collective-permute-start(f32[3,16,512]{2,1,0:T(8,128)S(1)} %get-tuple-element.82), channel_id=1, source_target_pairs={{1,4},{4,1},{5,8},{8,5},{9,12},{12,9},{3,6},{6,3},{7,10},{10,7},{1... | collective-permute-start | bytes 294920 | tf_op jit(solution)/shard_map/ppermute | solution.py:546
  76.7 5.6 %collective-permute-start.19 = (f32[3,16,512]{2,1,0:T(8,128)S(1)}, f32[3,16,512]{2,1,0:T(8,128)S(1)}, u32[]{:S(2)}, u32[]{:S(2)}) collective-permute-start(f32[3,16,512]{2,1,0:T(8,128)S(1)} %get-tuple-element.83), channel_id=1, source_target_pairs={{0,1},{1,0},{2,3},{3,2},{4,5},{5,4},{6,7},{7,6},{8,9},{9,8},{10,11... | collective-permute-start | bytes 294920 | tf_op jit(solution)/shard_map/ppermute | solution.py:543
  79.3 3.0 %collective-permute-start.24 = (f32[6,8,512]{2,1,0:T(8,128)S(1)}, f32[6,8,512]{2,1,0:T(8,128)S(1)}, u32[]{:S(2)}, u32[]{:S(2)}) collective-permute-start(f32[6,8,512]{2,1,0:T(8,128)S(1)} %collective-permute-done.22.refs_11_), channel_id=1, source_target_pairs={{0,1},{1,0},{2,3},{3,2},{4,5},{5,4},{6,7},{7,6},{8,9},{9,8},{10,11... | collective-permute-start | bytes 294920 | tf_op jit(solution)/shard_map/ppermute | solution.py:543
  79.3 3.0 %collective-permute-start.23 = (f32[2,8,512]{2,1,0:T(8,128)S(1)}, f32[2,8,512]{2,1,0:T(8,128)S(1)}, u32[]{:S(2)}, u32[]{:S(2)}) collective-permute-start(f32[2,8,512]{2,1,0:T(8,128)S(1)} %get-tuple-element.87), channel_id=1, source_target_pairs={{1,6},{3,4},{4,3},{6,1},{5,10},{7,8},{8,7},{10,5},{9,14},{11,12},{... | collective-permute-start | bytes 98312 | tf_op jit(solution)/shard_map/ppermute | solution.py:548
  84.9 7.7 %collective-permute-start.27 = (f32[2,8,512]{2,1,0:T(8,128)S(1)}, f32[2,8,512]{2,1,0:T(8,128)S(1)}, u32[]{:S(2)}, u32[]{:S(2)}) collective-permute-start(f32[2,8,512]{2,1,0:T(8,128)S(1)} %get-tuple-element.92), channel_id=1, source_target_pairs={{0,2},{2,0},{1,3},{3,1},{4,6},{6,4},{5,7},{7,5},{8,10},{10,8},{9,1... | collective-permute-start | bytes 98312 | tf_op jit(solution)/shard_map/ppermute | solution.py:550
  86.5 9.8 %collective-permute-start.25 = (f32[1,16,512]{2,1,0:T(8,128)S(1)}, f32[1,16,512]{2,1,0:T(8,128)S(1)}, u32[]{:S(2)}, u32[]{:S(2)}) collective-permute-start(f32[1,16,512]{2,1,0:T(8,128)S(1)} %get-tuple-element.90), channel_id=1, source_target_pairs={{1,4},{4,1},{5,8},{8,5},{9,12},{12,9},{3,6},{6,3},{7,10},{10,7},{1... | collective-permute-start | bytes 98312 | tf_op jit(solution)/shard_map/ppermute | solution.py:546
  87.1 9.2 %collective-permute-start.26 = (f32[1,16,512]{2,1,0:T(8,128)S(1)}, f32[1,16,512]{2,1,0:T(8,128)S(1)}, u32[]{:S(2)}, u32[]{:S(2)}) collective-permute-start(f32[1,16,512]{2,1,0:T(8,128)S(1)} %get-tuple-element.91), channel_id=1, source_target_pairs={{0,1},{1,0},{2,3},{3,2},{4,5},{5,4},{6,7},{7,6},{8,9},{9,8},{10,11... | collective-permute-start | bytes 98312 | tf_op jit(solution)/shard_map/ppermute | solution.py:543
  92.6 3.7 %collective-permute-start.29 = (f32[2,8,512]{2,1,0:T(8,128)S(1)}, f32[2,8,512]{2,1,0:T(8,128)S(1)}, u32[]{:S(2)}, u32[]{:S(2)}) collective-permute-start(f32[2,8,512]{2,1,0:T(8,128)S(1)} %collective-permute-done.27.refs_10_), channel_id=1, source_target_pairs={{0,1},{1,0},{2,3},{3,2},{4,5},{5,4},{6,7},{7,6},{8,9},{9,8},{10,11... | collective-permute-start | bytes 98312 | tf_op jit(solution)/shard_map/ppermute | solution.py:543
  92.7 3.6 %collective-permute-start.28 = (f32[1,8,512]{2,1,0:T(8,128)S(1)}, f32[1,8,512]{2,1,0:T(8,128)S(1)}, u32[]{:S(2)}, u32[]{:S(2)}) collective-permute-start(f32[1,8,512]{2,1,0:T(8,128)S(1)} %get-tuple-element.93), channel_id=1, source_target_pairs={{1,6},{3,4},{4,3},{6,1},{5,10},{7,8},{8,7},{10,5},{9,14},{11,12},{... | collective-permute-start | bytes 49160 | tf_op jit(solution)/shard_map/ppermute | solution.py:548
  93.3 7.0 %collective-permute-start.17 = (f32[16,16,256]{2,1,0:T(8,128)S(1)}, f32[16,16,256]{2,1,0:T(8,128)S(1)}, u32[]{:S(2)}, u32[]{:S(2)}) collective-permute-start(f32[16,16,256]{2,1,0:T(8,128)S(1)} %get-tuple-element.78), channel_id=1, source_target_pairs={{0,1},{1,0},{2,3},{3,2},{4,5},{5,4},{6,7},{7,6},{8,9},{9,8},{10,11... | collective-permute-start | bytes 786440 | tf_op jit(solution)/shard_map/ppermute | solution.py:543
  97.6 5.4 %collective-permute-start.30 = (f32[16,16,256]{2,1,0:T(8,128)S(1)}, f32[16,16,256]{2,1,0:T(8,128)S(1)}, u32[]{:S(2)}, u32[]{:S(2)}) collective-permute-start(f32[16,16,256]{2,1,0:T(8,128)S(1)} %get-tuple-element.94), channel_id=1, source_target_pairs={{0,1},{1,0},{2,3},{3,2},{4,5},{5,4},{6,7},{7,6},{8,9},{9,8},{10,11... | collective-permute-start | bytes 786440 | tf_op jit(solution)/shard_map/ppermute | solution.py:543

commit v5 on v4

v5 whole, which is shorter than its diff:
```python
import functools

import jax
import jax.numpy as jnp
from jax import lax
from jax.experimental import pallas as pl
from jax.experimental.pallas import tpu as pltpu
from jax.sharding import PartitionSpec as P


NOFF = 17
MARGIN = 16
TILE = 8
F32 = jnp.float32
UNROLL = 8
FIRST, SECOND, THIRD, LAST = (2, 1, 2, 2, 2), (2,), (2, 3), (3, 2, 1)
SLACK = 8 << 20


class Geometry:
    def __init__(self, rows, depth, half, sections):
        self.B, self.Z, self.H, self.Y = rows // 2, depth, half, 2 * half
        self.two = sections == 2
        self.sides = 1 if self.two else 2
        self.ZE = depth + TILE * self.sides
        assert self.B >= MARGIN and depth % TILE == 0 and half % 128 == 0


def halo_place(side, depth, k, geo):
    return (1 - side) * (geo.B - depth) + side * 2 * geo.B + k


def slot_of(depth):
    return 4 if depth > 2 else depth


def tile_mask(sender, depth, turn, width):
    place = lax.broadcasted_iota(jnp.int32, (TILE, width), 0)
    place = lax.rem(place + (TILE - turn), TILE)
    start = (1 - sender) * (TILE - depth)
    return (place >= start) & (place < start + depth)


def turned(value, turn):
    turn = turn % TILE
    return value if turn == 0 else pltpu.roll(value, turn, 0)


def senders(s, geo):
    return [s] if geo.two else [0, 1]


def receivers(s, geo):
    return [(geo.Z, 1 - s)] if geo.two else [(geo.ZE - TILE, 0), (geo.Z, 1)]


def edge_tile(ref, row, sender, geo):
    start = pl.multiple_of((1 - sender) * (geo.Z - TILE), TILE)
    return ref[row, pl.ds(start, TILE), :]


def tiles_of(depths, geo):
    starts, total = [], 0
    for depth in depths:
        starts.append(total)
        total += geo.B * slot_of(depth) // TILE
    return starts, total


def corner_slot(depths):
    return 4 if max(depths) > 2 else 2


def corner_tiles(depths):
    return -(-sum(depths) * corner_slot(depths) // TILE)


def pack_tiles(items, g, s, tiles, corners, geo):
    depths = [depth for _, depth in items]
    starts, _ = tiles_of(depths, geo)
    for sender, tile_ref, corner_ref in zip(senders(s, geo), tiles, corners):
        for (ref, depth), start in zip(items, starts):
            slot = slot_of(depth)
            per = TILE // slot
            masks = [tile_mask(sender, depth, k * slot, geo.Y) for k in range(1, per)]
            for q in range(geo.B // per):
                out = edge_tile(ref, q * per, sender, geo)
                for k in range(1, per):
                    value = turned(edge_tile(ref, q * per + k, sender, geo), k * slot)
                    out = jnp.where(masks[k - 1], value, out)
                tile_ref[start + q] = out
        slot, place = corner_slot(depths), 0
        for ref, depth in items:
            for k in range(depth):
                at, turn = divmod(place * slot, TILE)
                value = turned(edge_tile(ref, g * (geo.B - depth) + k, sender, geo), turn)
                if turn:
                    value = jnp.where(tile_mask(sender, depth, turn, geo.Y), value, corner_ref[at])
                corner_ref[at] = value
                place += 1


def unpack_row(ref, depths, index, x, geo):
    depth = depths[index]
    per = TILE // slot_of(depth)
    return turned(ref[tiles_of(depths, geo)[0][index] + x // per], TILE - (x % per) * slot_of(depth))


def unpack_corner(ref, depths, index, k):
    at, turn = divmod((sum(depths[:index]) + k) * corner_slot(depths), TILE)
    return turned(ref[at], TILE - turn)


def unpack_c(ref, depths, index, side, k, geo):
    low = unpack_row(ref, depths, index, k, geo)
    high = unpack_row(ref, depths, index, geo.B - depths[index] + k, geo)
    return jnp.where(side == 1, low, high)


def fill(dst, own, xrow, crow, halo, depths, index, g, s, geo):
    n = geo.sides
    depth = depths[index]
    ends = list(zip(receivers(s, geo), halo[:n], halo[n : 2 * n], halo[2 * n :]))

    def one(row, carry):
        dst[geo.B + row, 0 : geo.Z, :] = own[row]
        return carry

    lax.fori_loop(0, geo.B, one, 0, unroll=4)
    for (offset, sender), tile, xtile, ctile in ends:
        keep = tile_mask(sender, depth, 0, geo.Y)
        span = slice(offset, offset + TILE)
        for row in range(geo.B):
            dst[geo.B + row, span, :] = jnp.where(keep, unpack_row(tile, depths, index, row, geo), 0.0)
        for k in range(depth):
            dst[halo_place(g, depth, k, geo), span, :] = jnp.where(keep, unpack_corner(xtile, depths, index, k), 0.0)
            value = unpack_c(ctile, depths, index, 1 - g, k, geo)
            dst[halo_place(1 - g, depth, k, geo), span, :] = jnp.where(keep, value, 0.0)
    for side, get in ((g, xrow), (1 - g, crow)):
        for k in range(depth if get is not None else 0):
            dst[halo_place(side, depth, k, geo), 0 : geo.Z, :] = get(k)


def fill_blocks(dst, xblock, cblock, g, geo, own=None):
    def one(row, carry):
        dst[g * 2 * geo.B + row, 0 : geo.Z, :] = xblock[row]
        dst[(1 - g) * 2 * geo.B + row, 0 : geo.Z, :] = cblock[row]
        if own is not None:
            dst[geo.B + row, 0 : geo.Z, :] = own[row]
        return carry

    lax.fori_loop(0, geo.B, one, 0, unroll=2)


def each(first, count, body, group):
    group = max(k for k in range(1, group + 1) if count % k == 0)

    def trip(index, carry):
        for k in range(group):
            body(first + index * group + k)
        return carry

    lax.fori_loop(0, count // group, trip, 0)


def advance(src, off, first, count, top, prior, extra, store, coefs, dif, tot, geo, group=None):
    xx, zz, yy, xz, mid = coefs
    lane = lax.broadcasted_iota(jnp.int32, (top, 128), 1)
    low_edge, high_edge = lane == 0, lane == 127
    spans = [slice(k, k + 128) for k in range(0, geo.Y, 128)]

    def slopes(row):
        value = src[row - off]
        above = pltpu.roll(value, geo.ZE - 1, 0)[0:top]
        below = pltpu.roll(value, 1, 0)[0:top]
        dif[row, 0:top] = above - below
        return value[0:top], above + below

    def local(row):
        at = jnp.minimum(row - (geo.B - 2), geo.B + 3)
        whole, total = slopes(row)
        value = [whole[:, span] for span in spans]
        zero = jnp.zeros_like(value[0])
        right = [pltpu.roll(v, 127, 1) for v in value] + [zero]
        left = [zero] + [pltpu.roll(v, 1, 1) for v in value]
        for k, span in enumerate(spans):
            side = jnp.where(high_edge, right[k + 1], right[k]) + jnp.where(low_edge, left[k], left[k + 1])
            new = mid[at, 0:top, span] * value[k] + zz[at, 0:top, span] * total[:, span]
            tot[row, 0:top, span] = new + yy[at, 0:top, span] * side

    slopes(first - 1)
    local(first)

    def one(row):
        local(row + 1)
        at = row - (geo.B - 2)
        new = tot[row, 0:top] + xx[at, 0:top] * (src[row + 1 - off, 0:top] + src[row - 1 - off, 0:top])
        new = new + xz[at, 0:top] * (dif[row + 1, 0:top] - dif[row - 1, 0:top])
        last = prior(row)
        if last is not None:
            new = new - last[0:top]
        if extra is not None:
            new = new + extra(row)[0:top]
        store(row, new)

    each(first, count, one, group or UNROLL)


def make_source(ext, refl, refl_far, offsets, courant, out, g, geo):
    near = pl.multiple_of(g * geo.H, 128)
    far = pl.multiple_of((1 - g) * geo.H, 128)

    def one(row):
        acc = jnp.zeros((geo.Z, geo.H), F32)
        acc_far = jnp.zeros((geo.Z, geo.H), F32)
        for h in range(NOFF):
            place = geo.B + row + offsets[h]
            acc = acc + refl[h, row].astype(F32) * ext[place, 0 : geo.Z, pl.ds(near, geo.H)]
            acc_far = acc_far + refl_far[h, row] * ext[place, 0 : geo.Z, pl.ds(far, geo.H)]
        out[row, :, pl.ds(near, geo.H)] = courant[row, :, pl.ds(near, geo.H)] * acc
        out[row, :, pl.ds(far, geo.H)] = courant[row, :, pl.ds(far, geo.H)] * acc_far

    each(0, geo.B, one, 2)


def edge_rows(depth, side, geo):
    return side * (geo.B - depth)


def trig_products(angle):
    turns = jnp.floor(angle * 0.6366197723675814 + 0.5)
    rest = angle - turns * 1.5703125
    rest = rest - turns * 4.837512969970703125e-4
    rest = rest - turns * 7.549789954891882e-8
    odd = (turns - 2.0 * jnp.floor(turns * 0.5)) > 0.5
    square = rest * rest
    sine = rest + rest * square * (
        -1.6666654611e-1 + square * (8.3321608736e-3 + square * -1.9515295891e-4)
    )
    cosine = 1.0 - 0.5 * square + square * square * (
        4.166664568298827e-2 + square * (-1.388731625493765e-3 + square * 2.443315711809948e-5)
    )
    sine_square = jnp.where(odd, cosine * cosine, sine * sine)
    cosine_square = jnp.where(odd, sine * sine, cosine * cosine)
    product = sine * cosine
    return sine_square, cosine_square, jnp.where(odd, -product, product)


def half_kernel(geo, scal, *refs, other):
    *fields, out, sems = refs
    half = 1 - scal[0] if other else scal[0]
    start = pl.multiple_of(half * geo.B, TILE)
    copies = [
        pltpu.make_async_copy(field.at[pl.ds(start, geo.B)], out.at[k], sems.at[k]) for k, field in enumerate(fields)
    ]
    for copy in copies:
        copy.start()
    for copy in copies:
        copy.wait()


def widen_kernel(geo, scal, refl, out, held, sems):
    other = pl.multiple_of((1 - scal[0]) * geo.B, TILE)
    cuts = [0, 5, 9, 13, NOFF]
    copies = [
        pltpu.make_async_copy(refl.at[pl.ds(a, b - a), pl.ds(other, geo.B)], held.at[pl.ds(a, b - a)], sems.at[k])
        for k, (a, b) in enumerate(zip(cuts, cuts[1:]))
    ]
    for copy in copies:
        copy.start()
    for copy, a, b in zip(copies, cuts, cuts[1:]):
        copy.wait()

        def one(h, carry):
            for row in range(geo.B):
                out[h, row] = held[h, row].astype(F32)
            return carry

        lax.fori_loop(a, b, one, 0)


def own_refl_kernel(geo, scal, refl, out, sem):
    start = pl.multiple_of(scal[0] * geo.B, TILE)
    copy = pltpu.make_async_copy(refl.at[:, pl.ds(start, geo.B)], out, sem)
    copy.start()
    copy.wait()


def join_kernel(geo, scal, *refs):
    near, far = refs[:2]
    own = refs[2:7]
    px, pc = refs[7:9]
    tiles, corners = refs[9 : 9 + geo.sides], refs[9 + geo.sides :]
    g, s = scal[0], scal[1]
    near_y = pl.multiple_of(g * geo.H, 128)
    far_y = pl.multiple_of((1 - g) * geo.H, 128)

    def one(row, carry):
        for k in range(5):
            own[k][row, :, pl.ds(near_y, geo.H)] = near[k, row]
            own[k][row, :, pl.ds(far_y, geo.H)] = far[k, row]
        return carry

    lax.fori_loop(0, geo.B, one, 0, unroll=2)
    put_rows(list(zip(own, FIRST)), px, pc, 0, g, geo)
    pack_tiles(list(zip(own, FIRST)), g, s, tiles, corners, geo)


def put_rows(items, px, pc, start, g, geo):
    for side, out in ((g, px), (1 - g, pc)):
        at = start
        for ref, depth in items:
            for k in range(depth):
                out[at] = ref[edge_rows(depth, side, geo) + k]
                at += 1


def coefficients(speed, aniso, angle):
    stretch = 2.0 * aniso
    sine_square, cosine_square, product = trig_products(angle)
    cx = speed * (1.0 + stretch * cosine_square)
    cz = speed * (1.0 + stretch * sine_square)
    cy = speed * (1.0 + stretch)
    return cx, cz, cy, (0.5 * speed) * (stretch * product), 2.0 - 2.0 * (cx + cz + cy)


def coef_kernel(geo, scal, courant, aniso, tilt, *coefs):
    def one(row):
        for ref, value in zip(coefs, coefficients(courant[row], aniso[row], tilt[row])):
            ref[row + 2, 0 : geo.Z, :] = value

    each(0, geo.B, one, 2)


def coef_halo(coefs, xr, cr, halo, g, s, geo):
    n, depth, depths = geo.sides, FIRST[2], FIRST
    starts, _ = tiles_of(depths, geo)
    slot = slot_of(depth)
    per = TILE // slot
    for (offset, sender), tile, xtile, ctile in zip(receivers(s, geo), halo[:n], halo[n : 2 * n], halo[2 * n :]):
        keep = tile_mask(sender, depth, 0, geo.Y)
        span = slice(offset, offset + TILE)
        for q in range(geo.B // per):
            values = coefficients(*(tile[start + q] for start in starts[2:]))
            for k in range(per):
                for ref, value in zip(coefs, values):
                    ref[q * per + k + 2, span, :] = jnp.where(keep, turned(value, TILE - k * slot), 0.0)
        for k in range(depth):
            corner = [unpack_corner(xtile, depths, i, k) for i in (2, 3, 4)]
            for ref, value in zip(coefs, coefficients(*corner)):
                ref[halo_place(g, depth, k, geo) - (geo.B - 2), span, :] = jnp.where(keep, value, 0.0)
            other = [unpack_c(ctile, depths, i, 1 - g, k, geo) for i in (2, 3, 4)]
            for ref, value in zip(coefs, coefficients(*other)):
                ref[halo_place(1 - g, depth, k, geo) - (geo.B - 2), span, :] = jnp.where(keep, value, 0.0)
    for side, line in ((g, xr), (1 - g, cr)):
        for k in range(depth):
            for ref, value in zip(coefs, coefficients(line[3 + k], line[5 + k], line[7 + k])):
                ref[halo_place(side, depth, k, geo) - (geo.B - 2), 0 : geo.Z, :] = value


def first_kernel(geo, scal, *refs):
    n = geo.sides
    now, before, xr, cr = refs[:4]
    halo = refs[4 : 4 + 3 * n]
    out_block, prior_ext, *coefs = refs[9 + 3 * n : 16 + 3 * n]
    out_tiles, out_corners = refs[16 + 3 * n : 16 + 4 * n], refs[16 + 4 * n : 16 + 5 * n]
    ext, old, dif, tot = refs[16 + 5 * n :]
    g, s = scal[0], scal[1]
    coef_halo(coefs, xr, cr, halo, g, s, geo)
    fill(old, before, lambda k: xr[2 + k], lambda k: cr[2 + k], halo, FIRST, 1, g, s, geo)
    fill(ext, now, lambda k: xr[k], lambda k: cr[k], halo, FIRST, 0, g, s, geo)

    def keep_block(row, value):
        out_block[row - geo.B] = value

    two_steps(ext, 1, lambda row: old[row], prior_ext, keep_block, coefs, dif, tot, geo)
    pack_tiles([(out_block, 2)], g, s, out_tiles, out_corners, geo)


def two_steps(ext, beyond, prior, mid, store, coefs, dif, tot, geo):
    off = geo.B - beyond

    def keep(row, value):
        mid[row - off] = value

    advance(ext, 0, off, geo.B + 2 * beyond, geo.ZE, prior, None, keep, coefs, dif, tot, geo)
    advance(mid, off, geo.B, geo.B, geo.Z, lambda row: ext[row], None, store, coefs, dif, tot, geo)


def second_kernel(geo, scal, offsets, *refs):
    n = geo.sides
    now, before, xr, cr, courant, refl, refl_far, *coefs = refs[:12]
    halo = refs[12 : 12 + 3 * n]
    px, pc, prior_ext, force = refs[12 + 3 * n : 16 + 3 * n]
    out_tiles, out_corners = refs[16 + 3 * n : 16 + 4 * n], refs[16 + 4 * n : 16 + 5 * n]
    ext, dif, tot = refs[16 + 5 * n :]
    g, s = scal[0], scal[1]
    B = geo.B
    fill_blocks(ext, xr, cr, g, geo)
    fill(ext, now, None, None, halo, SECOND, 0, g, s, geo)

    def keep_block(row, value):
        px[row - B] = value
        pc[row - B] = value

    two_steps(ext, 1, lambda row: before[row - (B - 1)], prior_ext, keep_block, coefs, dif, tot, geo)
    make_source(ext, refl, refl_far, offsets, courant, force, g, geo)
    put_rows([(force, THIRD[1])], px, pc, B, g, geo)
    pack_tiles([(px, THIRD[0]), (force, THIRD[1])], g, s, out_tiles, out_corners, geo)


def third_kernel(geo, scal, *refs):
    n = geo.sides
    now, before, xr, cr, *coefs = refs[:9]
    halo = refs[9 : 9 + 3 * n]
    block, near, back = refs[9 + 3 * n : 12 + 3 * n]
    ext, dif, tot, mid = refs[12 + 3 * n :]
    g, s = scal[0], scal[1]
    B = geo.B

    def row_of(side, k):
        return (1 - side) * (B - 2) + k

    fill(ext, now, lambda k: xr[row_of(g, k)], lambda k: cr[row_of(1 - g, k)], halo, THIRD, 0, g, s, geo)

    def keep_block(row, value):
        block[row - B] = value
        low, high = value[:, 0 : geo.H], value[:, geo.H : geo.Y]
        near[row - B] = jnp.where(g == 0, low, high)
        back[row - B] = jnp.where(g == 0, high, low)

    two_steps(ext, 1, lambda row: before[row - (B - 1)], mid, keep_block, coefs, dif, tot, geo)


def scatter_kernel(geo, scal, offsets, *refs):
    n = geo.sides
    now, xr, cr, courant, refl, refl_far, *coefs = refs[:11]
    force = refs[11]
    halo = refs[12 : 12 + 3 * n]
    force_out, scat, scat_prior = refs[12 + 3 * n : 15 + 3 * n]
    ext, dif, tot, wave = refs[15 + 3 * n :]
    g, s = scal[0], scal[1]
    B = geo.B
    fill_blocks(ext, xr, cr, g, geo, now)
    make_source(ext, refl, refl_far, offsets, courant, force_out, g, geo)
    fill(wave, force, lambda k: xr[B + k], lambda k: cr[B + k], halo, THIRD, 1, g, s, geo)

    def keep_scat(row, value):
        scat[row - B] = value + force_out[row - B]

    two_steps(wave, 2, lambda row: -wave[row], scat_prior, keep_scat, coefs, dif, tot, geo)


def source_kernel(geo, scal, offsets, *refs):
    n = geo.sides
    now, xr, cr, courant, refl, refl_far, scat, force2 = refs[:8]
    force3, px, pc = refs[8:11]
    tiles, corners, ext = refs[11 : 11 + n], refs[11 + n : 11 + 2 * n], refs[11 + 2 * n]
    g, s = scal[0], scal[1]
    fill_blocks(ext, xr, cr, g, geo, now)
    make_source(ext, refl, refl_far, offsets, courant, force3, g, geo)
    items = list(zip((scat, force2, force3), LAST))
    put_rows(items, px, pc, 0, g, geo)
    pack_tiles(items, g, s, tiles, corners, geo)


def last_kernel(geo, scal, *refs):
    n = geo.sides
    scat, before, force2, force3, xr, cr, *coefs = refs[:11]
    halo = refs[11 : 11 + 3 * n]
    out_near, out_far = refs[11 + 3 * n : 13 + 3 * n]
    wave, second, third, dif, tot, mid4, mid5 = refs[13 + 3 * n :]
    g, s = scal[0], scal[1]
    B = geo.B
    fill(wave, scat, lambda k: xr[k], lambda k: cr[k], halo, LAST, 0, g, s, geo)
    fill(second, force2, lambda k: xr[3 + k], lambda k: cr[3 + k], halo, LAST, 1, g, s, geo)
    fill(third, force3, lambda k: xr[5 + k], lambda k: cr[5 + k], halo, LAST, 2, g, s, geo)

    def keep4(row, value):
        mid4[row - (B - 2)] = value

    def keep5(row, value):
        mid5[row - (B - 1)] = value

    def keep6(row, value):
        low, high = value[:, 0 : geo.H], value[:, geo.H : geo.Y]
        out_near[row - B] = jnp.where(g == 0, low, high)
        out_far[row - B] = jnp.where(g == 0, high, low)

    prior2 = lambda row: before[row - (B - 2)]
    prior4 = lambda row: mid4[row - (B - 2)]
    advance(wave, 0, B - 2, B + 4, geo.ZE, prior2, lambda row: second[row], keep4, coefs, dif, tot, geo)
    advance(mid4, B - 2, B - 1, B + 2, geo.ZE, lambda row: wave[row], lambda row: third[row], keep5, coefs, dif, tot, geo)
    advance(mid5, B - 1, B, B, geo.Z, prior4, lambda row: force3[row - B], keep6, coefs, dif, tot, geo)


def finish_kernel(geo, scal, near, far, out):
    g = scal[0]

    def one(row, carry):
        out[g * geo.B + row] = near[row]
        out[(1 - g) * geo.B + row] = far[row]
        return carry

    lax.fori_loop(0, geo.B, one, 0, unroll=4)


def place_kernel(geo, scal, *refs, other):
    half, out, sem = refs[0], refs[-2], refs[-1]
    start = pl.multiple_of((1 - scal[0] if other else scal[0]) * geo.B, TILE)
    copy = pltpu.make_async_copy(half, out.at[pl.ds(start, geo.B)], sem)
    copy.start()
    copy.wait()


def shards(sections, gx, wave_now, wave_before, courant, anisotropy, tilt, reflectivity, offsets):
    rows, depth, half = wave_now.shape
    geo = Geometry(rows, depth, half, sections)
    B, Z, H, Y, ZE, n = geo.B, geo.Z, geo.H, geo.Y, geo.ZE, geo.sides
    g = lax.axis_index("gy")
    s = lax.axis_index("section")
    scal = jnp.stack([g, s]).astype(jnp.int32)
    swap = [(0, 1), (1, 0)]
    pairs_x = [p for i in range(gx - 1) for p in ((2 * i + 1, 2 * i + 2), (2 * i + 2, 2 * i + 1))]

    def z_moves():
        if geo.two:
            return [[(0, 1), (1, 0)]]
        return [[(i, i + 1) for i in range(sections - 1)], [(i + 1, i) for i in range(sections - 1)]]

    def corner_pairs(move):
        out = []
        for a, b in pairs_x:
            for i, j in move:
                out.append((((a // 2) * sections + i) * 2 + a % 2, ((b // 2) * sections + j) * 2 + b % 2))
        return out

    def chip(value):
        return lax.ppermute(value, "gy", swap)

    def exchange(px, pc, tiles, corners):
        xr = lax.ppermute(px, ("gx", "gy"), pairs_x)
        xz = [
            lax.ppermute(t, ("gx", "section", "gy"), corner_pairs(m)) for t, m in zip(corners, z_moves())
        ]
        zr = [lax.ppermute(t, "section", m) for t, m in zip(tiles, z_moves())]
        cr = chip(pc)
        cz = [chip(t) for t in zr]
        return xr, cr, [*zr, *xz, *cz]

    def shape(*dims):
        return jax.ShapeDtypeStruct(dims, F32)

    def call(kernel, inputs, outs, scratch, smem=1, specs=None, extra=(), aliases=None, out_specs=None):
        if specs is None:
            specs = [pl.BlockSpec(memory_space=pltpu.SMEM)] * (smem - 1)
            specs += [pl.BlockSpec(memory_space=pltpu.VMEM)] * (len(inputs) - smem)
        used = sum(4 * d[0] * d[1] * d[2] for d in scratch)
        return pl.pallas_call(
            functools.partial(kernel, geo),
            out_shape=outs,
            grid_spec=pltpu.PrefetchScalarGridSpec(
                num_scalar_prefetch=1,
                grid=(1,),
                in_specs=specs,
                out_specs=out_specs or [pl.BlockSpec(memory_space=pltpu.VMEM)] * len(outs),
                scratch_shapes=[*(pltpu.VMEM(d, F32) for d in scratch), *extra],
            ),
            input_output_aliases=aliases or {},
            compiler_params=pltpu.CompilerParams(vmem_limit_bytes=used + SLACK),
        )(*inputs)

    block, wide, wider, ext = (B, Z, Y), (B + 2, ZE, Y), (B + 4, ZE, Y), (3 * B, ZE, Y)

    def tile_outs(depths):
        return [shape(tiles_of(depths, geo)[1], TILE, Y)] * n + [shape(corner_tiles(depths), TILE, Y)] * n

    in_hbm = lambda value: pltpu.with_memory_space_constraint(value, pltpu.HBM)
    fields = [in_hbm(f) for f in (wave_now, wave_before, courant, anisotropy, tilt)]
    reflectivity = in_hbm(reflectivity)
    hbm = pl.BlockSpec(memory_space=pltpu.HBM)
    whole = pl.BlockSpec(memory_space=pltpu.VMEM)

    def half_of(other):
        kernel = functools.partial(half_kernel, other=other)
        copies = [pltpu.SemaphoreType.DMA((5,))]
        (out,) = call(kernel, [scal, *fields], [shape(5, B, Z, H)], [], specs=[hbm] * 5, extra=copies)
        return out

    far = chip(half_of(True))
    near = half_of(False)
    *own, px, pc, r0, r1 = _split(
        call(
            join_kernel,
            [scal, near, far],
            [shape(*block)] * 5 + [shape(sum(FIRST), Z, Y)] * 2 + tile_outs(FIRST),
            [],
        ),
        7,
        n,
    )
    xr, cr, halo = exchange(px, pc, r0, r1)
    (refl_far,) = call(
        widen_kernel,
        [scal, reflectivity],
        [shape(NOFF, B, Z, H)],
        [],
        specs=[hbm],
        extra=[pltpu.VMEM((NOFF, B, Z, H), reflectivity.dtype), pltpu.SemaphoreType.DMA((4,))],
    )
    refl_far = chip(refl_far)
    coefs = call(coef_kernel, [scal, *own[2:]], [shape(*wider)] * 5, [])
    inputs = [scal, *own[:2], xr, cr, *halo, *coefs]
    first = len(inputs) - 5
    now, prior, *coefs, r0, r1 = _split(
        call(
            first_kernel,
            inputs,
            [shape(*block), shape(*wide)] + [shape(*wider)] * 5 + tile_outs(SECOND),
            [ext] * 4,
            aliases={first + k: 2 + k for k in range(5)},
        ),
        7,
        n,
    )
    courant_own = own[2]
    xr, cr, halo = exchange(now, now, r0, r1)
    (refl,) = call(
        own_refl_kernel,
        [scal, reflectivity],
        [jax.ShapeDtypeStruct((NOFF, B, Z, H), reflectivity.dtype)],
        [],
        specs=[hbm],
        extra=[pltpu.SemaphoreType.DMA],
    )
    px, pc, prior, force, r0, r1 = _split(
        call(
            second_kernel,
            [scal, offsets, now, prior, xr, cr, courant_own, refl, refl_far, *coefs, *halo],
            [shape(B + THIRD[1], Z, Y)] * 2 + [shape(*wide), shape(*block)] + tile_outs(THIRD),
            [ext] * 3,
            2,
        ),
        4,
        n,
    )
    xr, cr, halo = exchange(px, pc, r0, r1)
    wave, near_u, back = call(
        third_kernel, [scal, px, prior, xr, cr, *coefs, *halo], [shape(*block)] + [shape(B, Z, H)] * 2, [ext] * 3 + [wide]
    )
    wave_x = lax.ppermute(wave, ("gx", "gy"), pairs_x)
    wave_c = chip(wave)
    force2, scat, scat_prior = call(
        scatter_kernel,
        [scal, offsets, px, xr, cr, courant_own, refl, refl_far, *coefs, force, *halo],
        [shape(*block)] * 2 + [shape(*wider)],
        [ext] * 4,
        2,
    )
    force3, qx, qc, r0, r1 = _split(
        call(
            source_kernel,
            [scal, offsets, wave, wave_x, wave_c, courant_own, refl, refl_far, scat, force2],
            [shape(*block)] + [shape(sum(LAST), Z, Y)] * 2 + tile_outs(LAST),
            [ext],
            2,
        ),
        3,
        n,
    )
    xr, cr, halo = exchange(qx, qc, r0, r1)

    def placed(half, other, into=None):
        return call(
            functools.partial(place_kernel, other=other),
            [scal, half] + ([] if into is None else [into]),
            [shape(rows, Z, H)],
            [],
            specs=[whole] + ([] if into is None else [hbm]),
            extra=[pltpu.SemaphoreType.DMA],
            aliases={} if into is None else {2: 0},
            out_specs=[hbm],
        )[0]

    back = chip(back)
    (background,) = call(finish_kernel, [scal, near_u, back], [shape(rows, Z, H)], [])
    near_w, far_w = call(
        last_kernel,
        [scal, scat, scat_prior, force2, force3, xr, cr, *coefs, *halo],
        [shape(B, Z, H)] * 2,
        [ext] * 5 + [wider, wide],
    )
    far_w = chip(far_w)
    scattered = placed(near_w, False)
    scattered = placed(far_w, True, scattered)
    return background, scattered


def _split(values, count, n):
    return [*values[:count], values[count : count + n], values[count + n :]]


def solution(mesh):
    spec = P(("shot", "gx"), "section", "gy")
    assert mesh.shape["gy"] == 2
    return jax.shard_map(
        functools.partial(shards, mesh.shape["section"], mesh.shape["gx"]),
        mesh=mesh,
        in_specs=(spec,) * 5 + (P(None, ("shot", "gx"), "section", "gy"), P()),
        out_specs=(spec, spec),
        check_vma=False,
    )
```

time: 105 us -> 110 us (1.048)
  waiting for transfers between devices: 14.6 us -> 22.7 us
  starting transfers between devices: 54.8 us -> 51.3 us
    ppermute x5 -> x4, waiting for transfers between devices: 8.58 us -> 16.7 us  [exchange(): zr = [lax.ppermute(t, 'section', m) for t, m in zip(tiles, z_moves())]]
    ppermute x5 -> x4, starting transfers between devices: 9.01 us -> 7.45 us  [exchange(): zr = [lax.ppermute(t, 'section', m) for t, m in zip(tiles, z_moves())]]
    ppermute x5 -> x4, starting transfers between devices: 3.39 us -> 2.74 us  [exchange(): lax.ppermute(t, ('gx', 'section', 'gy'), corner_pairs(m))]
    ppermute x5 -> x4, starting transfers between devices: 3.36 us -> 2.72 us  [exchange(): xr = lax.ppermute(px, ('gx', 'gy'), pairs_x)]
    ppermute x15 -> x13, starting transfers between devices: 38.3 us -> 37.7 us  [chip(): return lax.ppermute(value, 'gy', swap)]
    pallas_call x16 -> x15, Pallas kernels: 33.9 us -> 34.2 us  [call(): pl.pallas_call(functools.partial(kernel, geo), out_shape=outs, grid_spec=...]
    ppermute x15 -> x13, waiting for transfers between devices: 5.94 us -> 6.03 us  [chip(): return lax.ppermute(value, 'gy', swap)]
  transfers between devices with their start and end apart: 31 -> 26, of which waited for: 6 -> 6; matrix products, arithmetic and copies ran while one was open for 0% -> 0% of each run, Pallas kernels for 21% -> 20%
where the time goes in v5:
time: 110 us; the launch traced here: 109 us
  starting transfers between devices  51.3 us (47%)
  Pallas kernels  34.2 us (31%)
  waiting for transfers between devices  22.7 us (21%)
    ppermute x13, starting transfers between devices, chip(): return lax.ppermute(value, 'gy', swap)  37.7 us
    pallas_call x15, Pallas kernels, call(): pl.pallas_call(functools.partial(kernel, geo), out_shape=outs, grid_spec=...  34.2 us
    ppermute x4, waiting for transfers between devices, exchange(): zr = [lax.ppermute(t, 'section', m) for t, m in zip(tiles, z_moves())]  16.7 us
    ppermute x4, starting transfers between devices, exchange(): zr = [lax.ppermute(t, 'section', m) for t, m in zip(tiles, z_moves())]  7.45 us
    ppermute x13, waiting for transfers between devices, chip(): return lax.ppermute(value, 'gy', swap)  6.03 us
    ppermute x4, starting transfers between devices, exchange(): lax.ppermute(t, ('gx', 'section', 'gy'), corner_pairs(m))  2.74 us
    ppermute x4, starting transfers between devices, exchange(): xr = lax.ppermute(px, ('gx', 'gy'), pairs_x)  2.72 us
  transfers between devices with their start and end apart: 26, of which 6 were waited for; matrix products, arithmetic and copies ran while one was open for 0% of the time, Pallas kernels for 20%

profile of v5, /device:TPU:0, one launch (start us, length us, event | category | flops | bytes accessed | tf_op | source)
XLA Modules:
  0.0 109.3 jit_solution(10494099453232522814)
XLA Ops:
  0.6 0.1 pad_add_fusion.scal
  0.7 2.2 %shard_map.92 = f32[17,16,16,256]{3,2,1,0:T(8,128)S(1)} custom-call(s32[2]{0:T(128)S(1)} %pad_add_fusion.scal, bf16[17,32,16,256]{3,2,1,0:T(8,128)(2,1)} %refl.3), custom_call_target="tpu_custom_call" | custom-call | tf_op jit(solution)/shard_map/pallas_call | solution.py:559
  2.9 0.6 collective-permute-start.8
  3.5 1.9 %shard_map.87 = f32[5,16,16,256]{3,2,1,0:T(8,128)S(1)} custom-call(s32[2]{0:T(128)S(1)} %pad_add_fusion.scal, f32[32,16,256]{2,1,0:T(8,128)} %refs_0_.3, f32[32,16,256]{2,1,0:T(8,128)} %refs_1_.3, f32[32,16,256]{2,1,0:T(8,128)} %refs_2_.3, f32[32,16,256]{2,1,0:T(8,128)} %refs_3_.3, f32[32,16,256]{2,1,0:T(8,128)} %refs_4_.3), custom_call_target="tpu_custom_call" | custom-call | tf_op jit(solution)/shard_map/pallas_call | solution.py:559
  5.3 0.1 collective-permute-start
  5.4 1.9 %shard_map.86.refs_0_ = f32[5,16,16,256]{3,2,1,0:T(8,128)S(1)} custom-call(s32[2]{0:T(128)S(1)} %pad_add_fusion.scal, f32[32,16,256]{2,1,0:T(8,128)} %refs_0_.3, f32[32,16,256]{2,1,0:T(8,128)} %refs_1_.3, f32[32,16,256]{2,1,0:T(8,128)} %refs_2_.3, f32[32,16,256]{2,1,0:T(8,128)} %refs_3_.3, f32[32,16,256]{2,1,0:T(8,128)} %refs_4_.3), custom_call_target="tpu_custom_call" | custom-call | tf_op jit(solution)/shard_map/pallas_call | solution.py:559
  7.3 5.2 %collective-permute-done.refs_1_ = f32[5,16,16,256]{3,2,1,0:T(8,128)S(1)} collective-permute-done((f32[5,16,16,256]{3,2,1,0:T(8,128)S(1)}, f32[5,16,16,256]{3,2,1,0:T(8,128)S(1)}, u32[]{:S(2)}, u32[]{:S(2)}) %collective-permute-start) | collective-permute-done | bytes 1310752 | tf_op jit(solution)/shard_map/ppermute | solution.py:539
  12.5 0.9 shard_map.88
  13.4 2.9 %collective-permute-start.3 = (f32[18,8,512]{2,1,0:T(8,128)S(1)}, f32[18,8,512]{2,1,0:T(8,128)S(1)}, u32[]{:S(2)}, u32[]{:S(2)}) collective-permute-start(f32[18,8,512]{2,1,0:T(8,128)S(1)} %get-tuple-element.48), channel_id=1, source_target_pairs={{0,2},{2,0},{1,3},{3,1},{4,6},{6,4},{5,7},{7,5},{8,10},{10,8},{9,1... | collective-permute-start | bytes 884744 | tf_op jit(solution)/shard_map/ppermute | solution.py:546
  16.3 0.7 collective-permute-start.1
  17.0 3.0 %collective-permute-start.2 = (f32[9,16,512]{2,1,0:T(8,128)S(1)}, f32[9,16,512]{2,1,0:T(8,128)S(1)}, u32[]{:S(2)}, u32[]{:S(2)}) collective-permute-start(f32[9,16,512]{2,1,0:T(8,128)S(1)} %get-tuple-element.47), channel_id=1, source_target_pairs={{0,1},{1,0},{2,3},{3,2},{4,5},{5,4},{6,7},{7,6},{8,9},{9,8},{10,11... | collective-permute-start | bytes 884744 | tf_op jit(solution)/shard_map/ppermute | solution.py:539
  20.0 3.6 %collective-permute-done.3.refs_4_ = f32[18,8,512]{2,1,0:T(8,128)S(1)} collective-permute-done((f32[18,8,512]{2,1,0:T(8,128)S(1)}, f32[18,8,512]{2,1,0:T(8,128)S(1)}, u32[]{:S(2)}, u32[]{:S(2)}) %collective-permute-start.3) | collective-permute-done | bytes 294944 | tf_op jit(solution)/shard_map/ppermute | solution.py:546
  23.6 0.7 collective-permute-start.4
  24.3 1.6 %shard_map.89 = (f32[20,24,512]{2,1,0:T(8,128)S(1)}, f32[20,24,512]{2,1,0:T(8,128)S(1)}, f32[20,24,512]{2,1,0:T(8,128)S(1)}, f32[20,24,512]{2,1,0:T(8,128)S(1)}, f32[20,24,512]{2,1,0:T(8,128)S(1)}) custom-call(s32[2]{0:T(128)S(1)} %pad_add_fusion.scal, f32[16,16,512]{2,1,0:T(8,128)S(1)} %get-tuple-element.50.courant.refs_4_.refs_3_, ...), custom_call_target="tpu_custom_call" | custom-call | tf_op jit(solution)/shard_map/pallas_call | solution.py:559
  25.8 0.0 collective-permute-done.4.refs_5_
  25.8 0.0 collective-permute-done.2.refs_3_
  25.9 0.0 collective-permute-done.5.refs_6_
  25.9 3.0 %shard_map.90 = (f32[16,16,512]{2,1,0:T(8,128)S(1)}, f32[18,24,512]{2,1,0:T(8,128)S(1)}, f32[20,24,512]{2,1,0:T(8,128)S(1)}, f32[20,24,512]{2,1,0:T(8,128)S(1)},...) custom-call(s32[2]{0:T(128)S(1)} %pad_add_fusion.scal, ...), custom_call_target="tpu_custom_call", output_to_operand_aliasing={{2}: (8, {}), {3}: (9, {}), {4}: (10, {}), {5}: (11, {}), {... | custom-call | tf_op jit(solution)/shard_map/pallas_call | solution.py:559
  28.9 0.7 collective-permute-start.6
  29.6 7.3 %collective-permute-start.7 = (f32[16,16,512]{2,1,0:T(8,128)S(1)}, f32[16,16,512]{2,1,0:T(8,128)S(1)}, u32[]{:S(2)}, u32[]{:S(2)}) collective-permute-start(f32[16,16,512]{2,1,0:T(8,128)S(1)} %get-tuple-element.58.refs_0_), channel_id=1, source_target_pairs={{0,1},{1,0},{2,3},{3,2},{4,5},{5,4},{6,7},{7,6},{8,9},{9,8},{10,11... | collective-permute-start | bytes 1572872 | tf_op jit(solution)/shard_map/ppermute | solution.py:539
  36.9 1.5 %collective-permute-start.9 = (f32[4,8,512]{2,1,0:T(8,128)S(1)}, f32[4,8,512]{2,1,0:T(8,128)S(1)}, u32[]{:S(2)}, u32[]{:S(2)}) collective-permute-start(f32[4,8,512]{2,1,0:T(8,128)S(1)} %get-tuple-element.65), channel_id=1, source_target_pairs={{0,2},{2,0},{1,3},{3,1},{4,6},{6,4},{5,7},{7,5},{8,10},{10,8},{9,1... | collective-permute-start | bytes 196616 | tf_op jit(solution)/shard_map/ppermute | solution.py:546
  38.3 2.8 %collective-permute-done.9.refs_12_ = f32[4,8,512]{2,1,0:T(8,128)S(1)} collective-permute-done((f32[4,8,512]{2,1,0:T(8,128)S(1)}, f32[4,8,512]{2,1,0:T(8,128)S(1)}, u32[]{:S(2)}, u32[]{:S(2)}) %collective-permute-start.9) | collective-permute-done | bytes 65568 | tf_op jit(solution)/shard_map/ppermute | solution.py:546
  41.1 0.8 collective-permute-start.10
  41.9 2.2 %shard_map.91.refs_5_.refs_4_ = bf16[17,16,16,256]{3,2,1,0:T(8,128)(2,1)S(1)} custom-call(s32[2]{0:T(128)S(1)} %pad_add_fusion.scal, bf16[17,32,16,256]{3,2,1,0:T(8,128)(2,1)} %refl.3), custom_call_target="tpu_custom_call" | custom-call | tf_op jit(solution)/shard_map/pallas_call | solution.py:559
  44.2 4.1 %shard_map.93 = (f32[19,16,512]{2,1,0:T(8,128)S(1)}, f32[19,16,512]{2,1,0:T(8,128)S(1)}, f32[18,24,512]{2,1,0:T(8,128)S(1)}, f32[16,16,512]{2,1,0:T(8,128)S(1)},...) custom-call(s32[2]{0:T(128)S(1)} %pad_add_fusion.scal, s32[17]{0:T(128)S(1)} %copy-done, ...), custom_call_target="tpu_custom_call" | custom-call | tf_op jit(solution)/shard_map/pallas_call | solution.py:559
  48.3 0.7 collective-permute-start.12
  49.0 6.0 %collective-permute-start.13 = (f32[19,16,512]{2,1,0:T(8,128)S(1)}, f32[19,16,512]{2,1,0:T(8,128)S(1)}, u32[]{:S(2)}, u32[]{:S(2)}) collective-permute-start(f32[19,16,512]{2,1,0:T(8,128)S(1)} %get-tuple-element.69), channel_id=1, source_target_pairs={{0,1},{1,0},{2,3},{3,2},{4,5},{5,4},{6,7},{7,6},{8,9},{9,8},{10,11... | collective-permute-start | bytes 1867784 | tf_op jit(solution)/shard_map/ppermute | solution.py:539
  55.0 1.5 %collective-permute-start.14 = (f32[12,8,512]{2,1,0:T(8,128)S(1)}, f32[12,8,512]{2,1,0:T(8,128)S(1)}, u32[]{:S(2)}, u32[]{:S(2)}) collective-permute-start(f32[12,8,512]{2,1,0:T(8,128)S(1)} %get-tuple-element.70), channel_id=1, source_target_pairs={{0,2},{2,0},{1,3},{3,1},{4,6},{6,4},{5,7},{7,5},{8,10},{10,8},{9,1... | collective-permute-start | bytes 589832 | tf_op jit(solution)/shard_map/ppermute | solution.py:546
  56.5 5.4 %collective-permute-done.14.refs_9_.refs_12_ = f32[12,8,512]{2,1,0:T(8,128)S(1)} collective-permute-done((f32[12,8,512]{2,1,0:T(8,128)S(1)}, f32[12,8,512]{2,1,0:T(8,128)S(1)}, u32[]{:S(2)}, u32[]{:S(2)}) %collective-permute-start.14) | collective-permute-done | bytes 196640 | tf_op jit(solution)/shard_map/ppermute | solution.py:546
  61.9 0.7 collective-permute-start.15
  62.6 0.8 collective-permute-done.16.refs_11_.refs_14_
  63.3 2.3 %shard_map.94 = (f32[16,16,512]{2,1,0:T(8,128)S(1)}, f32[16,16,256]{2,1,0:T(8,128)S(1)}, f32[16,16,256]{2,1,0:T(8,128)S(1)}) custom-call(s32[2]{0:T(128)S(1)} %pad_add_fusion.scal, f32[19,16,512]{2,1,0:T(8,128)S(1)} %get-tuple-element.67.refs_0_, f32[18,24,512]{2,1,0:T(8,128)S(1)} %get-tuple-element.68.refs_1_, ...), custom_call_target="tpu_custom_call" | custom-call | tf_op jit(solution)/shard_map/pallas_call | solution.py:559
  65.7 0.7 collective-permute-start.18
  66.4 7.8 %collective-permute-start.19 = (f32[16,16,512]{2,1,0:T(8,128)S(1)}, f32[16,16,512]{2,1,0:T(8,128)S(1)}, u32[]{:S(2)}, u32[]{:S(2)}) collective-permute-start(f32[16,16,512]{2,1,0:T(8,128)S(1)} %get-tuple-element.78.refs_0_), channel_id=1, source_target_pairs={{0,1},{1,0},{2,3},{3,2},{4,5},{5,4},{6,7},{7,6},{8,9},{9,8},{10,11... | collective-permute-start | bytes 1572872 | tf_op jit(solution)/shard_map/ppermute | solution.py:539
  74.2 4.2 %shard_map.96 = (f32[16,16,512]{2,1,0:T(8,128)S(1)}, f32[16,16,512]{2,1,0:T(8,128)S(1)}, f32[20,24,512]{2,1,0:T(8,128)S(1)}) custom-call(s32[2]{0:T(128)S(1)} %pad_add_fusion.scal, s32[17]{0:T(128)S(1)} %copy-done, f32[19,16,512]{2,1,0:T(8,128)S(1)} %get-tuple-element.67.refs_0_, f32[19,16,512]{2,1,0:T(8,128)S(1)} %collective-permute-done.12.refs_2_.refs_1_, ...), custom_call_target="tpu_custom_call" | custom-call | tf_op jit(solution)/shard_map/pallas_call | solution.py:559
  78.5 2.4 %shard_map.97 = (f32[16,16,512]{2,1,0:T(8,128)S(1)}, f32[6,16,512]{2,1,0:T(8,128)S(1)}, f32[6,16,512]{2,1,0:T(8,128)S(1)}, f32[14,8,512]{2,1,0:T(8,128)S(1)}, f32[3,8,512]{2,1,0:T(8,128)S(1)}) custom-call(s32[2]{0:T(128)S(1)} %pad_add_fusion.scal, s32[17]{0:T(128)S(1)} %copy-done, f32[16,16,512]{2,1,0:T(8,128)S(1)} %get-tuple-element.78.refs_0_, ...), custom_call_target="tpu_custom_call" | custom-call | tf_op jit(solution)/shard_map/pallas_call | solution.py:559
  80.9 1.6 %collective-permute-start.22 = (f32[14,8,512]{2,1,0:T(8,128)S(1)}, f32[14,8,512]{2,1,0:T(8,128)S(1)}, u32[]{:S(2)}, u32[]{:S(2)}) collective-permute-start(f32[14,8,512]{2,1,0:T(8,128)S(1)} %get-tuple-element.82), channel_id=1, source_target_pairs={{0,2},{2,0},{1,3},{3,1},{4,6},{6,4},{5,7},{7,5},{8,10},{10,8},{9,1... | collective-permute-start | bytes 688136 | tf_op jit(solution)/shard_map/ppermute | solution.py:546
  82.4 4.9 %collective-permute-done.22.refs_11_ = f32[14,8,512]{2,1,0:T(8,128)S(1)} collective-permute-done((f32[14,8,512]{2,1,0:T(8,128)S(1)}, f32[14,8,512]{2,1,0:T(8,128)S(1)}, u32[]{:S(2)}, u32[]{:S(2)}) %collective-permute-start.22) | collective-permute-done | bytes 229408 | tf_op jit(solution)/shard_map/ppermute | solution.py:546
  87.3 1.9 %collective-permute-start.24 = (f32[14,8,512]{2,1,0:T(8,128)S(1)}, f32[14,8,512]{2,1,0:T(8,128)S(1)}, u32[]{:S(2)}, u32[]{:S(2)}) collective-permute-start(f32[14,8,512]{2,1,0:T(8,128)S(1)} %collective-permute-done.22.refs_11_), channel_id=1, source_target_pairs={{0,1},{1,0},{2,3},{3,2},{4,5},{5,4},{6,7},{7,6},{8,9},{9,8},{10,11... | collective-permute-start | bytes 688136 | tf_op jit(solution)/shard_map/ppermute | solution.py:539
  89.3 0.7 collective-permute-start.20
  89.9 5.3 %collective-permute-start.21 = (f32[6,16,512]{2,1,0:T(8,128)S(1)}, f32[6,16,512]{2,1,0:T(8,128)S(1)}, u32[]{:S(2)}, u32[]{:S(2)}) collective-permute-start(f32[6,16,512]{2,1,0:T(8,128)S(1)} %get-tuple-element.81), channel_id=1, source_target_pairs={{0,1},{1,0},{2,3},{3,2},{4,5},{5,4},{6,7},{7,6},{8,9},{9,8},{10,11... | collective-permute-start | bytes 589832 | tf_op jit(solution)/shard_map/ppermute | solution.py:539
  95.2 0.7 collective-permute-start.23
  95.9 3.3 %collective-permute-start.17 = (f32[16,16,256]{2,1,0:T(8,128)S(1)}, f32[16,16,256]{2,1,0:T(8,128)S(1)}, u32[]{:S(2)}, u32[]{:S(2)}) collective-permute-start(f32[16,16,256]{2,1,0:T(8,128)S(1)} %get-tuple-element.73), channel_id=1, source_target_pairs={{0,1},{1,0},{2,3},{3,2},{4,5},{5,4},{6,7},{7,6},{8,9},{9,8},{10,11... | collective-permute-start | bytes 786440 | tf_op jit(solution)/shard_map/ppermute | solution.py:539
  99.1 3.7 %shard_map.98 = (f32[16,16,256]{2,1,0:T(8,128)S(1)}, f32[16,16,256]{2,1,0:T(8,128)S(1)}) custom-call(s32[2]{0:T(128)S(1)} %pad_add_fusion.scal, f32[16,16,512]{2,1,0:T(8,128)S(1)} %get-tuple-element.75.refs_6_.refs_0_, f32[20,24,512]{2,1,0:T(8,128)S(1)} %get-tuple-element.76.refs_1_, f32[16,16,512]{2,1,0:T(8,128)S(1)} %get-tuple-element.77.refs_7_.refs_2_, ...), custom_call_target="tpu_custom_call" | custom-call | tf_op jit(solution)/shard_map/pallas_call | solution.py:559
  102.9 2.5 %collective-permute-start.25 = (f32[16,16,256]{2,1,0:T(8,128)S(1)}, f32[16,16,256]{2,1,0:T(8,128)S(1)}, u32[]{:S(2)}, u32[]{:S(2)}) collective-permute-start(f32[16,16,256]{2,1,0:T(8,128)S(1)} %get-tuple-element.84), channel_id=1, source_target_pairs={{0,1},{1,0},{2,3},{3,2},{4,5},{5,4},{6,7},{7,6},{8,9},{9,8},{10,11... | collective-permute-start | bytes 786440 | tf_op jit(solution)/shard_map/ppermute | solution.py:539
  105.4 1.4 %shard_map.95 = f32[32,16,256]{2,1,0:T(8,128)} custom-call(s32[2]{0:T(128)S(1)} %pad_add_fusion.scal, f32[16,16,256]{2,1,0:T(8,128)S(1)} %get-tuple-element.72.near, f32[16,16,256]{2,1,0:T(8,128)S(1)} %collective-permute-done.17.far), custom_call_target="tpu_custom_call" | custom-call | tf_op jit(solution)/shard_map/pallas_call | solution.py:559
  106.7 1.3 %shard_map.99.refs_1_ = f32[32,16,256]{2,1,0:T(8,128)} custom-call(s32[2]{0:T(128)S(1)} %pad_add_fusion.scal, f32[16,16,256]{2,1,0:T(8,128)S(1)} %get-tuple-element.85.refs_0_), custom_call_target="tpu_custom_call" | custom-call | tf_op jit(solution)/shard_map/pallas_call | solution.py:559
  108.0 1.3 %shard_map.100 = f32[32,16,256]{2,1,0:T(8,128)} custom-call(s32[2]{0:T(128)S(1)} %pad_add_fusion.scal, f32[16,16,256]{2,1,0:T(8,128)S(1)} %collective-permute-done.25.refs_0_, f32[32,16,256]{2,1,0:T(8,128)} %shard_map.99.refs_1_), custom_call_target="tpu_custom_call", output_to_operand_aliasing={{}: (2, {})} | custom-call | tf_op jit(solution)/shard_map/pallas_call | solution.py:559
  (22 shorter events, 0.1 us)
Async XLA Ops:
  2.9 41.2 %collective-permute-start.8 = (f32[17,16,16,256]{3,2,1,0:T(8,128)S(1)}, f32[17,16,16,256]{3,2,1,0:T(8,128)S(1)}, u32[]{:S(2)}, u32[]{:S(2)}) collective-permute-start(f32[17,16,16,256]{3,2,1,0:T(8,128)S(1)} %shard_map.92), channel_id=1, source_target_pairs={{0,1},{1,0},{2,3},{3,2},{4,5},{5,4},{6,7},{7,6},{8,9},{9,8},{10,11... | collective-permute-start | bytes 13369352 | tf_op jit(solution)/shard_map/ppermute | solution.py:539
  5.3 7.2 %collective-permute-start = (f32[5,16,16,256]{3,2,1,0:T(8,128)S(1)}, f32[5,16,16,256]{3,2,1,0:T(8,128)S(1)}, u32[]{:S(2)}, u32[]{:S(2)}) collective-permute-start(f32[5,16,16,256]{3,2,1,0:T(8,128)S(1)} %shard_map.87), channel_id=1, source_target_pairs={{0,1},{1,0},{2,3},{3,2},{4,5},{5,4},{6,7},{7,6},{8,9},{9,8},{10,11... | collective-permute-start | bytes 3932168 | tf_op jit(solution)/shard_map/ppermute | solution.py:539
  13.4 10.2 %collective-permute-start.3 = (f32[18,8,512]{2,1,0:T(8,128)S(1)}, f32[18,8,512]{2,1,0:T(8,128)S(1)}, u32[]{:S(2)}, u32[]{:S(2)}) collective-permute-start(f32[18,8,512]{2,1,0:T(8,128)S(1)} %get-tuple-element.48), channel_id=1, source_target_pairs={{0,2},{2,0},{1,3},{3,1},{4,6},{6,4},{5,7},{7,5},{8,10},{10,8},{9,1... | collective-permute-start | bytes 884744 | tf_op jit(solution)/shard_map/ppermute | solution.py:546
  16.3 9.5 %collective-permute-start.1 = (f32[9,16,512]{2,1,0:T(8,128)S(1)}, f32[9,16,512]{2,1,0:T(8,128)S(1)}, u32[]{:S(2)}, u32[]{:S(2)}) collective-permute-start(f32[9,16,512]{2,1,0:T(8,128)S(1)} %get-tuple-element.46), channel_id=1, source_target_pairs={{1,4},{4,1},{5,8},{8,5},{9,12},{12,9},{3,6},{6,3},{7,10},{10,7},{1... | collective-permute-start | bytes 884744 | tf_op jit(solution)/shard_map/ppermute | solution.py:542
  17.0 8.9 %collective-permute-start.2 = (f32[9,16,512]{2,1,0:T(8,128)S(1)}, f32[9,16,512]{2,1,0:T(8,128)S(1)}, u32[]{:S(2)}, u32[]{:S(2)}) collective-permute-start(f32[9,16,512]{2,1,0:T(8,128)S(1)} %get-tuple-element.47), channel_id=1, source_target_pairs={{0,1},{1,0},{2,3},{3,2},{4,5},{5,4},{6,7},{7,6},{8,9},{9,8},{10,11... | collective-permute-start | bytes 884744 | tf_op jit(solution)/shard_map/ppermute | solution.py:539
  23.6 2.3 %collective-permute-start.5 = (f32[18,8,512]{2,1,0:T(8,128)S(1)}, f32[18,8,512]{2,1,0:T(8,128)S(1)}, u32[]{:S(2)}, u32[]{:S(2)}) collective-permute-start(f32[18,8,512]{2,1,0:T(8,128)S(1)} %collective-permute-done.3.refs_4_), channel_id=1, source_target_pairs={{0,1},{1,0},{2,3},{3,2},{4,5},{5,4},{6,7},{7,6},{8,9},{9,8},{10,11... | collective-permute-start | bytes 884744 | tf_op jit(solution)/shard_map/ppermute | solution.py:539
  23.6 2.2 %collective-permute-start.4 = (f32[3,8,512]{2,1,0:T(8,128)S(1)}, f32[3,8,512]{2,1,0:T(8,128)S(1)}, u32[]{:S(2)}, u32[]{:S(2)}) collective-permute-start(f32[3,8,512]{2,1,0:T(8,128)S(1)} %get-tuple-element.49), channel_id=1, source_target_pairs={{1,6},{3,4},{4,3},{6,1},{5,10},{7,8},{8,7},{10,5},{9,14},{11,12},{... | collective-permute-start | bytes 147464 | tf_op jit(solution)/shard_map/ppermute | solution.py:544
  28.9 15.2 %collective-permute-start.6 = (f32[16,16,512]{2,1,0:T(8,128)S(1)}, f32[16,16,512]{2,1,0:T(8,128)S(1)}, u32[]{:S(2)}, u32[]{:S(2)}) collective-permute-start(f32[16,16,512]{2,1,0:T(8,128)S(1)} %get-tuple-element.58.refs_0_), channel_id=1, source_target_pairs={{1,4},{4,1},{5,8},{8,5},{9,12},{12,9},{3,6},{6,3},{7,10},{10,7},{1... | collective-permute-start | bytes 1572872 | tf_op jit(solution)/shard_map/ppermute | solution.py:542
  29.6 14.6 %collective-permute-start.7 = (f32[16,16,512]{2,1,0:T(8,128)S(1)}, f32[16,16,512]{2,1,0:T(8,128)S(1)}, u32[]{:S(2)}, u32[]{:S(2)}) collective-permute-start(f32[16,16,512]{2,1,0:T(8,128)S(1)} %get-tuple-element.58.refs_0_), channel_id=1, source_target_pairs={{0,1},{1,0},{2,3},{3,2},{4,5},{5,4},{6,7},{7,6},{8,9},{9,8},{10,11... | collective-permute-start | bytes 1572872 | tf_op jit(solution)/shard_map/ppermute | solution.py:539
  36.9 4.3 %collective-permute-start.9 = (f32[4,8,512]{2,1,0:T(8,128)S(1)}, f32[4,8,512]{2,1,0:T(8,128)S(1)}, u32[]{:S(2)}, u32[]{:S(2)}) collective-permute-start(f32[4,8,512]{2,1,0:T(8,128)S(1)} %get-tuple-element.65), channel_id=1, source_target_pairs={{0,2},{2,0},{1,3},{3,1},{4,6},{6,4},{5,7},{7,5},{8,10},{10,8},{9,1... | collective-permute-start | bytes 196616 | tf_op jit(solution)/shard_map/ppermute | solution.py:546
  41.1 3.0 %collective-permute-start.11 = (f32[4,8,512]{2,1,0:T(8,128)S(1)}, f32[4,8,512]{2,1,0:T(8,128)S(1)}, u32[]{:S(2)}, u32[]{:S(2)}) collective-permute-start(f32[4,8,512]{2,1,0:T(8,128)S(1)} %collective-permute-done.9.refs_12_), channel_id=1, source_target_pairs={{0,1},{1,0},{2,3},{3,2},{4,5},{5,4},{6,7},{7,6},{8,9},{9,8},{10,11... | collective-permute-start | bytes 196616 | tf_op jit(solution)/shard_map/ppermute | solution.py:539
  41.1 3.0 %copy-start = (s32[17]{0:T(128)S(1)}, s32[17]{0:T(128)}, u32[]{:S(2)}) copy-start(s32[17]{0:T(128)} %offsets.5) | copy-start | bytes 208
  41.1 3.0 %collective-permute-start.10 = (f32[1,8,512]{2,1,0:T(8,128)S(1)}, f32[1,8,512]{2,1,0:T(8,128)S(1)}, u32[]{:S(2)}, u32[]{:S(2)}) collective-permute-start(f32[1,8,512]{2,1,0:T(8,128)S(1)} %get-tuple-element.66), channel_id=1, source_target_pairs={{1,6},{3,4},{4,3},{6,1},{5,10},{7,8},{8,7},{10,5},{9,14},{11,12},{... | collective-permute-start | bytes 49160 | tf_op jit(solution)/shard_map/ppermute | solution.py:544
  48.3 15.1 %collective-permute-start.12 = (f32[19,16,512]{2,1,0:T(8,128)S(1)}, f32[19,16,512]{2,1,0:T(8,128)S(1)}, u32[]{:S(2)}, u32[]{:S(2)}) collective-permute-start(f32[19,16,512]{2,1,0:T(8,128)S(1)} %get-tuple-element.67.refs_0_), channel_id=1, source_target_pairs={{1,4},{4,1},{5,8},{8,5},{9,12},{12,9},{3,6},{6,3},{7,10},{10,7},{1... | collective-permute-start | bytes 1867784 | tf_op jit(solution)/shard_map/ppermute | solution.py:542
  49.0 14.4 %collective-permute-start.13 = (f32[19,16,512]{2,1,0:T(8,128)S(1)}, f32[19,16,512]{2,1,0:T(8,128)S(1)}, u32[]{:S(2)}, u32[]{:S(2)}) collective-permute-start(f32[19,16,512]{2,1,0:T(8,128)S(1)} %get-tuple-element.69), channel_id=1, source_target_pairs={{0,1},{1,0},{2,3},{3,2},{4,5},{5,4},{6,7},{7,6},{8,9},{9,8},{10,11... | collective-permute-start | bytes 1867784 | tf_op jit(solution)/shard_map/ppermute | solution.py:539
  55.0 6.9 %collective-permute-start.14 = (f32[12,8,512]{2,1,0:T(8,128)S(1)}, f32[12,8,512]{2,1,0:T(8,128)S(1)}, u32[]{:S(2)}, u32[]{:S(2)}) collective-permute-start(f32[12,8,512]{2,1,0:T(8,128)S(1)} %get-tuple-element.70), channel_id=1, source_target_pairs={{0,2},{2,0},{1,3},{3,1},{4,6},{6,4},{5,7},{7,5},{8,10},{10,8},{9,1... | collective-permute-start | bytes 589832 | tf_op jit(solution)/shard_map/ppermute | solution.py:546
  61.9 1.4 %collective-permute-start.16 = (f32[12,8,512]{2,1,0:T(8,128)S(1)}, f32[12,8,512]{2,1,0:T(8,128)S(1)}, u32[]{:S(2)}, u32[]{:S(2)}) collective-permute-start(f32[12,8,512]{2,1,0:T(8,128)S(1)} %collective-permute-done.14.refs_9_.refs_12_), channel_id=1, source_target_pairs={{0,1},{1,0},{2,3},{3,2},{4,5},{5,4},{6,7},{7,6},{8,9},{9,8},{10,11... | collective-permute-start | bytes 589832 | tf_op jit(solution)/shard_map/ppermute | solution.py:539
  61.9 0.7 collective-permute-start.15
  65.7 12.8 %collective-permute-start.18 = (f32[16,16,512]{2,1,0:T(8,128)S(1)}, f32[16,16,512]{2,1,0:T(8,128)S(1)}, u32[]{:S(2)}, u32[]{:S(2)}) collective-permute-start(f32[16,16,512]{2,1,0:T(8,128)S(1)} %get-tuple-element.78.refs_0_), channel_id=1, source_target_pairs={{1,4},{4,1},{5,8},{8,5},{9,12},{12,9},{3,6},{6,3},{7,10},{10,7},{1... | collective-permute-start | bytes 1572872 | tf_op jit(solution)/shard_map/ppermute | solution.py:651
  66.4 12.1 %collective-permute-start.19 = (f32[16,16,512]{2,1,0:T(8,128)S(1)}, f32[16,16,512]{2,1,0:T(8,128)S(1)}, u32[]{:S(2)}, u32[]{:S(2)}) collective-permute-start(f32[16,16,512]{2,1,0:T(8,128)S(1)} %get-tuple-element.78.refs_0_), channel_id=1, source_target_pairs={{0,1},{1,0},{2,3},{3,2},{4,5},{5,4},{6,7},{7,6},{8,9},{9,8},{10,11... | collective-permute-start | bytes 1572872 | tf_op jit(solution)/shard_map/ppermute | solution.py:539
  80.9 6.4 %collective-permute-start.22 = (f32[14,8,512]{2,1,0:T(8,128)S(1)}, f32[14,8,512]{2,1,0:T(8,128)S(1)}, u32[]{:S(2)}, u32[]{:S(2)}) collective-permute-start(f32[14,8,512]{2,1,0:T(8,128)S(1)} %get-tuple-element.82), channel_id=1, source_target_pairs={{0,2},{2,0},{1,3},{3,1},{4,6},{6,4},{5,7},{7,5},{8,10},{10,8},{9,1... | collective-permute-start | bytes 688136 | tf_op jit(solution)/shard_map/ppermute | solution.py:546
  87.3 11.8 %collective-permute-start.24 = (f32[14,8,512]{2,1,0:T(8,128)S(1)}, f32[14,8,512]{2,1,0:T(8,128)S(1)}, u32[]{:S(2)}, u32[]{:S(2)}) collective-permute-start(f32[14,8,512]{2,1,0:T(8,128)S(1)} %collective-permute-done.22.refs_11_), channel_id=1, source_target_pairs={{0,1},{1,0},{2,3},{3,2},{4,5},{5,4},{6,7},{7,6},{8,9},{9,8},{10,11... | collective-permute-start | bytes 688136 | tf_op jit(solution)/shard_map/ppermute | solution.py:539
  89.3 9.9 %collective-permute-start.20 = (f32[6,16,512]{2,1,0:T(8,128)S(1)}, f32[6,16,512]{2,1,0:T(8,128)S(1)}, u32[]{:S(2)}, u32[]{:S(2)}) collective-permute-start(f32[6,16,512]{2,1,0:T(8,128)S(1)} %get-tuple-element.80), channel_id=1, source_target_pairs={{1,4},{4,1},{5,8},{8,5},{9,12},{12,9},{3,6},{6,3},{7,10},{10,7},{1... | collective-permute-start | bytes 589832 | tf_op jit(solution)/shard_map/ppermute | solution.py:542
  89.9 9.2 %collective-permute-start.21 = (f32[6,16,512]{2,1,0:T(8,128)S(1)}, f32[6,16,512]{2,1,0:T(8,128)S(1)}, u32[]{:S(2)}, u32[]{:S(2)}) collective-permute-start(f32[6,16,512]{2,1,0:T(8,128)S(1)} %get-tuple-element.81), channel_id=1, source_target_pairs={{0,1},{1,0},{2,3},{3,2},{4,5},{5,4},{6,7},{7,6},{8,9},{9,8},{10,11... | collective-permute-start | bytes 589832 | tf_op jit(solution)/shard_map/ppermute | solution.py:539
  95.2 3.9 %collective-permute-start.23 = (f32[3,8,512]{2,1,0:T(8,128)S(1)}, f32[3,8,512]{2,1,0:T(8,128)S(1)}, u32[]{:S(2)}, u32[]{:S(2)}) collective-permute-start(f32[3,8,512]{2,1,0:T(8,128)S(1)} %get-tuple-element.83), channel_id=1, source_target_pairs={{1,6},{3,4},{4,3},{6,1},{5,10},{7,8},{8,7},{10,5},{9,14},{11,12},{... | collective-permute-start | bytes 147464 | tf_op jit(solution)/shard_map/ppermute | solution.py:544
  95.9 9.5 %collective-permute-start.17 = (f32[16,16,256]{2,1,0:T(8,128)S(1)}, f32[16,16,256]{2,1,0:T(8,128)S(1)}, u32[]{:S(2)}, u32[]{:S(2)}) collective-permute-start(f32[16,16,256]{2,1,0:T(8,128)S(1)} %get-tuple-element.73), channel_id=1, source_target_pairs={{0,1},{1,0},{2,3},{3,2},{4,5},{5,4},{6,7},{7,6},{8,9},{9,8},{10,11... | collective-permute-start | bytes 786440 | tf_op jit(solution)/shard_map/ppermute | solution.py:539
  102.9 5.1 %collective-permute-start.25 = (f32[16,16,256]{2,1,0:T(8,128)S(1)}, f32[16,16,256]{2,1,0:T(8,128)S(1)}, u32[]{:S(2)}, u32[]{:S(2)}) collective-permute-start(f32[16,16,256]{2,1,0:T(8,128)S(1)} %get-tuple-element.84), channel_id=1, source_target_pairs={{0,1},{1,0},{2,3},{3,2},{4,5},{5,4},{6,7},{7,6},{8,9},{9,8},{10,11... | collective-permute-start | bytes 786440 | tf_op jit(solution)/shard_map/ppermute | solution.py:539

commit v6 on v5

--- a/solution.py
+++ b/solution.py
@@ -259,7 +259,46 @@
         copy.wait()
 
 
-def widen_kernel(geo, scal, refl, out, held, sems):
+def join_kernel(geo, scal, *refs):
+    near, far = refs[:2]
+    own = refs[2:7]
+    px, pc = refs[7:9]
+    tiles, corners = refs[9 : 9 + geo.sides], refs[9 + geo.sides :]
+    g, s = scal[0], scal[1]
+    near_y = pl.multiple_of(g * geo.H, 128)
+    far_y = pl.multiple_of((1 - g) * geo.H, 128)
+
+    def one(row, carry):
+        for k in range(5):
+            own[k][row, :, pl.ds(near_y, geo.H)] = near[k, row]
+            own[k][row, :, pl.ds(far_y, geo.H)] = far[k, row]
+        return carry
+
+    lax.fori_loop(0, geo.B, one, 0, unroll=2)
+    put_rows(list(zip(own, FIRST)), px, pc, 0, g, geo)
+    pack_tiles(list(zip(own, FIRST)), g, s, tiles, corners, geo)
+
+
+def put_rows(items, px, pc, start, g, geo):
+    for side, out in ((g, px), (1 - g, pc)):
+        at = start
+        for ref, depth in items:
+            for k in range(depth):
+                out[at] = ref[edge_rows(depth, side, geo) + k]
+                at += 1
+
+
+def coefficients(speed, aniso, angle):
+    stretch = 2.0 * aniso
+    sine_square, cosine_square, product = trig_products(angle)
+    cx = speed * (1.0 + stretch * cosine_square)
+    cz = speed * (1.0 + stretch * sine_square)
+    cy = speed * (1.0 + stretch)
+    return cx, cz, cy, (0.5 * speed) * (stretch * product), 2.0 - 2.0 * (cx + cz + cy)
+
+
+def prepare_kernel(geo, scal, courant, aniso, tilt, refl, *refs):
+    *coefs, out, held, sems = refs
     other = pl.multiple_of((1 - scal[0]) * geo.B, TILE)
     cuts = [0, 5, 9, 13, NOFF]
     copies = [
@@ -268,68 +307,21 @@
     ]
     for copy in copies:
         copy.start()
+
+    def one(row):
+        for ref, value in zip(coefs, coefficients(courant[row], aniso[row], tilt[row])):
+            ref[row + 2, 0 : geo.Z, :] = value
+
+    each(0, geo.B, one, 2)
     for copy, a, b in zip(copies, cuts, cuts[1:]):
         copy.wait()
 
-        def one(h, carry):
+        def widen(h, carry):
             for row in range(geo.B):
                 out[h, row] = held[h, row].astype(F32)
             return carry
 
-        lax.fori_loop(a, b, one, 0)
-
-
-def own_refl_kernel(geo, scal, refl, out, sem):
-    start = pl.multiple_of(scal[0] * geo.B, TILE)
-    copy = pltpu.make_async_copy(refl.at[:, pl.ds(start, geo.B)], out, sem)
-    copy.start()
-    copy.wait()
-
-
-def join_kernel(geo, scal, *refs):
-    near, far = refs[:2]
-    own = refs[2:7]
-    px, pc = refs[7:9]
-    tiles, corners = refs[9 : 9 + geo.sides], refs[9 + geo.sides :]
-    g, s = scal[0], scal[1]
-    near_y = pl.multiple_of(g * geo.H, 128)
-    far_y = pl.multiple_of((1 - g) * geo.H, 128)
-
-    def one(row, carry):
-        for k in range(5):
-            own[k][row, :, pl.ds(near_y, geo.H)] = near[k, row]
-            own[k][row, :, pl.ds(far_y, geo.H)] = far[k, row]
-        return carry
-
-    lax.fori_loop(0, geo.B, one, 0, unroll=2)
-    put_rows(list(zip(own, FIRST)), px, pc, 0, g, geo)
-    pack_tiles(list(zip(own, FIRST)), g, s, tiles, corners, geo)
-
-
-def put_rows(items, px, pc, start, g, geo):
-    for side, out in ((g, px), (1 - g, pc)):
-        at = start
-        for ref, depth in items:
-            for k in range(depth):
-                out[at] = ref[edge_rows(depth, side, geo) + k]
-                at += 1
-
-
-def coefficients(speed, aniso, angle):
-    stretch = 2.0 * aniso
-    sine_square, cosine_square, product = trig_products(angle)
-    cx = speed * (1.0 + stretch * cosine_square)
-    cz = speed * (1.0 + stretch * sine_square)
-    cy = speed * (1.0 + stretch)
-    return cx, cz, cy, (0.5 * speed) * (stretch * product), 2.0 - 2.0 * (cx + cz + cy)
-
-
-def coef_kernel(geo, scal, courant, aniso, tilt, *coefs):
-    def one(row):
-        for ref, value in zip(coefs, coefficients(courant[row], aniso[row], tilt[row])):
-            ref[row + 2, 0 : geo.Z, :] = value
-
-    each(0, geo.B, one, 2)
+        lax.fori_loop(a, b, widen, 0)
 
 
 def coef_halo(coefs, xr, cr, halo, g, s, geo):
@@ -362,10 +354,13 @@
     n = geo.sides
     now, before, xr, cr = refs[:4]
     halo = refs[4 : 4 + 3 * n]
-    out_block, prior_ext, *coefs = refs[9 + 3 * n : 16 + 3 * n]
-    out_tiles, out_corners = refs[16 + 3 * n : 16 + 4 * n], refs[16 + 4 * n : 16 + 5 * n]
-    ext, old, dif, tot = refs[16 + 5 * n :]
+    refl = refs[9 + 3 * n]
+    out_block, prior_ext, *coefs = refs[10 + 3 * n : 17 + 3 * n]
+    out_tiles, out_corners = refs[17 + 3 * n : 17 + 4 * n], refs[17 + 4 * n : 17 + 5 * n]
+    near_refl, ext, old, dif, tot, sem = refs[17 + 5 * n :]
     g, s = scal[0], scal[1]
+    copy = pltpu.make_async_copy(refl.at[:, pl.ds(pl.multiple_of(g * geo.B, TILE), geo.B)], near_refl, sem)
+    copy.start()
     coef_halo(coefs, xr, cr, halo, g, s, geo)
     fill(old, before, lambda k: xr[2 + k], lambda k: cr[2 + k], halo, FIRST, 1, g, s, geo)
     fill(ext, now, lambda k: xr[k], lambda k: cr[k], halo, FIRST, 0, g, s, geo)
@@ -375,6 +370,7 @@
 
     two_steps(ext, 1, lambda row: old[row], prior_ext, keep_block, coefs, dif, tot, geo)
     pack_tiles([(out_block, 2)], g, s, out_tiles, out_corners, geo)
+    copy.wait()
 
 
 def two_steps(ext, beyond, prior, mid, store, coefs, dif, tot, geo):
@@ -387,26 +383,33 @@
     advance(mid, off, geo.B, geo.B, geo.Z, lambda row: ext[row], None, store, coefs, dif, tot, geo)
 
 
-def second_kernel(geo, scal, offsets, *refs):
+def second_kernel(geo, scal, *refs):
     n = geo.sides
-    now, before, xr, cr, courant, refl, refl_far, *coefs = refs[:12]
-    halo = refs[12 : 12 + 3 * n]
-    px, pc, prior_ext, force = refs[12 + 3 * n : 16 + 3 * n]
-    out_tiles, out_corners = refs[16 + 3 * n : 16 + 4 * n], refs[16 + 4 * n : 16 + 5 * n]
-    ext, dif, tot = refs[16 + 5 * n :]
+    now, before, xr, cr, force, *coefs = refs[:10]
+    halo = refs[10 : 10 + 3 * n]
+    px, pc, prior_ext = refs[10 + 3 * n : 13 + 3 * n]
+    out_tiles, out_corners = refs[13 + 3 * n : 13 + 4 * n], refs[13 + 4 * n : 13 + 5 * n]
+    ext, dif, tot = refs[13 + 5 * n :]
     g, s = scal[0], scal[1]
     B = geo.B
-    fill_blocks(ext, xr, cr, g, geo)
-    fill(ext, now, None, None, halo, SECOND, 0, g, s, geo)
+    fill(ext, now, lambda k: xr[row_of(g, k, geo)], lambda k: cr[row_of(1 - g, k, geo)], halo, SECOND, 0, g, s, geo)
 
     def keep_block(row, value):
         px[row - B] = value
         pc[row - B] = value
 
     two_steps(ext, 1, lambda row: before[row - (B - 1)], prior_ext, keep_block, coefs, dif, tot, geo)
-    make_source(ext, refl, refl_far, offsets, courant, force, g, geo)
     put_rows([(force, THIRD[1])], px, pc, B, g, geo)
     pack_tiles([(px, THIRD[0]), (force, THIRD[1])], g, s, out_tiles, out_corners, geo)
+
+
+def row_of(side, k, geo):
+    return (1 - side) * (geo.B - 2) + k
+
+
+def source_only_kernel(geo, scal, offsets, now, xr, cr, courant, refl, refl_far, force, ext):
+    fill_blocks(ext, xr, cr, scal[0], geo, now)
+    make_source(ext, refl, refl_far, offsets, courant, force, scal[0], geo)
 
 
 def third_kernel(geo, scal, *refs):
@@ -418,10 +421,7 @@
     g, s = scal[0], scal[1]
     B = geo.B
 
-    def row_of(side, k):
-        return (1 - side) * (B - 2) + k
-
-    fill(ext, now, lambda k: xr[row_of(g, k)], lambda k: cr[row_of(1 - g, k)], halo, THIRD, 0, g, s, geo)
+    fill(ext, now, lambda k: xr[row_of(g, k, geo)], lambda k: cr[row_of(1 - g, k, geo)], halo, THIRD, 0, g, s, geo)
 
     def keep_block(row, value):
         block[row - B] = value
@@ -600,48 +600,51 @@
         n,
     )
     xr, cr, halo = exchange(px, pc, r0, r1)
-    (refl_far,) = call(
-        widen_kernel,
-        [scal, reflectivity],
-        [shape(NOFF, B, Z, H)],
+    *coefs, refl_far = call(
+        prepare_kernel,
+        [scal, *own[2:], reflectivity],
+        [shape(*wider)] * 5 + [shape(NOFF, B, Z, H)],
         [],
-        specs=[hbm],
+        specs=[whole] * 3 + [hbm],
         extra=[pltpu.VMEM((NOFF, B, Z, H), reflectivity.dtype), pltpu.SemaphoreType.DMA((4,))],
     )
     refl_far = chip(refl_far)
-    coefs = call(coef_kernel, [scal, *own[2:]], [shape(*wider)] * 5, [])
-    inputs = [scal, *own[:2], xr, cr, *halo, *coefs]
-    first = len(inputs) - 5
+    inputs = [scal, *own[:2], xr, cr, *halo, *coefs, reflectivity]
+    first = len(inputs) - 6
     now, prior, *coefs, r0, r1 = _split(
         call(
             first_kernel,
             inputs,
-            [shape(*block), shape(*wide)] + [shape(*wider)] * 5 + tile_outs(SECOND),
+            [shape(*block), shape(*wide)]
+            + [shape(*wider)] * 5
+            + tile_outs(SECOND)
+            + [jax.ShapeDtypeStruct((NOFF, B, Z, H), reflectivity.dtype)],
             [ext] * 4,
+            specs=[whole] * (len(inputs) - 2) + [hbm],
+            extra=[pltpu.SemaphoreType.DMA],
             aliases={first + k: 2 + k for k in range(5)},
         ),
         7,
         n,
     )
+    *r1, refl = r1
     courant_own = own[2]
     xr, cr, halo = exchange(now, now, r0, r1)
-    (refl,) = call(
-        own_refl_kernel,
-        [scal, reflectivity],
-        [jax.ShapeDtypeStruct((NOFF, B, Z, H), reflectivity.dtype)],
-        [],
-        specs=[hbm],
-        extra=[pltpu.SemaphoreType.DMA],
-    )
-    px, pc, prior, force, r0, r1 = _split(
+    (force,) = call(
+        source_only_kernel,
+        [scal, offsets, now, xr, cr, courant_own, refl, refl_far],
+        [shape(*block)],
+        [ext],
+        2,
+    )
+    px, pc, prior, r0, r1 = _split(
         call(
             second_kernel,
-            [scal, offsets, now, prior, xr, cr, courant_own, refl, refl_far, *coefs, *halo],
-            [shape(B + THIRD[1], Z, Y)] * 2 + [shape(*wide), shape(*block)] + tile_outs(THIRD),
+            [scal, now, prior, xr, cr, force, *coefs, *halo],
+            [shape(B + THIRD[1], Z, Y)] * 2 + [shape(*wide)] + tile_outs(THIRD),
             [ext] * 3,
-            2,
         ),
-        4,
+        3,
         n,
     )
     xr, cr, halo = exchange(px, pc, r0, r1)

time: 110 us -> 104 us (0.945)
  waiting for transfers between devices: 22.7 us -> 18.7 us
  Pallas kernels: 34.2 us -> 31.5 us
  starting transfers between devices: 51.3 us -> 52.5 us
    ppermute x13, waiting for transfers between devices: 6.03 us -> 2.12 us  [chip(): return lax.ppermute(value, 'gy', swap)]
    pallas_call x15 -> x14, Pallas kernels: 34.2 us -> 31.5 us  [call(): pl.pallas_call(functools.partial(kernel, geo), out_shape=outs, grid_spec=...]
    ppermute x13, starting transfers between devices: 37.7 us -> 40.2 us  [chip(): return lax.ppermute(value, 'gy', swap)]
    ppermute x4, starting transfers between devices: 7.45 us -> 6.29 us  [exchange(): zr = [lax.ppermute(t, 'section', m) for t, m in zip(tiles, z_moves())]]
  transfers between devices with their start and end apart: 26 -> 26, of which waited for: 6 -> 7; matrix products, arithmetic and copies ran while one was open for 0% -> 0% of each run, Pallas kernels for 20% -> 17%
where the time goes in v6:
time: 104 us
  starting transfers between devices  52.5 us (50%)
  Pallas kernels  31.5 us (30%)
  waiting for transfers between devices  18.7 us (18%)
    ppermute x13, starting transfers between devices, chip(): return lax.ppermute(value, 'gy', swap)  40.2 us
    pallas_call x14, Pallas kernels, call(): pl.pallas_call(functools.partial(kernel, geo), out_shape=outs, grid_spec=...  31.5 us
    ppermute x4, waiting for transfers between devices, exchange(): zr = [lax.ppermute(t, 'section', m) for t, m in zip(tiles, z_moves())]  16.5 us
    ppermute x4, starting transfers between devices, exchange(): zr = [lax.ppermute(t, 'section', m) for t, m in zip(tiles, z_moves())]  6.29 us
    ppermute x4, starting transfers between devices, exchange(): xr = lax.ppermute(px, ('gx', 'gy'), pairs_x)  2.7 us
    ppermute x4, starting transfers between devices, exchange(): lax.ppermute(t, ('gx', 'section', 'gy'), corner_pairs(m))  2.61 us
    ppermute x13, waiting for transfers between devices, chip(): return lax.ppermute(value, 'gy', swap)  2.12 us
  transfers between devices with their start and end apart: 26, of which 7 were waited for; matrix products, arithmetic and copies ran while one was open for 0% of the time, Pallas kernels for 17%

profile of v6, /device:TPU:0, one launch (start us, length us, event | category | flops | bytes accessed | tf_op | source)
XLA Modules:
  0.0 103.6 jit_solution(12838491033919240351)
XLA Ops:
  0.6 0.1 pad_add_fusion.scal
  0.7 1.9 %shard_map.87 = f32[5,16,16,256]{3,2,1,0:T(8,128)S(1)} custom-call(s32[2]{0:T(128)S(1)} %pad_add_fusion.scal, f32[32,16,256]{2,1,0:T(8,128)} %refs_0_.3, f32[32,16,256]{2,1,0:T(8,128)} %refs_1_.3, f32[32,16,256]{2,1,0:T(8,128)} %refs_2_.3, f32[32,16,256]{2,1,0:T(8,128)} %refs_3_.3, f32[32,16,256]{2,1,0:T(8,128)} %refs_4_.3), custom_call_target="tpu_custom_call" | custom-call | tf_op jit(solution)/shard_map/pallas_call | solution.py:559
  2.6 0.6 collective-permute-start
  3.1 1.9 %shard_map.86.refs_0_ = f32[5,16,16,256]{3,2,1,0:T(8,128)S(1)} custom-call(s32[2]{0:T(128)S(1)} %pad_add_fusion.scal, f32[32,16,256]{2,1,0:T(8,128)} %refs_0_.3, f32[32,16,256]{2,1,0:T(8,128)} %refs_1_.3, f32[32,16,256]{2,1,0:T(8,128)} %refs_2_.3, f32[32,16,256]{2,1,0:T(8,128)} %refs_3_.3, f32[32,16,256]{2,1,0:T(8,128)} %refs_4_.3), custom_call_target="tpu_custom_call" | custom-call | tf_op jit(solution)/shard_map/pallas_call | solution.py:559
  5.0 0.8 collective-permute-done.refs_1_
  5.8 0.9 shard_map.88
  6.7 2.2 %shard_map.89 = (f32[20,24,512]{2,1,0:T(8,128)S(1)}, f32[20,24,512]{2,1,0:T(8,128)S(1)}, f32[20,24,512]{2,1,0:T(8,128)S(1)}, f32[20,24,512]{2,1,0:T(8,128)S(1)},...) custom-call(s32[2]{0:T(128)S(1)} %pad_add_fusion.scal, ...), custom_call_target="tpu_custom_call" | custom-call | tf_op jit(solution)/shard_map/pallas_call | solution.py:559
  8.9 0.4 collective-permute-start.8
  9.3 2.6 %collective-permute-start.3 = (f32[18,8,512]{2,1,0:T(8,128)S(1)}, f32[18,8,512]{2,1,0:T(8,128)S(1)}, u32[]{:S(2)}, u32[]{:S(2)}) collective-permute-start(f32[18,8,512]{2,1,0:T(8,128)S(1)} %get-tuple-element.49), channel_id=1, source_target_pairs={{0,2},{2,0},{1,3},{3,1},{4,6},{6,4},{5,7},{7,5},{8,10},{10,8},{9,1... | collective-permute-start | bytes 884744 | tf_op jit(solution)/shard_map/ppermute | solution.py:546
  11.9 0.7 collective-permute-start.1
  12.6 3.0 %collective-permute-start.2 = (f32[9,16,512]{2,1,0:T(8,128)S(1)}, f32[9,16,512]{2,1,0:T(8,128)S(1)}, u32[]{:S(2)}, u32[]{:S(2)}) collective-permute-start(f32[9,16,512]{2,1,0:T(8,128)S(1)} %get-tuple-element.48), channel_id=1, source_target_pairs={{0,1},{1,0},{2,3},{3,2},{4,5},{5,4},{6,7},{7,6},{8,9},{9,8},{10,11... | collective-permute-start | bytes 884744 | tf_op jit(solution)/shard_map/ppermute | solution.py:539
  15.6 3.9 %collective-permute-done.3.refs_4_ = f32[18,8,512]{2,1,0:T(8,128)S(1)} collective-permute-done((f32[18,8,512]{2,1,0:T(8,128)S(1)}, f32[18,8,512]{2,1,0:T(8,128)S(1)}, u32[]{:S(2)}, u32[]{:S(2)}) %collective-permute-start.3) | collective-permute-done | bytes 294944 | tf_op jit(solution)/shard_map/ppermute | solution.py:546
  19.5 0.0 collective-permute-start.5
  19.5 0.7 collective-permute-start.4
  20.2 0.9 collective-permute-done.5.refs_6_
  21.0 3.0 %shard_map.90 = (f32[16,16,512]{2,1,0:T(8,128)S(1)}, f32[18,24,512]{2,1,0:T(8,128)S(1)}, f32[20,24,512]{2,1,0:T(8,128)S(1)}, f32[20,24,512]{2,1,0:T(8,128)S(1)},...) custom-call(s32[2]{0:T(128)S(1)} %pad_add_fusion.scal, ...), custom_call_target="tpu_custom_call", output_to_operand_aliasing={{2}: (8, {}), {3}: (9, {}), {4}: (10, {}), {5}: (11, {}), {... | custom-call | tf_op jit(solution)/shard_map/pallas_call | solution.py:559
  24.1 5.3 %collective-permute-start.7 = (f32[16,16,512]{2,1,0:T(8,128)S(1)}, f32[16,16,512]{2,1,0:T(8,128)S(1)}, u32[]{:S(2)}, u32[]{:S(2)}) collective-permute-start(f32[16,16,512]{2,1,0:T(8,128)S(1)} %get-tuple-element.59.now.refs_0_), channel_id=1, source_target_pairs={{0,1},{1,0},{2,3},{3,2},{4,5},{5,4},{6,7},{7,6},{8,9},{9,8},{10,11... | collective-permute-start | bytes 1572872 | tf_op jit(solution)/shard_map/ppermute | solution.py:539
  29.4 0.7 collective-permute-start.6
  30.1 1.8 %collective-permute-start.9 = (f32[4,8,512]{2,1,0:T(8,128)S(1)}, f32[4,8,512]{2,1,0:T(8,128)S(1)}, u32[]{:S(2)}, u32[]{:S(2)}) collective-permute-start(f32[4,8,512]{2,1,0:T(8,128)S(1)} %get-tuple-element.68), channel_id=1, source_target_pairs={{0,2},{2,0},{1,3},{3,1},{4,6},{6,4},{5,7},{7,5},{8,10},{10,8},{9,1... | collective-permute-start | bytes 196616 | tf_op jit(solution)/shard_map/ppermute | solution.py:546
  31.9 2.5 %collective-permute-done.9.refs_10_ = f32[4,8,512]{2,1,0:T(8,128)S(1)} collective-permute-done((f32[4,8,512]{2,1,0:T(8,128)S(1)}, f32[4,8,512]{2,1,0:T(8,128)S(1)}, u32[]{:S(2)}, u32[]{:S(2)}) %collective-permute-start.9) | collective-permute-done | bytes 65568 | tf_op jit(solution)/shard_map/ppermute | solution.py:546
  34.4 2.0 %collective-permute-start.11 = (f32[4,8,512]{2,1,0:T(8,128)S(1)}, f32[4,8,512]{2,1,0:T(8,128)S(1)}, u32[]{:S(2)}, u32[]{:S(2)}) collective-permute-start(f32[4,8,512]{2,1,0:T(8,128)S(1)} %collective-permute-done.9.refs_10_), channel_id=1, source_target_pairs={{0,1},{1,0},{2,3},{3,2},{4,5},{5,4},{6,7},{7,6},{8,9},{9,8},{10,11... | collective-permute-start | bytes 196616 | tf_op jit(solution)/shard_map/ppermute | solution.py:539
  36.5 0.7 collective-permute-start.10
  37.2 2.4 %shard_map.91.refs_4_.refs_11_ = f32[16,16,512]{2,1,0:T(8,128)S(1)} custom-call(s32[2]{0:T(128)S(1)} %pad_add_fusion.scal, s32[17]{0:T(128)S(1)} %copy-done, f32[16,16,512]{2,1,0:T(8,128)S(1)} %get-tuple-element.59.now.refs_0_, f32[16,16,512]{2,1,0:T(8,128)S(1)} %collective-permute-done.6.xr.refs_2_, f32[16,16,512]{2,1,0:T(8,128)S(1)} %collective-permute-done.7.cr.refs_3_, ...), custom_call_target="tpu_custom_call" | custom-call | tf_op jit(solution)/shard_map/pallas_call | solution.py:559
  39.6 2.4 %shard_map.92 = (f32[19,16,512]{2,1,0:T(8,128)S(1)}, f32[19,16,512]{2,1,0:T(8,128)S(1)}, f32[18,24,512]{2,1,0:T(8,128)S(1)}, f32[12,8,512]{2,1,0:T(8,128)S(1)}, f32[3,8,512]{2,1,0:T(8,128)S(1)}) custom-call(s32[2]{0:T(128)S(1)} %pad_add_fusion.scal, f32[16,16,512]{2,1,0:T(8,128)S(1)} %get-tuple-element.59.now.refs_0_, ...), custom_call_target="tpu_custom_call" | custom-call | tf_op jit(solution)/shard_map/pallas_call | solution.py:559
  42.0 4.3 %collective-permute-start.13 = (f32[19,16,512]{2,1,0:T(8,128)S(1)}, f32[19,16,512]{2,1,0:T(8,128)S(1)}, u32[]{:S(2)}, u32[]{:S(2)}) collective-permute-start(f32[19,16,512]{2,1,0:T(8,128)S(1)} %get-tuple-element.72), channel_id=1, source_target_pairs={{0,1},{1,0},{2,3},{3,2},{4,5},{5,4},{6,7},{7,6},{8,9},{9,8},{10,11... | collective-permute-start | bytes 1867784 | tf_op jit(solution)/shard_map/ppermute | solution.py:539
  46.3 0.7 collective-permute-start.12
  47.0 0.5 collective-permute-start.14
  47.5 5.4 %collective-permute-done.14.refs_9_.refs_12_ = f32[12,8,512]{2,1,0:T(8,128)S(1)} collective-permute-done((f32[12,8,512]{2,1,0:T(8,128)S(1)}, f32[12,8,512]{2,1,0:T(8,128)S(1)}, u32[]{:S(2)}, u32[]{:S(2)}) %collective-permute-start.14) | collective-permute-done | bytes 196640 | tf_op jit(solution)/shard_map/ppermute | solution.py:546
  52.9 1.8 %collective-permute-start.16 = (f32[12,8,512]{2,1,0:T(8,128)S(1)}, f32[12,8,512]{2,1,0:T(8,128)S(1)}, u32[]{:S(2)}, u32[]{:S(2)}) collective-permute-start(f32[12,8,512]{2,1,0:T(8,128)S(1)} %collective-permute-done.14.refs_9_.refs_12_), channel_id=1, source_target_pairs={{0,1},{1,0},{2,3},{3,2},{4,5},{5,4},{6,7},{7,6},{8,9},{9,8},{10,11... | collective-permute-start | bytes 589832 | tf_op jit(solution)/shard_map/ppermute | solution.py:539
  54.7 0.7 collective-permute-start.15
  55.3 0.4 collective-permute-done.16.refs_11_.refs_14_
  55.7 2.3 %shard_map.93 = (f32[16,16,512]{2,1,0:T(8,128)S(1)}, f32[16,16,256]{2,1,0:T(8,128)S(1)}, f32[16,16,256]{2,1,0:T(8,128)S(1)}) custom-call(s32[2]{0:T(128)S(1)} %pad_add_fusion.scal, f32[19,16,512]{2,1,0:T(8,128)S(1)} %get-tuple-element.70.refs_0_, f32[18,24,512]{2,1,0:T(8,128)S(1)} %get-tuple-element.71.refs_1_, ...), custom_call_target="tpu_custom_call" | custom-call | tf_op jit(solution)/shard_map/pallas_call | solution.py:559
  58.1 5.9 %collective-permute-start.19 = (f32[16,16,512]{2,1,0:T(8,128)S(1)}, f32[16,16,512]{2,1,0:T(8,128)S(1)}, u32[]{:S(2)}, u32[]{:S(2)}) collective-permute-start(f32[16,16,512]{2,1,0:T(8,128)S(1)} %get-tuple-element.80.refs_0_), channel_id=1, source_target_pairs={{0,1},{1,0},{2,3},{3,2},{4,5},{5,4},{6,7},{7,6},{8,9},{9,8},{10,11... | collective-permute-start | bytes 1572872 | tf_op jit(solution)/shard_map/ppermute | solution.py:539
  63.9 0.7 collective-permute-start.18
  64.6 4.3 %shard_map.95 = (f32[16,16,512]{2,1,0:T(8,128)S(1)}, f32[16,16,512]{2,1,0:T(8,128)S(1)}, f32[20,24,512]{2,1,0:T(8,128)S(1)}) custom-call(s32[2]{0:T(128)S(1)} %pad_add_fusion.scal, s32[17]{0:T(128)S(1)} %copy-done, f32[19,16,512]{2,1,0:T(8,128)S(1)} %get-tuple-element.70.refs_0_, f32[19,16,512]{2,1,0:T(8,128)S(1)} %collective-permute-done.12.refs_2_.refs_1_, ...), custom_call_target="tpu_custom_call" | custom-call | tf_op jit(solution)/shard_map/pallas_call | solution.py:559
  69.0 2.5 %shard_map.96 = (f32[16,16,512]{2,1,0:T(8,128)S(1)}, f32[6,16,512]{2,1,0:T(8,128)S(1)}, f32[6,16,512]{2,1,0:T(8,128)S(1)}, f32[14,8,512]{2,1,0:T(8,128)S(1)}, f32[3,8,512]{2,1,0:T(8,128)S(1)}) custom-call(s32[2]{0:T(128)S(1)} %pad_add_fusion.scal, s32[17]{0:T(128)S(1)} %copy-done, f32[16,16,512]{2,1,0:T(8,128)S(1)} %get-tuple-element.80.refs_0_, ...), custom_call_target="tpu_custom_call" | custom-call | tf_op jit(solution)/shard_map/pallas_call | solution.py:559
  71.5 1.3 %collective-permute-start.22 = (f32[14,8,512]{2,1,0:T(8,128)S(1)}, f32[14,8,512]{2,1,0:T(8,128)S(1)}, u32[]{:S(2)}, u32[]{:S(2)}) collective-permute-start(f32[14,8,512]{2,1,0:T(8,128)S(1)} %get-tuple-element.84), channel_id=1, source_target_pairs={{0,2},{2,0},{1,3},{3,1},{4,6},{6,4},{5,7},{7,5},{8,10},{10,8},{9,1... | collective-permute-start | bytes 688136 | tf_op jit(solution)/shard_map/ppermute | solution.py:546
  72.8 4.8 %collective-permute-done.22.refs_11_ = f32[14,8,512]{2,1,0:T(8,128)S(1)} collective-permute-done((f32[14,8,512]{2,1,0:T(8,128)S(1)}, f32[14,8,512]{2,1,0:T(8,128)S(1)}, u32[]{:S(2)}, u32[]{:S(2)}) %collective-permute-start.22) | collective-permute-done | bytes 229408 | tf_op jit(solution)/shard_map/ppermute | solution.py:546
  77.6 5.8 %collective-permute-start.24 = (f32[14,8,512]{2,1,0:T(8,128)S(1)}, f32[14,8,512]{2,1,0:T(8,128)S(1)}, u32[]{:S(2)}, u32[]{:S(2)}) collective-permute-start(f32[14,8,512]{2,1,0:T(8,128)S(1)} %collective-permute-done.22.refs_11_), channel_id=1, source_target_pairs={{0,1},{1,0},{2,3},{3,2},{4,5},{5,4},{6,7},{7,6},{8,9},{9,8},{10,11... | collective-permute-start | bytes 688136 | tf_op jit(solution)/shard_map/ppermute | solution.py:539
  83.4 0.7 collective-permute-start.20
  84.0 5.5 %collective-permute-start.21 = (f32[6,16,512]{2,1,0:T(8,128)S(1)}, f32[6,16,512]{2,1,0:T(8,128)S(1)}, u32[]{:S(2)}, u32[]{:S(2)}) collective-permute-start(f32[6,16,512]{2,1,0:T(8,128)S(1)} %get-tuple-element.83), channel_id=1, source_target_pairs={{0,1},{1,0},{2,3},{3,2},{4,5},{5,4},{6,7},{7,6},{8,9},{9,8},{10,11... | collective-permute-start | bytes 589832 | tf_op jit(solution)/shard_map/ppermute | solution.py:539
  89.5 0.7 collective-permute-start.23
  90.2 3.1 %collective-permute-start.17 = (f32[16,16,256]{2,1,0:T(8,128)S(1)}, f32[16,16,256]{2,1,0:T(8,128)S(1)}, u32[]{:S(2)}, u32[]{:S(2)}) collective-permute-start(f32[16,16,256]{2,1,0:T(8,128)S(1)} %get-tuple-element.76), channel_id=1, source_target_pairs={{0,1},{1,0},{2,3},{3,2},{4,5},{5,4},{6,7},{7,6},{8,9},{9,8},{10,11... | collective-permute-start | bytes 786440 | tf_op jit(solution)/shard_map/ppermute | solution.py:539
  93.3 3.7 %shard_map.97 = (f32[16,16,256]{2,1,0:T(8,128)S(1)}, f32[16,16,256]{2,1,0:T(8,128)S(1)}) custom-call(s32[2]{0:T(128)S(1)} %pad_add_fusion.scal, f32[16,16,512]{2,1,0:T(8,128)S(1)} %get-tuple-element.77.refs_6_.refs_0_, f32[20,24,512]{2,1,0:T(8,128)S(1)} %get-tuple-element.78.refs_1_, f32[16,16,512]{2,1,0:T(8,128)S(1)} %get-tuple-element.79.refs_7_.refs_2_, ...), custom_call_target="tpu_custom_call" | custom-call | tf_op jit(solution)/shard_map/pallas_call | solution.py:559
  97.0 2.6 %collective-permute-start.25 = (f32[16,16,256]{2,1,0:T(8,128)S(1)}, f32[16,16,256]{2,1,0:T(8,128)S(1)}, u32[]{:S(2)}, u32[]{:S(2)}) collective-permute-start(f32[16,16,256]{2,1,0:T(8,128)S(1)} %get-tuple-element.86), channel_id=1, source_target_pairs={{0,1},{1,0},{2,3},{3,2},{4,5},{5,4},{6,7},{7,6},{8,9},{9,8},{10,11... | collective-permute-start | bytes 786440 | tf_op jit(solution)/shard_map/ppermute | solution.py:539
  99.7 1.4 %shard_map.94 = f32[32,16,256]{2,1,0:T(8,128)} custom-call(s32[2]{0:T(128)S(1)} %pad_add_fusion.scal, f32[16,16,256]{2,1,0:T(8,128)S(1)} %get-tuple-element.75.near, f32[16,16,256]{2,1,0:T(8,128)S(1)} %collective-permute-done.17.far), custom_call_target="tpu_custom_call" | custom-call | tf_op jit(solution)/shard_map/pallas_call | solution.py:559
  101.1 1.3 %shard_map.98.refs_1_ = f32[32,16,256]{2,1,0:T(8,128)} custom-call(s32[2]{0:T(128)S(1)} %pad_add_fusion.scal, f32[16,16,256]{2,1,0:T(8,128)S(1)} %get-tuple-element.87.refs_0_), custom_call_target="tpu_custom_call" | custom-call | tf_op jit(solution)/shard_map/pallas_call | solution.py:559
  102.3 1.3 %shard_map.99 = f32[32,16,256]{2,1,0:T(8,128)} custom-call(s32[2]{0:T(128)S(1)} %pad_add_fusion.scal, f32[16,16,256]{2,1,0:T(8,128)S(1)} %collective-permute-done.25.refs_0_, f32[32,16,256]{2,1,0:T(8,128)} %shard_map.98.refs_1_), custom_call_target="tpu_custom_call", output_to_operand_aliasing={{}: (2, {})} | custom-call | tf_op jit(solution)/shard_map/pallas_call | solution.py:559
  (21 shorter events, 0.1 us)
Async XLA Ops:
  2.6 3.2 %collective-permute-start = (f32[5,16,16,256]{3,2,1,0:T(8,128)S(1)}, f32[5,16,16,256]{3,2,1,0:T(8,128)S(1)}, u32[]{:S(2)}, u32[]{:S(2)}) collective-permute-start(f32[5,16,16,256]{3,2,1,0:T(8,128)S(1)} %shard_map.87), channel_id=1, source_target_pairs={{0,1},{1,0},{2,3},{3,2},{4,5},{5,4},{6,7},{7,6},{8,9},{9,8},{10,11... | collective-permute-start | bytes 3932168 | tf_op jit(solution)/shard_map/ppermute | solution.py:539
  8.9 28.3 %collective-permute-start.8 = (f32[17,16,16,256]{3,2,1,0:T(8,128)S(1)}, f32[17,16,16,256]{3,2,1,0:T(8,128)S(1)}, u32[]{:S(2)}, u32[]{:S(2)}) collective-permute-start(f32[17,16,16,256]{3,2,1,0:T(8,128)S(1)} %get-tuple-element.62), channel_id=1, source_target_pairs={{0,1},{1,0},{2,3},{3,2},{4,5},{5,4},{6,7},{7,6},{8,9},{9,8},{10,11... | collective-permute-start | bytes 13369352 | tf_op jit(solution)/shard_map/ppermute | solution.py:539
  9.3 10.2 %collective-permute-start.3 = (f32[18,8,512]{2,1,0:T(8,128)S(1)}, f32[18,8,512]{2,1,0:T(8,128)S(1)}, u32[]{:S(2)}, u32[]{:S(2)}) collective-permute-start(f32[18,8,512]{2,1,0:T(8,128)S(1)} %get-tuple-element.49), channel_id=1, source_target_pairs={{0,2},{2,0},{1,3},{3,1},{4,6},{6,4},{5,7},{7,5},{8,10},{10,8},{9,1... | collective-permute-start | bytes 884744 | tf_op jit(solution)/shard_map/ppermute | solution.py:546
  11.9 8.2 %collective-permute-start.1 = (f32[9,16,512]{2,1,0:T(8,128)S(1)}, f32[9,16,512]{2,1,0:T(8,128)S(1)}, u32[]{:S(2)}, u32[]{:S(2)}) collective-permute-start(f32[9,16,512]{2,1,0:T(8,128)S(1)} %get-tuple-element.47), channel_id=1, source_target_pairs={{1,4},{4,1},{5,8},{8,5},{9,12},{12,9},{3,6},{6,3},{7,10},{10,7},{1... | collective-permute-start | bytes 884744 | tf_op jit(solution)/shard_map/ppermute | solution.py:542
  12.6 7.6 %collective-permute-start.2 = (f32[9,16,512]{2,1,0:T(8,128)S(1)}, f32[9,16,512]{2,1,0:T(8,128)S(1)}, u32[]{:S(2)}, u32[]{:S(2)}) collective-permute-start(f32[9,16,512]{2,1,0:T(8,128)S(1)} %get-tuple-element.48), channel_id=1, source_target_pairs={{0,1},{1,0},{2,3},{3,2},{4,5},{5,4},{6,7},{7,6},{8,9},{9,8},{10,11... | collective-permute-start | bytes 884744 | tf_op jit(solution)/shard_map/ppermute | solution.py:539
  19.5 1.6 %collective-permute-start.5 = (f32[18,8,512]{2,1,0:T(8,128)S(1)}, f32[18,8,512]{2,1,0:T(8,128)S(1)}, u32[]{:S(2)}, u32[]{:S(2)}) collective-permute-start(f32[18,8,512]{2,1,0:T(8,128)S(1)} %collective-permute-done.3.refs_4_), channel_id=1, source_target_pairs={{0,1},{1,0},{2,3},{3,2},{4,5},{5,4},{6,7},{7,6},{8,9},{9,8},{10,11... | collective-permute-start | bytes 884744 | tf_op jit(solution)/shard_map/ppermute | solution.py:539
  19.5 0.7 collective-permute-start.4
  21.0 16.1 %copy-start = (s32[17]{0:T(128)S(1)}, s32[17]{0:T(128)}, u32[]{:S(2)}) copy-start(s32[17]{0:T(128)} %offsets.5) | copy-start | bytes 208
  24.1 13.0 %collective-permute-start.7 = (f32[16,16,512]{2,1,0:T(8,128)S(1)}, f32[16,16,512]{2,1,0:T(8,128)S(1)}, u32[]{:S(2)}, u32[]{:S(2)}) collective-permute-start(f32[16,16,512]{2,1,0:T(8,128)S(1)} %get-tuple-element.59.now.refs_0_), channel_id=1, source_target_pairs={{0,1},{1,0},{2,3},{3,2},{4,5},{5,4},{6,7},{7,6},{8,9},{9,8},{10,11... | collective-permute-start | bytes 1572872 | tf_op jit(solution)/shard_map/ppermute | solution.py:539
  29.4 7.7 %collective-permute-start.6 = (f32[16,16,512]{2,1,0:T(8,128)S(1)}, f32[16,16,512]{2,1,0:T(8,128)S(1)}, u32[]{:S(2)}, u32[]{:S(2)}) collective-permute-start(f32[16,16,512]{2,1,0:T(8,128)S(1)} %get-tuple-element.59.now.refs_0_), channel_id=1, source_target_pairs={{1,4},{4,1},{5,8},{8,5},{9,12},{12,9},{3,6},{6,3},{7,10},{10,7},{1... | collective-permute-start | bytes 1572872 | tf_op jit(solution)/shard_map/ppermute | solution.py:542
  30.1 4.3 %collective-permute-start.9 = (f32[4,8,512]{2,1,0:T(8,128)S(1)}, f32[4,8,512]{2,1,0:T(8,128)S(1)}, u32[]{:S(2)}, u32[]{:S(2)}) collective-permute-start(f32[4,8,512]{2,1,0:T(8,128)S(1)} %get-tuple-element.68), channel_id=1, source_target_pairs={{0,2},{2,0},{1,3},{3,1},{4,6},{6,4},{5,7},{7,5},{8,10},{10,8},{9,1... | collective-permute-start | bytes 196616 | tf_op jit(solution)/shard_map/ppermute | solution.py:546
  34.4 5.2 %collective-permute-start.11 = (f32[4,8,512]{2,1,0:T(8,128)S(1)}, f32[4,8,512]{2,1,0:T(8,128)S(1)}, u32[]{:S(2)}, u32[]{:S(2)}) collective-permute-start(f32[4,8,512]{2,1,0:T(8,128)S(1)} %collective-permute-done.9.refs_10_), channel_id=1, source_target_pairs={{0,1},{1,0},{2,3},{3,2},{4,5},{5,4},{6,7},{7,6},{8,9},{9,8},{10,11... | collective-permute-start | bytes 196616 | tf_op jit(solution)/shard_map/ppermute | solution.py:539
  36.5 3.1 %collective-permute-start.10 = (f32[1,8,512]{2,1,0:T(8,128)S(1)}, f32[1,8,512]{2,1,0:T(8,128)S(1)}, u32[]{:S(2)}, u32[]{:S(2)}) collective-permute-start(f32[1,8,512]{2,1,0:T(8,128)S(1)} %get-tuple-element.69), channel_id=1, source_target_pairs={{1,6},{3,4},{4,3},{6,1},{5,10},{7,8},{8,7},{10,5},{9,14},{11,12},{... | collective-permute-start | bytes 49160 | tf_op jit(solution)/shard_map/ppermute | solution.py:544
  42.0 13.7 %collective-permute-start.13 = (f32[19,16,512]{2,1,0:T(8,128)S(1)}, f32[19,16,512]{2,1,0:T(8,128)S(1)}, u32[]{:S(2)}, u32[]{:S(2)}) collective-permute-start(f32[19,16,512]{2,1,0:T(8,128)S(1)} %get-tuple-element.72), channel_id=1, source_target_pairs={{0,1},{1,0},{2,3},{3,2},{4,5},{5,4},{6,7},{7,6},{8,9},{9,8},{10,11... | collective-permute-start | bytes 1867784 | tf_op jit(solution)/shard_map/ppermute | solution.py:539
  46.3 9.4 %collective-permute-start.12 = (f32[19,16,512]{2,1,0:T(8,128)S(1)}, f32[19,16,512]{2,1,0:T(8,128)S(1)}, u32[]{:S(2)}, u32[]{:S(2)}) collective-permute-start(f32[19,16,512]{2,1,0:T(8,128)S(1)} %get-tuple-element.70.refs_0_), channel_id=1, source_target_pairs={{1,4},{4,1},{5,8},{8,5},{9,12},{12,9},{3,6},{6,3},{7,10},{10,7},{1... | collective-permute-start | bytes 1867784 | tf_op jit(solution)/shard_map/ppermute | solution.py:542
  47.0 5.9 %collective-permute-start.14 = (f32[12,8,512]{2,1,0:T(8,128)S(1)}, f32[12,8,512]{2,1,0:T(8,128)S(1)}, u32[]{:S(2)}, u32[]{:S(2)}) collective-permute-start(f32[12,8,512]{2,1,0:T(8,128)S(1)} %get-tuple-element.73), channel_id=1, source_target_pairs={{0,2},{2,0},{1,3},{3,1},{4,6},{6,4},{5,7},{7,5},{8,10},{10,8},{9,1... | collective-permute-start | bytes 589832 | tf_op jit(solution)/shard_map/ppermute | solution.py:546
  52.9 2.8 %collective-permute-start.16 = (f32[12,8,512]{2,1,0:T(8,128)S(1)}, f32[12,8,512]{2,1,0:T(8,128)S(1)}, u32[]{:S(2)}, u32[]{:S(2)}) collective-permute-start(f32[12,8,512]{2,1,0:T(8,128)S(1)} %collective-permute-done.14.refs_9_.refs_12_), channel_id=1, source_target_pairs={{0,1},{1,0},{2,3},{3,2},{4,5},{5,4},{6,7},{7,6},{8,9},{9,8},{10,11... | collective-permute-start | bytes 589832 | tf_op jit(solution)/shard_map/ppermute | solution.py:539
  54.7 0.7 collective-permute-start.15
  58.1 10.9 %collective-permute-start.19 = (f32[16,16,512]{2,1,0:T(8,128)S(1)}, f32[16,16,512]{2,1,0:T(8,128)S(1)}, u32[]{:S(2)}, u32[]{:S(2)}) collective-permute-start(f32[16,16,512]{2,1,0:T(8,128)S(1)} %get-tuple-element.80.refs_0_), channel_id=1, source_target_pairs={{0,1},{1,0},{2,3},{3,2},{4,5},{5,4},{6,7},{7,6},{8,9},{9,8},{10,11... | collective-permute-start | bytes 1572872 | tf_op jit(solution)/shard_map/ppermute | solution.py:539
  63.9 5.1 %collective-permute-start.18 = (f32[16,16,512]{2,1,0:T(8,128)S(1)}, f32[16,16,512]{2,1,0:T(8,128)S(1)}, u32[]{:S(2)}, u32[]{:S(2)}) collective-permute-start(f32[16,16,512]{2,1,0:T(8,128)S(1)} %get-tuple-element.80.refs_0_), channel_id=1, source_target_pairs={{1,4},{4,1},{5,8},{8,5},{9,12},{12,9},{3,6},{6,3},{7,10},{10,7},{1... | collective-permute-start | bytes 1572872 | tf_op jit(solution)/shard_map/ppermute | solution.py:654
  71.5 6.1 %collective-permute-start.22 = (f32[14,8,512]{2,1,0:T(8,128)S(1)}, f32[14,8,512]{2,1,0:T(8,128)S(1)}, u32[]{:S(2)}, u32[]{:S(2)}) collective-permute-start(f32[14,8,512]{2,1,0:T(8,128)S(1)} %get-tuple-element.84), channel_id=1, source_target_pairs={{0,2},{2,0},{1,3},{3,1},{4,6},{6,4},{5,7},{7,5},{8,10},{10,8},{9,1... | collective-permute-start | bytes 688136 | tf_op jit(solution)/shard_map/ppermute | solution.py:546
  77.6 15.7 %collective-permute-start.24 = (f32[14,8,512]{2,1,0:T(8,128)S(1)}, f32[14,8,512]{2,1,0:T(8,128)S(1)}, u32[]{:S(2)}, u32[]{:S(2)}) collective-permute-start(f32[14,8,512]{2,1,0:T(8,128)S(1)} %collective-permute-done.22.refs_11_), channel_id=1, source_target_pairs={{0,1},{1,0},{2,3},{3,2},{4,5},{5,4},{6,7},{7,6},{8,9},{9,8},{10,11... | collective-permute-start | bytes 688136 | tf_op jit(solution)/shard_map/ppermute | solution.py:539
  83.4 9.9 %collective-permute-start.20 = (f32[6,16,512]{2,1,0:T(8,128)S(1)}, f32[6,16,512]{2,1,0:T(8,128)S(1)}, u32[]{:S(2)}, u32[]{:S(2)}) collective-permute-start(f32[6,16,512]{2,1,0:T(8,128)S(1)} %get-tuple-element.82), channel_id=1, source_target_pairs={{1,4},{4,1},{5,8},{8,5},{9,12},{12,9},{3,6},{6,3},{7,10},{10,7},{1... | collective-permute-start | bytes 589832 | tf_op jit(solution)/shard_map/ppermute | solution.py:542
  84.0 9.2 %collective-permute-start.21 = (f32[6,16,512]{2,1,0:T(8,128)S(1)}, f32[6,16,512]{2,1,0:T(8,128)S(1)}, u32[]{:S(2)}, u32[]{:S(2)}) collective-permute-start(f32[6,16,512]{2,1,0:T(8,128)S(1)} %get-tuple-element.83), channel_id=1, source_target_pairs={{0,1},{1,0},{2,3},{3,2},{4,5},{5,4},{6,7},{7,6},{8,9},{9,8},{10,11... | collective-permute-start | bytes 589832 | tf_op jit(solution)/shard_map/ppermute | solution.py:539
  89.5 3.7 %collective-permute-start.23 = (f32[3,8,512]{2,1,0:T(8,128)S(1)}, f32[3,8,512]{2,1,0:T(8,128)S(1)}, u32[]{:S(2)}, u32[]{:S(2)}) collective-permute-start(f32[3,8,512]{2,1,0:T(8,128)S(1)} %get-tuple-element.85), channel_id=1, source_target_pairs={{1,6},{3,4},{4,3},{6,1},{5,10},{7,8},{8,7},{10,5},{9,14},{11,12},{... | collective-permute-start | bytes 147464 | tf_op jit(solution)/shard_map/ppermute | solution.py:544
  90.2 9.5 %collective-permute-start.17 = (f32[16,16,256]{2,1,0:T(8,128)S(1)}, f32[16,16,256]{2,1,0:T(8,128)S(1)}, u32[]{:S(2)}, u32[]{:S(2)}) collective-permute-start(f32[16,16,256]{2,1,0:T(8,128)S(1)} %get-tuple-element.76), channel_id=1, source_target_pairs={{0,1},{1,0},{2,3},{3,2},{4,5},{5,4},{6,7},{7,6},{8,9},{9,8},{10,11... | collective-permute-start | bytes 786440 | tf_op jit(solution)/shard_map/ppermute | solution.py:539
  97.0 5.3 %collective-permute-start.25 = (f32[16,16,256]{2,1,0:T(8,128)S(1)}, f32[16,16,256]{2,1,0:T(8,128)S(1)}, u32[]{:S(2)}, u32[]{:S(2)}) collective-permute-start(f32[16,16,256]{2,1,0:T(8,128)S(1)} %get-tuple-element.86), channel_id=1, source_target_pairs={{0,1},{1,0},{2,3},{3,2},{4,5},{5,4},{6,7},{7,6},{8,9},{9,8},{10,11... | collective-permute-start | bytes 786440 | tf_op jit(solution)/shard_map/ppermute | solution.py:539

commit v7 on v6

--- a/solution.py
+++ b/solution.py
@@ -387,20 +387,20 @@
     n = geo.sides
     now, before, xr, cr, force, *coefs = refs[:10]
     halo = refs[10 : 10 + 3 * n]
-    px, pc, prior_ext = refs[10 + 3 * n : 13 + 3 * n]
-    out_tiles, out_corners = refs[13 + 3 * n : 13 + 4 * n], refs[13 + 4 * n : 13 + 5 * n]
-    ext, dif, tot = refs[13 + 5 * n :]
+    block, px, pc, prior_ext = refs[10 + 3 * n : 14 + 3 * n]
+    out_tiles, out_corners = refs[14 + 3 * n : 14 + 4 * n], refs[14 + 4 * n : 14 + 5 * n]
+    ext, dif, tot = refs[14 + 5 * n :]
     g, s = scal[0], scal[1]
     B = geo.B
     fill(ext, now, lambda k: xr[row_of(g, k, geo)], lambda k: cr[row_of(1 - g, k, geo)], halo, SECOND, 0, g, s, geo)
 
     def keep_block(row, value):
-        px[row - B] = value
-        pc[row - B] = value
+        block[row - B] = value
 
     two_steps(ext, 1, lambda row: before[row - (B - 1)], prior_ext, keep_block, coefs, dif, tot, geo)
-    put_rows([(force, THIRD[1])], px, pc, B, g, geo)
-    pack_tiles([(px, THIRD[0]), (force, THIRD[1])], g, s, out_tiles, out_corners, geo)
+    items = list(zip((block, force), THIRD))
+    put_rows(items, px, pc, 0, g, geo)
+    pack_tiles(items, g, s, out_tiles, out_corners, geo)
 
 
 def row_of(side, k, geo):
@@ -421,7 +421,7 @@
     g, s = scal[0], scal[1]
     B = geo.B
 
-    fill(ext, now, lambda k: xr[row_of(g, k, geo)], lambda k: cr[row_of(1 - g, k, geo)], halo, THIRD, 0, g, s, geo)
+    fill(ext, now, lambda k: xr[k], lambda k: cr[k], halo, THIRD, 0, g, s, geo)
 
     def keep_block(row, value):
         block[row - B] = value
@@ -434,16 +434,16 @@
 
 def scatter_kernel(geo, scal, offsets, *refs):
     n = geo.sides
-    now, xr, cr, courant, refl, refl_far, *coefs = refs[:11]
-    force = refs[11]
-    halo = refs[12 : 12 + 3 * n]
-    force_out, scat, scat_prior = refs[12 + 3 * n : 15 + 3 * n]
-    ext, dif, tot, wave = refs[15 + 3 * n :]
+    now, xblock, cblock, xr, cr, courant, refl, refl_far, *coefs = refs[:13]
+    force = refs[13]
+    halo = refs[14 : 14 + 3 * n]
+    force_out, scat, scat_prior = refs[14 + 3 * n : 17 + 3 * n]
+    ext, dif, tot, wave = refs[17 + 3 * n :]
     g, s = scal[0], scal[1]
     B = geo.B
-    fill_blocks(ext, xr, cr, g, geo, now)
+    fill_blocks(ext, xblock, cblock, g, geo, now)
     make_source(ext, refl, refl_far, offsets, courant, force_out, g, geo)
-    fill(wave, force, lambda k: xr[B + k], lambda k: cr[B + k], halo, THIRD, 1, g, s, geo)
+    fill(wave, force, lambda k: xr[THIRD[0] + k], lambda k: cr[THIRD[0] + k], halo, THIRD, 1, g, s, geo)
 
     def keep_scat(row, value):
         scat[row - B] = value + force_out[row - B]
@@ -503,14 +503,6 @@
         return carry
 
     lax.fori_loop(0, geo.B, one, 0, unroll=4)
-
-
-def place_kernel(geo, scal, *refs, other):
-    half, out, sem = refs[0], refs[-2], refs[-1]
-    start = pl.multiple_of((1 - scal[0] if other else scal[0]) * geo.B, TILE)
-    copy = pltpu.make_async_copy(half, out.at[pl.ds(start, geo.B)], sem)
-    copy.start()
-    copy.wait()
 
 
 def shards(sections, gx, wave_now, wave_before, courant, anisotropy, tilt, reflectivity, offsets):
@@ -637,25 +629,27 @@
         [ext],
         2,
     )
-    px, pc, prior, r0, r1 = _split(
+    now, px, pc, prior, r0, r1 = _split(
         call(
             second_kernel,
             [scal, now, prior, xr, cr, force, *coefs, *halo],
-            [shape(B + THIRD[1], Z, Y)] * 2 + [shape(*wide)] + tile_outs(THIRD),
+            [shape(*block)] + [shape(sum(THIRD), Z, Y)] * 2 + [shape(*wide)] + tile_outs(THIRD),
             [ext] * 3,
         ),
-        3,
+        4,
         n,
     )
     xr, cr, halo = exchange(px, pc, r0, r1)
+    now_x = lax.ppermute(now, ("gx", "gy"), pairs_x)
+    now_c = chip(now)
     wave, near_u, back = call(
-        third_kernel, [scal, px, prior, xr, cr, *coefs, *halo], [shape(*block)] + [shape(B, Z, H)] * 2, [ext] * 3 + [wide]
+        third_kernel, [scal, now, prior, xr, cr, *coefs, *halo], [shape(*block)] + [shape(B, Z, H)] * 2, [ext] * 3 + [wide]
     )
     wave_x = lax.ppermute(wave, ("gx", "gy"), pairs_x)
     wave_c = chip(wave)
     force2, scat, scat_prior = call(
         scatter_kernel,
-        [scal, offsets, px, xr, cr, courant_own, refl, refl_far, *coefs, force, *halo],
+        [scal, offsets, now, now_x, now_c, xr, cr, courant_own, refl, refl_far, *coefs, force, *halo],
         [shape(*block)] * 2 + [shape(*wider)],
         [ext] * 4,
         2,
@@ -673,18 +667,6 @@
     )
     xr, cr, halo = exchange(qx, qc, r0, r1)
 
-    def placed(half, other, into=None):
-        return call(
-            functools.partial(place_kernel, other=other),
-            [scal, half] + ([] if into is None else [into]),
-            [shape(rows, Z, H)],
-            [],
-            specs=[whole] + ([] if into is None else [hbm]),
-            extra=[pltpu.SemaphoreType.DMA],
-            aliases={} if into is None else {2: 0},
-            out_specs=[hbm],
-        )[0]
-
     back = chip(back)
     (background,) = call(finish_kernel, [scal, near_u, back], [shape(rows, Z, H)], [])
     near_w, far_w = call(
@@ -694,8 +676,9 @@
         [ext] * 5 + [wider, wide],
     )
     far_w = chip(far_w)
-    scattered = placed(near_w, False)
-    scattered = placed(far_w, True, scattered)
+    low_half = jnp.where(g == 0, near_w, far_w)
+    high_half = jnp.where(g == 0, far_w, near_w)
+    scattered = jnp.concatenate([low_half, high_half], 0)
     return background, scattered
 
 

time: 104 us -> 105 us (level)
  starting transfers between devices: 52.5 us -> 57.2 us
  Pallas kernels: 31.5 us -> 29 us
  waiting for transfers between devices: 18.7 us -> 16.9 us
    ppermute x13 -> x14, starting transfers between devices: 40.2 us -> 43.1 us  [chip(): return lax.ppermute(value, 'gy', swap)]
    pallas_call x14 -> x12, Pallas kernels: 31.5 us -> 29 us  [call(): pl.pallas_call(functools.partial(kernel, geo), out_shape=outs, grid_spec=...]
    ppermute x4, waiting for transfers between devices: 16.5 us -> 15.1 us  [exchange(): zr = [lax.ppermute(t, 'section', m) for t, m in zip(tiles, z_moves())]]
    ppermute x4, starting transfers between devices: 6.29 us -> 7.5 us  [exchange(): zr = [lax.ppermute(t, 'section', m) for t, m in zip(tiles, z_moves())]]
    ppermute x13 -> x14, waiting for transfers between devices: 2.12 us -> 1.72 us  [chip(): return lax.ppermute(value, 'gy', swap)]
  transfers between devices with their start and end apart: 26 -> 28, of which waited for: 7 -> 6; matrix products, arithmetic and copies ran while one was open for 0% -> 0% of each run, Pallas kernels for 17% -> 18%
where the time goes in v7:
time: 105 us
  starting transfers between devices  57.2 us (54%)
  Pallas kernels  29 us (28%)
  waiting for transfers between devices  16.9 us (16%)
    ppermute x14, starting transfers between devices, chip(): return lax.ppermute(value, 'gy', swap)  43.1 us
    pallas_call x12, Pallas kernels, call(): pl.pallas_call(functools.partial(kernel, geo), out_shape=outs, grid_spec=...  29 us
    ppermute x4, waiting for transfers between devices, exchange(): zr = [lax.ppermute(t, 'section', m) for t, m in zip(tiles, z_moves())]  15.1 us
    ppermute x4, starting transfers between devices, exchange(): zr = [lax.ppermute(t, 'section', m) for t, m in zip(tiles, z_moves())]  7.5 us
    ppermute x4, starting transfers between devices, exchange(): xr = lax.ppermute(px, ('gx', 'gy'), pairs_x)  2.67 us
    ppermute x4, starting transfers between devices, exchange(): lax.ppermute(t, ('gx', 'section', 'gy'), corner_pairs(m))  2.61 us
  transfers between devices with their start and end apart: 28, of which 6 were waited for; matrix products, arithmetic and copies ran while one was open for 0% of the time, Pallas kernels for 18%

profile of v7, /device:TPU:0, one launch (start us, length us, event | category | flops | bytes accessed | tf_op | source)
XLA Modules:
  0.0 105.0 jit_solution(13407892077258045266)
XLA Ops:
  0.6 0.1 pad_add_fusion.scal
  0.7 1.9 %shard_map.87 = f32[5,16,16,256]{3,2,1,0:T(8,128)S(1)} custom-call(s32[2]{0:T(128)S(1)} %pad_add_fusion.scal, f32[32,16,256]{2,1,0:T(8,128)} %refs_0_.3, f32[32,16,256]{2,1,0:T(8,128)} %refs_1_.3, f32[32,16,256]{2,1,0:T(8,128)} %refs_2_.3, f32[32,16,256]{2,1,0:T(8,128)} %refs_3_.3, f32[32,16,256]{2,1,0:T(8,128)} %refs_4_.3), custom_call_target="tpu_custom_call" | custom-call | tf_op jit(solution)/shard_map/pallas_call | solution.py:551
  2.6 0.6 collective-permute-start
  3.1 1.9 %shard_map.86.refs_0_ = f32[5,16,16,256]{3,2,1,0:T(8,128)S(1)} custom-call(s32[2]{0:T(128)S(1)} %pad_add_fusion.scal, f32[32,16,256]{2,1,0:T(8,128)} %refs_0_.3, f32[32,16,256]{2,1,0:T(8,128)} %refs_1_.3, f32[32,16,256]{2,1,0:T(8,128)} %refs_2_.3, f32[32,16,256]{2,1,0:T(8,128)} %refs_3_.3, f32[32,16,256]{2,1,0:T(8,128)} %refs_4_.3), custom_call_target="tpu_custom_call" | custom-call | tf_op jit(solution)/shard_map/pallas_call | solution.py:551
  5.0 0.8 collective-permute-done.refs_1_
  5.8 0.9 shard_map.88
  6.7 2.2 %shard_map.89 = (f32[20,24,512]{2,1,0:T(8,128)S(1)}, f32[20,24,512]{2,1,0:T(8,128)S(1)}, f32[20,24,512]{2,1,0:T(8,128)S(1)}, f32[20,24,512]{2,1,0:T(8,128)S(1)},...) custom-call(s32[2]{0:T(128)S(1)} %pad_add_fusion.scal, ...), custom_call_target="tpu_custom_call" | custom-call | tf_op jit(solution)/shard_map/pallas_call | solution.py:551
  8.9 0.4 collective-permute-start.8
  9.3 2.6 %collective-permute-start.3 = (f32[18,8,512]{2,1,0:T(8,128)S(1)}, f32[18,8,512]{2,1,0:T(8,128)S(1)}, u32[]{:S(2)}, u32[]{:S(2)}) collective-permute-start(f32[18,8,512]{2,1,0:T(8,128)S(1)} %get-tuple-element.50), channel_id=1, source_target_pairs={{0,2},{2,0},{1,3},{3,1},{4,6},{6,4},{5,7},{7,5},{8,10},{10,8},{9,1... | collective-permute-start | bytes 884744 | tf_op jit(solution)/shard_map/ppermute | solution.py:538
  11.9 0.7 collective-permute-start.1
  12.6 3.0 %collective-permute-start.2 = (f32[9,16,512]{2,1,0:T(8,128)S(1)}, f32[9,16,512]{2,1,0:T(8,128)S(1)}, u32[]{:S(2)}, u32[]{:S(2)}) collective-permute-start(f32[9,16,512]{2,1,0:T(8,128)S(1)} %get-tuple-element.49), channel_id=1, source_target_pairs={{0,1},{1,0},{2,3},{3,2},{4,5},{5,4},{6,7},{7,6},{8,9},{9,8},{10,11... | collective-permute-start | bytes 884744 | tf_op jit(solution)/shard_map/ppermute | solution.py:531
  15.6 3.9 %collective-permute-done.3.refs_4_ = f32[18,8,512]{2,1,0:T(8,128)S(1)} collective-permute-done((f32[18,8,512]{2,1,0:T(8,128)S(1)}, f32[18,8,512]{2,1,0:T(8,128)S(1)}, u32[]{:S(2)}, u32[]{:S(2)}) %collective-permute-start.3) | collective-permute-done | bytes 294944 | tf_op jit(solution)/shard_map/ppermute | solution.py:538
  19.5 0.0 collective-permute-start.5
  19.5 0.7 collective-permute-start.4
  20.2 0.9 collective-permute-done.5.refs_6_
  21.0 3.0 %shard_map.90 = (f32[16,16,512]{2,1,0:T(8,128)S(1)}, f32[18,24,512]{2,1,0:T(8,128)S(1)}, f32[20,24,512]{2,1,0:T(8,128)S(1)}, f32[20,24,512]{2,1,0:T(8,128)S(1)},...) custom-call(s32[2]{0:T(128)S(1)} %pad_add_fusion.scal, ...), custom_call_target="tpu_custom_call", output_to_operand_aliasing={{2}: (8, {}), {3}: (9, {}), {4}: (10, {}), {5}: (11, {}), {... | custom-call | tf_op jit(solution)/shard_map/pallas_call | solution.py:551
  24.1 5.3 %collective-permute-start.7 = (f32[16,16,512]{2,1,0:T(8,128)S(1)}, f32[16,16,512]{2,1,0:T(8,128)S(1)}, u32[]{:S(2)}, u32[]{:S(2)}) collective-permute-start(f32[16,16,512]{2,1,0:T(8,128)S(1)} %get-tuple-element.60.now.refs_0_), channel_id=1, source_target_pairs={{0,1},{1,0},{2,3},{3,2},{4,5},{5,4},{6,7},{7,6},{8,9},{9,8},{10,11... | collective-permute-start | bytes 1572872 | tf_op jit(solution)/shard_map/ppermute | solution.py:531
  29.4 0.7 collective-permute-start.6
  30.1 1.8 %collective-permute-start.9 = (f32[4,8,512]{2,1,0:T(8,128)S(1)}, f32[4,8,512]{2,1,0:T(8,128)S(1)}, u32[]{:S(2)}, u32[]{:S(2)}) collective-permute-start(f32[4,8,512]{2,1,0:T(8,128)S(1)} %get-tuple-element.69), channel_id=1, source_target_pairs={{0,2},{2,0},{1,3},{3,1},{4,6},{6,4},{5,7},{7,5},{8,10},{10,8},{9,1... | collective-permute-start | bytes 196616 | tf_op jit(solution)/shard_map/ppermute | solution.py:538
  31.9 2.5 %collective-permute-done.9.refs_10_ = f32[4,8,512]{2,1,0:T(8,128)S(1)} collective-permute-done((f32[4,8,512]{2,1,0:T(8,128)S(1)}, f32[4,8,512]{2,1,0:T(8,128)S(1)}, u32[]{:S(2)}, u32[]{:S(2)}) %collective-permute-start.9) | collective-permute-done | bytes 65568 | tf_op jit(solution)/shard_map/ppermute | solution.py:538
  34.4 2.0 %collective-permute-start.11 = (f32[4,8,512]{2,1,0:T(8,128)S(1)}, f32[4,8,512]{2,1,0:T(8,128)S(1)}, u32[]{:S(2)}, u32[]{:S(2)}) collective-permute-start(f32[4,8,512]{2,1,0:T(8,128)S(1)} %collective-permute-done.9.refs_10_), channel_id=1, source_target_pairs={{0,1},{1,0},{2,3},{3,2},{4,5},{5,4},{6,7},{7,6},{8,9},{9,8},{10,11... | collective-permute-start | bytes 196616 | tf_op jit(solution)/shard_map/ppermute | solution.py:531
  36.5 0.7 collective-permute-start.10
  37.2 2.4 %shard_map.91.refs_4_.refs_13_ = f32[16,16,512]{2,1,0:T(8,128)S(1)} custom-call(s32[2]{0:T(128)S(1)} %pad_add_fusion.scal, s32[17]{0:T(128)S(1)} %copy-done, f32[16,16,512]{2,1,0:T(8,128)S(1)} %get-tuple-element.60.now.refs_0_, f32[16,16,512]{2,1,0:T(8,128)S(1)} %collective-permute-done.6.xr.refs_2_, f32[16,16,512]{2,1,0:T(8,128)S(1)} %collective-permute-done.7.cr.refs_3_, ...), custom_call_target="tpu_custom_call" | custom-call | tf_op jit(solution)/shard_map/pallas_call | solution.py:551
  39.6 2.4 %shard_map.92 = (f32[16,16,512]{2,1,0:T(8,128)S(1)}, f32[5,16,512]{2,1,0:T(8,128)S(1)}, f32[5,16,512]{2,1,0:T(8,128)S(1)}, f32[18,24,512]{2,1,0:T(8,128)S(1)}, f...) custom-call(s32[2]{0:T(128)S(1)} %pad_add_fusion.scal, f32[16,16,512]{2,1,0:T(8,128)S(1)} %get-tuple-element.60.now.refs_0_, ...), custom_call_target="tpu_custom_call" | custom-call | tf_op jit(solution)/shard_map/pallas_call | solution.py:551
  42.0 1.6 %collective-permute-start.14 = (f32[12,8,512]{2,1,0:T(8,128)S(1)}, f32[12,8,512]{2,1,0:T(8,128)S(1)}, u32[]{:S(2)}, u32[]{:S(2)}) collective-permute-start(f32[12,8,512]{2,1,0:T(8,128)S(1)} %get-tuple-element.75), channel_id=1, source_target_pairs={{0,2},{2,0},{1,3},{3,1},{4,6},{6,4},{5,7},{7,5},{8,10},{10,8},{9,1... | collective-permute-start | bytes 589832 | tf_op jit(solution)/shard_map/ppermute | solution.py:538
  43.6 4.2 %collective-permute-done.14.refs_9_.refs_14_ = f32[12,8,512]{2,1,0:T(8,128)S(1)} collective-permute-done((f32[12,8,512]{2,1,0:T(8,128)S(1)}, f32[12,8,512]{2,1,0:T(8,128)S(1)}, u32[]{:S(2)}, u32[]{:S(2)}) %collective-permute-start.14) | collective-permute-done | bytes 196640 | tf_op jit(solution)/shard_map/ppermute | solution.py:538
  47.8 3.1 %collective-permute-start.16 = (f32[12,8,512]{2,1,0:T(8,128)S(1)}, f32[12,8,512]{2,1,0:T(8,128)S(1)}, u32[]{:S(2)}, u32[]{:S(2)}) collective-permute-start(f32[12,8,512]{2,1,0:T(8,128)S(1)} %collective-permute-done.14.refs_9_.refs_14_), channel_id=1, source_target_pairs={{0,1},{1,0},{2,3},{3,2},{4,5},{5,4},{6,7},{7,6},{8,9},{9,8},{10,11... | collective-permute-start | bytes 589832 | tf_op jit(solution)/shard_map/ppermute | solution.py:531
  50.8 0.7 collective-permute-start.12
  51.5 5.0 %collective-permute-start.13 = (f32[5,16,512]{2,1,0:T(8,128)S(1)}, f32[5,16,512]{2,1,0:T(8,128)S(1)}, u32[]{:S(2)}, u32[]{:S(2)}) collective-permute-start(f32[5,16,512]{2,1,0:T(8,128)S(1)} %get-tuple-element.74), channel_id=1, source_target_pairs={{0,1},{1,0},{2,3},{3,2},{4,5},{5,4},{6,7},{7,6},{8,9},{9,8},{10,11... | collective-permute-start | bytes 491528 | tf_op jit(solution)/shard_map/ppermute | solution.py:531
  56.6 0.7 collective-permute-start.15
  57.2 3.3 %collective-permute-start.19 = (f32[16,16,512]{2,1,0:T(8,128)S(1)}, f32[16,16,512]{2,1,0:T(8,128)S(1)}, u32[]{:S(2)}, u32[]{:S(2)}) collective-permute-start(f32[16,16,512]{2,1,0:T(8,128)S(1)} %get-tuple-element.71.refs_0_), channel_id=1, source_target_pairs={{0,1},{1,0},{2,3},{3,2},{4,5},{5,4},{6,7},{7,6},{8,9},{9,8},{10,11... | collective-permute-start | bytes 1572872 | tf_op jit(solution)/shard_map/ppermute | solution.py:531
  60.5 0.7 collective-permute-start.18
  61.3 2.3 %shard_map.93 = (f32[16,16,512]{2,1,0:T(8,128)S(1)}, f32[16,16,256]{2,1,0:T(8,128)S(1)}, f32[16,16,256]{2,1,0:T(8,128)S(1)}) custom-call(s32[2]{0:T(128)S(1)} %pad_add_fusion.scal, f32[16,16,512]{2,1,0:T(8,128)S(1)} %get-tuple-element.71.refs_0_, f32[18,24,512]{2,1,0:T(8,128)S(1)} %get-tuple-element.72.refs_1_, ...), custom_call_target="tpu_custom_call" | custom-call | tf_op jit(solution)/shard_map/pallas_call | solution.py:551
  63.6 5.0 %collective-permute-start.21 = (f32[16,16,512]{2,1,0:T(8,128)S(1)}, f32[16,16,512]{2,1,0:T(8,128)S(1)}, u32[]{:S(2)}, u32[]{:S(2)}) collective-permute-start(f32[16,16,512]{2,1,0:T(8,128)S(1)} %get-tuple-element.82.refs_0_), channel_id=1, source_target_pairs={{0,1},{1,0},{2,3},{3,2},{4,5},{5,4},{6,7},{7,6},{8,9},{9,8},{10,11... | collective-permute-start | bytes 1572872 | tf_op jit(solution)/shard_map/ppermute | solution.py:531
  68.6 0.7 collective-permute-start.20
  69.3 4.4 %shard_map.95 = (f32[16,16,512]{2,1,0:T(8,128)S(1)}, f32[16,16,512]{2,1,0:T(8,128)S(1)}, f32[20,24,512]{2,1,0:T(8,128)S(1)}) custom-call(s32[2]{0:T(128)S(1)} %pad_add_fusion.scal, s32[17]{0:T(128)S(1)} %copy-done, f32[16,16,512]{2,1,0:T(8,128)S(1)} %get-tuple-element.71.refs_0_, f32[16,16,512]{2,1,0:T(8,128)S(1)} %collective-permute-done.18.refs_1_, ...), custom_call_target="tpu_custom_call" | custom-call | tf_op jit(solution)/shard_map/pallas_call | solution.py:551
  73.7 2.5 %shard_map.96 = (f32[16,16,512]{2,1,0:T(8,128)S(1)}, f32[6,16,512]{2,1,0:T(8,128)S(1)}, f32[6,16,512]{2,1,0:T(8,128)S(1)}, f32[14,8,512]{2,1,0:T(8,128)S(1)}, f32[3,8,512]{2,1,0:T(8,128)S(1)}) custom-call(s32[2]{0:T(128)S(1)} %pad_add_fusion.scal, s32[17]{0:T(128)S(1)} %copy-done, f32[16,16,512]{2,1,0:T(8,128)S(1)} %get-tuple-element.82.refs_0_, ...), custom_call_target="tpu_custom_call" | custom-call | tf_op jit(solution)/shard_map/pallas_call | solution.py:551
  76.2 1.5 %collective-permute-start.24 = (f32[14,8,512]{2,1,0:T(8,128)S(1)}, f32[14,8,512]{2,1,0:T(8,128)S(1)}, u32[]{:S(2)}, u32[]{:S(2)}) collective-permute-start(f32[14,8,512]{2,1,0:T(8,128)S(1)} %get-tuple-element.86), channel_id=1, source_target_pairs={{0,2},{2,0},{1,3},{3,1},{4,6},{6,4},{5,7},{7,5},{8,10},{10,8},{9,1... | collective-permute-start | bytes 688136 | tf_op jit(solution)/shard_map/ppermute | solution.py:538
  77.8 4.6 %collective-permute-done.24.refs_11_ = f32[14,8,512]{2,1,0:T(8,128)S(1)} collective-permute-done((f32[14,8,512]{2,1,0:T(8,128)S(1)}, f32[14,8,512]{2,1,0:T(8,128)S(1)}, u32[]{:S(2)}, u32[]{:S(2)}) %collective-permute-start.24) | collective-permute-done | bytes 229408 | tf_op jit(solution)/shard_map/ppermute | solution.py:538
  82.3 4.3 %collective-permute-start.26 = (f32[14,8,512]{2,1,0:T(8,128)S(1)}, f32[14,8,512]{2,1,0:T(8,128)S(1)}, u32[]{:S(2)}, u32[]{:S(2)}) collective-permute-start(f32[14,8,512]{2,1,0:T(8,128)S(1)} %collective-permute-done.24.refs_11_), channel_id=1, source_target_pairs={{0,1},{1,0},{2,3},{3,2},{4,5},{5,4},{6,7},{7,6},{8,9},{9,8},{10,11... | collective-permute-start | bytes 688136 | tf_op jit(solution)/shard_map/ppermute | solution.py:531
  86.6 0.7 collective-permute-start.22
  87.3 5.3 %collective-permute-start.23 = (f32[6,16,512]{2,1,0:T(8,128)S(1)}, f32[6,16,512]{2,1,0:T(8,128)S(1)}, u32[]{:S(2)}, u32[]{:S(2)}) collective-permute-start(f32[6,16,512]{2,1,0:T(8,128)S(1)} %get-tuple-element.85), channel_id=1, source_target_pairs={{0,1},{1,0},{2,3},{3,2},{4,5},{5,4},{6,7},{7,6},{8,9},{9,8},{10,11... | collective-permute-start | bytes 589832 | tf_op jit(solution)/shard_map/ppermute | solution.py:531
  92.6 0.7 collective-permute-start.25
  93.2 3.1 %collective-permute-start.17 = (f32[16,16,256]{2,1,0:T(8,128)S(1)}, f32[16,16,256]{2,1,0:T(8,128)S(1)}, u32[]{:S(2)}, u32[]{:S(2)}) collective-permute-start(f32[16,16,256]{2,1,0:T(8,128)S(1)} %get-tuple-element.78), channel_id=1, source_target_pairs={{0,1},{1,0},{2,3},{3,2},{4,5},{5,4},{6,7},{7,6},{8,9},{9,8},{10,11... | collective-permute-start | bytes 786440 | tf_op jit(solution)/shard_map/ppermute | solution.py:531
  96.3 3.7 %shard_map.97 = (f32[16,16,256]{2,1,0:T(8,128)S(1)}, f32[16,16,256]{2,1,0:T(8,128)S(1)}) custom-call(s32[2]{0:T(128)S(1)} %pad_add_fusion.scal, f32[16,16,512]{2,1,0:T(8,128)S(1)} %get-tuple-element.79.refs_6_.refs_0_, f32[20,24,512]{2,1,0:T(8,128)S(1)} %get-tuple-element.80.refs_1_, f32[16,16,512]{2,1,0:T(8,128)S(1)} %get-tuple-element.81.refs_7_.refs_2_, ...), custom_call_target="tpu_custom_call" | custom-call | tf_op jit(solution)/shard_map/pallas_call | solution.py:551
  100.1 2.6 %collective-permute-start.27 = (f32[16,16,256]{2,1,0:T(8,128)S(1)}, f32[16,16,256]{2,1,0:T(8,128)S(1)}, u32[]{:S(2)}, u32[]{:S(2)}) collective-permute-start(f32[16,16,256]{2,1,0:T(8,128)S(1)} %get-tuple-element.89), channel_id=1, source_target_pairs={{0,1},{1,0},{2,3},{3,2},{4,5},{5,4},{6,7},{7,6},{8,9},{9,8},{10,11... | collective-permute-start | bytes 786440 | tf_op jit(solution)/shard_map/ppermute | solution.py:531
  102.7 1.4 %shard_map.94 = f32[32,16,256]{2,1,0:T(8,128)} custom-call(s32[2]{0:T(128)S(1)} %pad_add_fusion.scal, f32[16,16,256]{2,1,0:T(8,128)S(1)} %get-tuple-element.77.near, f32[16,16,256]{2,1,0:T(8,128)S(1)} %collective-permute-done.17.far), custom_call_target="tpu_custom_call" | custom-call | tf_op jit(solution)/shard_map/pallas_call | solution.py:551
  104.2 0.8 pad_maximum_fusion
  (25 shorter events, 0.1 us)
Async XLA Ops:
  2.6 3.2 %collective-permute-start = (f32[5,16,16,256]{3,2,1,0:T(8,128)S(1)}, f32[5,16,16,256]{3,2,1,0:T(8,128)S(1)}, u32[]{:S(2)}, u32[]{:S(2)}) collective-permute-start(f32[5,16,16,256]{3,2,1,0:T(8,128)S(1)} %shard_map.87), channel_id=1, source_target_pairs={{0,1},{1,0},{2,3},{3,2},{4,5},{5,4},{6,7},{7,6},{8,9},{9,8},{10,11... | collective-permute-start | bytes 3932168 | tf_op jit(solution)/shard_map/ppermute | solution.py:531
  8.9 28.3 %collective-permute-start.8 = (f32[17,16,16,256]{3,2,1,0:T(8,128)S(1)}, f32[17,16,16,256]{3,2,1,0:T(8,128)S(1)}, u32[]{:S(2)}, u32[]{:S(2)}) collective-permute-start(f32[17,16,16,256]{3,2,1,0:T(8,128)S(1)} %get-tuple-element.63), channel_id=1, source_target_pairs={{0,1},{1,0},{2,3},{3,2},{4,5},{5,4},{6,7},{7,6},{8,9},{9,8},{10,11... | collective-permute-start | bytes 13369352 | tf_op jit(solution)/shard_map/ppermute | solution.py:531
  9.3 10.2 %collective-permute-start.3 = (f32[18,8,512]{2,1,0:T(8,128)S(1)}, f32[18,8,512]{2,1,0:T(8,128)S(1)}, u32[]{:S(2)}, u32[]{:S(2)}) collective-permute-start(f32[18,8,512]{2,1,0:T(8,128)S(1)} %get-tuple-element.50), channel_id=1, source_target_pairs={{0,2},{2,0},{1,3},{3,1},{4,6},{6,4},{5,7},{7,5},{8,10},{10,8},{9,1... | collective-permute-start | bytes 884744 | tf_op jit(solution)/shard_map/ppermute | solution.py:538
  11.9 8.2 %collective-permute-start.1 = (f32[9,16,512]{2,1,0:T(8,128)S(1)}, f32[9,16,512]{2,1,0:T(8,128)S(1)}, u32[]{:S(2)}, u32[]{:S(2)}) collective-permute-start(f32[9,16,512]{2,1,0:T(8,128)S(1)} %get-tuple-element.48), channel_id=1, source_target_pairs={{1,4},{4,1},{5,8},{8,5},{9,12},{12,9},{3,6},{6,3},{7,10},{10,7},{1... | collective-permute-start | bytes 884744 | tf_op jit(solution)/shard_map/ppermute | solution.py:534
  12.6 7.6 %collective-permute-start.2 = (f32[9,16,512]{2,1,0:T(8,128)S(1)}, f32[9,16,512]{2,1,0:T(8,128)S(1)}, u32[]{:S(2)}, u32[]{:S(2)}) collective-permute-start(f32[9,16,512]{2,1,0:T(8,128)S(1)} %get-tuple-element.49), channel_id=1, source_target_pairs={{0,1},{1,0},{2,3},{3,2},{4,5},{5,4},{6,7},{7,6},{8,9},{9,8},{10,11... | collective-permute-start | bytes 884744 | tf_op jit(solution)/shard_map/ppermute | solution.py:531
  19.5 1.6 %collective-permute-start.5 = (f32[18,8,512]{2,1,0:T(8,128)S(1)}, f32[18,8,512]{2,1,0:T(8,128)S(1)}, u32[]{:S(2)}, u32[]{:S(2)}) collective-permute-start(f32[18,8,512]{2,1,0:T(8,128)S(1)} %collective-permute-done.3.refs_4_), channel_id=1, source_target_pairs={{0,1},{1,0},{2,3},{3,2},{4,5},{5,4},{6,7},{7,6},{8,9},{9,8},{10,11... | collective-permute-start | bytes 884744 | tf_op jit(solution)/shard_map/ppermute | solution.py:531
  19.5 0.7 collective-permute-start.4
  21.0 16.1 %copy-start = (s32[17]{0:T(128)S(1)}, s32[17]{0:T(128)}, u32[]{:S(2)}) copy-start(s32[17]{0:T(128)} %offsets.5) | copy-start | bytes 208
  24.1 13.0 %collective-permute-start.7 = (f32[16,16,512]{2,1,0:T(8,128)S(1)}, f32[16,16,512]{2,1,0:T(8,128)S(1)}, u32[]{:S(2)}, u32[]{:S(2)}) collective-permute-start(f32[16,16,512]{2,1,0:T(8,128)S(1)} %get-tuple-element.60.now.refs_0_), channel_id=1, source_target_pairs={{0,1},{1,0},{2,3},{3,2},{4,5},{5,4},{6,7},{7,6},{8,9},{9,8},{10,11... | collective-permute-start | bytes 1572872 | tf_op jit(solution)/shard_map/ppermute | solution.py:531
  29.4 7.7 %collective-permute-start.6 = (f32[16,16,512]{2,1,0:T(8,128)S(1)}, f32[16,16,512]{2,1,0:T(8,128)S(1)}, u32[]{:S(2)}, u32[]{:S(2)}) collective-permute-start(f32[16,16,512]{2,1,0:T(8,128)S(1)} %get-tuple-element.60.now.refs_0_), channel_id=1, source_target_pairs={{1,4},{4,1},{5,8},{8,5},{9,12},{12,9},{3,6},{6,3},{7,10},{10,7},{1... | collective-permute-start | bytes 1572872 | tf_op jit(solution)/shard_map/ppermute | solution.py:534
  30.1 4.3 %collective-permute-start.9 = (f32[4,8,512]{2,1,0:T(8,128)S(1)}, f32[4,8,512]{2,1,0:T(8,128)S(1)}, u32[]{:S(2)}, u32[]{:S(2)}) collective-permute-start(f32[4,8,512]{2,1,0:T(8,128)S(1)} %get-tuple-element.69), channel_id=1, source_target_pairs={{0,2},{2,0},{1,3},{3,1},{4,6},{6,4},{5,7},{7,5},{8,10},{10,8},{9,1... | collective-permute-start | bytes 196616 | tf_op jit(solution)/shard_map/ppermute | solution.py:538
  34.4 5.2 %collective-permute-start.11 = (f32[4,8,512]{2,1,0:T(8,128)S(1)}, f32[4,8,512]{2,1,0:T(8,128)S(1)}, u32[]{:S(2)}, u32[]{:S(2)}) collective-permute-start(f32[4,8,512]{2,1,0:T(8,128)S(1)} %collective-permute-done.9.refs_10_), channel_id=1, source_target_pairs={{0,1},{1,0},{2,3},{3,2},{4,5},{5,4},{6,7},{7,6},{8,9},{9,8},{10,11... | collective-permute-start | bytes 196616 | tf_op jit(solution)/shard_map/ppermute | solution.py:531
  36.5 3.1 %collective-permute-start.10 = (f32[1,8,512]{2,1,0:T(8,128)S(1)}, f32[1,8,512]{2,1,0:T(8,128)S(1)}, u32[]{:S(2)}, u32[]{:S(2)}) collective-permute-start(f32[1,8,512]{2,1,0:T(8,128)S(1)} %get-tuple-element.70), channel_id=1, source_target_pairs={{1,6},{3,4},{4,3},{6,1},{5,10},{7,8},{8,7},{10,5},{9,14},{11,12},{... | collective-permute-start | bytes 49160 | tf_op jit(solution)/shard_map/ppermute | solution.py:536
  42.0 5.7 %collective-permute-start.14 = (f32[12,8,512]{2,1,0:T(8,128)S(1)}, f32[12,8,512]{2,1,0:T(8,128)S(1)}, u32[]{:S(2)}, u32[]{:S(2)}) collective-permute-start(f32[12,8,512]{2,1,0:T(8,128)S(1)} %get-tuple-element.75), channel_id=1, source_target_pairs={{0,2},{2,0},{1,3},{3,1},{4,6},{6,4},{5,7},{7,5},{8,10},{10,8},{9,1... | collective-permute-start | bytes 589832 | tf_op jit(solution)/shard_map/ppermute | solution.py:538
  47.8 13.5 %collective-permute-start.16 = (f32[12,8,512]{2,1,0:T(8,128)S(1)}, f32[12,8,512]{2,1,0:T(8,128)S(1)}, u32[]{:S(2)}, u32[]{:S(2)}) collective-permute-start(f32[12,8,512]{2,1,0:T(8,128)S(1)} %collective-permute-done.14.refs_9_.refs_14_), channel_id=1, source_target_pairs={{0,1},{1,0},{2,3},{3,2},{4,5},{5,4},{6,7},{7,6},{8,9},{9,8},{10,11... | collective-permute-start | bytes 589832 | tf_op jit(solution)/shard_map/ppermute | solution.py:531
  50.8 10.4 %collective-permute-start.12 = (f32[5,16,512]{2,1,0:T(8,128)S(1)}, f32[5,16,512]{2,1,0:T(8,128)S(1)}, u32[]{:S(2)}, u32[]{:S(2)}) collective-permute-start(f32[5,16,512]{2,1,0:T(8,128)S(1)} %get-tuple-element.73), channel_id=1, source_target_pairs={{1,4},{4,1},{5,8},{8,5},{9,12},{12,9},{3,6},{6,3},{7,10},{10,7},{1... | collective-permute-start | bytes 491528 | tf_op jit(solution)/shard_map/ppermute | solution.py:534
  51.5 9.7 %collective-permute-start.13 = (f32[5,16,512]{2,1,0:T(8,128)S(1)}, f32[5,16,512]{2,1,0:T(8,128)S(1)}, u32[]{:S(2)}, u32[]{:S(2)}) collective-permute-start(f32[5,16,512]{2,1,0:T(8,128)S(1)} %get-tuple-element.74), channel_id=1, source_target_pairs={{0,1},{1,0},{2,3},{3,2},{4,5},{5,4},{6,7},{7,6},{8,9},{9,8},{10,11... | collective-permute-start | bytes 491528 | tf_op jit(solution)/shard_map/ppermute | solution.py:531
  56.6 4.0 %collective-permute-start.15 = (f32[3,8,512]{2,1,0:T(8,128)S(1)}, f32[3,8,512]{2,1,0:T(8,128)S(1)}, u32[]{:S(2)}, u32[]{:S(2)}) collective-permute-start(f32[3,8,512]{2,1,0:T(8,128)S(1)} %get-tuple-element.76), channel_id=1, source_target_pairs={{1,6},{3,4},{4,3},{6,1},{5,10},{7,8},{8,7},{10,5},{9,14},{11,12},{... | collective-permute-start | bytes 147464 | tf_op jit(solution)/shard_map/ppermute | solution.py:536
  57.2 12.1 %collective-permute-start.19 = (f32[16,16,512]{2,1,0:T(8,128)S(1)}, f32[16,16,512]{2,1,0:T(8,128)S(1)}, u32[]{:S(2)}, u32[]{:S(2)}) collective-permute-start(f32[16,16,512]{2,1,0:T(8,128)S(1)} %get-tuple-element.71.refs_0_), channel_id=1, source_target_pairs={{0,1},{1,0},{2,3},{3,2},{4,5},{5,4},{6,7},{7,6},{8,9},{9,8},{10,11... | collective-permute-start | bytes 1572872 | tf_op jit(solution)/shard_map/ppermute | solution.py:531
  60.5 8.8 %collective-permute-start.18 = (f32[16,16,512]{2,1,0:T(8,128)S(1)}, f32[16,16,512]{2,1,0:T(8,128)S(1)}, u32[]{:S(2)}, u32[]{:S(2)}) collective-permute-start(f32[16,16,512]{2,1,0:T(8,128)S(1)} %get-tuple-element.71.refs_0_), channel_id=1, source_target_pairs={{1,4},{4,1},{5,8},{8,5},{9,12},{12,9},{3,6},{6,3},{7,10},{10,7},{1... | collective-permute-start | bytes 1572872 | tf_op jit(solution)/shard_map/ppermute | solution.py:643
  63.6 10.1 %collective-permute-start.21 = (f32[16,16,512]{2,1,0:T(8,128)S(1)}, f32[16,16,512]{2,1,0:T(8,128)S(1)}, u32[]{:S(2)}, u32[]{:S(2)}) collective-permute-start(f32[16,16,512]{2,1,0:T(8,128)S(1)} %get-tuple-element.82.refs_0_), channel_id=1, source_target_pairs={{0,1},{1,0},{2,3},{3,2},{4,5},{5,4},{6,7},{7,6},{8,9},{9,8},{10,11... | collective-permute-start | bytes 1572872 | tf_op jit(solution)/shard_map/ppermute | solution.py:531
  68.6 5.1 %collective-permute-start.20 = (f32[16,16,512]{2,1,0:T(8,128)S(1)}, f32[16,16,512]{2,1,0:T(8,128)S(1)}, u32[]{:S(2)}, u32[]{:S(2)}) collective-permute-start(f32[16,16,512]{2,1,0:T(8,128)S(1)} %get-tuple-element.82.refs_0_), channel_id=1, source_target_pairs={{1,4},{4,1},{5,8},{8,5},{9,12},{12,9},{3,6},{6,3},{7,10},{10,7},{1... | collective-permute-start | bytes 1572872 | tf_op jit(solution)/shard_map/ppermute | solution.py:648
  76.2 6.1 %collective-permute-start.24 = (f32[14,8,512]{2,1,0:T(8,128)S(1)}, f32[14,8,512]{2,1,0:T(8,128)S(1)}, u32[]{:S(2)}, u32[]{:S(2)}) collective-permute-start(f32[14,8,512]{2,1,0:T(8,128)S(1)} %get-tuple-element.86), channel_id=1, source_target_pairs={{0,2},{2,0},{1,3},{3,1},{4,6},{6,4},{5,7},{7,5},{8,10},{10,8},{9,1... | collective-permute-start | bytes 688136 | tf_op jit(solution)/shard_map/ppermute | solution.py:538
  82.3 14.0 %collective-permute-start.26 = (f32[14,8,512]{2,1,0:T(8,128)S(1)}, f32[14,8,512]{2,1,0:T(8,128)S(1)}, u32[]{:S(2)}, u32[]{:S(2)}) collective-permute-start(f32[14,8,512]{2,1,0:T(8,128)S(1)} %collective-permute-done.24.refs_11_), channel_id=1, source_target_pairs={{0,1},{1,0},{2,3},{3,2},{4,5},{5,4},{6,7},{7,6},{8,9},{9,8},{10,11... | collective-permute-start | bytes 688136 | tf_op jit(solution)/shard_map/ppermute | solution.py:531
  86.6 9.7 %collective-permute-start.22 = (f32[6,16,512]{2,1,0:T(8,128)S(1)}, f32[6,16,512]{2,1,0:T(8,128)S(1)}, u32[]{:S(2)}, u32[]{:S(2)}) collective-permute-start(f32[6,16,512]{2,1,0:T(8,128)S(1)} %get-tuple-element.84), channel_id=1, source_target_pairs={{1,4},{4,1},{5,8},{8,5},{9,12},{12,9},{3,6},{6,3},{7,10},{10,7},{1... | collective-permute-start | bytes 589832 | tf_op jit(solution)/shard_map/ppermute | solution.py:534
  87.3 9.1 %collective-permute-start.23 = (f32[6,16,512]{2,1,0:T(8,128)S(1)}, f32[6,16,512]{2,1,0:T(8,128)S(1)}, u32[]{:S(2)}, u32[]{:S(2)}) collective-permute-start(f32[6,16,512]{2,1,0:T(8,128)S(1)} %get-tuple-element.85), channel_id=1, source_target_pairs={{0,1},{1,0},{2,3},{3,2},{4,5},{5,4},{6,7},{7,6},{8,9},{9,8},{10,11... | collective-permute-start | bytes 589832 | tf_op jit(solution)/shard_map/ppermute | solution.py:531
  92.6 3.8 %collective-permute-start.25 = (f32[3,8,512]{2,1,0:T(8,128)S(1)}, f32[3,8,512]{2,1,0:T(8,128)S(1)}, u32[]{:S(2)}, u32[]{:S(2)}) collective-permute-start(f32[3,8,512]{2,1,0:T(8,128)S(1)} %get-tuple-element.87), channel_id=1, source_target_pairs={{1,6},{3,4},{4,3},{6,1},{5,10},{7,8},{8,7},{10,5},{9,14},{11,12},{... | collective-permute-start | bytes 147464 | tf_op jit(solution)/shard_map/ppermute | solution.py:536
  93.2 9.5 %collective-permute-start.17 = (f32[16,16,256]{2,1,0:T(8,128)S(1)}, f32[16,16,256]{2,1,0:T(8,128)S(1)}, u32[]{:S(2)}, u32[]{:S(2)}) collective-permute-start(f32[16,16,256]{2,1,0:T(8,128)S(1)} %get-tuple-element.78), channel_id=1, source_target_pairs={{0,1},{1,0},{2,3},{3,2},{4,5},{5,4},{6,7},{7,6},{8,9},{9,8},{10,11... | collective-permute-start | bytes 786440 | tf_op jit(solution)/shard_map/ppermute | solution.py:531
  100.1 4.0 %collective-permute-start.27 = (f32[16,16,256]{2,1,0:T(8,128)S(1)}, f32[16,16,256]{2,1,0:T(8,128)S(1)}, u32[]{:S(2)}, u32[]{:S(2)}) collective-permute-start(f32[16,16,256]{2,1,0:T(8,128)S(1)} %get-tuple-element.89), channel_id=1, source_target_pairs={{0,1},{1,0},{2,3},{3,2},{4,5},{5,4},{6,7},{7,6},{8,9},{9,8},{10,11... | collective-permute-start | bytes 786440 | tf_op jit(solution)/shard_map/ppermute | solution.py:531

commit v8 on v7

--- a/solution.py
+++ b/solution.py
@@ -80,6 +80,8 @@
     starts, _ = tiles_of(depths, geo)
     for sender, tile_ref, corner_ref in zip(senders(s, geo), tiles, corners):
         for (ref, depth), start in zip(items, starts):
+            if ref is None:
+                continue
             slot = slot_of(depth)
             per = TILE // slot
             masks = [tile_mask(sender, depth, k * slot, geo.Y) for k in range(1, per)]
@@ -93,11 +95,13 @@
         for ref, depth in items:
             for k in range(depth):
                 at, turn = divmod(place * slot, TILE)
+                place += 1
+                if ref is None:
+                    continue
                 value = turned(edge_tile(ref, g * (geo.B - depth) + k, sender, geo), turn)
                 if turn:
                     value = jnp.where(tile_mask(sender, depth, turn, geo.Y), value, corner_ref[at])
                 corner_ref[at] = value
-                place += 1
 
 
 def unpack_row(ref, depths, index, x, geo):
@@ -437,8 +441,9 @@
     now, xblock, cblock, xr, cr, courant, refl, refl_far, *coefs = refs[:13]
     force = refs[13]
     halo = refs[14 : 14 + 3 * n]
-    force_out, scat, scat_prior = refs[14 + 3 * n : 17 + 3 * n]
-    ext, dif, tot, wave = refs[17 + 3 * n :]
+    force_out, scat, scat_prior, px, pc = refs[14 + 3 * n : 19 + 3 * n]
+    out_tiles, out_corners = refs[19 + 3 * n : 19 + 4 * n], refs[19 + 4 * n : 19 + 5 * n]
+    ext, dif, tot, wave = refs[19 + 5 * n :]
     g, s = scal[0], scal[1]
     B = geo.B
     fill_blocks(ext, xblock, cblock, g, geo, now)
@@ -449,19 +454,20 @@
         scat[row - B] = value + force_out[row - B]
 
     two_steps(wave, 2, lambda row: -wave[row], scat_prior, keep_scat, coefs, dif, tot, geo)
+    put_rows([(scat, LAST[0]), (force_out, LAST[1])], px, pc, 0, g, geo)
+    pack_tiles(list(zip((scat, force_out, None), LAST)), g, s, out_tiles, out_corners, geo)
 
 
 def source_kernel(geo, scal, offsets, *refs):
     n = geo.sides
-    now, xr, cr, courant, refl, refl_far, scat, force2 = refs[:8]
-    force3, px, pc = refs[8:11]
-    tiles, corners, ext = refs[11 : 11 + n], refs[11 + n : 11 + 2 * n], refs[11 + 2 * n]
+    now, xr, cr, courant, refl, refl_far = refs[:6]
+    force3, px, pc = refs[8 + 2 * n : 11 + 2 * n]
+    tiles, corners, ext = refs[11 + 2 * n : 11 + 3 * n], refs[11 + 3 * n : 11 + 4 * n], refs[11 + 4 * n]
     g, s = scal[0], scal[1]
     fill_blocks(ext, xr, cr, g, geo, now)
     make_source(ext, refl, refl_far, offsets, courant, force3, g, geo)
-    items = list(zip((scat, force2, force3), LAST))
-    put_rows(items, px, pc, 0, g, geo)
-    pack_tiles(items, g, s, tiles, corners, geo)
+    put_rows([(force3, LAST[2])], px, pc, LAST[0] + LAST[1], g, geo)
+    pack_tiles(list(zip((None, None, force3), LAST)), g, s, tiles, corners, geo)
 
 
 def last_kernel(geo, scal, *refs):
@@ -510,8 +516,7 @@
     geo = Geometry(rows, depth, half, sections)
     B, Z, H, Y, ZE, n = geo.B, geo.Z, geo.H, geo.Y, geo.ZE, geo.sides
     g = lax.axis_index("gy")
-    s = lax.axis_index("section")
-    scal = jnp.stack([g, s]).astype(jnp.int32)
+    scal = None
     swap = [(0, 1), (1, 0)]
     pairs_x = [p for i in range(gx - 1) for p in ((2 * i + 1, 2 * i + 2), (2 * i + 2, 2 * i + 1))]
 
@@ -548,19 +553,23 @@
             specs = [pl.BlockSpec(memory_space=pltpu.SMEM)] * (smem - 1)
             specs += [pl.BlockSpec(memory_space=pltpu.VMEM)] * (len(inputs) - smem)
         used = sum(4 * d[0] * d[1] * d[2] for d in scratch)
+
+        def body(*refs):
+            kernel(geo, (lax.axis_index("gy"), lax.axis_index("section")), *refs)
+
         return pl.pallas_call(
-            functools.partial(kernel, geo),
+            body,
             out_shape=outs,
             grid_spec=pltpu.PrefetchScalarGridSpec(
-                num_scalar_prefetch=1,
+                num_scalar_prefetch=0,
                 grid=(1,),
                 in_specs=specs,
                 out_specs=out_specs or [pl.BlockSpec(memory_space=pltpu.VMEM)] * len(outs),
                 scratch_shapes=[*(pltpu.VMEM(d, F32) for d in scratch), *extra],
             ),
-            input_output_aliases=aliases or {},
+            input_output_aliases={k - 1: v for k, v in (aliases or {}).items()},
             compiler_params=pltpu.CompilerParams(vmem_limit_bytes=used + SLACK),
-        )(*inputs)
+        )(*inputs[1:])
 
     block, wide, wider, ext = (B, Z, Y), (B + 2, ZE, Y), (B + 4, ZE, Y), (3 * B, ZE, Y)
 
@@ -647,26 +656,26 @@
     )
     wave_x = lax.ppermute(wave, ("gx", "gy"), pairs_x)
     wave_c = chip(wave)
-    force2, scat, scat_prior = call(
+    force2, scat, scat_prior, *payload = call(
         scatter_kernel,
         [scal, offsets, now, now_x, now_c, xr, cr, courant_own, refl, refl_far, *coefs, force, *halo],
-        [shape(*block)] * 2 + [shape(*wider)],
+        [shape(*block)] * 2 + [shape(*wider)] + [shape(sum(LAST), Z, Y)] * 2 + tile_outs(LAST),
         [ext] * 4,
         2,
     )
     force3, qx, qc, r0, r1 = _split(
         call(
             source_kernel,
-            [scal, offsets, wave, wave_x, wave_c, courant_own, refl, refl_far, scat, force2],
+            [scal, offsets, wave, wave_x, wave_c, courant_own, refl, refl_far, *payload],
             [shape(*block)] + [shape(sum(LAST), Z, Y)] * 2 + tile_outs(LAST),
             [ext],
             2,
+            aliases={8 + k: 1 + k for k in range(len(payload))},
         ),
         3,
         n,
     )
     xr, cr, halo = exchange(qx, qc, r0, r1)
-
     back = chip(back)
     (background,) = call(finish_kernel, [scal, near_u, back], [shape(rows, Z, H)], [])
     near_w, far_w = call(

time: 105 us -> 98.5 us (0.938)
  Pallas kernels: 29 us -> 22.8 us
  starting transfers between devices: 57.2 us -> 55.5 us
  waiting for transfers between devices: 16.9 us -> 18 us
    pallas_call x12, Pallas kernels: 29 us -> 22.8 us  [call(): pl.pallas_call(body, out_shape=outs, grid_spec=pltpu.PrefetchScalarGridSp...]
    ppermute x14, starting transfers between devices: 43.1 us -> 41.6 us  [chip(): return lax.ppermute(value, 'gy', swap)]
  transfers between devices with their start and end apart: 28 -> 28, of which waited for: 6 -> 7; matrix products, arithmetic and copies ran while one was open for 0% -> 0% of each run, Pallas kernels for 18% -> 16%
where the time goes in v8:
time: 98.5 us; the launch traced here: 98 us
  starting transfers between devices  55.5 us (56%)
  Pallas kernels  22.8 us (23%)
  waiting for transfers between devices  18 us (18%)
    ppermute x14, starting transfers between devices, chip(): return lax.ppermute(value, 'gy', swap)  41.6 us
    pallas_call x12, Pallas kernels, call(): pl.pallas_call(body, out_shape=outs, grid_spec=pltpu.PrefetchScalarGridSp...  22.8 us
    ppermute x4, waiting for transfers between devices, exchange(): zr = [lax.ppermute(t, 'section', m) for t, m in zip(tiles, z_moves())]  15.4 us
    ppermute x4, starting transfers between devices, exchange(): zr = [lax.ppermute(t, 'section', m) for t, m in zip(tiles, z_moves())]  7.21 us
    ppermute x4, starting transfers between devices, exchange(): xr = lax.ppermute(px, ('gx', 'gy'), pairs_x)  2.68 us
    ppermute x4, starting transfers between devices, exchange(): lax.ppermute(t, ('gx', 'section', 'gy'), corner_pairs(m))  2.61 us
    ppermute x14, waiting for transfers between devices, chip(): return lax.ppermute(value, 'gy', swap)  2.59 us
  transfers between devices with their start and end apart: 28, of which 7 were waited for; matrix products, arithmetic and copies ran while one was open for 0% of the time, Pallas kernels for 16%

profile of v8, /device:TPU:0, one launch (start us, length us, event | category | flops | bytes accessed | tf_op | source)
XLA Modules:
  0.0 98.0 jit_solution(4323015364514506959)
XLA Ops:
  0.6 1.3 %shard_map.87 = f32[5,16,16,256]{3,2,1,0:T(8,128)S(1)} custom-call(f32[32,16,256]{2,1,0:T(8,128)} %refs_0_.6, f32[32,16,256]{2,1,0:T(8,128)} %refs_1_.3, f32[32,16,256]{2,1,0:T(8,128)} %refs_2_.3, f32[32,16,256]{2,1,0:T(8,128)} %refs_3_.4, f32[32,16,256]{2,1,0:T(8,128)} %refs_4_.3), custom_call_target="tpu_custom_call" | custom-call | tf_op jit(solution)/shard_map/pallas_call | solution.py:560
  2.0 0.6 collective-permute-start
  2.5 1.3 %shard_map.86.refs_0_ = f32[5,16,16,256]{3,2,1,0:T(8,128)S(1)} custom-call(f32[32,16,256]{2,1,0:T(8,128)} %refs_0_.6, f32[32,16,256]{2,1,0:T(8,128)} %refs_1_.3, f32[32,16,256]{2,1,0:T(8,128)} %refs_2_.3, f32[32,16,256]{2,1,0:T(8,128)} %refs_3_.4, f32[32,16,256]{2,1,0:T(8,128)} %refs_4_.3), custom_call_target="tpu_custom_call" | custom-call | tf_op jit(solution)/shard_map/pallas_call | solution.py:560
  3.8 1.3 %collective-permute-done.refs_1_ = f32[5,16,16,256]{3,2,1,0:T(8,128)S(1)} collective-permute-done((f32[5,16,16,256]{3,2,1,0:T(8,128)S(1)}, f32[5,16,16,256]{3,2,1,0:T(8,128)S(1)}, u32[]{:S(2)}, u32[]{:S(2)}) %collective-permute-start) | collective-permute-done | bytes 1310752 | tf_op jit(solution)/shard_map/ppermute | solution.py:536
  5.2 0.3 shard_map.88
  5.5 1.7 %shard_map.89 = (f32[20,24,512]{2,1,0:T(8,128)S(1)}, f32[20,24,512]{2,1,0:T(8,128)S(1)}, f32[20,24,512]{2,1,0:T(8,128)S(1)}, f32[20,24,512]{2,1,0:T(8,128)S(1)},...) custom-call(f32[16,16,512]{2,1,0:T(8,128)S(1)} %get-tuple-element.56.refs_0_.refs_4_.refs_6_, ...), custom_call_target="tpu_custom_call" | custom-call | tf_op jit(solution)/shard_map/pallas_call | solution.py:560
  7.2 0.4 collective-permute-start.8
  7.6 2.6 %collective-permute-start.3 = (f32[18,8,512]{2,1,0:T(8,128)S(1)}, f32[18,8,512]{2,1,0:T(8,128)S(1)}, u32[]{:S(2)}, u32[]{:S(2)}) collective-permute-start(f32[18,8,512]{2,1,0:T(8,128)S(1)} %get-tuple-element.54), channel_id=1, source_target_pairs={{0,2},{2,0},{1,3},{3,1},{4,6},{6,4},{5,7},{7,5},{8,10},{10,8},{9,1... | collective-permute-start | bytes 884744 | tf_op jit(solution)/shard_map/ppermute | solution.py:543
  10.2 0.7 collective-permute-start.1
  10.9 3.0 %collective-permute-start.2 = (f32[9,16,512]{2,1,0:T(8,128)S(1)}, f32[9,16,512]{2,1,0:T(8,128)S(1)}, u32[]{:S(2)}, u32[]{:S(2)}) collective-permute-start(f32[9,16,512]{2,1,0:T(8,128)S(1)} %get-tuple-element.53), channel_id=1, source_target_pairs={{0,1},{1,0},{2,3},{3,2},{4,5},{5,4},{6,7},{7,6},{8,9},{9,8},{10,11... | collective-permute-start | bytes 884744 | tf_op jit(solution)/shard_map/ppermute | solution.py:536
  13.9 3.9 %collective-permute-done.3.refs_4_ = f32[18,8,512]{2,1,0:T(8,128)S(1)} collective-permute-done((f32[18,8,512]{2,1,0:T(8,128)S(1)}, f32[18,8,512]{2,1,0:T(8,128)S(1)}, u32[]{:S(2)}, u32[]{:S(2)}) %collective-permute-start.3) | collective-permute-done | bytes 294944 | tf_op jit(solution)/shard_map/ppermute | solution.py:543
  17.8 0.0 collective-permute-start.5
  17.8 0.7 collective-permute-start.4
  18.4 0.0 collective-permute-done.2.refs_3_
  18.5 0.9 collective-permute-done.5.refs_6_
  19.3 2.5 %shard_map.90 = (f32[16,16,512]{2,1,0:T(8,128)S(1)}, f32[18,24,512]{2,1,0:T(8,128)S(1)}, f32[20,24,512]{2,1,0:T(8,128)S(1)}, f32[20,24,512]{2,1,0:T(8,128)S(1)},...) custom-call(f32[16,16,512]{2,1,0:T(8,128)S(1)} %get-tuple-element.50, ...), custom_call_target="tpu_custom_call", output_to_operand_aliasing={{2}: (7, {}), {3}: (8, {}), {4}: (9, {}), {5}: (10, {}), {6... | custom-call | tf_op jit(solution)/shard_map/pallas_call | solution.py:560
  21.8 0.7 collective-permute-start.6
  22.5 8.0 %collective-permute-start.7 = (f32[16,16,512]{2,1,0:T(8,128)S(1)}, f32[16,16,512]{2,1,0:T(8,128)S(1)}, u32[]{:S(2)}, u32[]{:S(2)}) collective-permute-start(f32[16,16,512]{2,1,0:T(8,128)S(1)} %get-tuple-element.64.refs_1_.refs_0_), channel_id=1, source_target_pairs={{0,1},{1,0},{2,3},{3,2},{4,5},{5,4},{6,7},{7,6},{8,9},{9,8},{10,11... | collective-permute-start | bytes 1572872 | tf_op jit(solution)/shard_map/ppermute | solution.py:536
  30.5 1.5 %collective-permute-start.9 = (f32[4,8,512]{2,1,0:T(8,128)S(1)}, f32[4,8,512]{2,1,0:T(8,128)S(1)}, u32[]{:S(2)}, u32[]{:S(2)}) collective-permute-start(f32[4,8,512]{2,1,0:T(8,128)S(1)} %get-tuple-element.73), channel_id=1, source_target_pairs={{0,2},{2,0},{1,3},{3,1},{4,6},{6,4},{5,7},{7,5},{8,10},{10,8},{9,1... | collective-permute-start | bytes 196616 | tf_op jit(solution)/shard_map/ppermute | solution.py:543
  32.0 2.8 %collective-permute-done.9.refs_10_ = f32[4,8,512]{2,1,0:T(8,128)S(1)} collective-permute-done((f32[4,8,512]{2,1,0:T(8,128)S(1)}, f32[4,8,512]{2,1,0:T(8,128)S(1)}, u32[]{:S(2)}, u32[]{:S(2)}) %collective-permute-start.9) | collective-permute-done | bytes 65568 | tf_op jit(solution)/shard_map/ppermute | solution.py:543
  34.8 0.7 collective-permute-start.10
  35.5 1.9 %shard_map.91.refs_4_.refs_14_ = f32[16,16,512]{2,1,0:T(8,128)S(1)} custom-call(s32[17]{0:T(128)S(1)} %copy-done, f32[16,16,512]{2,1,0:T(8,128)S(1)} %get-tuple-element.64.refs_1_.refs_0_, f32[16,16,512]{2,1,0:T(8,128)S(1)} %collective-permute-done.6.refs_2_, f32[16,16,512]{2,1,0:T(8,128)S(1)} %collective-permute-done.7.refs_3_, ...), custom_call_target="tpu_custom_call" | custom-call | tf_op jit(solution)/shard_map/pallas_call | solution.py:560
  37.4 1.9 %shard_map.92 = (f32[16,16,512]{2,1,0:T(8,128)S(1)}, f32[5,16,512]{2,1,0:T(8,128)S(1)}, f32[5,16,512]{2,1,0:T(8,128)S(1)}, f32[18,24,512]{2,1,0:T(8,128)S(1)}, f...) custom-call(f32[16,16,512]{2,1,0:T(8,128)S(1)} %get-tuple-element.64.refs_1_.refs_0_, ...), custom_call_target="tpu_custom_call" | custom-call | tf_op jit(solution)/shard_map/pallas_call | solution.py:560
  39.3 1.6 %collective-permute-start.14 = (f32[12,8,512]{2,1,0:T(8,128)S(1)}, f32[12,8,512]{2,1,0:T(8,128)S(1)}, u32[]{:S(2)}, u32[]{:S(2)}) collective-permute-start(f32[12,8,512]{2,1,0:T(8,128)S(1)} %get-tuple-element.79), channel_id=1, source_target_pairs={{0,2},{2,0},{1,3},{3,1},{4,6},{6,4},{5,7},{7,5},{8,10},{10,8},{9,1... | collective-permute-start | bytes 589832 | tf_op jit(solution)/shard_map/ppermute | solution.py:543
  40.9 4.2 %collective-permute-done.14.refs_9_.refs_15_ = f32[12,8,512]{2,1,0:T(8,128)S(1)} collective-permute-done((f32[12,8,512]{2,1,0:T(8,128)S(1)}, f32[12,8,512]{2,1,0:T(8,128)S(1)}, u32[]{:S(2)}, u32[]{:S(2)}) %collective-permute-start.14) | collective-permute-done | bytes 196640 | tf_op jit(solution)/shard_map/ppermute | solution.py:543
  45.0 2.7 %collective-permute-start.16 = (f32[12,8,512]{2,1,0:T(8,128)S(1)}, f32[12,8,512]{2,1,0:T(8,128)S(1)}, u32[]{:S(2)}, u32[]{:S(2)}) collective-permute-start(f32[12,8,512]{2,1,0:T(8,128)S(1)} %collective-permute-done.14.refs_9_.refs_15_), channel_id=1, source_target_pairs={{0,1},{1,0},{2,3},{3,2},{4,5},{5,4},{6,7},{7,6},{8,9},{9,8},{10,11... | collective-permute-start | bytes 589832 | tf_op jit(solution)/shard_map/ppermute | solution.py:536
  47.7 0.7 collective-permute-start.12
  48.4 5.3 %collective-permute-start.13 = (f32[5,16,512]{2,1,0:T(8,128)S(1)}, f32[5,16,512]{2,1,0:T(8,128)S(1)}, u32[]{:S(2)}, u32[]{:S(2)}) collective-permute-start(f32[5,16,512]{2,1,0:T(8,128)S(1)} %get-tuple-element.78), channel_id=1, source_target_pairs={{0,1},{1,0},{2,3},{3,2},{4,5},{5,4},{6,7},{7,6},{8,9},{9,8},{10,11... | collective-permute-start | bytes 491528 | tf_op jit(solution)/shard_map/ppermute | solution.py:536
  53.6 0.7 collective-permute-start.15
  54.3 0.7 collective-permute-start.18
  55.0 5.2 %collective-permute-start.19 = (f32[16,16,512]{2,1,0:T(8,128)S(1)}, f32[16,16,512]{2,1,0:T(8,128)S(1)}, u32[]{:S(2)}, u32[]{:S(2)}) collective-permute-start(f32[16,16,512]{2,1,0:T(8,128)S(1)} %get-tuple-element.75.refs_0_.refs_1_), channel_id=1, source_target_pairs={{0,1},{1,0},{2,3},{3,2},{4,5},{5,4},{6,7},{7,6},{8,9},{9,8},{10,11... | collective-permute-start | bytes 1572872 | tf_op jit(solution)/shard_map/ppermute | solution.py:536
  60.2 1.8 %shard_map.93 = (f32[16,16,512]{2,1,0:T(8,128)S(1)}, f32[16,16,256]{2,1,0:T(8,128)S(1)}, f32[16,16,256]{2,1,0:T(8,128)S(1)}) custom-call(f32[16,16,512]{2,1,0:T(8,128)S(1)} %get-tuple-element.75.refs_0_.refs_1_, f32[18,24,512]{2,1,0:T(8,128)S(1)} %get-tuple-element.76.refs_1_, f32[5,16,512]{2,1,0:T(8,128)S(1)} %collective-permute-done.12.refs_2_.refs_4_, ...), custom_call_target="tpu_custom_call" | custom-call | tf_op jit(solution)/shard_map/pallas_call | solution.py:560
  62.1 0.7 collective-permute-start.20
  62.8 3.0 %collective-permute-start.21 = (f32[16,16,512]{2,1,0:T(8,128)S(1)}, f32[16,16,512]{2,1,0:T(8,128)S(1)}, u32[]{:S(2)}, u32[]{:S(2)}) collective-permute-start(f32[16,16,512]{2,1,0:T(8,128)S(1)} %get-tuple-element.86.refs_1_), channel_id=1, source_target_pairs={{0,1},{1,0},{2,3},{3,2},{4,5},{5,4},{6,7},{7,6},{8,9},{9,8},{10,11... | collective-permute-start | bytes 1572872 | tf_op jit(solution)/shard_map/ppermute | solution.py:536
  65.8 4.0 %shard_map.95 = (f32[16,16,512]{2,1,0:T(8,128)S(1)}, f32[16,16,512]{2,1,0:T(8,128)S(1)}, f32[20,24,512]{2,1,0:T(8,128)S(1)}, f32[6,16,512]{2,1,0:T(8,128)S(1)}, ...) custom-call(s32[17]{0:T(128)S(1)} %copy-done, ...), custom_call_target="tpu_custom_call" | custom-call | tf_op jit(solution)/shard_map/pallas_call | solution.py:560
  69.8 2.0 %shard_map.96 = (f32[16,16,512]{2,1,0:T(8,128)S(1)}, f32[6,16,512]{2,1,0:T(8,128)S(1)}, f32[6,16,512]{2,1,0:T(8,128)S(1)}, f32[14,8,512]{2,1,0:T(8,128)S(1)}, f32[3,8,512]{2,1,0:T(8,128)S(1)}) custom-call(s32[17]{0:T(128)S(1)} %copy-done, ...), custom_call_target="tpu_custom_call", output_to_operand_aliasing={{1}: (7, {}), {2}: (8, {}), {3}: (9, {}), {4}: (10, {})} | custom-call | tf_op jit(solution)/shard_map/pallas_call | solution.py:560
  71.8 1.6 %collective-permute-start.24 = (f32[14,8,512]{2,1,0:T(8,128)S(1)}, f32[14,8,512]{2,1,0:T(8,128)S(1)}, u32[]{:S(2)}, u32[]{:S(2)}) collective-permute-start(f32[14,8,512]{2,1,0:T(8,128)S(1)} %get-tuple-element.94), channel_id=1, source_target_pairs={{0,2},{2,0},{1,3},{3,1},{4,6},{6,4},{5,7},{7,5},{8,10},{10,8},{9,1... | collective-permute-start | bytes 688136 | tf_op jit(solution)/shard_map/ppermute | solution.py:543
  73.4 4.5 %collective-permute-done.24.refs_11_ = f32[14,8,512]{2,1,0:T(8,128)S(1)} collective-permute-done((f32[14,8,512]{2,1,0:T(8,128)S(1)}, f32[14,8,512]{2,1,0:T(8,128)S(1)}, u32[]{:S(2)}, u32[]{:S(2)}) %collective-permute-start.24) | collective-permute-done | bytes 229408 | tf_op jit(solution)/shard_map/ppermute | solution.py:543
  77.9 3.2 %collective-permute-start.26 = (f32[14,8,512]{2,1,0:T(8,128)S(1)}, f32[14,8,512]{2,1,0:T(8,128)S(1)}, u32[]{:S(2)}, u32[]{:S(2)}) collective-permute-start(f32[14,8,512]{2,1,0:T(8,128)S(1)} %collective-permute-done.24.refs_11_), channel_id=1, source_target_pairs={{0,1},{1,0},{2,3},{3,2},{4,5},{5,4},{6,7},{7,6},{8,9},{9,8},{10,11... | collective-permute-start | bytes 688136 | tf_op jit(solution)/shard_map/ppermute | solution.py:536
  81.1 0.7 collective-permute-start.22
  81.8 4.5 %collective-permute-start.23 = (f32[6,16,512]{2,1,0:T(8,128)S(1)}, f32[6,16,512]{2,1,0:T(8,128)S(1)}, u32[]{:S(2)}, u32[]{:S(2)}) collective-permute-start(f32[6,16,512]{2,1,0:T(8,128)S(1)} %get-tuple-element.93), channel_id=1, source_target_pairs={{0,1},{1,0},{2,3},{3,2},{4,5},{5,4},{6,7},{7,6},{8,9},{9,8},{10,11... | collective-permute-start | bytes 589832 | tf_op jit(solution)/shard_map/ppermute | solution.py:536
  86.3 0.7 collective-permute-start.25
  87.0 3.0 %collective-permute-start.17 = (f32[16,16,256]{2,1,0:T(8,128)S(1)}, f32[16,16,256]{2,1,0:T(8,128)S(1)}, u32[]{:S(2)}, u32[]{:S(2)}) collective-permute-start(f32[16,16,256]{2,1,0:T(8,128)S(1)} %get-tuple-element.82), channel_id=1, source_target_pairs={{0,1},{1,0},{2,3},{3,2},{4,5},{5,4},{6,7},{7,6},{8,9},{9,8},{10,11... | collective-permute-start | bytes 786440 | tf_op jit(solution)/shard_map/ppermute | solution.py:536
  90.0 3.3 %shard_map.97 = (f32[16,16,256]{2,1,0:T(8,128)S(1)}, f32[16,16,256]{2,1,0:T(8,128)S(1)}) custom-call(f32[16,16,512]{2,1,0:T(8,128)S(1)} %get-tuple-element.83.refs_0_, f32[20,24,512]{2,1,0:T(8,128)S(1)} %get-tuple-element.84.refs_1_, f32[16,16,512]{2,1,0:T(8,128)S(1)} %get-tuple-element.85.refs_2_, f32[16,16,512]{2,1,0:T(8,128)S(1)} %get-tuple-element.91.refs_3_, ...), custom_call_target="tpu_custom_call" | custom-call | tf_op jit(solution)/shard_map/pallas_call | solution.py:560
  93.3 2.7 %collective-permute-start.27 = (f32[16,16,256]{2,1,0:T(8,128)S(1)}, f32[16,16,256]{2,1,0:T(8,128)S(1)}, u32[]{:S(2)}, u32[]{:S(2)}) collective-permute-start(f32[16,16,256]{2,1,0:T(8,128)S(1)} %get-tuple-element.97), channel_id=1, source_target_pairs={{0,1},{1,0},{2,3},{3,2},{4,5},{5,4},{6,7},{7,6},{8,9},{9,8},{10,11... | collective-permute-start | bytes 786440 | tf_op jit(solution)/shard_map/ppermute | solution.py:536
  96.0 0.8 shard_map.94
  96.8 0.3 collective-permute-done.27
  97.2 0.8 pad_maximum_fusion
  (24 shorter events, 0.1 us)
Async XLA Ops:
  2.0 3.2 %collective-permute-start = (f32[5,16,16,256]{3,2,1,0:T(8,128)S(1)}, f32[5,16,16,256]{3,2,1,0:T(8,128)S(1)}, u32[]{:S(2)}, u32[]{:S(2)}) collective-permute-start(f32[5,16,16,256]{3,2,1,0:T(8,128)S(1)} %shard_map.87), channel_id=1, source_target_pairs={{0,1},{1,0},{2,3},{3,2},{4,5},{5,4},{6,7},{7,6},{8,9},{9,8},{10,11... | collective-permute-start | bytes 3932168 | tf_op jit(solution)/shard_map/ppermute | solution.py:536
  7.2 28.3 %collective-permute-start.8 = (f32[17,16,16,256]{3,2,1,0:T(8,128)S(1)}, f32[17,16,16,256]{3,2,1,0:T(8,128)S(1)}, u32[]{:S(2)}, u32[]{:S(2)}) collective-permute-start(f32[17,16,16,256]{3,2,1,0:T(8,128)S(1)} %get-tuple-element.67), channel_id=1, source_target_pairs={{0,1},{1,0},{2,3},{3,2},{4,5},{5,4},{6,7},{7,6},{8,9},{9,8},{10,11... | collective-permute-start | bytes 13369352 | tf_op jit(solution)/shard_map/ppermute | solution.py:536
  7.6 10.2 %collective-permute-start.3 = (f32[18,8,512]{2,1,0:T(8,128)S(1)}, f32[18,8,512]{2,1,0:T(8,128)S(1)}, u32[]{:S(2)}, u32[]{:S(2)}) collective-permute-start(f32[18,8,512]{2,1,0:T(8,128)S(1)} %get-tuple-element.54), channel_id=1, source_target_pairs={{0,2},{2,0},{1,3},{3,1},{4,6},{6,4},{5,7},{7,5},{8,10},{10,8},{9,1... | collective-permute-start | bytes 884744 | tf_op jit(solution)/shard_map/ppermute | solution.py:543
  10.2 8.2 %collective-permute-start.1 = (f32[9,16,512]{2,1,0:T(8,128)S(1)}, f32[9,16,512]{2,1,0:T(8,128)S(1)}, u32[]{:S(2)}, u32[]{:S(2)}) collective-permute-start(f32[9,16,512]{2,1,0:T(8,128)S(1)} %get-tuple-element.52), channel_id=1, source_target_pairs={{1,4},{4,1},{5,8},{8,5},{9,12},{12,9},{3,6},{6,3},{7,10},{10,7},{1... | collective-permute-start | bytes 884744 | tf_op jit(solution)/shard_map/ppermute | solution.py:539
  10.9 7.6 %collective-permute-start.2 = (f32[9,16,512]{2,1,0:T(8,128)S(1)}, f32[9,16,512]{2,1,0:T(8,128)S(1)}, u32[]{:S(2)}, u32[]{:S(2)}) collective-permute-start(f32[9,16,512]{2,1,0:T(8,128)S(1)} %get-tuple-element.53), channel_id=1, source_target_pairs={{0,1},{1,0},{2,3},{3,2},{4,5},{5,4},{6,7},{7,6},{8,9},{9,8},{10,11... | collective-permute-start | bytes 884744 | tf_op jit(solution)/shard_map/ppermute | solution.py:536
  17.8 1.6 %collective-permute-start.5 = (f32[18,8,512]{2,1,0:T(8,128)S(1)}, f32[18,8,512]{2,1,0:T(8,128)S(1)}, u32[]{:S(2)}, u32[]{:S(2)}) collective-permute-start(f32[18,8,512]{2,1,0:T(8,128)S(1)} %collective-permute-done.3.refs_4_), channel_id=1, source_target_pairs={{0,1},{1,0},{2,3},{3,2},{4,5},{5,4},{6,7},{7,6},{8,9},{9,8},{10,11... | collective-permute-start | bytes 884744 | tf_op jit(solution)/shard_map/ppermute | solution.py:536
  17.8 0.7 collective-permute-start.4
  19.3 16.1 %copy-start = (s32[17]{0:T(128)S(1)}, s32[17]{0:T(128)}, u32[]{:S(2)}) copy-start(s32[17]{0:T(128)} %refs_0_.9) | copy-start | bytes 208
  21.8 13.6 %collective-permute-start.6 = (f32[16,16,512]{2,1,0:T(8,128)S(1)}, f32[16,16,512]{2,1,0:T(8,128)S(1)}, u32[]{:S(2)}, u32[]{:S(2)}) collective-permute-start(f32[16,16,512]{2,1,0:T(8,128)S(1)} %get-tuple-element.64.refs_1_.refs_0_), channel_id=1, source_target_pairs={{1,4},{4,1},{5,8},{8,5},{9,12},{12,9},{3,6},{6,3},{7,10},{10,7},{1... | collective-permute-start | bytes 1572872 | tf_op jit(solution)/shard_map/ppermute | solution.py:539
  22.5 12.9 %collective-permute-start.7 = (f32[16,16,512]{2,1,0:T(8,128)S(1)}, f32[16,16,512]{2,1,0:T(8,128)S(1)}, u32[]{:S(2)}, u32[]{:S(2)}) collective-permute-start(f32[16,16,512]{2,1,0:T(8,128)S(1)} %get-tuple-element.64.refs_1_.refs_0_), channel_id=1, source_target_pairs={{0,1},{1,0},{2,3},{3,2},{4,5},{5,4},{6,7},{7,6},{8,9},{9,8},{10,11... | collective-permute-start | bytes 1572872 | tf_op jit(solution)/shard_map/ppermute | solution.py:536
  30.5 4.3 %collective-permute-start.9 = (f32[4,8,512]{2,1,0:T(8,128)S(1)}, f32[4,8,512]{2,1,0:T(8,128)S(1)}, u32[]{:S(2)}, u32[]{:S(2)}) collective-permute-start(f32[4,8,512]{2,1,0:T(8,128)S(1)} %get-tuple-element.73), channel_id=1, source_target_pairs={{0,2},{2,0},{1,3},{3,1},{4,6},{6,4},{5,7},{7,5},{8,10},{10,8},{9,1... | collective-permute-start | bytes 196616 | tf_op jit(solution)/shard_map/ppermute | solution.py:543
  34.8 2.6 %collective-permute-start.11 = (f32[4,8,512]{2,1,0:T(8,128)S(1)}, f32[4,8,512]{2,1,0:T(8,128)S(1)}, u32[]{:S(2)}, u32[]{:S(2)}) collective-permute-start(f32[4,8,512]{2,1,0:T(8,128)S(1)} %collective-permute-done.9.refs_10_), channel_id=1, source_target_pairs={{0,1},{1,0},{2,3},{3,2},{4,5},{5,4},{6,7},{7,6},{8,9},{9,8},{10,11... | collective-permute-start | bytes 196616 | tf_op jit(solution)/shard_map/ppermute | solution.py:536
  34.8 2.6 %collective-permute-start.10 = (f32[1,8,512]{2,1,0:T(8,128)S(1)}, f32[1,8,512]{2,1,0:T(8,128)S(1)}, u32[]{:S(2)}, u32[]{:S(2)}) collective-permute-start(f32[1,8,512]{2,1,0:T(8,128)S(1)} %get-tuple-element.74), channel_id=1, source_target_pairs={{1,6},{3,4},{4,3},{6,1},{5,10},{7,8},{8,7},{10,5},{9,14},{11,12},{... | collective-permute-start | bytes 49160 | tf_op jit(solution)/shard_map/ppermute | solution.py:541
  39.3 5.7 %collective-permute-start.14 = (f32[12,8,512]{2,1,0:T(8,128)S(1)}, f32[12,8,512]{2,1,0:T(8,128)S(1)}, u32[]{:S(2)}, u32[]{:S(2)}) collective-permute-start(f32[12,8,512]{2,1,0:T(8,128)S(1)} %get-tuple-element.79), channel_id=1, source_target_pairs={{0,2},{2,0},{1,3},{3,1},{4,6},{6,4},{5,7},{7,5},{8,10},{10,8},{9,1... | collective-permute-start | bytes 589832 | tf_op jit(solution)/shard_map/ppermute | solution.py:543
  45.0 15.2 %collective-permute-start.16 = (f32[12,8,512]{2,1,0:T(8,128)S(1)}, f32[12,8,512]{2,1,0:T(8,128)S(1)}, u32[]{:S(2)}, u32[]{:S(2)}) collective-permute-start(f32[12,8,512]{2,1,0:T(8,128)S(1)} %collective-permute-done.14.refs_9_.refs_15_), channel_id=1, source_target_pairs={{0,1},{1,0},{2,3},{3,2},{4,5},{5,4},{6,7},{7,6},{8,9},{9,8},{10,11... | collective-permute-start | bytes 589832 | tf_op jit(solution)/shard_map/ppermute | solution.py:536
  47.7 12.5 %collective-permute-start.12 = (f32[5,16,512]{2,1,0:T(8,128)S(1)}, f32[5,16,512]{2,1,0:T(8,128)S(1)}, u32[]{:S(2)}, u32[]{:S(2)}) collective-permute-start(f32[5,16,512]{2,1,0:T(8,128)S(1)} %get-tuple-element.77), channel_id=1, source_target_pairs={{1,4},{4,1},{5,8},{8,5},{9,12},{12,9},{3,6},{6,3},{7,10},{10,7},{1... | collective-permute-start | bytes 491528 | tf_op jit(solution)/shard_map/ppermute | solution.py:539
  48.4 11.9 %collective-permute-start.13 = (f32[5,16,512]{2,1,0:T(8,128)S(1)}, f32[5,16,512]{2,1,0:T(8,128)S(1)}, u32[]{:S(2)}, u32[]{:S(2)}) collective-permute-start(f32[5,16,512]{2,1,0:T(8,128)S(1)} %get-tuple-element.78), channel_id=1, source_target_pairs={{0,1},{1,0},{2,3},{3,2},{4,5},{5,4},{6,7},{7,6},{8,9},{9,8},{10,11... | collective-permute-start | bytes 491528 | tf_op jit(solution)/shard_map/ppermute | solution.py:536
  53.6 1.4 %collective-permute-start.15 = (f32[3,8,512]{2,1,0:T(8,128)S(1)}, f32[3,8,512]{2,1,0:T(8,128)S(1)}, u32[]{:S(2)}, u32[]{:S(2)}) collective-permute-start(f32[3,8,512]{2,1,0:T(8,128)S(1)} %get-tuple-element.80), channel_id=1, source_target_pairs={{1,6},{3,4},{4,3},{6,1},{5,10},{7,8},{8,7},{10,5},{9,14},{11,12},{... | collective-permute-start | bytes 147464 | tf_op jit(solution)/shard_map/ppermute | solution.py:541
  54.3 11.5 %collective-permute-start.18 = (f32[16,16,512]{2,1,0:T(8,128)S(1)}, f32[16,16,512]{2,1,0:T(8,128)S(1)}, u32[]{:S(2)}, u32[]{:S(2)}) collective-permute-start(f32[16,16,512]{2,1,0:T(8,128)S(1)} %get-tuple-element.75.refs_0_.refs_1_), channel_id=1, source_target_pairs={{1,4},{4,1},{5,8},{8,5},{9,12},{12,9},{3,6},{6,3},{7,10},{10,7},{1... | collective-permute-start | bytes 1572872 | tf_op jit(solution)/shard_map/ppermute | solution.py:652
  55.0 10.8 %collective-permute-start.19 = (f32[16,16,512]{2,1,0:T(8,128)S(1)}, f32[16,16,512]{2,1,0:T(8,128)S(1)}, u32[]{:S(2)}, u32[]{:S(2)}) collective-permute-start(f32[16,16,512]{2,1,0:T(8,128)S(1)} %get-tuple-element.75.refs_0_.refs_1_), channel_id=1, source_target_pairs={{0,1},{1,0},{2,3},{3,2},{4,5},{5,4},{6,7},{7,6},{8,9},{9,8},{10,11... | collective-permute-start | bytes 1572872 | tf_op jit(solution)/shard_map/ppermute | solution.py:536
  62.1 7.7 %collective-permute-start.20 = (f32[16,16,512]{2,1,0:T(8,128)S(1)}, f32[16,16,512]{2,1,0:T(8,128)S(1)}, u32[]{:S(2)}, u32[]{:S(2)}) collective-permute-start(f32[16,16,512]{2,1,0:T(8,128)S(1)} %get-tuple-element.86.refs_1_), channel_id=1, source_target_pairs={{1,4},{4,1},{5,8},{8,5},{9,12},{12,9},{3,6},{6,3},{7,10},{10,7},{1... | collective-permute-start | bytes 1572872 | tf_op jit(solution)/shard_map/ppermute | solution.py:657
  62.8 7.0 %collective-permute-start.21 = (f32[16,16,512]{2,1,0:T(8,128)S(1)}, f32[16,16,512]{2,1,0:T(8,128)S(1)}, u32[]{:S(2)}, u32[]{:S(2)}) collective-permute-start(f32[16,16,512]{2,1,0:T(8,128)S(1)} %get-tuple-element.86.refs_1_), channel_id=1, source_target_pairs={{0,1},{1,0},{2,3},{3,2},{4,5},{5,4},{6,7},{7,6},{8,9},{9,8},{10,11... | collective-permute-start | bytes 1572872 | tf_op jit(solution)/shard_map/ppermute | solution.py:536
  71.8 6.1 %collective-permute-start.24 = (f32[14,8,512]{2,1,0:T(8,128)S(1)}, f32[14,8,512]{2,1,0:T(8,128)S(1)}, u32[]{:S(2)}, u32[]{:S(2)}) collective-permute-start(f32[14,8,512]{2,1,0:T(8,128)S(1)} %get-tuple-element.94), channel_id=1, source_target_pairs={{0,2},{2,0},{1,3},{3,1},{4,6},{6,4},{5,7},{7,5},{8,10},{10,8},{9,1... | collective-permute-start | bytes 688136 | tf_op jit(solution)/shard_map/ppermute | solution.py:543
  77.9 12.1 %collective-permute-start.26 = (f32[14,8,512]{2,1,0:T(8,128)S(1)}, f32[14,8,512]{2,1,0:T(8,128)S(1)}, u32[]{:S(2)}, u32[]{:S(2)}) collective-permute-start(f32[14,8,512]{2,1,0:T(8,128)S(1)} %collective-permute-done.24.refs_11_), channel_id=1, source_target_pairs={{0,1},{1,0},{2,3},{3,2},{4,5},{5,4},{6,7},{7,6},{8,9},{9,8},{10,11... | collective-permute-start | bytes 688136 | tf_op jit(solution)/shard_map/ppermute | solution.py:536
  81.1 8.8 %collective-permute-start.22 = (f32[6,16,512]{2,1,0:T(8,128)S(1)}, f32[6,16,512]{2,1,0:T(8,128)S(1)}, u32[]{:S(2)}, u32[]{:S(2)}) collective-permute-start(f32[6,16,512]{2,1,0:T(8,128)S(1)} %get-tuple-element.92), channel_id=1, source_target_pairs={{1,4},{4,1},{5,8},{8,5},{9,12},{12,9},{3,6},{6,3},{7,10},{10,7},{1... | collective-permute-start | bytes 589832 | tf_op jit(solution)/shard_map/ppermute | solution.py:539
  81.8 8.2 %collective-permute-start.23 = (f32[6,16,512]{2,1,0:T(8,128)S(1)}, f32[6,16,512]{2,1,0:T(8,128)S(1)}, u32[]{:S(2)}, u32[]{:S(2)}) collective-permute-start(f32[6,16,512]{2,1,0:T(8,128)S(1)} %get-tuple-element.93), channel_id=1, source_target_pairs={{0,1},{1,0},{2,3},{3,2},{4,5},{5,4},{6,7},{7,6},{8,9},{9,8},{10,11... | collective-permute-start | bytes 589832 | tf_op jit(solution)/shard_map/ppermute | solution.py:536
  86.3 3.6 %collective-permute-start.25 = (f32[3,8,512]{2,1,0:T(8,128)S(1)}, f32[3,8,512]{2,1,0:T(8,128)S(1)}, u32[]{:S(2)}, u32[]{:S(2)}) collective-permute-start(f32[3,8,512]{2,1,0:T(8,128)S(1)} %get-tuple-element.95), channel_id=1, source_target_pairs={{1,6},{3,4},{4,3},{6,1},{5,10},{7,8},{8,7},{10,5},{9,14},{11,12},{... | collective-permute-start | bytes 147464 | tf_op jit(solution)/shard_map/ppermute | solution.py:541
  87.0 9.0 %collective-permute-start.17 = (f32[16,16,256]{2,1,0:T(8,128)S(1)}, f32[16,16,256]{2,1,0:T(8,128)S(1)}, u32[]{:S(2)}, u32[]{:S(2)}) collective-permute-start(f32[16,16,256]{2,1,0:T(8,128)S(1)} %get-tuple-element.82), channel_id=1, source_target_pairs={{0,1},{1,0},{2,3},{3,2},{4,5},{5,4},{6,7},{7,6},{8,9},{9,8},{10,11... | collective-permute-start | bytes 786440 | tf_op jit(solution)/shard_map/ppermute | solution.py:536
  93.3 3.9 %collective-permute-start.27 = (f32[16,16,256]{2,1,0:T(8,128)S(1)}, f32[16,16,256]{2,1,0:T(8,128)S(1)}, u32[]{:S(2)}, u32[]{:S(2)}) collective-permute-start(f32[16,16,256]{2,1,0:T(8,128)S(1)} %get-tuple-element.97), channel_id=1, source_target_pairs={{0,1},{1,0},{2,3},{3,2},{4,5},{5,4},{6,7},{7,6},{8,9},{9,8},{10,11... | collective-permute-start | bytes 786440 | tf_op jit(solution)/shard_map/ppermute | solution.py:536

commit v9 on v8

--- a/solution.py
+++ b/solution.py
@@ -211,6 +211,8 @@
 
 
 def make_source(ext, refl, refl_far, offsets, courant, out, g, geo):
+    copy, offsets = offsets
+    copy.wait()
     near = pl.multiple_of(g * geo.H, 128)
     far = pl.multiple_of((1 - g) * geo.H, 128)
 
@@ -550,12 +552,20 @@
 
     def call(kernel, inputs, outs, scratch, smem=1, specs=None, extra=(), aliases=None, out_specs=None):
         if specs is None:
-            specs = [pl.BlockSpec(memory_space=pltpu.SMEM)] * (smem - 1)
+            specs = [pl.BlockSpec(memory_space=pltpu.HBM)] * (smem - 1)
             specs += [pl.BlockSpec(memory_space=pltpu.VMEM)] * (len(inputs) - smem)
+        if smem == 2:
+            extra = (*extra, pltpu.SMEM((NOFF,), jnp.int32), pltpu.SemaphoreType.DMA)
         used = sum(4 * d[0] * d[1] * d[2] for d in scratch)
 
         def body(*refs):
-            kernel(geo, (lax.axis_index("gy"), lax.axis_index("section")), *refs)
+            place = (lax.axis_index("gy"), lax.axis_index("section"))
+            if smem == 1:
+                return kernel(geo, place, *refs)
+            *refs, held, sem = refs
+            copy = pltpu.make_async_copy(refs[0], held, sem)
+            copy.start()
+            kernel(geo, place, (copy, held), *refs[1:])
 
         return pl.pallas_call(
             body,
@@ -579,6 +589,7 @@
     in_hbm = lambda value: pltpu.with_memory_space_constraint(value, pltpu.HBM)
     fields = [in_hbm(f) for f in (wave_now, wave_before, courant, anisotropy, tilt)]
     reflectivity = in_hbm(reflectivity)
+    offsets = in_hbm(offsets)
     hbm = pl.BlockSpec(memory_space=pltpu.HBM)
     whole = pl.BlockSpec(memory_space=pltpu.VMEM)
 

time: 98.5 us -> 97.3 us (0.988)
  Pallas kernels: 22.8 us -> 20.7 us
    pallas_call x12, Pallas kernels: 22.8 us -> 20.7 us  [call(): pl.pallas_call(body, out_shape=outs, grid_spec=pltpu.PrefetchScalarGridSp...]
  transfers between devices with their start and end apart: 28 -> 28, of which waited for: 7 -> 7; matrix products, arithmetic and copies ran while one was open for 0% -> 0% of each run, Pallas kernels for 16% -> 14%
where the time goes in v9:
time: 97.3 us; the launch traced here: 96.9 us
  starting transfers between devices  56.4 us (58%)
  Pallas kernels  20.7 us (21%)
  waiting for transfers between devices  18 us (18%)
    ppermute x14, starting transfers between devices, chip(): return lax.ppermute(value, 'gy', swap)  42.5 us
    pallas_call x12, Pallas kernels, call(): pl.pallas_call(body, out_shape=outs, grid_spec=pltpu.PrefetchScalarGridSp...  20.7 us
    ppermute x4, waiting for transfers between devices, exchange(): zr = [lax.ppermute(t, 'section', m) for t, m in zip(tiles, z_moves())]  15.4 us
    ppermute x4, starting transfers between devices, exchange(): zr = [lax.ppermute(t, 'section', m) for t, m in zip(tiles, z_moves())]  7.21 us
    ppermute x4, starting transfers between devices, exchange(): xr = lax.ppermute(px, ('gx', 'gy'), pairs_x)  2.68 us
    ppermute x4, starting transfers between devices, exchange(): lax.ppermute(t, ('gx', 'section', 'gy'), corner_pairs(m))  2.61 us
    ppermute x14, waiting for transfers between devices, chip(): return lax.ppermute(value, 'gy', swap)  2.59 us
  transfers between devices with their start and end apart: 28, of which 7 were waited for; matrix products, arithmetic and copies ran while one was open for 0% of the time, Pallas kernels for 14%

profile of v9, /device:TPU:0, one launch (start us, length us, event | category | flops | bytes accessed | tf_op | source)
XLA Modules:
  0.0 96.9 jit_solution(14718368073746935644)
XLA Ops:
  0.6 1.3 %shard_map.87 = f32[5,16,16,256]{3,2,1,0:T(8,128)S(1)} custom-call(f32[32,16,256]{2,1,0:T(8,128)} %refs_0_.6, f32[32,16,256]{2,1,0:T(8,128)} %refs_1_.3, f32[32,16,256]{2,1,0:T(8,128)} %refs_2_.3, f32[32,16,256]{2,1,0:T(8,128)} %refs_3_.4, f32[32,16,256]{2,1,0:T(8,128)} %refs_4_.3), custom_call_target="tpu_custom_call" | custom-call | tf_op jit(solution)/shard_map/pallas_call | solution.py:570
  2.0 0.6 collective-permute-start
  2.5 1.3 %shard_map.86.refs_0_ = f32[5,16,16,256]{3,2,1,0:T(8,128)S(1)} custom-call(f32[32,16,256]{2,1,0:T(8,128)} %refs_0_.6, f32[32,16,256]{2,1,0:T(8,128)} %refs_1_.3, f32[32,16,256]{2,1,0:T(8,128)} %refs_2_.3, f32[32,16,256]{2,1,0:T(8,128)} %refs_3_.4, f32[32,16,256]{2,1,0:T(8,128)} %refs_4_.3), custom_call_target="tpu_custom_call" | custom-call | tf_op jit(solution)/shard_map/pallas_call | solution.py:570
  3.8 1.3 %collective-permute-done.refs_1_ = f32[5,16,16,256]{3,2,1,0:T(8,128)S(1)} collective-permute-done((f32[5,16,16,256]{3,2,1,0:T(8,128)S(1)}, f32[5,16,16,256]{3,2,1,0:T(8,128)S(1)}, u32[]{:S(2)}, u32[]{:S(2)}) %collective-permute-start) | collective-permute-done | bytes 1310752 | tf_op jit(solution)/shard_map/ppermute | solution.py:538
  5.2 0.3 shard_map.88
  5.5 1.7 %shard_map.89 = (f32[20,24,512]{2,1,0:T(8,128)S(1)}, f32[20,24,512]{2,1,0:T(8,128)S(1)}, f32[20,24,512]{2,1,0:T(8,128)S(1)}, f32[20,24,512]{2,1,0:T(8,128)S(1)},...) custom-call(f32[16,16,512]{2,1,0:T(8,128)S(1)} %get-tuple-element.56.refs_0_.refs_4_.refs_6_, ...), custom_call_target="tpu_custom_call" | custom-call | tf_op jit(solution)/shard_map/pallas_call | solution.py:570
  7.2 0.4 collective-permute-start.8
  7.6 2.6 %collective-permute-start.3 = (f32[18,8,512]{2,1,0:T(8,128)S(1)}, f32[18,8,512]{2,1,0:T(8,128)S(1)}, u32[]{:S(2)}, u32[]{:S(2)}) collective-permute-start(f32[18,8,512]{2,1,0:T(8,128)S(1)} %get-tuple-element.54), channel_id=1, source_target_pairs={{0,2},{2,0},{1,3},{3,1},{4,6},{6,4},{5,7},{7,5},{8,10},{10,8},{9,1... | collective-permute-start | bytes 884744 | tf_op jit(solution)/shard_map/ppermute | solution.py:545
  10.2 0.7 collective-permute-start.1
  10.9 3.0 %collective-permute-start.2 = (f32[9,16,512]{2,1,0:T(8,128)S(1)}, f32[9,16,512]{2,1,0:T(8,128)S(1)}, u32[]{:S(2)}, u32[]{:S(2)}) collective-permute-start(f32[9,16,512]{2,1,0:T(8,128)S(1)} %get-tuple-element.53), channel_id=1, source_target_pairs={{0,1},{1,0},{2,3},{3,2},{4,5},{5,4},{6,7},{7,6},{8,9},{9,8},{10,11... | collective-permute-start | bytes 884744 | tf_op jit(solution)/shard_map/ppermute | solution.py:538
  13.9 3.9 %collective-permute-done.3.refs_4_ = f32[18,8,512]{2,1,0:T(8,128)S(1)} collective-permute-done((f32[18,8,512]{2,1,0:T(8,128)S(1)}, f32[18,8,512]{2,1,0:T(8,128)S(1)}, u32[]{:S(2)}, u32[]{:S(2)}) %collective-permute-start.3) | collective-permute-done | bytes 294944 | tf_op jit(solution)/shard_map/ppermute | solution.py:545
  17.8 0.0 collective-permute-start.5
  17.8 0.7 collective-permute-start.4
  18.4 0.0 collective-permute-done.2.refs_3_
  18.5 0.9 collective-permute-done.5.refs_6_
  19.3 2.2 %shard_map.90 = (f32[16,16,512]{2,1,0:T(8,128)S(1)}, f32[18,24,512]{2,1,0:T(8,128)S(1)}, f32[20,24,512]{2,1,0:T(8,128)S(1)}, f32[20,24,512]{2,1,0:T(8,128)S(1)},...) custom-call(f32[16,16,512]{2,1,0:T(8,128)S(1)} %get-tuple-element.50, ...), custom_call_target="tpu_custom_call", output_to_operand_aliasing={{2}: (7, {}), {3}: (8, {}), {4}: (9, {}), {5}: (10, {}), {6... | custom-call | tf_op jit(solution)/shard_map/pallas_call | solution.py:570
  21.6 0.7 collective-permute-start.6
  22.3 8.0 %collective-permute-start.7 = (f32[16,16,512]{2,1,0:T(8,128)S(1)}, f32[16,16,512]{2,1,0:T(8,128)S(1)}, u32[]{:S(2)}, u32[]{:S(2)}) collective-permute-start(f32[16,16,512]{2,1,0:T(8,128)S(1)} %get-tuple-element.64.refs_1_.refs_0_), channel_id=1, source_target_pairs={{0,1},{1,0},{2,3},{3,2},{4,5},{5,4},{6,7},{7,6},{8,9},{9,8},{10,11... | collective-permute-start | bytes 1572872 | tf_op jit(solution)/shard_map/ppermute | solution.py:538
  30.2 1.5 %collective-permute-start.9 = (f32[4,8,512]{2,1,0:T(8,128)S(1)}, f32[4,8,512]{2,1,0:T(8,128)S(1)}, u32[]{:S(2)}, u32[]{:S(2)}) collective-permute-start(f32[4,8,512]{2,1,0:T(8,128)S(1)} %get-tuple-element.73), channel_id=1, source_target_pairs={{0,2},{2,0},{1,3},{3,1},{4,6},{6,4},{5,7},{7,5},{8,10},{10,8},{9,1... | collective-permute-start | bytes 196616 | tf_op jit(solution)/shard_map/ppermute | solution.py:545
  31.7 2.8 %collective-permute-done.9.refs_10_ = f32[4,8,512]{2,1,0:T(8,128)S(1)} collective-permute-done((f32[4,8,512]{2,1,0:T(8,128)S(1)}, f32[4,8,512]{2,1,0:T(8,128)S(1)}, u32[]{:S(2)}, u32[]{:S(2)}) %collective-permute-start.9) | collective-permute-done | bytes 65568 | tf_op jit(solution)/shard_map/ppermute | solution.py:545
  34.5 0.7 collective-permute-start.10
  35.2 1.8 %shard_map.91.refs_4_.refs_14_ = f32[16,16,512]{2,1,0:T(8,128)S(1)} custom-call(s32[17]{0:T(128)} %refs_0_.9, f32[16,16,512]{2,1,0:T(8,128)S(1)} %get-tuple-element.64.refs_1_.refs_0_, f32[16,16,512]{2,1,0:T(8,128)S(1)} %collective-permute-done.6.refs_2_, f32[16,16,512]{2,1,0:T(8,128)S(1)} %collective-permute-done.7.refs_3_, ...), custom_call_target="tpu_custom_call" | custom-call | tf_op jit(solution)/shard_map/pallas_call | solution.py:570
  37.0 1.6 %shard_map.92 = (f32[16,16,512]{2,1,0:T(8,128)S(1)}, f32[5,16,512]{2,1,0:T(8,128)S(1)}, f32[5,16,512]{2,1,0:T(8,128)S(1)}, f32[18,24,512]{2,1,0:T(8,128)S(1)}, f...) custom-call(f32[16,16,512]{2,1,0:T(8,128)S(1)} %get-tuple-element.64.refs_1_.refs_0_, ...), custom_call_target="tpu_custom_call" | custom-call | tf_op jit(solution)/shard_map/pallas_call | solution.py:570
  38.6 1.6 %collective-permute-start.14 = (f32[12,8,512]{2,1,0:T(8,128)S(1)}, f32[12,8,512]{2,1,0:T(8,128)S(1)}, u32[]{:S(2)}, u32[]{:S(2)}) collective-permute-start(f32[12,8,512]{2,1,0:T(8,128)S(1)} %get-tuple-element.79), channel_id=1, source_target_pairs={{0,2},{2,0},{1,3},{3,1},{4,6},{6,4},{5,7},{7,5},{8,10},{10,8},{9,1... | collective-permute-start | bytes 589832 | tf_op jit(solution)/shard_map/ppermute | solution.py:545
  40.2 4.2 %collective-permute-done.14.refs_9_.refs_15_ = f32[12,8,512]{2,1,0:T(8,128)S(1)} collective-permute-done((f32[12,8,512]{2,1,0:T(8,128)S(1)}, f32[12,8,512]{2,1,0:T(8,128)S(1)}, u32[]{:S(2)}, u32[]{:S(2)}) %collective-permute-start.14) | collective-permute-done | bytes 196640 | tf_op jit(solution)/shard_map/ppermute | solution.py:545
  44.3 2.8 %collective-permute-start.16 = (f32[12,8,512]{2,1,0:T(8,128)S(1)}, f32[12,8,512]{2,1,0:T(8,128)S(1)}, u32[]{:S(2)}, u32[]{:S(2)}) collective-permute-start(f32[12,8,512]{2,1,0:T(8,128)S(1)} %collective-permute-done.14.refs_9_.refs_15_), channel_id=1, source_target_pairs={{0,1},{1,0},{2,3},{3,2},{4,5},{5,4},{6,7},{7,6},{8,9},{9,8},{10,11... | collective-permute-start | bytes 589832 | tf_op jit(solution)/shard_map/ppermute | solution.py:538
  47.1 0.7 collective-permute-start.12
  47.8 5.3 %collective-permute-start.13 = (f32[5,16,512]{2,1,0:T(8,128)S(1)}, f32[5,16,512]{2,1,0:T(8,128)S(1)}, u32[]{:S(2)}, u32[]{:S(2)}) collective-permute-start(f32[5,16,512]{2,1,0:T(8,128)S(1)} %get-tuple-element.78), channel_id=1, source_target_pairs={{0,1},{1,0},{2,3},{3,2},{4,5},{5,4},{6,7},{7,6},{8,9},{9,8},{10,11... | collective-permute-start | bytes 491528 | tf_op jit(solution)/shard_map/ppermute | solution.py:538
  53.1 0.7 collective-permute-start.15
  53.7 0.7 collective-permute-start.18
  54.4 5.2 %collective-permute-start.19 = (f32[16,16,512]{2,1,0:T(8,128)S(1)}, f32[16,16,512]{2,1,0:T(8,128)S(1)}, u32[]{:S(2)}, u32[]{:S(2)}) collective-permute-start(f32[16,16,512]{2,1,0:T(8,128)S(1)} %get-tuple-element.75.refs_0_.refs_1_), channel_id=1, source_target_pairs={{0,1},{1,0},{2,3},{3,2},{4,5},{5,4},{6,7},{7,6},{8,9},{9,8},{10,11... | collective-permute-start | bytes 1572872 | tf_op jit(solution)/shard_map/ppermute | solution.py:538
  59.7 1.6 %shard_map.93 = (f32[16,16,512]{2,1,0:T(8,128)S(1)}, f32[16,16,256]{2,1,0:T(8,128)S(1)}, f32[16,16,256]{2,1,0:T(8,128)S(1)}) custom-call(f32[16,16,512]{2,1,0:T(8,128)S(1)} %get-tuple-element.75.refs_0_.refs_1_, f32[18,24,512]{2,1,0:T(8,128)S(1)} %get-tuple-element.76.refs_1_, f32[5,16,512]{2,1,0:T(8,128)S(1)} %collective-permute-done.12.refs_2_.refs_4_, ...), custom_call_target="tpu_custom_call" | custom-call | tf_op jit(solution)/shard_map/pallas_call | solution.py:570
  61.2 0.7 collective-permute-start.20
  61.9 3.0 %collective-permute-start.21 = (f32[16,16,512]{2,1,0:T(8,128)S(1)}, f32[16,16,512]{2,1,0:T(8,128)S(1)}, u32[]{:S(2)}, u32[]{:S(2)}) collective-permute-start(f32[16,16,512]{2,1,0:T(8,128)S(1)} %get-tuple-element.86.refs_1_), channel_id=1, source_target_pairs={{0,1},{1,0},{2,3},{3,2},{4,5},{5,4},{6,7},{7,6},{8,9},{9,8},{10,11... | collective-permute-start | bytes 1572872 | tf_op jit(solution)/shard_map/ppermute | solution.py:538
  65.0 3.5 %shard_map.95 = (f32[16,16,512]{2,1,0:T(8,128)S(1)}, f32[16,16,512]{2,1,0:T(8,128)S(1)}, f32[20,24,512]{2,1,0:T(8,128)S(1)}, f32[6,16,512]{2,1,0:T(8,128)S(1)}, ...) custom-call(s32[17]{0:T(128)} %refs_0_.9, ...), custom_call_target="tpu_custom_call" | custom-call | tf_op jit(solution)/shard_map/pallas_call | solution.py:570
  68.5 1.8 %shard_map.96 = (f32[16,16,512]{2,1,0:T(8,128)S(1)}, f32[6,16,512]{2,1,0:T(8,128)S(1)}, f32[6,16,512]{2,1,0:T(8,128)S(1)}, f32[14,8,512]{2,1,0:T(8,128)S(1)}, f32[3,8,512]{2,1,0:T(8,128)S(1)}) custom-call(s32[17]{0:T(128)} %refs_0_.9, ...), custom_call_target="tpu_custom_call", output_to_operand_aliasing={{1}: (7, {}), {2}: (8, {}), {3}: (9, {}), {4}: (10, {})} | custom-call | tf_op jit(solution)/shard_map/pallas_call | solution.py:570
  70.4 1.6 %collective-permute-start.24 = (f32[14,8,512]{2,1,0:T(8,128)S(1)}, f32[14,8,512]{2,1,0:T(8,128)S(1)}, u32[]{:S(2)}, u32[]{:S(2)}) collective-permute-start(f32[14,8,512]{2,1,0:T(8,128)S(1)} %get-tuple-element.94), channel_id=1, source_target_pairs={{0,2},{2,0},{1,3},{3,1},{4,6},{6,4},{5,7},{7,5},{8,10},{10,8},{9,1... | collective-permute-start | bytes 688136 | tf_op jit(solution)/shard_map/ppermute | solution.py:545
  71.9 4.5 %collective-permute-done.24.refs_11_ = f32[14,8,512]{2,1,0:T(8,128)S(1)} collective-permute-done((f32[14,8,512]{2,1,0:T(8,128)S(1)}, f32[14,8,512]{2,1,0:T(8,128)S(1)}, u32[]{:S(2)}, u32[]{:S(2)}) %collective-permute-start.24) | collective-permute-done | bytes 229408 | tf_op jit(solution)/shard_map/ppermute | solution.py:545
  76.5 4.0 %collective-permute-start.26 = (f32[14,8,512]{2,1,0:T(8,128)S(1)}, f32[14,8,512]{2,1,0:T(8,128)S(1)}, u32[]{:S(2)}, u32[]{:S(2)}) collective-permute-start(f32[14,8,512]{2,1,0:T(8,128)S(1)} %collective-permute-done.24.refs_11_), channel_id=1, source_target_pairs={{0,1},{1,0},{2,3},{3,2},{4,5},{5,4},{6,7},{7,6},{8,9},{9,8},{10,11... | collective-permute-start | bytes 688136 | tf_op jit(solution)/shard_map/ppermute | solution.py:538
  80.5 0.7 collective-permute-start.22
  81.2 4.5 %collective-permute-start.23 = (f32[6,16,512]{2,1,0:T(8,128)S(1)}, f32[6,16,512]{2,1,0:T(8,128)S(1)}, u32[]{:S(2)}, u32[]{:S(2)}) collective-permute-start(f32[6,16,512]{2,1,0:T(8,128)S(1)} %get-tuple-element.93), channel_id=1, source_target_pairs={{0,1},{1,0},{2,3},{3,2},{4,5},{5,4},{6,7},{7,6},{8,9},{9,8},{10,11... | collective-permute-start | bytes 589832 | tf_op jit(solution)/shard_map/ppermute | solution.py:538
  85.7 0.7 collective-permute-start.25
  86.3 3.0 %collective-permute-start.17 = (f32[16,16,256]{2,1,0:T(8,128)S(1)}, f32[16,16,256]{2,1,0:T(8,128)S(1)}, u32[]{:S(2)}, u32[]{:S(2)}) collective-permute-start(f32[16,16,256]{2,1,0:T(8,128)S(1)} %get-tuple-element.82), channel_id=1, source_target_pairs={{0,1},{1,0},{2,3},{3,2},{4,5},{5,4},{6,7},{7,6},{8,9},{9,8},{10,11... | collective-permute-start | bytes 786440 | tf_op jit(solution)/shard_map/ppermute | solution.py:538
  89.3 2.8 %shard_map.97 = (f32[16,16,256]{2,1,0:T(8,128)S(1)}, f32[16,16,256]{2,1,0:T(8,128)S(1)}) custom-call(f32[16,16,512]{2,1,0:T(8,128)S(1)} %get-tuple-element.83.refs_0_, f32[20,24,512]{2,1,0:T(8,128)S(1)} %get-tuple-element.84.refs_1_, f32[16,16,512]{2,1,0:T(8,128)S(1)} %get-tuple-element.85.refs_2_, f32[16,16,512]{2,1,0:T(8,128)S(1)} %get-tuple-element.91.refs_3_, ...), custom_call_target="tpu_custom_call" | custom-call | tf_op jit(solution)/shard_map/pallas_call | solution.py:570
  92.1 2.7 %collective-permute-start.27 = (f32[16,16,256]{2,1,0:T(8,128)S(1)}, f32[16,16,256]{2,1,0:T(8,128)S(1)}, u32[]{:S(2)}, u32[]{:S(2)}) collective-permute-start(f32[16,16,256]{2,1,0:T(8,128)S(1)} %get-tuple-element.97), channel_id=1, source_target_pairs={{0,1},{1,0},{2,3},{3,2},{4,5},{5,4},{6,7},{7,6},{8,9},{9,8},{10,11... | collective-permute-start | bytes 786440 | tf_op jit(solution)/shard_map/ppermute | solution.py:538
  94.9 0.8 shard_map.94
  95.7 0.3 collective-permute-done.27
  96.1 0.8 pad_maximum_fusion
  (22 shorter events, 0.1 us)
Async XLA Ops:
  2.0 3.2 %collective-permute-start = (f32[5,16,16,256]{3,2,1,0:T(8,128)S(1)}, f32[5,16,16,256]{3,2,1,0:T(8,128)S(1)}, u32[]{:S(2)}, u32[]{:S(2)}) collective-permute-start(f32[5,16,16,256]{3,2,1,0:T(8,128)S(1)} %shard_map.87), channel_id=1, source_target_pairs={{0,1},{1,0},{2,3},{3,2},{4,5},{5,4},{6,7},{7,6},{8,9},{9,8},{10,11... | collective-permute-start | bytes 3932168 | tf_op jit(solution)/shard_map/ppermute | solution.py:538
  7.2 28.0 %collective-permute-start.8 = (f32[17,16,16,256]{3,2,1,0:T(8,128)S(1)}, f32[17,16,16,256]{3,2,1,0:T(8,128)S(1)}, u32[]{:S(2)}, u32[]{:S(2)}) collective-permute-start(f32[17,16,16,256]{3,2,1,0:T(8,128)S(1)} %get-tuple-element.67), channel_id=1, source_target_pairs={{0,1},{1,0},{2,3},{3,2},{4,5},{5,4},{6,7},{7,6},{8,9},{9,8},{10,11... | collective-permute-start | bytes 13369352 | tf_op jit(solution)/shard_map/ppermute | solution.py:538
  7.6 10.2 %collective-permute-start.3 = (f32[18,8,512]{2,1,0:T(8,128)S(1)}, f32[18,8,512]{2,1,0:T(8,128)S(1)}, u32[]{:S(2)}, u32[]{:S(2)}) collective-permute-start(f32[18,8,512]{2,1,0:T(8,128)S(1)} %get-tuple-element.54), channel_id=1, source_target_pairs={{0,2},{2,0},{1,3},{3,1},{4,6},{6,4},{5,7},{7,5},{8,10},{10,8},{9,1... | collective-permute-start | bytes 884744 | tf_op jit(solution)/shard_map/ppermute | solution.py:545
  10.2 8.2 %collective-permute-start.1 = (f32[9,16,512]{2,1,0:T(8,128)S(1)}, f32[9,16,512]{2,1,0:T(8,128)S(1)}, u32[]{:S(2)}, u32[]{:S(2)}) collective-permute-start(f32[9,16,512]{2,1,0:T(8,128)S(1)} %get-tuple-element.52), channel_id=1, source_target_pairs={{1,4},{4,1},{5,8},{8,5},{9,12},{12,9},{3,6},{6,3},{7,10},{10,7},{1... | collective-permute-start | bytes 884744 | tf_op jit(solution)/shard_map/ppermute | solution.py:541
  10.9 7.6 %collective-permute-start.2 = (f32[9,16,512]{2,1,0:T(8,128)S(1)}, f32[9,16,512]{2,1,0:T(8,128)S(1)}, u32[]{:S(2)}, u32[]{:S(2)}) collective-permute-start(f32[9,16,512]{2,1,0:T(8,128)S(1)} %get-tuple-element.53), channel_id=1, source_target_pairs={{0,1},{1,0},{2,3},{3,2},{4,5},{5,4},{6,7},{7,6},{8,9},{9,8},{10,11... | collective-permute-start | bytes 884744 | tf_op jit(solution)/shard_map/ppermute | solution.py:538
  17.8 1.6 %collective-permute-start.5 = (f32[18,8,512]{2,1,0:T(8,128)S(1)}, f32[18,8,512]{2,1,0:T(8,128)S(1)}, u32[]{:S(2)}, u32[]{:S(2)}) collective-permute-start(f32[18,8,512]{2,1,0:T(8,128)S(1)} %collective-permute-done.3.refs_4_), channel_id=1, source_target_pairs={{0,1},{1,0},{2,3},{3,2},{4,5},{5,4},{6,7},{7,6},{8,9},{9,8},{10,11... | collective-permute-start | bytes 884744 | tf_op jit(solution)/shard_map/ppermute | solution.py:538
  17.8 0.7 collective-permute-start.4
  21.6 13.6 %collective-permute-start.6 = (f32[16,16,512]{2,1,0:T(8,128)S(1)}, f32[16,16,512]{2,1,0:T(8,128)S(1)}, u32[]{:S(2)}, u32[]{:S(2)}) collective-permute-start(f32[16,16,512]{2,1,0:T(8,128)S(1)} %get-tuple-element.64.refs_1_.refs_0_), channel_id=1, source_target_pairs={{1,4},{4,1},{5,8},{8,5},{9,12},{12,9},{3,6},{6,3},{7,10},{10,7},{1... | collective-permute-start | bytes 1572872 | tf_op jit(solution)/shard_map/ppermute | solution.py:541
  22.3 12.9 %collective-permute-start.7 = (f32[16,16,512]{2,1,0:T(8,128)S(1)}, f32[16,16,512]{2,1,0:T(8,128)S(1)}, u32[]{:S(2)}, u32[]{:S(2)}) collective-permute-start(f32[16,16,512]{2,1,0:T(8,128)S(1)} %get-tuple-element.64.refs_1_.refs_0_), channel_id=1, source_target_pairs={{0,1},{1,0},{2,3},{3,2},{4,5},{5,4},{6,7},{7,6},{8,9},{9,8},{10,11... | collective-permute-start | bytes 1572872 | tf_op jit(solution)/shard_map/ppermute | solution.py:538
  30.2 4.3 %collective-permute-start.9 = (f32[4,8,512]{2,1,0:T(8,128)S(1)}, f32[4,8,512]{2,1,0:T(8,128)S(1)}, u32[]{:S(2)}, u32[]{:S(2)}) collective-permute-start(f32[4,8,512]{2,1,0:T(8,128)S(1)} %get-tuple-element.73), channel_id=1, source_target_pairs={{0,2},{2,0},{1,3},{3,1},{4,6},{6,4},{5,7},{7,5},{8,10},{10,8},{9,1... | collective-permute-start | bytes 196616 | tf_op jit(solution)/shard_map/ppermute | solution.py:545
  34.5 2.5 %collective-permute-start.11 = (f32[4,8,512]{2,1,0:T(8,128)S(1)}, f32[4,8,512]{2,1,0:T(8,128)S(1)}, u32[]{:S(2)}, u32[]{:S(2)}) collective-permute-start(f32[4,8,512]{2,1,0:T(8,128)S(1)} %collective-permute-done.9.refs_10_), channel_id=1, source_target_pairs={{0,1},{1,0},{2,3},{3,2},{4,5},{5,4},{6,7},{7,6},{8,9},{9,8},{10,11... | collective-permute-start | bytes 196616 | tf_op jit(solution)/shard_map/ppermute | solution.py:538
  34.5 2.5 %collective-permute-start.10 = (f32[1,8,512]{2,1,0:T(8,128)S(1)}, f32[1,8,512]{2,1,0:T(8,128)S(1)}, u32[]{:S(2)}, u32[]{:S(2)}) collective-permute-start(f32[1,8,512]{2,1,0:T(8,128)S(1)} %get-tuple-element.74), channel_id=1, source_target_pairs={{1,6},{3,4},{4,3},{6,1},{5,10},{7,8},{8,7},{10,5},{9,14},{11,12},{... | collective-permute-start | bytes 49160 | tf_op jit(solution)/shard_map/ppermute | solution.py:543
  38.6 5.7 %collective-permute-start.14 = (f32[12,8,512]{2,1,0:T(8,128)S(1)}, f32[12,8,512]{2,1,0:T(8,128)S(1)}, u32[]{:S(2)}, u32[]{:S(2)}) collective-permute-start(f32[12,8,512]{2,1,0:T(8,128)S(1)} %get-tuple-element.79), channel_id=1, source_target_pairs={{0,2},{2,0},{1,3},{3,1},{4,6},{6,4},{5,7},{7,5},{8,10},{10,8},{9,1... | collective-permute-start | bytes 589832 | tf_op jit(solution)/shard_map/ppermute | solution.py:545
  44.3 15.3 %collective-permute-start.16 = (f32[12,8,512]{2,1,0:T(8,128)S(1)}, f32[12,8,512]{2,1,0:T(8,128)S(1)}, u32[]{:S(2)}, u32[]{:S(2)}) collective-permute-start(f32[12,8,512]{2,1,0:T(8,128)S(1)} %collective-permute-done.14.refs_9_.refs_15_), channel_id=1, source_target_pairs={{0,1},{1,0},{2,3},{3,2},{4,5},{5,4},{6,7},{7,6},{8,9},{9,8},{10,11... | collective-permute-start | bytes 589832 | tf_op jit(solution)/shard_map/ppermute | solution.py:538
  47.1 12.5 %collective-permute-start.12 = (f32[5,16,512]{2,1,0:T(8,128)S(1)}, f32[5,16,512]{2,1,0:T(8,128)S(1)}, u32[]{:S(2)}, u32[]{:S(2)}) collective-permute-start(f32[5,16,512]{2,1,0:T(8,128)S(1)} %get-tuple-element.77), channel_id=1, source_target_pairs={{1,4},{4,1},{5,8},{8,5},{9,12},{12,9},{3,6},{6,3},{7,10},{10,7},{1... | collective-permute-start | bytes 491528 | tf_op jit(solution)/shard_map/ppermute | solution.py:541
  47.8 11.9 %collective-permute-start.13 = (f32[5,16,512]{2,1,0:T(8,128)S(1)}, f32[5,16,512]{2,1,0:T(8,128)S(1)}, u32[]{:S(2)}, u32[]{:S(2)}) collective-permute-start(f32[5,16,512]{2,1,0:T(8,128)S(1)} %get-tuple-element.78), channel_id=1, source_target_pairs={{0,1},{1,0},{2,3},{3,2},{4,5},{5,4},{6,7},{7,6},{8,9},{9,8},{10,11... | collective-permute-start | bytes 491528 | tf_op jit(solution)/shard_map/ppermute | solution.py:538
  53.1 1.4 %collective-permute-start.15 = (f32[3,8,512]{2,1,0:T(8,128)S(1)}, f32[3,8,512]{2,1,0:T(8,128)S(1)}, u32[]{:S(2)}, u32[]{:S(2)}) collective-permute-start(f32[3,8,512]{2,1,0:T(8,128)S(1)} %get-tuple-element.80), channel_id=1, source_target_pairs={{1,6},{3,4},{4,3},{6,1},{5,10},{7,8},{8,7},{10,5},{9,14},{11,12},{... | collective-permute-start | bytes 147464 | tf_op jit(solution)/shard_map/ppermute | solution.py:543
  53.7 11.2 %collective-permute-start.18 = (f32[16,16,512]{2,1,0:T(8,128)S(1)}, f32[16,16,512]{2,1,0:T(8,128)S(1)}, u32[]{:S(2)}, u32[]{:S(2)}) collective-permute-start(f32[16,16,512]{2,1,0:T(8,128)S(1)} %get-tuple-element.75.refs_0_.refs_1_), channel_id=1, source_target_pairs={{1,4},{4,1},{5,8},{8,5},{9,12},{12,9},{3,6},{6,3},{7,10},{10,7},{1... | collective-permute-start | bytes 1572872 | tf_op jit(solution)/shard_map/ppermute | solution.py:663
  54.4 10.5 %collective-permute-start.19 = (f32[16,16,512]{2,1,0:T(8,128)S(1)}, f32[16,16,512]{2,1,0:T(8,128)S(1)}, u32[]{:S(2)}, u32[]{:S(2)}) collective-permute-start(f32[16,16,512]{2,1,0:T(8,128)S(1)} %get-tuple-element.75.refs_0_.refs_1_), channel_id=1, source_target_pairs={{0,1},{1,0},{2,3},{3,2},{4,5},{5,4},{6,7},{7,6},{8,9},{9,8},{10,11... | collective-permute-start | bytes 1572872 | tf_op jit(solution)/shard_map/ppermute | solution.py:538
  61.2 7.3 %collective-permute-start.20 = (f32[16,16,512]{2,1,0:T(8,128)S(1)}, f32[16,16,512]{2,1,0:T(8,128)S(1)}, u32[]{:S(2)}, u32[]{:S(2)}) collective-permute-start(f32[16,16,512]{2,1,0:T(8,128)S(1)} %get-tuple-element.86.refs_1_), channel_id=1, source_target_pairs={{1,4},{4,1},{5,8},{8,5},{9,12},{12,9},{3,6},{6,3},{7,10},{10,7},{1... | collective-permute-start | bytes 1572872 | tf_op jit(solution)/shard_map/ppermute | solution.py:668
  61.9 6.6 %collective-permute-start.21 = (f32[16,16,512]{2,1,0:T(8,128)S(1)}, f32[16,16,512]{2,1,0:T(8,128)S(1)}, u32[]{:S(2)}, u32[]{:S(2)}) collective-permute-start(f32[16,16,512]{2,1,0:T(8,128)S(1)} %get-tuple-element.86.refs_1_), channel_id=1, source_target_pairs={{0,1},{1,0},{2,3},{3,2},{4,5},{5,4},{6,7},{7,6},{8,9},{9,8},{10,11... | collective-permute-start | bytes 1572872 | tf_op jit(solution)/shard_map/ppermute | solution.py:538
  70.4 6.1 %collective-permute-start.24 = (f32[14,8,512]{2,1,0:T(8,128)S(1)}, f32[14,8,512]{2,1,0:T(8,128)S(1)}, u32[]{:S(2)}, u32[]{:S(2)}) collective-permute-start(f32[14,8,512]{2,1,0:T(8,128)S(1)} %get-tuple-element.94), channel_id=1, source_target_pairs={{0,2},{2,0},{1,3},{3,1},{4,6},{6,4},{5,7},{7,5},{8,10},{10,8},{9,1... | collective-permute-start | bytes 688136 | tf_op jit(solution)/shard_map/ppermute | solution.py:545
  76.5 12.9 %collective-permute-start.26 = (f32[14,8,512]{2,1,0:T(8,128)S(1)}, f32[14,8,512]{2,1,0:T(8,128)S(1)}, u32[]{:S(2)}, u32[]{:S(2)}) collective-permute-start(f32[14,8,512]{2,1,0:T(8,128)S(1)} %collective-permute-done.24.refs_11_), channel_id=1, source_target_pairs={{0,1},{1,0},{2,3},{3,2},{4,5},{5,4},{6,7},{7,6},{8,9},{9,8},{10,11... | collective-permute-start | bytes 688136 | tf_op jit(solution)/shard_map/ppermute | solution.py:538
  80.5 8.8 %collective-permute-start.22 = (f32[6,16,512]{2,1,0:T(8,128)S(1)}, f32[6,16,512]{2,1,0:T(8,128)S(1)}, u32[]{:S(2)}, u32[]{:S(2)}) collective-permute-start(f32[6,16,512]{2,1,0:T(8,128)S(1)} %get-tuple-element.92), channel_id=1, source_target_pairs={{1,4},{4,1},{5,8},{8,5},{9,12},{12,9},{3,6},{6,3},{7,10},{10,7},{1... | collective-permute-start | bytes 589832 | tf_op jit(solution)/shard_map/ppermute | solution.py:541
  81.2 8.2 %collective-permute-start.23 = (f32[6,16,512]{2,1,0:T(8,128)S(1)}, f32[6,16,512]{2,1,0:T(8,128)S(1)}, u32[]{:S(2)}, u32[]{:S(2)}) collective-permute-start(f32[6,16,512]{2,1,0:T(8,128)S(1)} %get-tuple-element.93), channel_id=1, source_target_pairs={{0,1},{1,0},{2,3},{3,2},{4,5},{5,4},{6,7},{7,6},{8,9},{9,8},{10,11... | collective-permute-start | bytes 589832 | tf_op jit(solution)/shard_map/ppermute | solution.py:538
  85.7 3.6 %collective-permute-start.25 = (f32[3,8,512]{2,1,0:T(8,128)S(1)}, f32[3,8,512]{2,1,0:T(8,128)S(1)}, u32[]{:S(2)}, u32[]{:S(2)}) collective-permute-start(f32[3,8,512]{2,1,0:T(8,128)S(1)} %get-tuple-element.95), channel_id=1, source_target_pairs={{1,6},{3,4},{4,3},{6,1},{5,10},{7,8},{8,7},{10,5},{9,14},{11,12},{... | collective-permute-start | bytes 147464 | tf_op jit(solution)/shard_map/ppermute | solution.py:543
  86.3 8.5 %collective-permute-start.17 = (f32[16,16,256]{2,1,0:T(8,128)S(1)}, f32[16,16,256]{2,1,0:T(8,128)S(1)}, u32[]{:S(2)}, u32[]{:S(2)}) collective-permute-start(f32[16,16,256]{2,1,0:T(8,128)S(1)} %get-tuple-element.82), channel_id=1, source_target_pairs={{0,1},{1,0},{2,3},{3,2},{4,5},{5,4},{6,7},{7,6},{8,9},{9,8},{10,11... | collective-permute-start | bytes 786440 | tf_op jit(solution)/shard_map/ppermute | solution.py:538
  92.1 3.9 %collective-permute-start.27 = (f32[16,16,256]{2,1,0:T(8,128)S(1)}, f32[16,16,256]{2,1,0:T(8,128)S(1)}, u32[]{:S(2)}, u32[]{:S(2)}) collective-permute-start(f32[16,16,256]{2,1,0:T(8,128)S(1)} %get-tuple-element.97), channel_id=1, source_target_pairs={{0,1},{1,0},{2,3},{3,2},{4,5},{5,4},{6,7},{7,6},{8,9},{9,8},{10,11... | collective-permute-start | bytes 786440 | tf_op jit(solution)/shard_map/ppermute | solution.py:538
